TPU v7x, 128 devices: a whole 4x4x4 slice. The times are simulated.
128 devices in a mesh: img: 4 (over z), depth: 32 (over y, x, core).
Axes of the slice: x: 4, y: 4, z: 4, core: 2. Of those that a mesh axis runs over, the one named last changes fastest.
Arguments:
- volume: bfloat16 [128, 2048, 512], P('depth', 'img'), may hold values from 0 to 1
- transfer_table: bfloat16 [4, 128], replicated, may hold values from 0 to 3
Outputs:
- image: float32 [4, 1048576], P(None, ('img', 'depth'))
All inputs are finite; a program needn't handle non-finite values.
Results may differ from a plain program's by a relative error of at most 0.00044.
Values may be sent and summed in bfloat16 or wider, within the bound.
No kernel may reach another device: no remote copies, remote signals or barrier semaphores. Data moves between devices by JAX's collectives and lax.ppermute only.
A program may use at most 64 MiB of HBM per device.

v0:
```python
import jax
import jax.numpy as jnp
from jax import lax
from jax.sharding import PartitionSpec as P


def padded(cells, sides, width):
    for axis, dim in sides:
        count = lax.axis_size(axis)
        ends = count - 1
        head = lax.slice_in_dim(cells, 0, width, axis=dim)
        tail = lax.slice_in_dim(cells, cells.shape[dim] - width, cells.shape[dim], axis=dim)
        cells = jnp.concatenate(
            [
                lax.ppermute(tail, axis, [(i, (i + 1) % count) for i in range(ends)]),
                cells,
                lax.ppermute(head, axis, [((i + 1) % count, i) for i in range(ends)]),
            ],
            axis=dim,
        )
    return cells


def colorize(center, grad_z, grad_x, grad_y, transfer_table, depth_total):
    lambert = jnp.abs(2.0 / 3.0 * grad_z + 1.0 / 3.0 * grad_x + 2.0 / 3.0 * grad_y)
    shading = 0.3 + 0.7 * lambert / jnp.sqrt(
        grad_z * grad_z + grad_x * grad_x + grad_y * grad_y + 0.01
    )
    entries = transfer_table.shape[1]
    position = center.reshape(-1) * jnp.float32(entries - 1)
    knot_list = jnp.arange(entries, dtype=jnp.float32)
    weights = jnp.maximum(0.0, 1.0 - jnp.abs(position[None, :] - knot_list[:, None])).astype(
        jnp.bfloat16
    )
    values = jnp.dot(transfer_table, weights, preferred_element_type=jnp.float32)
    colour = values[0:3] * shading.reshape(-1)[None, :]
    opacity = 1.0 - jnp.exp(-values[3] / jnp.float32(depth_total))
    return (colour, opacity)


def composite(nearer, farther):
    colour = nearer[0:3] + nearer[3:4] * farther[0:3]
    return jnp.concatenate([colour, nearer[3:4] * farther[3:4]], axis=0)


def shards(volume, transfer_table):
    slabs = volume.shape[0]
    pixels = volume.shape[1] * volume.shape[2]
    depth_count = lax.axis_size("depth")
    depth_total = slabs * depth_count
    ghosted = padded(volume, (("depth", 0), ("img", 1)), 1)

    def advance(state_pair, slab_index):
        accum, transmit = state_pair
        before = lax.dynamic_index_in_dim(ghosted, slab_index, 0, False)[1:-1].astype(jnp.float32)
        middle = lax.dynamic_index_in_dim(ghosted, slab_index + 1, 0, False).astype(jnp.float32)
        middle = jnp.pad(middle, ((0, 0), (1, 1)))
        after = lax.dynamic_index_in_dim(ghosted, slab_index + 2, 0, False)[1:-1].astype(
            jnp.float32
        )
        center = middle[1:-1, 1:-1]
        grad_z = (after - before) * 0.5
        grad_x = (middle[2:, 1:-1] - middle[:-2, 1:-1]) * 0.5
        grad_y = (middle[1:-1, 2:] - middle[1:-1, :-2]) * 0.5
        colour, opacity = colorize(center, grad_z, grad_x, grad_y, transfer_table, depth_total)
        accum = accum + transmit[None, :] * opacity[None, :] * colour
        transmit = transmit * (1.0 - opacity)
        return ((accum, transmit), None)

    start = (jnp.zeros((3, pixels), jnp.float32), jnp.ones((pixels,), jnp.float32))
    (accum, transmit), _ = lax.scan(advance, start, jnp.arange(slabs, dtype=jnp.int32))
    partial_image = jnp.concatenate([accum, transmit[None, :]], axis=0)
    piece_size = pixels // depth_count
    pieces_in = partial_image.reshape(4, depth_count, piece_size)
    received = lax.all_to_all(pieces_in, "depth", split_axis=1, concat_axis=1, tiled=True)
    while received.shape[1] > 1:
        received = composite(received[:, 0::2], received[:, 1::2])
    merged = received[:, 0]
    return jnp.concatenate([merged[0:3], 1.0 - merged[3:4]], axis=0)


def solution(mesh):
    placed = (P("depth", "img", None), P())
    return jax.shard_map(
        shards, mesh=mesh, in_specs=placed, out_specs=P(None, ("img", "depth")), check_vma=False
    )
```

profile of v0, /device:TPU:64, one launch (start us, length us, event | category | flops | bytes accessed | tf_op | source)
XLA Modules:
  0.0 238.2 jit_solution(12438480775967424843)
XLA Ops:
  0.0 1.4 fusion.32
  1.4 1.8 collective-permute-start
  3.2 1.3 collective-permute-start.1
  4.9 3.4 %collective-permute-done.1 = bf16[1,512,512]{2,1,0:T(8,128)(2,1)S(1)} collective-permute-done((bf16[1,512,512]{2,1,0:T(8,128)(2,1)S(1)}, bf16[1,512,512]{2,1,0:T(8,128)(2,1)S(1)}, u32[]{:S(2)}, u32[]{:S(2)}) %collective-permute-start.1) | collective-permute-done | bytes 524320 | tf_op jit(solution)/shard_map/ppermute | solution.py:17
  8.3 1.7 copy-done.5
  10.0 3.5 %collective-permute-start.2 = (bf16[6,1,512]{2,1,0:T(2,128)(2,1)S(1)}, bf16[6,1,512]{2,1,0:T(2,128)(2,1)S(1)}, u32[]{:S(2)}, u32[]{:S(2)}) collective-permute-start(bf16[6,1,512]{2,1,0:T(2,128)(2,1)S(1)} %get-tuple-element.154), channel_id=1, source_target_pairs={{0,32},{32,64},{64,96},{1,33},{33,65},{65,97},{2,34},{34,66},{66,9... | collective-permute-start | bytes 18440 | tf_op jit(solution)/shard_map/ppermute | solution.py:15
  13.6 2.3 collective-permute-start.3
  15.9 3.2 %collective-permute-done.3 = bf16[6,1,512]{2,1,0:T(2,128)(2,1)S(1)} collective-permute-done((bf16[6,1,512]{2,1,0:T(2,128)(2,1)S(1)}, bf16[6,1,512]{2,1,0:T(2,128)(2,1)S(1)}, u32[]{:S(2)}, u32[]{:S(2)}) %collective-permute-start.3) | collective-permute-done | bytes 6176 | tf_op jit(solution)/shard_map/ppermute | solution.py:17
  19.1 2.7 %pad_maximum_fusion.1 = bf16[6,514,512]{2,1,0:T(8,128)(2,1)S(1)} fusion(bf16[6,1,512]{2,1,0:T(2,128)(2,1)S(1)} %collective-permute-done.3, bf16[6,512,512]{2,1,0:T(8,128)(2,1)} %copy-done.5, bf16[6,1,512]{2,1,0:T(2,128)(2,1)S(1)} %collective-permute-done.2), kind=kLoop, calls=%fused_computation.34 | loop fusion | flops 9474048 | bytes 6316032 | tf_op jit(solution)/shard_map/concatenate | solution.py:13
  21.8 139.3 %while.16 = (s32[]{:T(128)}, f32[3,262144]{1,0:T(4,128)}, f32[262144]{0:T(1024)}, s32[4]{0:T(128)S(1)}, bf16[6,514,512]{2,1,0:T(8,128)(2,1)S(1)}, /*index=5*/bf1...) while((s32[]{:T(128)}, f32[3,262144]{1,0:T(4,128)}, ...), condition=%wide.region_1.2_spmd.clone, body=%wide.region_0.1_spmd.clone.sunk | while | flops 447742976 | bytes 70794656 | solution.py:71
  21.8 0.7 dynamic_slice.40
  27.5 1.5 fusion.49
  29.7 19.8 %convolution_bitcast_fusion.2 = f32[4,262144]{1,0:T(4,128)S(1)} fusion(bf16[4,128]{1,0:T(4,128)(2,1)S(1)} %get-tuple-element.250, f32[262144]{0:T(1024)S(1)} %bitcast.78), kind=kOutput, calls=%fused_computation.clone.1 | convolution fusion | flops 436207616 | bytes 5243904 | tf_op jit(solution)/shard_map/while/body/eval_jaxpr/dot_general | solution.py:35
  49.5 1.9 fusion.50
  51.5 0.7 subtract_multiply_fusion.2
  52.1 2.6 %fusion.51 = f32[3,262144]{1,0:T(4,128)S(1)} fusion(f32[4,262144]{1,0:T(4,128)S(1)} %convolution_bitcast_fusion.2, f32[3,262144]{1,0:T(4,128)S(1)} %copy-done, f32[262144]{0:T(1024)S(1)} %bitcast.75, f32[262144]{0:T(1024)S(1)} %get-tuple-element.217, pred[]{:T(512)S(6)} %compare.4), kind=kLoop, calls=%fused_computation.7.clone.1 | loop fusion | flops 3145728 | bytes 11534337 | tf_op jit(solution)/shard_map/while/body/eval_jaxpr/add | solution.py:66
  54.7 1.9 copy-done.1
  56.7 0.6 dynamic_slice.40
  62.3 1.5 fusion.49
  64.5 19.8 %convolution_bitcast_fusion.2 = f32[4,262144]{1,0:T(4,128)S(1)} fusion(bf16[4,128]{1,0:T(4,128)(2,1)S(1)} %get-tuple-element.250, f32[262144]{0:T(1024)S(1)} %bitcast.78), kind=kOutput, calls=%fused_computation.clone.1 | convolution fusion | flops 436207616 | bytes 5243904 | tf_op jit(solution)/shard_map/while/body/eval_jaxpr/dot_general | solution.py:35
  84.4 1.9 fusion.50
  86.3 0.7 subtract_multiply_fusion.2
  87.0 2.6 %fusion.51 = f32[3,262144]{1,0:T(4,128)S(1)} fusion(f32[4,262144]{1,0:T(4,128)S(1)} %convolution_bitcast_fusion.2, f32[3,262144]{1,0:T(4,128)S(1)} %copy-done, f32[262144]{0:T(1024)S(1)} %bitcast.75, f32[262144]{0:T(1024)S(1)} %get-tuple-element.217, pred[]{:T(512)S(6)} %compare.4), kind=kLoop, calls=%fused_computation.7.clone.1 | loop fusion | flops 3145728 | bytes 11534337 | tf_op jit(solution)/shard_map/while/body/eval_jaxpr/add | solution.py:66
  89.5 1.9 copy-done.1
  91.5 0.6 dynamic_slice.40
  97.1 1.5 fusion.49
  99.3 19.8 %convolution_bitcast_fusion.2 = f32[4,262144]{1,0:T(4,128)S(1)} fusion(bf16[4,128]{1,0:T(4,128)(2,1)S(1)} %get-tuple-element.250, f32[262144]{0:T(1024)S(1)} %bitcast.78), kind=kOutput, calls=%fused_computation.clone.1 | convolution fusion | flops 436207616 | bytes 5243904 | tf_op jit(solution)/shard_map/while/body/eval_jaxpr/dot_general | solution.py:35
  119.2 1.9 fusion.50
  121.1 0.7 subtract_multiply_fusion.2
  121.8 2.6 %fusion.51 = f32[3,262144]{1,0:T(4,128)S(1)} fusion(f32[4,262144]{1,0:T(4,128)S(1)} %convolution_bitcast_fusion.2, f32[3,262144]{1,0:T(4,128)S(1)} %copy-done, f32[262144]{0:T(1024)S(1)} %bitcast.75, f32[262144]{0:T(1024)S(1)} %get-tuple-element.217, pred[]{:T(512)S(6)} %compare.4), kind=kLoop, calls=%fused_computation.7.clone.1 | loop fusion | flops 3145728 | bytes 11534337 | tf_op jit(solution)/shard_map/while/body/eval_jaxpr/add | solution.py:66
  124.3 1.9 copy-done.1
  126.3 0.6 dynamic_slice.40
  131.9 1.5 fusion.49
  134.1 19.8 %convolution_bitcast_fusion.2 = f32[4,262144]{1,0:T(4,128)S(1)} fusion(bf16[4,128]{1,0:T(4,128)(2,1)S(1)} %get-tuple-element.250, f32[262144]{0:T(1024)S(1)} %bitcast.78), kind=kOutput, calls=%fused_computation.clone.1 | convolution fusion | flops 436207616 | bytes 5243904 | tf_op jit(solution)/shard_map/while/body/eval_jaxpr/dot_general | solution.py:35
  154.0 1.9 fusion.50
  155.9 0.7 subtract_multiply_fusion.2
  156.6 2.6 %fusion.51 = f32[3,262144]{1,0:T(4,128)S(1)} fusion(f32[4,262144]{1,0:T(4,128)S(1)} %convolution_bitcast_fusion.2, f32[3,262144]{1,0:T(4,128)S(1)} %copy-done, f32[262144]{0:T(1024)S(1)} %bitcast.75, f32[262144]{0:T(1024)S(1)} %get-tuple-element.217, pred[]{:T(512)S(6)} %compare.4), kind=kLoop, calls=%fused_computation.7.clone.1 | loop fusion | flops 3145728 | bytes 11534337 | tf_op jit(solution)/shard_map/while/body/eval_jaxpr/add | solution.py:66
  159.2 1.9 copy-done.1
  161.1 4.4 %pad_maximum_fusion = f32[4,32,8192]{2,0,1:T(4,128)S(1)} fusion(f32[1,32,8192]{2,0,1:T(1,128)} %bitcast.77, f32[3,32,8192]{2,0,1:T(4,128)} %bitcast.74), kind=kLoop, calls=%fused_computation.33 | loop fusion | flops 1048576 | bytes 8388608 | tf_op jit(solution)/shard_map/concatenate | solution.py:72
  165.5 65.1 %all_to_all.5 = f32[4,32,8192]{2,0,1:T(4,128)S(1)} all-to-all(f32[4,32,8192]{2,0,1:T(4,128)S(1)} %pad_maximum_fusion), channel_id=1, replica_groups=mesh['img'=4,'depth'=32] {'depth'}, dimensions={1} | all-to-all | bytes 8388608 | tf_op jit(solution)/shard_map/all_to_all | solution.py:75
  230.6 0.4 fusion.28
  231.0 1.2 fusion.31
  232.5 0.9 fusion.20
  233.4 1.0 pad_maximum_fusion.2
  234.5 0.6 fusion.34
  235.3 0.4 fusion.21
  235.6 0.5 pad_maximum_fusion.3
  237.5 0.7 pad_maximum_fusion.5
  (72 shorter events, 6.2 us)
Async XLA Ops:
  0.0 4.7 %copy-start.4 = (bf16[4,512,512]{2,1,0:T(8,128)(2,1)S(1)}, bf16[4,512,512]{2,1,0:T(8,128)(2,1)}, u32[]{:S(2)}) copy-start(bf16[4,512,512]{2,1,0:T(8,128)(2,1)} %param.4) | copy-start | bytes 6291460
  1.4 3.3 %collective-permute-start = (bf16[1,512,512]{2,1,0:T(8,128)(2,1)S(1)}, bf16[1,512,512]{2,1,0:T(8,128)(2,1)S(1)}, u32[]{:S(2)}, u32[]{:S(2)}) collective-permute-start(bf16[1,512,512]{2,1,0:T(8,128)(2,1)S(1)} %get-tuple-element.161), channel_id=1, source_target_pairs={{0,1},{1,2},{2,3},{3,4},{4,5},{5,6},{6,7},{7,8},{8,9},{9,10},{10,1... | collective-permute-start | bytes 1572872 | tf_op jit(solution)/shard_map/ppermute | solution.py:15
  3.2 5.0 %collective-permute-start.1 = (bf16[1,512,512]{2,1,0:T(8,128)(2,1)S(1)}, bf16[1,512,512]{2,1,0:T(8,128)(2,1)S(1)}, u32[]{:S(2)}, u32[]{:S(2)}) collective-permute-start(bf16[1,512,512]{2,1,0:T(8,128)(2,1)S(1)} %get-tuple-element.160), channel_id=1, source_target_pairs={{1,0},{2,1},{3,2},{4,3},{5,4},{6,5},{7,6},{8,7},{9,8},{10,9},{11,1... | collective-permute-start | bytes 1572872 | tf_op jit(solution)/shard_map/ppermute | solution.py:17
  8.3 1.7 copy-start.5
  10.0 11.8 %copy-start.6 = (bf16[4,128]{1,0:T(4,128)(2,1)S(1)}, bf16[4,128]{1,0:T(4,128)(2,1)}, u32[]{:S(2)}) copy-start(bf16[4,128]{1,0:T(4,128)(2,1)} %param.5) | copy-start | bytes 3076
  10.0 5.9 %collective-permute-start.2 = (bf16[6,1,512]{2,1,0:T(2,128)(2,1)S(1)}, bf16[6,1,512]{2,1,0:T(2,128)(2,1)S(1)}, u32[]{:S(2)}, u32[]{:S(2)}) collective-permute-start(bf16[6,1,512]{2,1,0:T(2,128)(2,1)S(1)} %get-tuple-element.154), channel_id=1, source_target_pairs={{0,32},{32,64},{64,96},{1,33},{33,65},{65,97},{2,34},{34,66},{66,9... | collective-permute-start | bytes 18440 | tf_op jit(solution)/shard_map/ppermute | solution.py:15
  13.6 5.6 %collective-permute-start.3 = (bf16[6,1,512]{2,1,0:T(2,128)(2,1)S(1)}, bf16[6,1,512]{2,1,0:T(2,128)(2,1)S(1)}, u32[]{:S(2)}, u32[]{:S(2)}) collective-permute-start(bf16[6,1,512]{2,1,0:T(2,128)(2,1)S(1)} %get-tuple-element.155), channel_id=1, source_target_pairs={{32,0},{64,32},{96,64},{33,1},{65,33},{97,65},{34,2},{66,34},{98,6... | collective-permute-start | bytes 18440 | tf_op jit(solution)/shard_map/ppermute | solution.py:17
  29.7 21.8 %copy-start.2 = (f32[262144]{0:T(1024)S(1)}, f32[262144]{0:T(1024)}, u32[]{:S(2)}) copy-start(f32[262144]{0:T(1024)} %get-tuple-element.234) | copy-start | bytes 3145732 | tf_op jit(solution)/shard_map/while
  49.5 2.6 %copy-start = (f32[3,262144]{1,0:T(4,128)S(1)}, f32[3,262144]{1,0:T(4,128)}, u32[]{:S(2)}) copy-start(f32[3,262144]{1,0:T(4,128)} %get-tuple-element.233) | copy-start | bytes 9437188 | tf_op jit(solution)/shard_map/while
  52.1 2.6 %copy-start.3 = (f32[262144]{0:T(1024)}, f32[262144]{0:T(1024)S(1)}, u32[]{:S(2)}) copy-start(f32[262144]{0:T(1024)S(1)} %get-tuple-element.247) | copy-start | bytes 3145732 | tf_op jit(solution)/shard_map/while
  54.7 1.9 copy-start.1
  64.5 21.8 %copy-start.2 = (f32[262144]{0:T(1024)S(1)}, f32[262144]{0:T(1024)}, u32[]{:S(2)}) copy-start(f32[262144]{0:T(1024)} %get-tuple-element.234) | copy-start | bytes 3145732 | tf_op jit(solution)/shard_map/while
  84.4 2.6 %copy-start = (f32[3,262144]{1,0:T(4,128)S(1)}, f32[3,262144]{1,0:T(4,128)}, u32[]{:S(2)}) copy-start(f32[3,262144]{1,0:T(4,128)} %get-tuple-element.233) | copy-start | bytes 9437188 | tf_op jit(solution)/shard_map/while
  86.9 2.6 %copy-start.3 = (f32[262144]{0:T(1024)}, f32[262144]{0:T(1024)S(1)}, u32[]{:S(2)}) copy-start(f32[262144]{0:T(1024)S(1)} %get-tuple-element.247) | copy-start | bytes 3145732 | tf_op jit(solution)/shard_map/while
  89.5 1.9 copy-start.1
  99.3 21.8 %copy-start.2 = (f32[262144]{0:T(1024)S(1)}, f32[262144]{0:T(1024)}, u32[]{:S(2)}) copy-start(f32[262144]{0:T(1024)} %get-tuple-element.234) | copy-start | bytes 3145732 | tf_op jit(solution)/shard_map/while
  119.2 2.6 %copy-start = (f32[3,262144]{1,0:T(4,128)S(1)}, f32[3,262144]{1,0:T(4,128)}, u32[]{:S(2)}) copy-start(f32[3,262144]{1,0:T(4,128)} %get-tuple-element.233) | copy-start | bytes 9437188 | tf_op jit(solution)/shard_map/while
  121.7 2.6 %copy-start.3 = (f32[262144]{0:T(1024)}, f32[262144]{0:T(1024)S(1)}, u32[]{:S(2)}) copy-start(f32[262144]{0:T(1024)S(1)} %get-tuple-element.247) | copy-start | bytes 3145732 | tf_op jit(solution)/shard_map/while
  124.3 1.9 copy-start.1
  134.1 21.8 %copy-start.2 = (f32[262144]{0:T(1024)S(1)}, f32[262144]{0:T(1024)}, u32[]{:S(2)}) copy-start(f32[262144]{0:T(1024)} %get-tuple-element.234) | copy-start | bytes 3145732 | tf_op jit(solution)/shard_map/while
  154.0 2.6 %copy-start = (f32[3,262144]{1,0:T(4,128)S(1)}, f32[3,262144]{1,0:T(4,128)}, u32[]{:S(2)}) copy-start(f32[3,262144]{1,0:T(4,128)} %get-tuple-element.233) | copy-start | bytes 9437188 | tf_op jit(solution)/shard_map/while
  156.5 2.6 %copy-start.3 = (f32[262144]{0:T(1024)}, f32[262144]{0:T(1024)S(1)}, u32[]{:S(2)}) copy-start(f32[262144]{0:T(1024)S(1)} %get-tuple-element.247) | copy-start | bytes 3145732 | tf_op jit(solution)/shard_map/while
  159.1 1.9 copy-start.1
where the time goes:
time: 240 us; the launch traced here: 238 us
  matrix products  79.3 us (33%)
  blocking collectives  65.1 us (27%)
  other arithmetic  41.3 us (17%)
  loops' own time  19.3 us (8%)
  local copies, waits for them, and re-layouts  17.2 us (7%)
  starting transfers between devices  8.91 us (4%)
  waiting for transfers between devices  6.8 us (3%)
    dot_general x4, matrix products, colorize(): jnp.dot(transfer_table, weights, preferred_element_type=jnp.float32)  79.3 us
    all_to_all x1, blocking collectives, shards(): lax.all_to_all(pieces_in, 'depth', split_axis=1, concat_axis=1, tiled=True)  65.1 us
    another operation x1, loops' own time, shards(): lax.scan(advance, start, jnp.arange(slabs, dtype=jnp.int32))  19.3 us
    add x4, other arithmetic, advance(): accum = accum + transmit[None, :] * opacity[None, :] * colour  10.2 us
    while x40, local copies, waits for them, and re-layouts  9.98 us
    sub x4, other arithmetic, colorize(): opacity = 1.0 - jnp.exp(-values[3] / jnp.float32(depth_total))  7.6 us
    ppermute x2, waiting for transfers between devices, padded(): lax.ppermute(head, axis, [((i + 1) % count, i) for i in range(ends)])  6.61 us
    while x8, other arithmetic  6.54 us
  transfers between devices with their start and end apart: 4, of which 3 were waited for; matrix products, arithmetic and copies ran while one was open for 0% of the time, Pallas kernels for 0%

commit v1 on v0

v1 whole, which is shorter than its diff:
```python
import functools

import jax
import jax.numpy as jnp
import numpy as np
from jax import lax
from jax.experimental import pallas as pl
from jax.experimental.pallas import tpu as pltpu
from jax.sharding import PartitionSpec as P

F32 = jnp.float32
BF16 = jnp.bfloat16
BLOCK = 16
LANES = 128
CHUNKS = 2
TINY = 1e-30


def row_differences(rows):
    local = np.arange(rows // 2)
    out = np.zeros((2, rows // 2, rows), np.float32)
    for parity in range(2):
        own = local // BLOCK * (2 * BLOCK) + parity * BLOCK + local % BLOCK
        for step in (1, -1):
            there = own + step
            keep = (there >= 0) & (there < rows)
            out[parity, local[keep], there[keep]] += step
    return out


def column_differences(cols):
    k = np.arange(cols)
    return (k[:, None] == k[None, :] + 1).astype(np.float32) - (
        k[:, None] == k[None, :] - 1
    ).astype(np.float32)


def look_up(table, index):
    return jnp.take_along_axis(table, index, axis=1, mode="promise_in_bounds")


def slab_kernel(
    core, own, other, outer_own, outer_other, edge_own, edge_other, rows_op, cols_op, tables,
    out, dx_ref, dy_ref, *, chunk, width,
):
    slices = own.shape[0]
    blocks = own.shape[1]
    cols = own.shape[4]
    entries = tables.shape[2]
    left = chunk * width
    window = slice(left, left + width)

    def slab(near, far, before, after, near_edge, far_edge, parity):
        stack = [(near, s) for s in range(slices)] + [(far, s) for s in range(slices)]
        edges = [(near_edge, s) for s in range(slices)] + [(far_edge, s) for s in range(slices)]
        for s, (ref, z) in enumerate(stack):
            strip = ref[z, :, :, :, window].reshape(blocks * 2 * BLOCK, width)
            dx = jnp.dot(rows_op[parity], strip, preferred_element_type=F32)
            dx_ref[s] = dx
            mine = ref[z, :, parity].reshape(blocks * BLOCK, cols)
            dy_ref[s] = jnp.dot(mine, cols_op[:, window], preferred_element_type=F32)
            edge_ref, edge_z = edges[s]
            row = edge_ref[edge_z : edge_z + 1, window].astype(F32)
            if parity == 0:
                dx_ref[s, 0:1, :] = dx[0:1] - row
            else:
                last = blocks * BLOCK
                dx_ref[s, last - 1 : last, :] = dx[last - 1 : last] + row

        tabs = [jnp.broadcast_to(tables[i, 0:1], (BLOCK, entries)) for i in range(8)]

        def block(b, carry):
            rows = pl.ds(pl.multiple_of(b * BLOCK, BLOCK), BLOCK)
            for start in range(0, width, LANES):
                here = slice(left + start, left + start + LANES)
                local = slice(start, start + LANES)
                accum = [jnp.zeros((BLOCK, LANES), F32) for _ in range(3)]
                transmit = jnp.ones((BLOCK, LANES), F32)
                prev = before[b, :, here].astype(F32)
                centre = stack[0][0][stack[0][1], b, parity, :, here].astype(F32)
                for s in range(2 * slices):
                    if s + 1 < 2 * slices:
                        ref, z = stack[s + 1]
                        following = ref[z, b, parity, :, here].astype(F32)
                    else:
                        following = after[b, :, here].astype(F32)
                    dz = following - prev
                    dx = dx_ref[s, rows, local]
                    dy = dy_ref[s, rows, local]
                    position = centre * float(entries - 1)
                    knot = position.astype(jnp.int32)
                    part = position - knot.astype(F32)
                    upper = part.astype(BF16).astype(F32)
                    lower = (1.0 - part).astype(BF16).astype(F32)
                    values = [
                        lower * look_up(tabs[c], knot) + upper * look_up(tabs[c + 4], knot)
                        for c in range(4)
                    ]
                    lambert = jnp.abs(2.0 * (dz + dy) + dx) * (0.7 / 6.0)
                    square = 0.25 * (dz * dz + dx * dx + dy * dy) + 0.01
                    shading = 0.3 + lambert * lax.rsqrt(square)
                    clear = jnp.exp2(values[3])
                    gain = transmit * (1.0 - clear) * shading
                    transmit = transmit * clear
                    accum = [a + gain * v for a, v in zip(accum, values[:3])]
                    prev, centre = centre, following
                for c in range(3):
                    out[b, c * BLOCK : (c + 1) * BLOCK, local] = accum[c]
                out[b, 3 * BLOCK : 4 * BLOCK, local] = (1.0 - transmit) * tables[8, 0:1, 0:1]
            return carry

        lax.fori_loop(0, blocks, block, 0)

    @pl.when(core[0] == 0)
    def _():
        slab(own, other, outer_own, outer_other, edge_own, edge_other, 0)

    @pl.when(core[0] != 0)
    def _():
        slab(other, own, outer_other, outer_own, edge_other, edge_own, 1)


def merge_kernel(scales, *refs):
    ins, out = refs[:-1], refs[-1]
    width = ins[0].shape[2]
    cols = width * len(ins)
    for q, ref in enumerate(ins):
        for start in range(0, width, LANES):
            local = slice(start, start + LANES)
            accum = [jnp.zeros((BLOCK, LANES), F32) for _ in range(3)]
            transmit = jnp.ones((BLOCK, LANES), F32)
            for s in range(ref.shape[0]):
                for c in range(3):
                    accum[c] = accum[c] + transmit * ref[s, c * BLOCK : (c + 1) * BLOCK, local]
                opacity = ref[s, 3 * BLOCK : 4 * BLOCK, local] * scales[1]
                transmit = transmit - transmit * opacity
            image = [a * scales[0] for a in accum] + [1.0 - transmit]
            for c in range(4):
                for r in range(BLOCK):
                    at = r * cols + q * width + start
                    out[c : c + 1, at : at + LANES] = image[c][r : r + 1]


def shards(volume, transfer_table):
    slices, rows, cols = volume.shape
    depth_count = lax.axis_size("depth")
    img_count = lax.axis_size("img")
    chips = depth_count // 2
    depth_total = slices * depth_count
    entries = transfer_table.shape[1]
    blocks = rows // (2 * BLOCK)
    width = cols // CHUNKS
    core = lax.axis_index("depth") % 2

    def shift(x, img_step, depth_step):
        pairs = []
        for i in range(img_count):
            for d in range(depth_count):
                to_i, to_d = i + img_step(d % 2), d + depth_step(d % 2)
                if 0 <= to_i < img_count and 0 <= to_d < depth_count:
                    pairs.append((i * depth_count + d, to_i * depth_count + to_d))
        return lax.ppermute(x, ("img", "depth"), pairs)

    other = lax.ppermute(volume, "depth", [(d, d ^ 1) for d in range(depth_count)])
    plane = lax.dynamic_index_in_dim(volume, (slices - 1) * core, 0, False)
    plane = plane.reshape(blocks, 2, BLOCK, cols)
    to_other_core = lax.dynamic_index_in_dim(plane, 1 - core, 1, False)
    to_same_core = lax.dynamic_index_in_dim(plane, core, 1, False)
    outer_own = shift(to_other_core, lambda c: 0, lambda c: 1 if c else -1)
    outer_other = shift(to_same_core, lambda c: 0, lambda c: 2 if c else -2)
    edge_same = lax.dynamic_index_in_dim(volume, (rows - 1) * (1 - core), 1, False)
    edge_cross = lax.dynamic_index_in_dim(volume, (rows - 1) * core, 1, False)
    edge_own = shift(edge_same, lambda c: -1 if c else 1, lambda c: 0)
    edge_other = shift(edge_cross, lambda c: 1 if c else -1, lambda c: -1 if c else 1)

    table = transfer_table.astype(F32)
    colour_top = jnp.maximum(jnp.max(table[0:3]), TINY)
    opacity_top = jnp.maximum(jnp.max(table[3]) * (2.0 * slices / depth_total), TINY)
    factor = jnp.concatenate(
        [
            jnp.full((3, 1), 1.0 / (colour_top * opacity_top), F32),
            jnp.full((1, 1), -np.log2(np.e) / depth_total, F32),
        ]
    )
    lower = table * factor
    upper = jnp.concatenate([lower[:, 1:], lower[:, -1:]], axis=1)
    scale_row = jnp.full((1, entries), 1.0 / opacity_top, F32)
    tables = jnp.concatenate([lower, upper, scale_row])[:, None, :]
    scales = jnp.stack([colour_top * opacity_top, opacity_top])

    split = (slices, blocks, 2, BLOCK, cols)
    own_view, other_view = volume.reshape(split), other.reshape(split)
    rows_op = jnp.asarray(row_differences(rows), BF16)
    cols_op = jnp.asarray(column_differences(cols), BF16)
    core_arg = core.astype(jnp.int32).reshape(1)
    same_core = [[2 * j + c for j in range(chips)] for c in range(2)]
    vmem = pl.BlockSpec(memory_space=pltpu.MemorySpace.VMEM)
    smem = pl.BlockSpec(memory_space=pltpu.MemorySpace.SMEM)
    received = []
    for q in range(CHUNKS):
        partial_image = pl.pallas_call(
            functools.partial(slab_kernel, chunk=q, width=width),
            out_shape=jax.ShapeDtypeStruct((blocks, 4 * BLOCK, width), F32),
            in_specs=[smem] + [vmem] * 9,
            out_specs=vmem,
            scratch_shapes=[pltpu.VMEM((2 * slices, blocks * BLOCK, width), F32)] * 2,
            compiler_params=pltpu.CompilerParams(vmem_limit_bytes=40 << 20),
            name="slab",
        )(
            core_arg, own_view, other_view, outer_own, outer_other, edge_own, edge_other,
            rows_op, cols_op, tables,
        )
        pieces = partial_image.astype(jnp.float16)
        pieces = lax.all_to_all(
            pieces, "depth", split_axis=0, concat_axis=0, tiled=True, axis_index_groups=same_core
        )
        received.append(pieces.astype(F32))
    return pl.pallas_call(
        merge_kernel,
        out_shape=jax.ShapeDtypeStruct((4, BLOCK * cols), F32),
        in_specs=[smem] + [vmem] * CHUNKS,
        out_specs=vmem,
        name="merge",
    )(scales, *received)


def solution(mesh):
    placed = (P("depth", "img", None), P())
    return jax.shard_map(
        shards, mesh=mesh, in_specs=placed, out_specs=P(None, ("img", "depth")), check_vma=False
    )
```

time: 240 us -> 84 us (0.35)
  the two profiles are of different devices: /device:TPU:64 before, /device:TPU:1 now
where the time goes in v1:
time: 84 us; the launch traced here: 83.2 us
  starting transfers between devices  28.9 us (34%)
  Pallas kernels  28.4 us (34%)
  waiting for transfers between devices  11.3 us (13%)
  other arithmetic  6.98 us (8%)
  local copies, waits for them, and re-layouts  5.96 us (7%)
  between operations  1.58 us (2%)
    pallas_call x2, Pallas kernels, shards(): pl.pallas_call(functools.partial(slab_kernel, chunk=q, width=width), out_...  26 us
    all_to_all x2, starting transfers between devices, shards(): lax.all_to_all(pieces, 'depth', split_axis=0, concat_axis=0, tiled=True,...  14.9 us
    ppermute x4, starting transfers between devices, shift(): return lax.ppermute(x, ('img', 'depth'), pairs)  12.6 us
    all_to_all x2, waiting for transfers between devices, shards(): lax.all_to_all(pieces, 'depth', split_axis=0, concat_axis=0, tiled=True,...  8.68 us
    unnamed x18, local copies, waits for them, and re-layouts  3.74 us
    convert_element_type x2, other arithmetic, shards(): received.append(pieces.astype(F32))  3.2 us
    ppermute x4, waiting for transfers between devices, shift(): return lax.ppermute(x, ('img', 'depth'), pairs)  2.66 us
    pallas_call x1, Pallas kernels, shards(): pl.pallas_call(merge_kernel, out_shape=jax.ShapeDtypeStruct((4, BLOCK * c...  2.4 us
  transfers between devices with their start and end apart: 7, of which 2 were waited for; matrix products, arithmetic and copies ran while one was open for 9% of the time, Pallas kernels for 16%

profile of v1, /device:TPU:1, one launch (start us, length us, event | category | flops | bytes accessed | tf_op | source)
XLA Modules:
  0.0 83.2 jit_solution(10907370051739808751)
XLA Ops:
  0.0 0.0 copy-start
  0.0 0.0 copy-start.7
  0.0 1.4 %collective-permute-start = (bf16[4,512,512]{2,1,0:T(8,128)(2,1)}, bf16[4,512,512]{2,1,0:T(8,128)(2,1)}, u32[]{:S(2)}, u32[]{:S(2)}) collective-permute-start(bf16[4,512,512]{2,1,0:T(8,128)(2,1)} %param.4), channel_id=1, source_target_pairs={{0,1},{1,0},{2,3},{3,2},{4,5},{5,4},{6,7},{7,6},{8,9},{9,8},{10,11... | collective-permute-start | bytes 6291464 | tf_op jit(solution)/shard_map/ppermute | solution.py:164
  1.4 0.8 constant_dynamic-slice_fusion
  2.2 1.3 %collective-permute-start.3 = (bf16[4,512]{1,0:T(4,128)(2,1)S(1)}, bf16[4,512]{1,0:T(4,128)(2,1)S(1)}, u32[]{:S(2)}, u32[]{:S(2)}) collective-permute-start(bf16[4,512]{1,0:T(4,128)(2,1)S(1)} %bitcast.22), channel_id=1, source_target_pairs={{0,32},{2,34},{4,36},{6,38},{8,40},{10,42},{12,44},{14,46},{16,48}... | collective-permute-start | bytes 12296 | tf_op jit(solution)/shard_map/ppermute | solution.py:162
  3.5 6.2 %collective-permute-start.4 = (bf16[4,512]{1,0:T(4,128)(2,1)S(1)}, bf16[4,512]{1,0:T(4,128)(2,1)S(1)}, u32[]{:S(2)}, u32[]{:S(2)}) collective-permute-start(bf16[4,512]{1,0:T(4,128)(2,1)S(1)} %bitcast.23), channel_id=1, source_target_pairs={{1,32},{3,34},{5,36},{7,38},{9,40},{11,42},{13,44},{15,46},{17,48}... | collective-permute-start | bytes 12296 | tf_op jit(solution)/shard_map/ppermute | solution.py:162
  9.8 1.1 %constant_dynamic-slice_fusion.2 = bf16[1,512,512]{2,1,0:T(8,128)(2,1)S(1)} fusion(bf16[4,512,512]{2,1,0:T(8,128)(2,1)} %param.4, s32[]{:T(128)S(6)} %select_n.26), kind=kLoop, calls=%fused_computation.8 | loop fusion | bytes 1048580 | tf_op jit(solution)/shard_map/jit(dynamic_index_in_dim)/dynamic_slice | solution.py:165
  10.9 3.1 %collective-permute-start.2 = (bf16[16,16,512]{2,1,0:T(8,128)(2,1)S(1)}, bf16[16,16,512]{2,1,0:T(8,128)(2,1)S(1)}, u32[]{:S(2)}, u32[]{:S(2)}) collective-permute-start(bf16[16,16,512]{2,1,0:T(8,128)(2,1)S(1)} %get-tuple-element.7), channel_id=1, source_target_pairs={{1,3},{2,0},{3,5},{4,2},{5,7},{6,4},{7,9},{8,6},{9,11},{10,8},{11,... | collective-permute-start | bytes 786440 | tf_op jit(solution)/shard_map/ppermute | solution.py:162
  14.1 1.9 %collective-permute-start.1 = (bf16[16,16,512]{2,1,0:T(8,128)(2,1)S(1)}, bf16[16,16,512]{2,1,0:T(8,128)(2,1)S(1)}, u32[]{:S(2)}, u32[]{:S(2)}) collective-permute-start(bf16[16,16,512]{2,1,0:T(8,128)(2,1)S(1)} %get-tuple-element.8), channel_id=1, source_target_pairs={{1,2},{2,1},{3,4},{4,3},{5,6},{6,5},{7,8},{8,7},{9,10},{10,9},{11,... | collective-permute-start | bytes 786440 | tf_op jit(solution)/shard_map/ppermute | solution.py:162
  16.0 0.0 copy-done.7
  16.0 0.6 slice_reduce_fusion.1
  17.3 0.6 slice_reduce_fusion
  18.6 0.1 pad_bitcast_fusion
  18.7 0.1 broadcast_multiply_fusion
  18.8 0.1 slice.15
  18.9 0.1 slice.14
  18.9 0.1 pad.4.clone
  19.0 0.1 maximum_maximum_fusion
  19.1 0.0 collective-permute-done.3.edge_own
  19.1 0.0 collective-permute-done.4.edge_other
  19.1 0.0 collective-permute-done.2.outer_other
  19.1 2.6 %collective-permute-done.1.outer_own = bf16[16,16,512]{2,1,0:T(8,128)(2,1)S(1)} collective-permute-done((bf16[16,16,512]{2,1,0:T(8,128)(2,1)S(1)}, bf16[16,16,512]{2,1,0:T(8,128)(2,1)S(1)}, u32[]{:S(2)}, u32[]{:S(2)}) %collective-permute-start.1) | collective-permute-done | bytes 262176 | tf_op jit(solution)/shard_map/ppermute | solution.py:162
  21.8 0.0 collective-permute-done
  21.8 0.0 copy-done
  21.8 0.0 copy-start.1
  21.8 1.0 %copy-done.1 = bf16[512,512]{1,0:T(8,128)(2,1)S(1)} copy-done((bf16[512,512]{1,0:T(8,128)(2,1)S(1)}, bf16[512,512]{1,0:T(8,128)(2,1)}, u32[]{:S(2)}) %copy-start.1) | copy-done | bytes 524312
  22.8 0.0 copy-start.3
  22.8 1.0 %copy-done.3 = bf16[2,256,512]{2,1,0:T(8,128)(2,1)S(1)} copy-done((bf16[2,256,512]{2,1,0:T(8,128)(2,1)S(1)}, bf16[2,256,512]{2,1,0:T(8,128)(2,1)}, u32[]{:S(2)}) %copy-start.3) | copy-done | bytes 524312
  23.9 13.0 %slab.2 = f32[16,64,256]{2,1,0:T(8,128)S(1)} custom-call(s32[1]{0:T(128)} %bitcast.2.core, bf16[4,16,2,16,512]{4,3,2,1,0:T(8,128)(2,1)S(1)} %bitcast.19, bf16[4,16,2,16,512]{4,3,2,1,0:T(8,128)(2,1)} %bitcast.4.other, bf16[16,16,512]{2,1,0:T(8,128)(2,1)S(1)} %collective-permute-done.1.outer_own, bf16[16,16,512]{2,1,0:T(8,128)(2,1)S(1)} %collective-permute-done.2.outer_other, ...), custom_call_target="tpu_custom_call" | custom-call | tf_op jit(solution)/shard_map/slab/pallas_call | solution.py:201
  36.9 0.0 copy-start.5
  36.9 0.7 copy-done.5
  37.6 0.0 copy-start.2
  37.6 0.0 copy-start.4
  37.6 0.9 %convert_element_type.16 = f16[16,64,256]{2,1,0:T(8,128)(2,1)} convert(f32[16,64,256]{2,1,0:T(8,128)S(1)} %slab.2) | non-fusion elementwise | flops 262144 | bytes 1572864 | tf_op jit(solution)/shard_map/convert_element_type | solution.py:213
  38.5 8.3 %all-to-all-start = ((f16[16,64,256]{2,1,0:T(8,128)(2,1)}), f16[16,64,256]{2,1,0:T(8,128)(2,1)}, u32[]{:S(2)}, u32[]{:S(2)}) async-start(f16[16,64,256]{2,1,0:T(8,128)(2,1)} %convert_element_type.16), calls=%async_computation | async-start | bytes 1048576 | tf_op jit(solution)/shard_map/all_to_all | solution.py:214
  46.9 0.0 copy-done.2
  46.9 0.0 copy-done.4
  46.9 0.0 copy-start.6
  46.9 0.9 %copy-done.6 = bf16[16,16,512]{2,1,0:T(8,128)(2,1)S(1)} copy-done((bf16[16,16,512]{2,1,0:T(8,128)(2,1)S(1)}, bf16[16,16,512]{2,1,0:T(8,128)(2,1)}, u32[]{:S(2)}) %copy-start.6) | copy-done | bytes 262168
  47.8 13.0 %slab.3 = f32[16,64,256]{2,1,0:T(8,128)S(1)} custom-call(s32[1]{0:T(128)} %bitcast.2.core, bf16[4,16,2,16,512]{4,3,2,1,0:T(8,128)(2,1)S(1)} %bitcast.20, bf16[4,16,2,16,512]{4,3,2,1,0:T(8,128)(2,1)} %bitcast.4.other, bf16[16,16,512]{2,1,0:T(8,128)(2,1)S(1)} %copy-done.6, bf16[16,16,512]{2,1,0:T(8,128)(2,1)S(1)} %collective-permute-done.2.outer_other, ...), custom_call_target="tpu_custom_call" | custom-call | tf_op jit(solution)/shard_map/slab/pallas_call | solution.py:201
  60.8 0.9 %convert_element_type.18 = f16[16,64,256]{2,1,0:T(8,128)(2,1)} convert(f32[16,64,256]{2,1,0:T(8,128)S(1)} %slab.3) | non-fusion elementwise | flops 262144 | bytes 1572864 | tf_op jit(solution)/shard_map/convert_element_type | solution.py:213
  61.8 0.0 all-to-all-done
  61.8 6.6 %all-to-all-start.1 = ((f16[16,64,256]{2,1,0:T(8,128)(2,1)}), f16[16,64,256]{2,1,0:T(8,128)(2,1)S(1)}, u32[]{:S(2)}, u32[]{:S(2)}) async-start(f16[16,64,256]{2,1,0:T(8,128)(2,1)} %convert_element_type.18), calls=%async_computation.1 | async-start | bytes 1048576 | tf_op jit(solution)/shard_map/all_to_all | solution.py:214
  68.4 0.6 pad_maximum_fusion.scales
  68.9 2.1 %convert_element_type.17.refs_0_ = f32[16,64,256]{2,1,0:T(8,128)} convert(f16[16,64,256]{2,1,0:T(8,128)(2,1)} %all-to-all-done) | non-fusion elementwise | flops 262144 | bytes 1572864 | tf_op jit(solution)/shard_map/convert_element_type | solution.py:217
  71.1 8.7 %all-to-all-done.1 = f16[16,64,256]{2,1,0:T(8,128)(2,1)S(1)} async-done(((f16[16,64,256]{2,1,0:T(8,128)(2,1)}), f16[16,64,256]{2,1,0:T(8,128)(2,1)S(1)}, u32[]{:S(2)}, u32[]{:S(2)}) %all-to-all-start.1) | async-done | bytes 524320 | tf_op jit(solution)/shard_map/all_to_all | solution.py:214
  79.7 1.1 %convert_element_type.19.refs_1_ = f32[16,64,256]{2,1,0:T(8,128)} convert(f16[16,64,256]{2,1,0:T(8,128)(2,1)S(1)} %all-to-all-done.1) | non-fusion elementwise | flops 262144 | bytes 1572864 | tf_op jit(solution)/shard_map/convert_element_type | solution.py:217
  80.8 2.4 %merge.1 = f32[4,8192]{1,0:T(4,128)} custom-call(f32[2]{0:T(128)} %pad_maximum_fusion.scales, f32[16,64,256]{2,1,0:T(8,128)} %convert_element_type.17.refs_0_, f32[16,64,256]{2,1,0:T(8,128)} %convert_element_type.19.refs_1_), custom_call_target="tpu_custom_call" | custom-call | tf_op jit(solution)/shard_map/merge/pallas_call | solution.py:218
  (5 shorter events, 0.1 us)
Async XLA Ops:
  0.0 21.8 %copy-start = (bf16[4,512,512]{2,1,0:T(8,128)(2,1)S(1)}, bf16[4,512,512]{2,1,0:T(8,128)(2,1)}, u32[]{:S(2)}) copy-start(bf16[4,512,512]{2,1,0:T(8,128)(2,1)} %param.4) | copy-start | bytes 6291460
  0.0 16.0 %copy-start.7 = (bf16[4,128]{1,0:T(4,128)(2,1)S(1)}, bf16[4,128]{1,0:T(4,128)(2,1)}, u32[]{:S(2)}) copy-start(bf16[4,128]{1,0:T(4,128)(2,1)} %param.5) | copy-start | bytes 3076
  0.0 21.8 %collective-permute-start = (bf16[4,512,512]{2,1,0:T(8,128)(2,1)}, bf16[4,512,512]{2,1,0:T(8,128)(2,1)}, u32[]{:S(2)}, u32[]{:S(2)}) collective-permute-start(bf16[4,512,512]{2,1,0:T(8,128)(2,1)} %param.4), channel_id=1, source_target_pairs={{0,1},{1,0},{2,3},{3,2},{4,5},{5,4},{6,7},{7,6},{8,9},{9,8},{10,11... | collective-permute-start | bytes 6291464 | tf_op jit(solution)/shard_map/ppermute | solution.py:164
  2.2 16.9 %collective-permute-start.3 = (bf16[4,512]{1,0:T(4,128)(2,1)S(1)}, bf16[4,512]{1,0:T(4,128)(2,1)S(1)}, u32[]{:S(2)}, u32[]{:S(2)}) collective-permute-start(bf16[4,512]{1,0:T(4,128)(2,1)S(1)} %bitcast.22), channel_id=1, source_target_pairs={{0,32},{2,34},{4,36},{6,38},{8,40},{10,42},{12,44},{14,46},{16,48}... | collective-permute-start | bytes 12296 | tf_op jit(solution)/shard_map/ppermute | solution.py:162
  3.5 15.6 %collective-permute-start.4 = (bf16[4,512]{1,0:T(4,128)(2,1)S(1)}, bf16[4,512]{1,0:T(4,128)(2,1)S(1)}, u32[]{:S(2)}, u32[]{:S(2)}) collective-permute-start(bf16[4,512]{1,0:T(4,128)(2,1)S(1)} %bitcast.23), channel_id=1, source_target_pairs={{1,32},{3,34},{5,36},{7,38},{9,40},{11,42},{13,44},{15,46},{17,48}... | collective-permute-start | bytes 12296 | tf_op jit(solution)/shard_map/ppermute | solution.py:162
  10.9 8.2 %collective-permute-start.2 = (bf16[16,16,512]{2,1,0:T(8,128)(2,1)S(1)}, bf16[16,16,512]{2,1,0:T(8,128)(2,1)S(1)}, u32[]{:S(2)}, u32[]{:S(2)}) collective-permute-start(bf16[16,16,512]{2,1,0:T(8,128)(2,1)S(1)} %get-tuple-element.7), channel_id=1, source_target_pairs={{1,3},{2,0},{3,5},{4,2},{5,7},{6,4},{7,9},{8,6},{9,11},{10,8},{11,... | collective-permute-start | bytes 786440 | tf_op jit(solution)/shard_map/ppermute | solution.py:162
  14.1 7.7 %collective-permute-start.1 = (bf16[16,16,512]{2,1,0:T(8,128)(2,1)S(1)}, bf16[16,16,512]{2,1,0:T(8,128)(2,1)S(1)}, u32[]{:S(2)}, u32[]{:S(2)}) collective-permute-start(bf16[16,16,512]{2,1,0:T(8,128)(2,1)S(1)} %get-tuple-element.8), channel_id=1, source_target_pairs={{1,2},{2,1},{3,4},{4,3},{5,6},{6,5},{7,8},{8,7},{9,10},{10,9},{11,... | collective-permute-start | bytes 786440 | tf_op jit(solution)/shard_map/ppermute | solution.py:162
  21.8 1.0 %copy-start.1 = (bf16[512,512]{1,0:T(8,128)(2,1)S(1)}, bf16[512,512]{1,0:T(8,128)(2,1)}, u32[]{:S(2)}) copy-start(bf16[512,512]{1,0:T(8,128)(2,1)} %constant.56.clone.cols_op) | copy-start | bytes 1572868
  22.8 1.0 %copy-start.3 = (bf16[2,256,512]{2,1,0:T(8,128)(2,1)S(1)}, bf16[2,256,512]{2,1,0:T(8,128)(2,1)}, u32[]{:S(2)}) copy-start(bf16[2,256,512]{2,1,0:T(8,128)(2,1)} %constant.55.clone.rows_op) | copy-start | bytes 1572868
  36.9 0.7 copy-start.5
  37.6 9.3 %copy-start.2 = (bf16[512,512]{1,0:T(8,128)(2,1)S(1)}, bf16[512,512]{1,0:T(8,128)(2,1)}, u32[]{:S(2)}) copy-start(bf16[512,512]{1,0:T(8,128)(2,1)} %constant.56.clone.cols_op) | copy-start | bytes 1572868
  37.6 9.3 %copy-start.4 = (bf16[2,256,512]{2,1,0:T(8,128)(2,1)S(1)}, bf16[2,256,512]{2,1,0:T(8,128)(2,1)}, u32[]{:S(2)}) copy-start(bf16[2,256,512]{2,1,0:T(8,128)(2,1)} %constant.55.clone.rows_op) | copy-start | bytes 1572868
  38.5 23.3 %all-to-all-start = ((f16[16,64,256]{2,1,0:T(8,128)(2,1)}), f16[16,64,256]{2,1,0:T(8,128)(2,1)}, u32[]{:S(2)}, u32[]{:S(2)}) async-start(f16[16,64,256]{2,1,0:T(8,128)(2,1)} %convert_element_type.16), calls=%async_computation | async-start | bytes 1048576 | tf_op jit(solution)/shard_map/all_to_all | solution.py:214
  46.9 1.0 %copy-start.6 = (bf16[16,16,512]{2,1,0:T(8,128)(2,1)S(1)}, bf16[16,16,512]{2,1,0:T(8,128)(2,1)}, u32[]{:S(2)}) copy-start(bf16[16,16,512]{2,1,0:T(8,128)(2,1)} %copy-done.5) | copy-start | bytes 786436
  61.8 17.9 %all-to-all-start.1 = ((f16[16,64,256]{2,1,0:T(8,128)(2,1)}), f16[16,64,256]{2,1,0:T(8,128)(2,1)S(1)}, u32[]{:S(2)}, u32[]{:S(2)}) async-start(f16[16,64,256]{2,1,0:T(8,128)(2,1)} %convert_element_type.18), calls=%async_computation.1 | async-start | bytes 1048576 | tf_op jit(solution)/shard_map/all_to_all | solution.py:214

commit v2 on v0

v2 whole, which is shorter than its diff:
```python
import functools

import jax
import jax.numpy as jnp
import numpy as np
from jax import lax
from jax.experimental import pallas as pl
from jax.experimental.pallas import tpu as pltpu
from jax.sharding import PartitionSpec as P

F32 = jnp.float32
BF16 = jnp.bfloat16
LANES = 128
EARLY = 3


def column_differences(cols):
    k = np.arange(cols)
    return (k[:, None] == k[None, :] + 1).astype(np.float32) - (
        k[:, None] == k[None, :] - 1
    ).astype(np.float32)


def look_up(table, index):
    return jnp.take_along_axis(table, index, axis=1, mode="promise_in_bounds")


def classify(centre, tabs, entries):
    position = centre * float(entries - 1)
    knot = position.astype(jnp.int32)
    part = position - knot.astype(F32)
    upper = part.astype(BF16).astype(F32)
    lower = (1.0 - part).astype(BF16).astype(F32)
    values = [
        lower * look_up(tabs[c], knot) + upper * look_up(tabs[c + 4], knot) for c in range(4)
    ]
    return values[:3] + [jnp.exp2(values[3])]


def spread_tables(tables, rows):
    return [jnp.broadcast_to(tables[i, 0:1], (rows, tables.shape[2])) for i in range(8)]


def classify_kernel(cells, cols_op, tables, values, dy, *, rows):
    entries = tables.shape[2]
    total, cols = cells.shape
    tabs = spread_tables(tables, rows)
    dy[...] = jnp.dot(cells[...], cols_op[...], preferred_element_type=F32)

    def block(b, carry):
        here = pl.ds(pl.multiple_of(b * rows, rows), rows)
        for start in range(0, cols, LANES):
            lanes = slice(start, start + LANES)
            found = classify(cells[here, lanes].astype(F32), tabs, entries)
            for c in range(4):
                values[c, here, lanes] = found[c]
        return carry

    lax.fori_loop(0, total // rows, block, 0)


def composite_kernel(early, late, values, dy_early, cols_op, tables, out, dy_late, *, rows):
    slabs, early_rows, cols = early.shape
    entries = tables.shape[2]
    count = early_rows // rows
    slices = count + 1
    tabs = spread_tables(tables, rows)
    for s in range(slabs):
        dy_late[s * rows : (s + 1) * rows] = jnp.dot(
            late[s, 0:rows], cols_op[...], preferred_element_type=F32
        )
    row = lax.broadcasted_iota(jnp.int32, (rows, LANES), 0)
    first, last = row == 0, row == rows - 1

    for start in range(0, cols, LANES):
        lanes = slice(start, start + LANES)

        def slab(s, carry):
            accum, transmit, prev, centre = carry
            accum = list(accum)
            halo = late[s, rows : rows + 2 * slices, lanes].astype(F32)
            after = jnp.minimum(s + 1, slabs - 1)
            inside = jnp.where(s + 1 < slabs, 1.0, 0.0)
            stack = [early[s, q * rows : (q + 1) * rows, lanes].astype(F32) for q in range(1, count)]
            stack.append(late[s, 0:rows, lanes].astype(F32))
            stack.append(early[after, 0:rows, lanes].astype(F32) * inside)
            for q in range(slices):
                following = stack[q]
                if q < count:
                    here = pl.ds(pl.multiple_of(s * early_rows + q * rows, rows), rows)
                    found = [values[c, here, lanes] for c in range(4)]
                    dy = dy_early[here, lanes]
                else:
                    here = pl.ds(pl.multiple_of(s * rows, rows), rows)
                    found = classify(centre, tabs, entries)
                    dy = dy_late[here, lanes]
                above = jnp.where(first, halo[q : q + 1], pltpu.roll(centre, 1, 0))
                below = jnp.where(
                    last, halo[slices + q : slices + q + 1], pltpu.roll(centre, rows - 1, 0)
                )
                dx = below - above
                dz = following - prev
                lambert = jnp.abs(2.0 * (dz + dy) + dx) * (0.7 / 6.0)
                square = 0.25 * (dz * dz + dx * dx + dy * dy) + 0.01
                shading = 0.3 + lambert * lax.rsqrt(square)
                clear = found[3]
                gain = transmit * (1.0 - clear) * shading
                transmit = transmit * clear
                accum = [a + gain * v for a, v in zip(accum, found[:3])]
                prev, centre = centre, following
            return tuple(accum), transmit, prev, centre

        zero = jnp.zeros((rows, LANES), F32)
        state = ((zero, zero, zero), zero + 1.0, zero, early[0, 0:rows, lanes].astype(F32))
        accum, transmit, _, _ = lax.fori_loop(0, slabs, slab, state)
        image = list(accum) + [1.0 - transmit]
        for c in range(4):
            for r in range(rows):
                at = r * cols + start
                out[c : c + 1, at : at + LANES] = image[c][r : r + 1]


def shards(volume, transfer_table):
    slices, strip, cols = volume.shape
    slabs = lax.axis_size("depth")
    img_count = lax.axis_size("img")
    depth_total = slices * slabs
    entries = transfer_table.shape[1]
    rows = strip // slabs

    table = transfer_table.astype(F32)
    factor = np.array([[1.0], [1.0], [1.0], [-np.log2(np.e) / depth_total]], np.float32)
    lower = table * factor
    upper = jnp.concatenate([lower[:, 1:], lower[:, -1:]], axis=1)
    tables = jnp.concatenate([lower, upper])[:, None, :]
    cols_op = jnp.asarray(column_differences(cols), BF16)

    def exchange(pieces):
        return lax.all_to_all(pieces, "depth", split_axis=0, concat_axis=0, tiled=True)

    blocks = volume.reshape(slices, slabs, rows, cols)
    early = exchange(
        jnp.swapaxes(blocks[:EARLY], 0, 1).reshape(slabs, EARLY * rows, cols)
    )
    forward = [(i, i + 1) for i in range(img_count - 1)]
    backward = [(i + 1, i) for i in range(img_count - 1)]
    top_edge = lax.ppermute(volume[:, strip - 1], "img", forward)
    bottom_edge = lax.ppermute(volume[:, 0], "img", backward)
    top = jnp.concatenate([top_edge[:, None], blocks[:, :-1, rows - 1]], axis=1)
    bottom = jnp.concatenate([blocks[:, 1:, 0], bottom_edge[:, None]], axis=1)
    late = exchange(
        jnp.concatenate(
            [blocks[EARLY], jnp.swapaxes(top, 0, 1), jnp.swapaxes(bottom, 0, 1)], axis=1
        )
    )

    vmem = pl.BlockSpec(memory_space=pltpu.MemorySpace.VMEM)
    total = slabs * EARLY * rows
    values, dy_early = pl.pallas_call(
        functools.partial(classify_kernel, rows=rows),
        out_shape=(
            jax.ShapeDtypeStruct((4, total, cols), F32),
            jax.ShapeDtypeStruct((total, cols), F32),
        ),
        in_specs=[vmem] * 3,
        out_specs=(vmem, vmem),
        compiler_params=pltpu.CompilerParams(vmem_limit_bytes=40 << 20),
        name="classify",
    )(early.reshape(total, cols), cols_op, tables)
    return pl.pallas_call(
        functools.partial(composite_kernel, rows=rows),
        out_shape=jax.ShapeDtypeStruct((4, rows * cols), F32),
        in_specs=[vmem] * 6,
        out_specs=vmem,
        scratch_shapes=[pltpu.VMEM((slabs * rows, cols), F32)],
        compiler_params=pltpu.CompilerParams(vmem_limit_bytes=40 << 20),
        name="composite",
    )(early, late, values, dy_early, cols_op, tables)


def solution(mesh):
    placed = (P("depth", "img", None), P())
    return jax.shard_map(
        shards, mesh=mesh, in_specs=placed, out_specs=P(None, ("img", "depth")), check_vma=False
    )
```

time: 240 us -> 89.1 us (0.37)
  matrix products: 79.3 us -> 0 us
  blocking collectives: 65.1 us -> 0 us
  Pallas kernels: 0 us -> 45.6 us
  other arithmetic: 41.3 us -> 1.4 us
  loops' own time: 19.3 us -> 0 us
  starting transfers between devices: 8.91 us -> 17.1 us
  local copies, waits for them, and re-layouts: 17.2 us -> 10.4 us
  waiting for transfers between devices: 6.8 us -> 12.8 us
    dot_general x4 -> x0, matrix products: 79.3 us -> none  [colorize(): jnp.dot(transfer_table, weights, preferred_element_type=jnp.float32)]
    all_to_all x1 -> x0, blocking collectives: 65.1 us -> none  [shards(): lax.all_to_all(pieces_in, 'depth', split_axis=1, concat_axis=1, tiled=True)]
    pallas_call x0 -> x2, Pallas kernels: none -> 45.6 us  [the longest x1 25.2 us: shards(): pl.pallas_call(functools.partial(classify_kernel, rows=rows), out_shape=(...]
    another operation x1 -> x0, loops' own time: 19.3 us -> none  [shards(): lax.scan(advance, start, jnp.arange(slabs, dtype=jnp.int32))]
    all_to_all x0 -> x2, waiting for transfers between devices: none -> 12.8 us  [exchange(): lax.all_to_all(pieces, 'depth', split_axis=0, concat_axis=0, tiled=True)]
    add x8 -> x0, other arithmetic: 11.7 us -> none  [the longest x4 10.2 us: advance(): accum = accum + transmit[None, :] * opacity[None, :] * colour]
    all_to_all x0 -> x2, starting transfers between devices: none -> 11.2 us  [exchange(): lax.all_to_all(pieces, 'depth', split_axis=0, concat_axis=0, tiled=True)]
    while x40 -> x0, local copies, waits for them, and re-layouts: 9.98 us -> none
  transfers between devices with their start and end apart: 4 -> 4, of which waited for: 3 -> 1; matrix products, arithmetic and copies ran while one was open for 0% -> 6% of each run, Pallas kernels for 0% -> 29%
where the time goes in v2:
time: 89.1 us; the launch traced here: 87.4 us
  Pallas kernels  45.6 us (51%)
  starting transfers between devices  17.1 us (19%)
  waiting for transfers between devices  12.8 us (14%)
  local copies, waits for them, and re-layouts  10.4 us (12%)
  other arithmetic  1.4 us (2%)
    pallas_call x1, Pallas kernels, shards(): pl.pallas_call(functools.partial(classify_kernel, rows=rows), out_shape=(...  25.2 us
    pallas_call x1, Pallas kernels, shards(): pl.pallas_call(functools.partial(composite_kernel, rows=rows), out_shape=...  20.5 us
    all_to_all x2, waiting for transfers between devices, exchange(): lax.all_to_all(pieces, 'depth', split_axis=0, concat_axis=0, tiled=True)  12.8 us
    all_to_all x2, starting transfers between devices, exchange(): lax.all_to_all(pieces, 'depth', split_axis=0, concat_axis=0, tiled=True)  11.2 us
    ppermute x1, starting transfers between devices, shards(): top_edge = lax.ppermute(volume[:, strip - 1], 'img', forward)  3.82 us
    unnamed x12, local copies, waits for them, and re-layouts  3.56 us
    slice x3, local copies, waits for them, and re-layouts, shards(): blocks[:EARLY]  2.7 us
    ppermute x1, starting transfers between devices, shards(): bottom_edge = lax.ppermute(volume[:, 0], 'img', backward)  2.02 us
  transfers between devices with their start and end apart: 4, of which 1 were waited for; matrix products, arithmetic and copies ran while one was open for 6% of the time, Pallas kernels for 29%

profile of v2, /device:TPU:64, one launch (start us, length us, event | category | flops | bytes accessed | tf_op | source)
XLA Modules:
  0.0 87.4 jit_solution(18354464610667478915)
XLA Ops:
  0.0 0.0 slice-start
  0.0 1.4 %slice-done = bf16[3,512,512]{2,1,0:T(8,128)(2,1)S(1)} async-done(((bf16[4,512,512]{2,1,0:T(8,128)(2,1)}), bf16[3,512,512]{2,1,0:T(8,128)(2,1)S(1)}, s32[]{:S(2)}) %slice-start) | async-done | bytes 1572888 | tf_op jit(solution)/shard_map/slice | solution.py:143
  1.4 1.3 %copy.8 = bf16[3,32,16,512]{3,2,0,1:T(8,128)(2,1)} copy(bf16[3,32,16,512]{3,2,1,0:T(8,128)(2,1)S(1)} %bitcast.28) | data formatting | bytes 3145728 | tf_op jit(solution)/shard_map/slice | solution.py:143
  2.7 7.3 %all-to-all-start = ((bf16[32,48,512]{2,1,0:T(8,128)(2,1)}), bf16[32,48,512]{2,1,0:T(8,128)(2,1)S(1)}, u32[]{:S(2)}, u32[]{:S(2)}) async-start(bf16[32,48,512]{2,1,0:T(8,128)(2,1)} %bitcast.2), calls=%async_computation | async-start | bytes 3145728 | tf_op jit(solution)/shard_map/all_to_all | solution.py:139
  10.0 0.8 fusion
  10.8 2.0 %collective-permute-start.1 = (bf16[4,512]{1,0:T(4,128)(2,1)S(1)}, bf16[4,512]{1,0:T(4,128)(2,1)S(1)}, u32[]{:S(2)}, u32[]{:S(2)}) collective-permute-start(bf16[4,512]{1,0:T(4,128)(2,1)S(1)} %bitcast.32), channel_id=1, source_target_pairs={{32,0},{64,32},{96,64},{33,1},{65,33},{97,65},{34,2},{66,34},{98,6... | collective-permute-start | bytes 12296 | tf_op jit(solution)/shard_map/ppermute | solution.py:148
  12.9 3.8 %collective-permute-start = (bf16[4,512]{1,0:T(4,128)(2,1)S(1)}, bf16[4,512]{1,0:T(4,128)(2,1)S(1)}, u32[]{:S(2)}, u32[]{:S(2)}) collective-permute-start(bf16[4,512]{1,0:T(4,128)(2,1)S(1)} %bitcast.33), channel_id=1, source_target_pairs={{0,32},{32,64},{64,96},{1,33},{33,65},{65,97},{2,34},{34,66},{66,9... | collective-permute-start | bytes 12296 | tf_op jit(solution)/shard_map/ppermute | solution.py:147
  16.7 1.9 %fusion.1 = (bf16[4,31,1,512]{3,2,1,0:T(2,128)(2,1)S(1)}, bf16[4,31,1,512]{3,2,1,0:T(2,128)(2,1)S(1)}) fusion(bf16[4,32,16,512]{3,2,1,0:T(8,128)(2,1)} %bitcast.27), kind=kLoop, calls=%fused_computation.10 | loop fusion | bytes 507904 | tf_op jit(solution)/shard_map/slice | solution.py:149
  18.7 0.1 copy_bitcast_fusion
  18.8 1.1 %slice.30 = bf16[1,512,512]{2,1,0:T(8,128)(2,1)S(1)} slice(bf16[4,512,512]{2,1,0:T(8,128)(2,1)} %param.4), slice={[3:4], [0:512], [0:512]} | slice | bytes 1048576 | tf_op jit(solution)/shard_map/slice | solution.py:153
  19.9 0.0 collective-permute-done.1
  19.9 0.1 maximum_bitcast_fusion.1
  20.0 0.0 collective-permute-done
  20.0 0.1 maximum_bitcast_fusion
  20.1 0.0 copy-start.3
  20.1 0.0 copy-start.4
  20.1 0.0 copy-start.2
  20.1 1.1 %pad_maximum_fusion = bf16[32,24,512]{2,1,0:T(8,128)(2,1)} fusion(bf16[32,4,512]{2,1,0:T(4,128)(2,1)S(1)} %maximum_bitcast_fusion.1, bf16[32,4,512]{2,1,0:T(4,128)(2,1)S(1)} %maximum_bitcast_fusion, bf16[32,16,512]{2,1,0:T(8,128)(2,1)S(1)} %bitcast.29), kind=kLoop, calls=%fused_computation | loop fusion | flops 2359296 | bytes 1572864 | tf_op jit(solution)/shard_map/concatenate | solution.py:152
  21.2 12.8 %all-to-all-done.early = bf16[32,48,512]{2,1,0:T(8,128)(2,1)S(1)} async-done(((bf16[32,48,512]{2,1,0:T(8,128)(2,1)}), bf16[32,48,512]{2,1,0:T(8,128)(2,1)S(1)}, u32[]{:S(2)}, u32[]{:S(2)}) %all-to-all-start) | async-done | bytes 1572896 | tf_op jit(solution)/shard_map/all_to_all | solution.py:139
  34.0 3.9 %all-to-all-start.1 = ((bf16[32,24,512]{2,1,0:T(8,128)(2,1)}), bf16[32,24,512]{2,1,0:T(8,128)(2,1)S(1)}, u32[]{:S(2)}, u32[]{:S(2)}) async-start(bf16[32,24,512]{2,1,0:T(8,128)(2,1)} %pad_maximum_fusion), calls=%async_computation.1 | async-start | bytes 1572864 | tf_op jit(solution)/shard_map/all_to_all | solution.py:139
  37.9 0.0 copy-done.3
  37.9 0.0 copy-done.4
  37.9 0.1 convert_multiply_fusion
  38.0 0.1 slice.36
  38.1 0.1 slice.35
  38.1 0.1 maximum_maximum_fusion
  38.2 0.0 copy-done.2
  38.2 25.2 %classify.1 = (f32[4,1536,512]{2,1,0:T(8,128)}, f32[1536,512]{1,0:T(8,128)S(1)}) custom-call(bf16[1536,512]{1,0:T(8,128)(2,1)S(1)} %bitcast.24, bf16[512,512]{1,0:T(8,128)(2,1)S(1)} %copy-done.2, f32[8,1,128]{2,1,0:T(1,128)S(1)} %bitcast.25), custom_call_target="tpu_custom_call" | custom-call | tf_op jit(solution)/shard_map/classify/pallas_call | solution.py:159
  63.4 0.0 copy-start
  63.4 1.6 %copy-done = f32[1536,512]{1,0:T(8,128)} copy-done((f32[1536,512]{1,0:T(8,128)}, f32[1536,512]{1,0:T(8,128)S(1)}, u32[]{:S(2)}) %copy-start) | copy-done | bytes 3145752
  65.0 0.0 all-to-all-done.1.late
  65.0 0.0 copy-start.1
  65.0 1.9 %copy-done.1 = f32[1536,512]{1,0:T(8,128)S(1)} copy-done((f32[1536,512]{1,0:T(8,128)S(1)}, f32[1536,512]{1,0:T(8,128)}, u32[]{:S(2)}) %copy-start.1) | copy-done | bytes 3145752
  66.9 20.5 %composite.1 = f32[4,8192]{1,0:T(4,128)} custom-call(bf16[32,48,512]{2,1,0:T(8,128)(2,1)S(1)} %all-to-all-done.early, bf16[32,24,512]{2,1,0:T(8,128)(2,1)S(1)} %all-to-all-done.1.late, f32[4,1536,512]{2,1,0:T(8,128)} %get-tuple-element.7.values, f32[1536,512]{1,0:T(8,128)S(1)} %copy-done.1, bf16[512,512]{1,0:T(8,128)(2,1)S(1)} %copy-done.2, ...), custom_call_target="tpu_custom_call" | custom-call | tf_op jit(solution)/shard_map/composite/pallas_call | solution.py:170
  (2 shorter events, 0.0 us)
Async XLA Ops:
  0.0 1.4 %slice-start = ((bf16[4,512,512]{2,1,0:T(8,128)(2,1)}), bf16[3,512,512]{2,1,0:T(8,128)(2,1)S(1)}, s32[]{:S(2)}) async-start(bf16[4,512,512]{2,1,0:T(8,128)(2,1)} %param.4), calls=%async_computation.2 | async-start | bytes 3145728 | tf_op jit(solution)/shard_map/slice | solution.py:143
  2.7 31.3 %all-to-all-start = ((bf16[32,48,512]{2,1,0:T(8,128)(2,1)}), bf16[32,48,512]{2,1,0:T(8,128)(2,1)S(1)}, u32[]{:S(2)}, u32[]{:S(2)}) async-start(bf16[32,48,512]{2,1,0:T(8,128)(2,1)} %bitcast.2), calls=%async_computation | async-start | bytes 3145728 | tf_op jit(solution)/shard_map/all_to_all | solution.py:139
  10.8 9.0 %collective-permute-start.1 = (bf16[4,512]{1,0:T(4,128)(2,1)S(1)}, bf16[4,512]{1,0:T(4,128)(2,1)S(1)}, u32[]{:S(2)}, u32[]{:S(2)}) collective-permute-start(bf16[4,512]{1,0:T(4,128)(2,1)S(1)} %bitcast.32), channel_id=1, source_target_pairs={{32,0},{64,32},{96,64},{33,1},{65,33},{97,65},{34,2},{66,34},{98,6... | collective-permute-start | bytes 12296 | tf_op jit(solution)/shard_map/ppermute | solution.py:148
  12.9 7.1 %collective-permute-start = (bf16[4,512]{1,0:T(4,128)(2,1)S(1)}, bf16[4,512]{1,0:T(4,128)(2,1)S(1)}, u32[]{:S(2)}, u32[]{:S(2)}) collective-permute-start(bf16[4,512]{1,0:T(4,128)(2,1)S(1)} %bitcast.33), channel_id=1, source_target_pairs={{0,32},{32,64},{64,96},{1,33},{33,65},{65,97},{2,34},{34,66},{66,9... | collective-permute-start | bytes 12296 | tf_op jit(solution)/shard_map/ppermute | solution.py:147
  20.1 17.8 %copy-start.3 = (bf16[4,128]{1,0:T(4,128)(2,1)S(1)}, bf16[4,128]{1,0:T(4,128)(2,1)}, u32[]{:S(2)}) copy-start(bf16[4,128]{1,0:T(4,128)(2,1)} %param.5) | copy-start | bytes 3076
  20.1 17.8 %copy-start.4 = (f32[4]{0:T(128)S(1)}, f32[4]{0:T(128)}, u32[]{:S(2)}) copy-start(f32[4]{0:T(128)} %constant.7) | copy-start | bytes 52
  20.1 18.1 %copy-start.2 = (bf16[512,512]{1,0:T(8,128)(2,1)S(1)}, bf16[512,512]{1,0:T(8,128)(2,1)}, u32[]{:S(2)}) copy-start(bf16[512,512]{1,0:T(8,128)(2,1)} %constant.5.clone.cols_op) | copy-start | bytes 1572868
  34.0 31.0 %all-to-all-start.1 = ((bf16[32,24,512]{2,1,0:T(8,128)(2,1)}), bf16[32,24,512]{2,1,0:T(8,128)(2,1)S(1)}, u32[]{:S(2)}, u32[]{:S(2)}) async-start(bf16[32,24,512]{2,1,0:T(8,128)(2,1)} %pad_maximum_fusion), calls=%async_computation.1 | async-start | bytes 1572864 | tf_op jit(solution)/shard_map/all_to_all | solution.py:139
  63.4 1.6 %copy-start = (f32[1536,512]{1,0:T(8,128)}, f32[1536,512]{1,0:T(8,128)S(1)}, u32[]{:S(2)}) copy-start(f32[1536,512]{1,0:T(8,128)S(1)} %get-tuple-element.8.dy_early) | copy-start | bytes 9437188
  65.0 1.9 %copy-start.1 = (f32[1536,512]{1,0:T(8,128)S(1)}, f32[1536,512]{1,0:T(8,128)}, u32[]{:S(2)}) copy-start(f32[1536,512]{1,0:T(8,128)} %copy-done) | copy-start | bytes 9437188

commit v3 on v1

v3 whole, which is shorter than its diff:
```python
import jax
import jax.numpy as jnp
import numpy as np
from jax import lax
from jax.experimental import pallas as pl
from jax.experimental.pallas import tpu as pltpu
from jax.sharding import PartitionSpec as P

F32 = jnp.float32
BF16 = jnp.bfloat16
BLOCK = 16
HALF = 8
LANES = 128
TINY = 1e-30


def row_differences(rows):
    local = np.arange(rows // 2)
    out = np.zeros((2, rows // 2, rows), np.float32)
    for parity in range(2):
        own = local // BLOCK * (2 * BLOCK) + parity * BLOCK + local % BLOCK
        for step in (1, -1):
            there = own + step
            keep = (there >= 0) & (there < rows)
            out[parity, local[keep], there[keep]] += step
    return out


def column_differences(cols):
    k = np.arange(cols)
    return (k[:, None] == k[None, :] + 1).astype(np.float32) - (
        k[:, None] == k[None, :] - 1
    ).astype(np.float32)


def look_up(table, index):
    return jnp.take_along_axis(table, index, axis=1, mode="promise_in_bounds")


def classify(centre, tabs):
    position = centre * float(tabs[0].shape[1] - 1)
    knot = position.astype(jnp.int32)
    part = position - knot.astype(F32)
    upper = part.astype(BF16).astype(F32)
    lower = (1.0 - part).astype(BF16).astype(F32)
    values = [
        lower * look_up(tabs[c], knot) + upper * look_up(tabs[c + 4], knot) for c in range(4)
    ]
    return values[:3] + [jnp.exp2(values[3])]


def spread(tables):
    return [jnp.broadcast_to(tables[i, 0:1], (HALF, tables.shape[2])) for i in range(8)]


def plane_terms(cells, z, parity, edge, core, rows_op, cols_op, slope, norm):
    blocks, cols = cells.shape[1], cells.shape[4]
    rows = blocks * BLOCK
    dx = jnp.dot(
        rows_op[parity], cells[z].reshape(2 * rows, cols), preferred_element_type=F32
    )
    dy = jnp.dot(
        cells[z, :, parity].reshape(rows, cols), cols_op[...], preferred_element_type=F32
    )
    slope[z] = 2.0 * dy + dx
    norm[z] = dx * dx + dy * dy
    halo = edge[z : z + 1, :].astype(F32)
    for at, sign in ((0, jnp.where(core == 0, -1.0, 0.0)), (rows - 1, jnp.where(core == 0, 0.0, 1.0))):
        dx_row = dx[at : at + 1] + halo * sign
        dy_row = dy[at : at + 1]
        slope[z, at : at + 1, :] = 2.0 * dy_row + dx_row
        norm[z, at : at + 1, :] = dx_row * dx_row + dy_row * dy_row


def own_kernel(core_ref, own, edge, rows_op, cols_op, tables, values, slope, norm):
    slices, blocks, _, _, cols = own.shape
    core = core_ref[0]
    for z in range(slices):
        plane_terms(own, z, core, edge, core, rows_op, cols_op, slope, norm)
    tabs = spread(tables)

    def block(b, carry):
        for z in range(slices):
            for half in range(0, BLOCK, HALF):
                here = pl.ds(pl.multiple_of(b * BLOCK + half, HALF), HALF)
                for start in range(0, cols, LANES):
                    lanes = slice(start, start + LANES)
                    centre = own[z, b, core, half : half + HALF, lanes].astype(F32)
                    found = classify(centre, tabs)
                    for c in range(4):
                        values[c, z, here, lanes] = found[c]
        return carry

    lax.fori_loop(0, blocks, block, 0)


def slab_kernel(
    core_ref, own, other, outer_own, outer_other, edge, rows_op, cols_op, tables,
    values, own_slope, own_norm, out, slope, norm,
):
    slices, blocks, _, _, cols = own.shape
    core = core_ref[0]
    front = core == 0
    for z in range(slices):
        plane_terms(other, z, core, edge, core, rows_op, cols_op, slope, norm)
    tabs = spread(tables)
    opacity_scale = tables[8, 0:1, 0:1]

    def shade(accum, transmit, dz, slope_xy, norm_xy, found):
        lambert = jnp.abs(2.0 * dz + slope_xy) * (0.7 / 6.0)
        shading = 0.3 + lambert * lax.rsqrt(0.25 * (dz * dz + norm_xy) + 0.01)
        gain = transmit * (1.0 - found[3]) * shading
        return [a + gain * v for a, v in zip(accum, found[:3])], transmit * found[3]

    def block(b, carry):
        for half in range(0, BLOCK, HALF):
            here = pl.ds(pl.multiple_of(b * BLOCK + half, HALF), HALF)
            rows = slice(half, half + HALF)
            for start in range(0, cols, LANES):
                lanes = slice(start, start + LANES)
                mine = [own[z, b, core, rows, lanes].astype(F32) for z in range(slices)]
                theirs = [other[z, b, core, rows, lanes].astype(F32) for z in range(slices)]
                end_own = outer_own[b, rows, lanes].astype(F32)
                end_other = outer_other[b, rows, lanes].astype(F32)
                stack = (
                    [jnp.where(front, end_own, theirs[-1])]
                    + mine
                    + [jnp.where(front, theirs[0], end_own)]
                )
                accum = [jnp.zeros((HALF, LANES), F32) for _ in range(3)]
                transmit = jnp.ones((HALF, LANES), F32)
                for z in range(slices):
                    found = [values[c, z, here, lanes] for c in range(4)]
                    accum, transmit = shade(
                        accum, transmit, stack[z + 2] - stack[z],
                        own_slope[z, here, lanes], own_norm[z, here, lanes], found,
                    )
                own_part = accum + [transmit]
                stack = (
                    [jnp.where(front, mine[-1], end_other)]
                    + theirs
                    + [jnp.where(front, end_other, mine[0])]
                )
                accum = [jnp.zeros((HALF, LANES), F32) for _ in range(3)]
                transmit = jnp.ones((HALF, LANES), F32)
                for z in range(slices):
                    accum, transmit = shade(
                        accum, transmit, stack[z + 2] - stack[z],
                        slope[z, here, lanes], norm[z, here, lanes], classify(theirs[z], tabs),
                    )
                other_part = accum + [transmit]
                near = [jnp.where(front, a, o) for a, o in zip(own_part, other_part)]
                far = [jnp.where(front, o, a) for a, o in zip(own_part, other_part)]
                for c in range(3):
                    at = c * BLOCK + half
                    out[b, at : at + HALF, lanes] = near[c] + near[3] * far[c]
                at = 3 * BLOCK + half
                out[b, at : at + HALF, lanes] = (1.0 - near[3] * far[3]) * opacity_scale
        return carry

    lax.fori_loop(0, blocks, block, 0)


def merge_kernel(scales, parts, out):
    cols = parts.shape[2]
    for start in range(0, cols, LANES):
        lanes = slice(start, start + LANES)
        accum = [jnp.zeros((BLOCK, LANES), F32) for _ in range(3)]
        transmit = jnp.ones((BLOCK, LANES), F32)
        for s in range(parts.shape[0]):
            for c in range(3):
                accum[c] = accum[c] + transmit * parts[s, c * BLOCK : (c + 1) * BLOCK, lanes]
            opacity = parts[s, 3 * BLOCK : 4 * BLOCK, lanes] * scales[1]
            transmit = transmit - transmit * opacity
        image = [a * scales[0] for a in accum] + [1.0 - transmit]
        for c in range(4):
            for r in range(BLOCK):
                at = r * cols + start
                out[c : c + 1, at : at + LANES] = image[c][r : r + 1]


def shards(volume, transfer_table):
    slices, rows, cols = volume.shape
    depth_count = lax.axis_size("depth")
    img_count = lax.axis_size("img")
    chips = depth_count // 2
    depth_total = slices * depth_count
    entries = transfer_table.shape[1]
    blocks = rows // (2 * BLOCK)
    core = lax.axis_index("depth") % 2

    def shift(x, img_step, depth_step):
        pairs = []
        for i in range(img_count):
            for d in range(depth_count):
                to_i, to_d = i + img_step(d % 2), d + depth_step(d % 2)
                if 0 <= to_i < img_count and 0 <= to_d < depth_count:
                    pairs.append((i * depth_count + d, to_i * depth_count + to_d))
        return lax.ppermute(x, ("img", "depth"), pairs)

    edge_same = lax.dynamic_index_in_dim(volume, (rows - 1) * (1 - core), 1, False)
    edge_cross = lax.dynamic_index_in_dim(volume, (rows - 1) * core, 1, False)
    edge_own = shift(edge_same, lambda c: -1 if c else 1, lambda c: 0)
    edge_other = shift(edge_cross, lambda c: 1 if c else -1, lambda c: -1 if c else 1)
    plane = lax.dynamic_index_in_dim(volume, (slices - 1) * core, 0, False)
    plane = plane.reshape(blocks, 2, BLOCK, cols)
    to_other_core = lax.dynamic_index_in_dim(plane, 1 - core, 1, False)
    to_same_core = lax.dynamic_index_in_dim(plane, core, 1, False)
    outer_own = shift(to_other_core, lambda c: 0, lambda c: 1 if c else -1)
    outer_other = shift(to_same_core, lambda c: 0, lambda c: 2 if c else -2)
    other = lax.ppermute(volume, "depth", [(d, d ^ 1) for d in range(depth_count)])

    table = transfer_table.astype(F32)
    colour_top = jnp.maximum(jnp.max(table[0:3]), TINY)
    opacity_top = jnp.maximum(jnp.max(table[3]) * (2.0 * slices / depth_total), TINY)
    factor = jnp.concatenate(
        [
            jnp.full((3, 1), 1.0 / (colour_top * opacity_top), F32),
            jnp.full((1, 1), -np.log2(np.e) / depth_total, F32),
        ]
    )
    lower = table * factor
    upper = jnp.concatenate([lower[:, 1:], lower[:, -1:]], axis=1)
    scale_row = jnp.full((1, entries), 1.0 / opacity_top, F32)
    tables = jnp.concatenate([lower, upper, scale_row])[:, None, :]
    scales = jnp.stack([colour_top * opacity_top, opacity_top])

    split = (slices, blocks, 2, BLOCK, cols)
    own_view, other_view = volume.reshape(split), other.reshape(split)
    rows_op = jnp.asarray(row_differences(rows), BF16)
    cols_op = jnp.asarray(column_differences(cols), BF16)
    core_arg = core.astype(jnp.int32).reshape(1)
    same_core = [[2 * j + c for j in range(chips)] for c in range(2)]
    vmem = pl.BlockSpec(memory_space=pltpu.MemorySpace.VMEM)
    smem = pl.BlockSpec(memory_space=pltpu.MemorySpace.SMEM)
    half = rows // 2
    values, own_slope, own_norm = pl.pallas_call(
        own_kernel,
        out_shape=(
            jax.ShapeDtypeStruct((4, slices, half, cols), F32),
            jax.ShapeDtypeStruct((slices, half, cols), F32),
            jax.ShapeDtypeStruct((slices, half, cols), F32),
        ),
        in_specs=[smem] + [vmem] * 5,
        out_specs=(vmem,) * 3,
        compiler_params=pltpu.CompilerParams(vmem_limit_bytes=20 << 20),
        name="own",
    )(core_arg, own_view, edge_own, rows_op, cols_op, tables)
    partial_image = pl.pallas_call(
        slab_kernel,
        out_shape=jax.ShapeDtypeStruct((blocks, 4 * BLOCK, cols), F32),
        in_specs=[smem] + [vmem] * 11,
        out_specs=vmem,
        scratch_shapes=[pltpu.VMEM((slices, half, cols), F32)] * 2,
        compiler_params=pltpu.CompilerParams(vmem_limit_bytes=20 << 20),
        name="slab",
    )(
        core_arg, own_view, other_view, outer_own, outer_other, edge_other,
        rows_op, cols_op, tables, values, own_slope, own_norm,
    )
    pieces = lax.all_to_all(
        partial_image.astype(jnp.float16), "depth", split_axis=0, concat_axis=0, tiled=True,
        axis_index_groups=same_core,
    )
    return pl.pallas_call(
        merge_kernel,
        out_shape=jax.ShapeDtypeStruct((4, BLOCK * cols), F32),
        in_specs=[smem, vmem],
        out_specs=vmem,
        name="merge",
    )(scales, pieces.astype(F32))


def solution(mesh):
    placed = (P("depth", "img", None), P())
    return jax.shard_map(
        shards, mesh=mesh, in_specs=placed, out_specs=P(None, ("img", "depth")), check_vma=False
    )
```

time: 84 us -> 69.4 us (0.83)
  starting transfers between devices: 28.9 us -> 21.5 us
  Pallas kernels: 28.4 us -> 21.4 us
  waiting for transfers between devices: 11.3 us -> 15.2 us
  other arithmetic: 6.98 us -> 4.9 us
  local copies, waits for them, and re-layouts: 5.96 us -> 4.31 us
    pallas_call x2, Pallas kernels: 26 us -> 18.9 us  [the longest x1 10.3 us: shards(): pl.pallas_call(slab_kernel, out_shape=jax.ShapeDtypeStruct((blocks, 4 * B...]
    all_to_all x2 -> x1, waiting for transfers between devices: 8.68 us -> 15.2 us  [shards(): lax.all_to_all(partial_image.astype(jnp.float16), 'depth', split_axis=0,...]
    all_to_all x2 -> x1, starting transfers between devices: 14.9 us -> 8.63 us  [shards(): lax.all_to_all(partial_image.astype(jnp.float16), 'depth', split_axis=0,...]
    ppermute x4, waiting for transfers between devices: 2.66 us -> 0.01 us  [shift(): return lax.ppermute(x, ('img', 'depth'), pairs)]
    convert_element_type x4 -> x2, other arithmetic: 5.05 us -> 2.84 us  [the longest x1 1.61 us: shards(): pieces.astype(F32)]
    unnamed x18 -> x12, local copies, waits for them, and re-layouts: 3.74 us -> 2.1 us
    ppermute x4, starting transfers between devices: 12.6 us -> 11.5 us  [shift(): return lax.ppermute(x, ('img', 'depth'), pairs)]
  transfers between devices with their start and end apart: 7 -> 6, of which waited for: 2 -> 1; matrix products, arithmetic and copies ran while one was open for 9% -> 6% of each run, Pallas kernels for 16% -> 12%
where the time goes in v3:
time: 69.4 us; the launch traced here: 68.9 us
  starting transfers between devices  21.5 us (31%)
  Pallas kernels  21.4 us (31%)
  waiting for transfers between devices  15.2 us (22%)
  other arithmetic  4.9 us (7%)
  local copies, waits for them, and re-layouts  4.31 us (6%)
  between operations  1.56 us (2%)
    all_to_all x1, waiting for transfers between devices, shards(): lax.all_to_all(partial_image.astype(jnp.float16), 'depth', split_axis=0,...  15.2 us
    ppermute x4, starting transfers between devices, shift(): return lax.ppermute(x, ('img', 'depth'), pairs)  11.5 us
    pallas_call x1, Pallas kernels, shards(): pl.pallas_call(slab_kernel, out_shape=jax.ShapeDtypeStruct((blocks, 4 * B...  10.3 us
    all_to_all x1, starting transfers between devices, shards(): lax.all_to_all(partial_image.astype(jnp.float16), 'depth', split_axis=0,...  8.63 us
    pallas_call x1, Pallas kernels, shards(): pl.pallas_call(own_kernel, out_shape=(jax.ShapeDtypeStruct((4, slices, ha...  8.56 us
    pallas_call x1, Pallas kernels, shards(): pl.pallas_call(merge_kernel, out_shape=jax.ShapeDtypeStruct((4, BLOCK * c...  2.54 us
    unnamed x12, local copies, waits for them, and re-layouts  2.1 us
    convert_element_type x1, other arithmetic, shards(): pieces.astype(F32)  1.61 us
  transfers between devices with their start and end apart: 6, of which 1 were waited for; matrix products, arithmetic and copies ran while one was open for 6% of the time, Pallas kernels for 12%

profile of v3, /device:TPU:1, one launch (start us, length us, event | category | flops | bytes accessed | tf_op | source)
XLA Modules:
  0.0 68.9 jit_solution(6111263301060229679)
XLA Ops:
  0.0 0.0 copy-start
  0.0 0.0 copy-start.4
  0.0 1.4 %collective-permute-start = (bf16[4,512,512]{2,1,0:T(8,128)(2,1)}, bf16[4,512,512]{2,1,0:T(8,128)(2,1)}, u32[]{:S(2)}, u32[]{:S(2)}) collective-permute-start(bf16[4,512,512]{2,1,0:T(8,128)(2,1)} %param.4), channel_id=1, source_target_pairs={{0,1},{1,0},{2,3},{3,2},{4,5},{5,4},{6,7},{7,6},{8,9},{9,8},{10,11... | collective-permute-start | bytes 6291464 | tf_op jit(solution)/shard_map/ppermute | solution.py:211
  1.4 0.8 %constant_dynamic-slice_fusion = (bf16[4,1,512]{2,1,0:T(2,128)(2,1)S(1)}, bf16[4,1,512]{2,1,0:T(2,128)(2,1)S(1)}) fusion(bf16[4,512,512]{2,1,0:T(8,128)(2,1)} %param.4, s32[]{:T(128)S(6)} %select_n.30, s32[]{:T(128)S(6)} %select_n.29), kind=kLoop, calls=%fused_computation.6 | loop fusion | bytes 16392 | tf_op jit(solution)/shard_map/jit(dynamic_index_in_dim)/dynamic_slice | solution.py:201
  2.2 3.7 %collective-permute-start.3 = (bf16[4,512]{1,0:T(4,128)(2,1)S(1)}, bf16[4,512]{1,0:T(4,128)(2,1)S(1)}, u32[]{:S(2)}, u32[]{:S(2)}) collective-permute-start(bf16[4,512]{1,0:T(4,128)(2,1)S(1)} %bitcast.22), channel_id=1, source_target_pairs={{1,32},{3,34},{5,36},{7,38},{9,40},{11,42},{13,44},{15,46},{17,48}... | collective-permute-start | bytes 12296 | tf_op jit(solution)/shard_map/ppermute | solution.py:199
  6.0 1.3 %collective-permute-start.4 = (bf16[4,512]{1,0:T(4,128)(2,1)S(1)}, bf16[4,512]{1,0:T(4,128)(2,1)S(1)}, u32[]{:S(2)}, u32[]{:S(2)}) collective-permute-start(bf16[4,512]{1,0:T(4,128)(2,1)S(1)} %bitcast.23), channel_id=1, source_target_pairs={{0,32},{2,34},{4,36},{6,38},{8,40},{10,42},{12,44},{14,46},{16,48}... | collective-permute-start | bytes 12296 | tf_op jit(solution)/shard_map/ppermute | solution.py:199
  7.3 1.1 %constant_dynamic-slice_fusion.2 = bf16[1,512,512]{2,1,0:T(8,128)(2,1)S(1)} fusion(bf16[4,512,512]{2,1,0:T(8,128)(2,1)} %param.4, s32[]{:T(128)S(6)} %select_n.26), kind=kLoop, calls=%fused_computation.8 | loop fusion | bytes 1048580 | tf_op jit(solution)/shard_map/jit(dynamic_index_in_dim)/dynamic_slice | solution.py:205
  8.4 3.1 %collective-permute-start.2 = (bf16[16,16,512]{2,1,0:T(8,128)(2,1)S(1)}, bf16[16,16,512]{2,1,0:T(8,128)(2,1)S(1)}, u32[]{:S(2)}, u32[]{:S(2)}) collective-permute-start(bf16[16,16,512]{2,1,0:T(8,128)(2,1)S(1)} %get-tuple-element.13), channel_id=1, source_target_pairs={{1,3},{2,0},{3,5},{4,2},{5,7},{6,4},{7,9},{8,6},{9,11},{10,8},{11,... | collective-permute-start | bytes 786440 | tf_op jit(solution)/shard_map/ppermute | solution.py:199
  11.5 3.3 %collective-permute-start.1 = (bf16[16,16,512]{2,1,0:T(8,128)(2,1)S(1)}, bf16[16,16,512]{2,1,0:T(8,128)(2,1)S(1)}, u32[]{:S(2)}, u32[]{:S(2)}) collective-permute-start(bf16[16,16,512]{2,1,0:T(8,128)(2,1)S(1)} %get-tuple-element.14), channel_id=1, source_target_pairs={{1,2},{2,1},{3,4},{4,3},{5,6},{6,5},{7,8},{8,7},{9,10},{10,9},{11,... | collective-permute-start | bytes 786440 | tf_op jit(solution)/shard_map/ppermute | solution.py:199
  14.9 0.0 copy-done.4
  14.9 0.6 slice_reduce_fusion.1
  16.2 0.7 slice_reduce_fusion
  17.5 0.1 pad_bitcast_fusion
  17.6 0.1 broadcast_multiply_fusion
  17.7 0.1 slice.15
  17.8 0.1 slice.14
  17.8 0.1 pad.4.clone
  17.9 0.1 maximum_maximum_fusion
  18.0 0.0 collective-permute-done.4.edge
  18.0 0.0 copy-done
  18.0 0.0 copy-start.1
  18.0 1.0 %copy-done.1 = bf16[512,512]{1,0:T(8,128)(2,1)S(1)} copy-done((bf16[512,512]{1,0:T(8,128)(2,1)S(1)}, bf16[512,512]{1,0:T(8,128)(2,1)}, u32[]{:S(2)}) %copy-start.1) | copy-done | bytes 524312
  19.1 0.0 copy-start.3
  19.1 1.0 %copy-done.3 = bf16[2,256,512]{2,1,0:T(8,128)(2,1)S(1)} copy-done((bf16[2,256,512]{2,1,0:T(8,128)(2,1)S(1)}, bf16[2,256,512]{2,1,0:T(8,128)(2,1)}, u32[]{:S(2)}) %copy-start.3) | copy-done | bytes 524312
  20.1 0.0 copy-start.2
  20.1 8.6 %own.1 = (f32[4,4,256,512]{3,2,1,0:T(8,128)S(1)}, f32[4,256,512]{2,1,0:T(8,128)S(1)}, f32[4,256,512]{2,1,0:T(8,128)S(1)}) custom-call(s32[1]{0:T(128)} %bitcast.2.core_ref, bf16[4,16,2,16,512]{4,3,2,1,0:T(8,128)(2,1)S(1)} %bitcast.19, bf16[4,512]{1,0:T(4,128)(2,1)S(1)} %collective-permute-done.4.edge, bf16[2,256,512]{2,1,0:T(8,128)(2,1)S(1)} %copy-done.3, ...), custom_call_target="tpu_custom_call" | custom-call | tf_op jit(solution)/shard_map/own/pallas_call | solution.py:237
  28.7 0.0 collective-permute-done.3.edge
  28.7 0.0 collective-permute-done.2.outer_other
  28.7 0.0 collective-permute-done.1.outer_own
  28.7 0.0 collective-permute-done
  28.7 0.0 copy-done.2
  28.7 10.3 %slab.1 = f32[16,64,512]{2,1,0:T(8,128)S(1)} custom-call(s32[1]{0:T(128)} %bitcast.2.core_ref, bf16[4,16,2,16,512]{4,3,2,1,0:T(8,128)(2,1)S(1)} %bitcast.20, bf16[4,16,2,16,512]{4,3,2,1,0:T(8,128)(2,1)} %bitcast.4.other, bf16[16,16,512]{2,1,0:T(8,128)(2,1)S(1)} %collective-permute-done.1.outer_own, ...), custom_call_target="tpu_custom_call" | custom-call | tf_op jit(solution)/shard_map/slab/pallas_call | solution.py:249
  39.1 1.2 %convert_element_type.10 = f16[16,64,512]{2,1,0:T(8,128)(2,1)} convert(f32[16,64,512]{2,1,0:T(8,128)S(1)} %slab.1) | non-fusion elementwise | flops 524288 | bytes 3145728 | tf_op jit(solution)/shard_map/convert_element_type | solution.py:262
  40.3 8.6 %all-to-all-start = ((f16[16,64,512]{2,1,0:T(8,128)(2,1)}), f16[16,64,512]{2,1,0:T(8,128)(2,1)S(1)}, u32[]{:S(2)}, u32[]{:S(2)}) async-start(f16[16,64,512]{2,1,0:T(8,128)(2,1)} %convert_element_type.10), calls=%async_computation | async-start | bytes 2097152 | tf_op jit(solution)/shard_map/all_to_all | solution.py:261
  48.9 0.7 pad_maximum_fusion.scales
  49.6 15.2 %all-to-all-done = f16[16,64,512]{2,1,0:T(8,128)(2,1)S(1)} async-done(((f16[16,64,512]{2,1,0:T(8,128)(2,1)}), f16[16,64,512]{2,1,0:T(8,128)(2,1)S(1)}, u32[]{:S(2)}, u32[]{:S(2)}) %all-to-all-start) | async-done | bytes 1048608 | tf_op jit(solution)/shard_map/all_to_all | solution.py:261
  64.8 1.6 %convert_element_type.11.parts = f32[16,64,512]{2,1,0:T(8,128)} convert(f16[16,64,512]{2,1,0:T(8,128)(2,1)S(1)} %all-to-all-done) | non-fusion elementwise | flops 524288 | bytes 3145728 | tf_op jit(solution)/shard_map/convert_element_type | solution.py:271
  66.4 2.5 %merge.1 = f32[4,8192]{1,0:T(4,128)} custom-call(f32[2]{0:T(128)} %pad_maximum_fusion.scales, f32[16,64,512]{2,1,0:T(8,128)} %convert_element_type.11.parts), custom_call_target="tpu_custom_call" | custom-call | tf_op jit(solution)/shard_map/merge/pallas_call | solution.py:265
  (5 shorter events, 0.1 us)
Async XLA Ops:
  0.0 18.0 %copy-start = (bf16[4,512,512]{2,1,0:T(8,128)(2,1)S(1)}, bf16[4,512,512]{2,1,0:T(8,128)(2,1)}, u32[]{:S(2)}) copy-start(bf16[4,512,512]{2,1,0:T(8,128)(2,1)} %param.4) | copy-start | bytes 6291460
  0.0 14.9 %copy-start.4 = (bf16[4,128]{1,0:T(4,128)(2,1)S(1)}, bf16[4,128]{1,0:T(4,128)(2,1)}, u32[]{:S(2)}) copy-start(bf16[4,128]{1,0:T(4,128)(2,1)} %param.5) | copy-start | bytes 3076
  0.0 28.7 %collective-permute-start = (bf16[4,512,512]{2,1,0:T(8,128)(2,1)}, bf16[4,512,512]{2,1,0:T(8,128)(2,1)}, u32[]{:S(2)}, u32[]{:S(2)}) collective-permute-start(bf16[4,512,512]{2,1,0:T(8,128)(2,1)} %param.4), channel_id=1, source_target_pairs={{0,1},{1,0},{2,3},{3,2},{4,5},{5,4},{6,7},{7,6},{8,9},{9,8},{10,11... | collective-permute-start | bytes 6291464 | tf_op jit(solution)/shard_map/ppermute | solution.py:211
  2.2 26.4 %collective-permute-start.3 = (bf16[4,512]{1,0:T(4,128)(2,1)S(1)}, bf16[4,512]{1,0:T(4,128)(2,1)S(1)}, u32[]{:S(2)}, u32[]{:S(2)}) collective-permute-start(bf16[4,512]{1,0:T(4,128)(2,1)S(1)} %bitcast.22), channel_id=1, source_target_pairs={{1,32},{3,34},{5,36},{7,38},{9,40},{11,42},{13,44},{15,46},{17,48}... | collective-permute-start | bytes 12296 | tf_op jit(solution)/shard_map/ppermute | solution.py:199
  6.0 12.0 %collective-permute-start.4 = (bf16[4,512]{1,0:T(4,128)(2,1)S(1)}, bf16[4,512]{1,0:T(4,128)(2,1)S(1)}, u32[]{:S(2)}, u32[]{:S(2)}) collective-permute-start(bf16[4,512]{1,0:T(4,128)(2,1)S(1)} %bitcast.23), channel_id=1, source_target_pairs={{0,32},{2,34},{4,36},{6,38},{8,40},{10,42},{12,44},{14,46},{16,48}... | collective-permute-start | bytes 12296 | tf_op jit(solution)/shard_map/ppermute | solution.py:199
  8.4 20.3 %collective-permute-start.2 = (bf16[16,16,512]{2,1,0:T(8,128)(2,1)S(1)}, bf16[16,16,512]{2,1,0:T(8,128)(2,1)S(1)}, u32[]{:S(2)}, u32[]{:S(2)}) collective-permute-start(bf16[16,16,512]{2,1,0:T(8,128)(2,1)S(1)} %get-tuple-element.13), channel_id=1, source_target_pairs={{1,3},{2,0},{3,5},{4,2},{5,7},{6,4},{7,9},{8,6},{9,11},{10,8},{11,... | collective-permute-start | bytes 786440 | tf_op jit(solution)/shard_map/ppermute | solution.py:199
  11.5 17.1 %collective-permute-start.1 = (bf16[16,16,512]{2,1,0:T(8,128)(2,1)S(1)}, bf16[16,16,512]{2,1,0:T(8,128)(2,1)S(1)}, u32[]{:S(2)}, u32[]{:S(2)}) collective-permute-start(bf16[16,16,512]{2,1,0:T(8,128)(2,1)S(1)} %get-tuple-element.14), channel_id=1, source_target_pairs={{1,2},{2,1},{3,4},{4,3},{5,6},{6,5},{7,8},{8,7},{9,10},{10,9},{11,... | collective-permute-start | bytes 786440 | tf_op jit(solution)/shard_map/ppermute | solution.py:199
  18.0 1.0 %copy-start.1 = (bf16[512,512]{1,0:T(8,128)(2,1)S(1)}, bf16[512,512]{1,0:T(8,128)(2,1)}, u32[]{:S(2)}) copy-start(bf16[512,512]{1,0:T(8,128)(2,1)} %constant.56.clone.cols_op) | copy-start | bytes 1572868
  19.1 1.0 %copy-start.3 = (bf16[2,256,512]{2,1,0:T(8,128)(2,1)S(1)}, bf16[2,256,512]{2,1,0:T(8,128)(2,1)}, u32[]{:S(2)}) copy-start(bf16[2,256,512]{2,1,0:T(8,128)(2,1)} %constant.55.clone.rows_op) | copy-start | bytes 1572868
  20.1 8.6 %copy-start.2 = (bf16[512,512]{1,0:T(8,128)(2,1)S(1)}, bf16[512,512]{1,0:T(8,128)(2,1)}, u32[]{:S(2)}) copy-start(bf16[512,512]{1,0:T(8,128)(2,1)} %constant.56.clone.cols_op) | copy-start | bytes 1572868
  40.3 24.5 %all-to-all-start = ((f16[16,64,512]{2,1,0:T(8,128)(2,1)}), f16[16,64,512]{2,1,0:T(8,128)(2,1)S(1)}, u32[]{:S(2)}, u32[]{:S(2)}) async-start(f16[16,64,512]{2,1,0:T(8,128)(2,1)} %convert_element_type.10), calls=%async_computation | async-start | bytes 2097152 | tf_op jit(solution)/shard_map/all_to_all | solution.py:261

commit v4 on v3

v4 whole, which is shorter than its diff:
```python
import functools

import jax
import jax.numpy as jnp
import numpy as np
from jax import lax
from jax.experimental import pallas as pl
from jax.experimental.pallas import tpu as pltpu
from jax.sharding import PartitionSpec as P

F32 = jnp.float32
BF16 = jnp.bfloat16
BLOCK = 16
HALF = 8
LANES = 128
TINY = 1e-30


def row_differences(rows, core):
    shape = (rows // 2, rows)
    local = lax.broadcasted_iota(jnp.int32, shape, 0)
    there = lax.broadcasted_iota(jnp.int32, shape, 1)
    step = there - (local + (local & -BLOCK) + core * BLOCK)
    return jnp.where(step == 1, 1.0, jnp.where(step == -1, -1.0, 0.0)).astype(BF16)


def column_differences(cols):
    step = lax.broadcasted_iota(jnp.int32, (cols, cols), 0) - lax.broadcasted_iota(
        jnp.int32, (cols, cols), 1
    )
    return jnp.where(step == 1, 1.0, jnp.where(step == -1, -1.0, 0.0)).astype(BF16)


def tops(table, slab_share):
    colour = jnp.max(jnp.max(table[0:3], axis=0, keepdims=True), axis=1, keepdims=True)
    extinction = jnp.max(table[3:4], axis=1, keepdims=True)
    return jnp.maximum(colour, TINY), jnp.maximum(extinction * slab_share, TINY)


def spread(table, slab_share, depth_total):
    entries = table.shape[1]
    colour_top, opacity_top = tops(table, slab_share)
    scale = 1.0 / (colour_top * opacity_top)
    lower = [table[c : c + 1] * scale for c in range(3)]
    lower.append(table[3:4] * float(-np.log2(np.e) / depth_total))
    lower = [jnp.broadcast_to(t, (HALF, entries)) for t in lower]
    last = lax.broadcasted_iota(jnp.int32, (HALF, entries), 1) == entries - 1
    upper = [jnp.where(last, t, pltpu.roll(t, entries - 1, 1)) for t in lower]
    return lower + upper


def look_up(table, index):
    return jnp.take_along_axis(table, index, axis=1, mode="promise_in_bounds")


def classify(centre, tabs):
    position = centre * float(tabs[0].shape[1] - 1)
    knot = position.astype(jnp.int32)
    part = position - knot.astype(F32)
    upper = part.astype(BF16).astype(F32)
    lower = (1.0 - part).astype(BF16).astype(F32)
    values = [
        lower * look_up(tabs[c], knot) + upper * look_up(tabs[c + 4], knot) for c in range(4)
    ]
    return values[:3] + [jnp.exp2(values[3])]


def plane_terms(cells, z, edge, core, rows_op, cols_op, slope, norm):
    blocks, cols = cells.shape[1], cells.shape[4]
    rows = blocks * BLOCK
    dx = jnp.dot(rows_op[...], cells[z].reshape(2 * rows, cols), preferred_element_type=F32)
    dy = jnp.dot(
        cells[z, :, core].reshape(rows, cols), cols_op[...], preferred_element_type=F32
    )
    slope[z] = 2.0 * dy + dx
    norm[z] = dx * dx + dy * dy
    halo = edge[z : z + 1, :].astype(F32)
    top, bottom = jnp.where(core == 0, -1.0, 0.0), jnp.where(core == 0, 0.0, 1.0)
    for at, sign in ((0, top), (rows - 1, bottom)):
        dx_row = dx[at : at + 1] + halo * sign
        dy_row = dy[at : at + 1]
        slope[z, at : at + 1, :] = 2.0 * dy_row + dx_row
        norm[z, at : at + 1, :] = dx_row * dx_row + dy_row * dy_row


def shade(accum, transmit, dz, slope_xy, norm_xy, found):
    lambert = jnp.abs(2.0 * dz + slope_xy) * (0.7 / 6.0)
    shading = 0.3 + lambert * lax.rsqrt(0.25 * (dz * dz + norm_xy) + 0.01)
    gain = transmit * (1.0 - found[3]) * shading
    return [a + gain * v for a, v in zip(accum, found[:3])], transmit * found[3]


def over(near, far):
    return [n + near[3] * f for n, f in zip(near[:3], far[:3])] + [near[3] * far[3]]


def nothing():
    return [jnp.zeros((HALF, LANES), F32)] * 3, jnp.ones((HALF, LANES), F32)


def own_kernel(
    core_ref, own, edge, table, first, last, middle, slope, norm, rows_op, cols_op,
    *, slab_share, depth_total,
):
    slices, blocks, _, _, cols = own.shape
    core = core_ref[0]
    rows_op[...] = row_differences(2 * blocks * BLOCK, core)
    cols_op[...] = column_differences(cols)
    for z in range(slices):
        plane_terms(own, z, edge, core, rows_op, cols_op, slope, norm)
    tabs = spread(table[...].astype(F32), slab_share, depth_total)

    def block(b, carry):
        for half in range(0, BLOCK, HALF):
            here = pl.ds(pl.multiple_of(b * BLOCK + half, HALF), HALF)
            rows = slice(half, half + HALF)
            for start in range(0, cols, LANES):
                lanes = slice(start, start + LANES)
                mine = [own[z, b, core, rows, lanes].astype(F32) for z in range(slices)]
                accum, transmit = nothing()
                for z in range(slices):
                    found = classify(mine[z], tabs)
                    if z in (0, slices - 1):
                        ref = last if z else first
                        for c in range(4):
                            ref[c, here, lanes] = found[c]
                    else:
                        accum, transmit = shade(
                            accum, transmit, mine[z + 1] - mine[z - 1],
                            slope[z, here, lanes], norm[z, here, lanes], found,
                        )
                for c in range(3):
                    middle[c, here, lanes] = accum[c]
                middle[3, here, lanes] = transmit
        return carry

    lax.fori_loop(0, blocks, block, 0)


def slab_kernel(
    core_ref, own, other, outer_own, outer_other, edge, table,
    first, last, middle, own_slope, own_norm, rows_op, cols_op, out, slope, norm,
    *, slab_share, depth_total,
):
    slices, blocks, _, _, cols = own.shape
    core = core_ref[0]
    front = core == 0
    for z in range(slices):
        plane_terms(other, z, edge, core, rows_op, cols_op, slope, norm)
    table_values = table[...].astype(F32)
    tabs = spread(table_values, slab_share, depth_total)
    opacity_scale = 1.0 / tops(table_values, slab_share)[1]

    def block(b, carry):
        for half in range(0, BLOCK, HALF):
            here = pl.ds(pl.multiple_of(b * BLOCK + half, HALF), HALF)
            rows = slice(half, half + HALF)
            for start in range(0, cols, LANES):
                lanes = slice(start, start + LANES)
                mine = [own[z, b, core, rows, lanes].astype(F32) for z in range(slices)]
                theirs = [other[z, b, core, rows, lanes].astype(F32) for z in range(slices)]
                end_own = outer_own[b, rows, lanes].astype(F32)
                end_other = outer_other[b, rows, lanes].astype(F32)

                def one(found, dz, z):
                    accum, transmit = shade(
                        *nothing(), dz, own_slope[z, here, lanes], own_norm[z, here, lanes],
                        [found[c, here, lanes] for c in range(4)],
                    )
                    return accum + [transmit]

                end = slices - 1
                own_part = over(
                    one(first, mine[1] - jnp.where(front, end_own, theirs[end]), 0),
                    over(
                        [middle[c, here, lanes] for c in range(4)],
                        one(last, jnp.where(front, theirs[0], end_own) - mine[end - 1], end),
                    ),
                )
                stack = (
                    [jnp.where(front, mine[end], end_other)]
                    + theirs
                    + [jnp.where(front, end_other, mine[0])]
                )
                accum, transmit = nothing()
                for z in range(slices):
                    accum, transmit = shade(
                        accum, transmit, stack[z + 2] - stack[z],
                        slope[z, here, lanes], norm[z, here, lanes], classify(theirs[z], tabs),
                    )
                other_part = accum + [transmit]
                near = [jnp.where(front, a, o) for a, o in zip(own_part, other_part)]
                far = [jnp.where(front, o, a) for a, o in zip(own_part, other_part)]
                both = over(near, far)
                both[3] = (1.0 - both[3]) * opacity_scale
                for c in range(4):
                    at = c * BLOCK + half
                    out[b, at : at + HALF, lanes] = both[c]
        return carry

    lax.fori_loop(0, blocks, block, 0)


def merge_kernel(parts, table, out, image, *, slab_share):
    cols = parts.shape[2]
    colour_top, opacity_top = tops(table[...].astype(F32), slab_share)
    for half in range(0, BLOCK, HALF):
        for start in range(0, cols, LANES):
            lanes = slice(start, start + LANES)
            accum, transmit = nothing()
            for s in range(parts.shape[0]):
                part = [
                    parts[s, c * BLOCK + half : c * BLOCK + half + HALF, lanes] for c in range(4)
                ]
                accum = [a + transmit * p for a, p in zip(accum, part[:3])]
                transmit = transmit - transmit * (part[3] * opacity_top)
            whole = [a * (colour_top * opacity_top) for a in accum] + [1.0 - transmit]
            for c in range(4):
                at = start // LANES, slice(c * BLOCK + half, c * BLOCK + half + HALF)
                image[at] = whole[c]
    for r in range(BLOCK):
        for start in range(0, cols, LANES):
            out[:, r * cols + start : r * cols + start + LANES] = image[
                start // LANES, pl.ds(r, 4, stride=BLOCK)
            ]


def shards(volume, transfer_table):
    slices, rows, cols = volume.shape
    depth_count = lax.axis_size("depth")
    img_count = lax.axis_size("img")
    chips = depth_count // 2
    depth_total = slices * depth_count
    blocks = rows // (2 * BLOCK)
    core = lax.axis_index("depth") % 2

    def shift(x, img_step, depth_step):
        pairs = []
        for i in range(img_count):
            for d in range(depth_count):
                to_i, to_d = i + img_step(d % 2), d + depth_step(d % 2)
                if 0 <= to_i < img_count and 0 <= to_d < depth_count:
                    pairs.append((i * depth_count + d, to_i * depth_count + to_d))
        return lax.ppermute(x, ("img", "depth"), pairs)

    plane = lax.dynamic_index_in_dim(volume, (slices - 1) * core, 0, False)
    plane = plane.reshape(blocks, 2, BLOCK, cols)
    to_other_core = lax.dynamic_index_in_dim(plane, 1 - core, 1, False)
    to_same_core = lax.dynamic_index_in_dim(plane, core, 1, False)
    edge_same = lax.dynamic_index_in_dim(volume, (rows - 1) * (1 - core), 1, False)
    edge_cross = lax.dynamic_index_in_dim(volume, (rows - 1) * core, 1, False)
    to_other_core, to_same_core, edge_same, edge_cross = lax.optimization_barrier(
        (to_other_core, to_same_core, edge_same, edge_cross)
    )
    outer_other = shift(to_same_core, lambda c: 0, lambda c: 2 if c else -2)
    outer_own = shift(to_other_core, lambda c: 0, lambda c: 1 if c else -1)
    edge_own = shift(edge_same, lambda c: -1 if c else 1, lambda c: 0)
    edge_other = shift(edge_cross, lambda c: 1 if c else -1, lambda c: -1 if c else 1)
    held = lax.optimization_barrier((volume, edge_own, edge_other))[0]
    other = lax.ppermute(held, "depth", [(d, d ^ 1) for d in range(depth_count)])

    split = (slices, blocks, 2, BLOCK, cols)
    own_view, other_view = volume.reshape(split), other.reshape(split)
    core_arg = core.astype(jnp.int32).reshape(1)
    same_core = [[2 * j + c for j in range(chips)] for c in range(2)]
    vmem = pl.BlockSpec(memory_space=pltpu.MemorySpace.VMEM)
    smem = pl.BlockSpec(memory_space=pltpu.MemorySpace.SMEM)
    half = rows // 2
    shares = dict(slab_share=2.0 * slices / depth_total, depth_total=depth_total)
    params = pltpu.CompilerParams(vmem_limit_bytes=16 << 20)
    quad = jax.ShapeDtypeStruct((4, half, cols), F32)
    slab_terms = jax.ShapeDtypeStruct((slices, half, cols), F32)
    own_terms = pl.pallas_call(
        functools.partial(own_kernel, **shares),
        out_shape=(
            quad, quad, quad, slab_terms, slab_terms,
            jax.ShapeDtypeStruct((half, rows), BF16),
            jax.ShapeDtypeStruct((cols, cols), BF16),
        ),
        in_specs=[smem] + [vmem] * 3,
        out_specs=(vmem,) * 7,
        compiler_params=params,
        name="own",
    )(core_arg, own_view, edge_own, transfer_table)
    partial_image = pl.pallas_call(
        functools.partial(slab_kernel, **shares),
        out_shape=jax.ShapeDtypeStruct((blocks, 4 * BLOCK, cols), F32),
        in_specs=[smem] + [vmem] * 13,
        out_specs=vmem,
        scratch_shapes=[pltpu.VMEM((slices, half, cols), F32)] * 2,
        compiler_params=params,
        name="slab",
    )(
        core_arg, own_view, other_view, outer_own, outer_other, edge_other, transfer_table,
        *own_terms,
    )
    pieces = lax.all_to_all(
        partial_image.astype(jnp.float16), "depth", split_axis=0, concat_axis=0, tiled=True,
        axis_index_groups=same_core,
    )
    return pl.pallas_call(
        functools.partial(merge_kernel, slab_share=shares["slab_share"]),
        out_shape=jax.ShapeDtypeStruct((4, BLOCK * cols), F32),
        in_specs=[vmem, vmem],
        out_specs=vmem,
        scratch_shapes=[pltpu.VMEM((cols // LANES, 4 * BLOCK, LANES), F32)],
        compiler_params=params,
        name="merge",
    )(pieces.astype(F32), transfer_table)


def solution(mesh):
    placed = (P("depth", "img", None), P())
    return jax.shard_map(
        shards, mesh=mesh, in_specs=placed, out_specs=P(None, ("img", "depth")), check_vma=False
    )
```

time: 69.4 us -> 61.9 us (0.89)
  blocking collectives: 0 us -> 23.6 us
  waiting for transfers between devices: 15.2 us -> 1.28 us
  starting transfers between devices: 21.5 us -> 15.4 us
  other arithmetic: 4.9 us -> 0.53 us
  Pallas kernels: 21.4 us -> 18.6 us
  local copies, waits for them, and re-layouts: 4.31 us -> 2.09 us
  between operations: 1.56 us -> 0.13 us
    all_to_all x0 -> x1, blocking collectives: none -> 23.6 us  [shards(): lax.all_to_all(partial_image.astype(jnp.float16), 'depth', split_axis=0,...]
    all_to_all x1 -> x0, waiting for transfers between devices: 15.2 us -> none  [shards(): lax.all_to_all(partial_image.astype(jnp.float16), 'depth', split_axis=0,...]
    all_to_all x1 -> x0, starting transfers between devices: 8.63 us -> none  [shards(): lax.all_to_all(partial_image.astype(jnp.float16), 'depth', split_axis=0,...]
    ppermute x4, starting transfers between devices: 11.5 us -> 15.4 us  [shift(): return lax.ppermute(x, ('img', 'depth'), pairs)]
    pallas_call x3, Pallas kernels: 21.4 us -> 18.6 us  [the longest x1 8.86 us: shards(): pl.pallas_call(functools.partial(slab_kernel, **shares), out_shape=jax.Sh...]
    unnamed x12 -> x5, local copies, waits for them, and re-layouts: 2.1 us -> 0.01 us
    ppermute x1, starting transfers between devices: 1.42 us -> 0.01 us  [shards(): lax.ppermute(held, 'depth', [(d, d ^ 1) for d in range(depth_count)])]
    convert_element_type x1, other arithmetic: 1.61 us -> 0.26 us  [shards(): pieces.astype(F32)]
  transfers between devices with their start and end apart: 6 -> 5, of which waited for: 1 -> 1; matrix products, arithmetic and copies ran while one was open for 6% -> 0% of each run, Pallas kernels for 12% -> 14%
where the time goes in v4:
time: 61.9 us; the launch traced here: 61.6 us
  blocking collectives  23.6 us (38%)
  Pallas kernels  18.6 us (30%)
  starting transfers between devices  15.4 us (25%)
  local copies, waits for them, and re-layouts  2.09 us (3%)
  waiting for transfers between devices  1.28 us (2%)
    all_to_all x1, blocking collectives, shards(): lax.all_to_all(partial_image.astype(jnp.float16), 'depth', split_axis=0,...  23.6 us
    ppermute x4, starting transfers between devices, shift(): return lax.ppermute(x, ('img', 'depth'), pairs)  15.4 us
    pallas_call x1, Pallas kernels, shards(): pl.pallas_call(functools.partial(slab_kernel, **shares), out_shape=jax.Sh...  8.86 us
    pallas_call x1, Pallas kernels, shards(): pl.pallas_call(functools.partial(own_kernel, **shares), out_shape=(quad,...  8.8 us
    ppermute x4, waiting for transfers between devices, shift(): return lax.ppermute(x, ('img', 'depth'), pairs)  1.27 us
  transfers between devices with their start and end apart: 5, of which 1 were waited for; matrix products, arithmetic and copies ran while one was open for 0% of the time, Pallas kernels for 14%

profile of v4, /device:TPU:1, one launch (start us, length us, event | category | flops | bytes accessed | tf_op | source)
XLA Modules:
  0.0 61.6 jit_solution(18159473122711037560)
XLA Ops:
  0.0 0.0 copy-start
  0.0 0.0 copy-start.1
  0.0 1.2 %constant_dynamic-slice_fusion.2 = bf16[1,512,512]{2,1,0:T(8,128)(2,1)S(1)} fusion(bf16[4,512,512]{2,1,0:T(8,128)(2,1)} %param.2, s32[]{:T(128)S(6)} %select_n.26), kind=kLoop, calls=%fused_computation.6 | loop fusion | bytes 1048580 | tf_op jit(solution)/shard_map/jit(dynamic_index_in_dim)/dynamic_slice | solution.py:246
  1.2 0.8 %constant_dynamic-slice_fusion = (bf16[4,1,512]{2,1,0:T(2,128)(2,1)S(1)}, bf16[4,1,512]{2,1,0:T(2,128)(2,1)S(1)}) fusion(bf16[4,512,512]{2,1,0:T(8,128)(2,1)} %param.2, s32[]{:T(128)S(6)} %select_n.30, s32[]{:T(128)S(6)} %select_n.29), kind=kLoop, calls=%fused_computation.4 | loop fusion | bytes 16392 | tf_op jit(solution)/shard_map/jit(dynamic_index_in_dim)/dynamic_slice | solution.py:251
  2.1 1.3 %collective-permute-start = (bf16[4,512]{1,0:T(4,128)(2,1)S(1)}, bf16[4,512]{1,0:T(4,128)(2,1)S(1)}, u32[]{:S(2)}, u32[]{:S(2)}) collective-permute-start(bf16[4,512]{1,0:T(4,128)(2,1)S(1)} %get-tuple-element.17), channel_id=1, source_target_pairs={{0,32},{2,34},{4,36},{6,38},{8,40},{10,42},{12,44},{14,46},{16,48}... | collective-permute-start | bytes 12296 | tf_op jit(solution)/shard_map/ppermute | solution.py:244
  3.4 7.5 %collective-permute-start.1 = (bf16[4,512]{1,0:T(4,128)(2,1)S(1)}, bf16[4,512]{1,0:T(4,128)(2,1)S(1)}, u32[]{:S(2)}, u32[]{:S(2)}) collective-permute-start(bf16[4,512]{1,0:T(4,128)(2,1)S(1)} %get-tuple-element.18), channel_id=1, source_target_pairs={{1,32},{3,34},{5,36},{7,38},{9,40},{11,42},{13,44},{15,46},{17,48}... | collective-permute-start | bytes 12296 | tf_op jit(solution)/shard_map/ppermute | solution.py:244
  10.9 0.0 collective-permute-done.edge
  10.9 1.3 %collective-permute-done.1.edge = bf16[4,512]{1,0:T(4,128)(2,1)S(1)} collective-permute-done((bf16[4,512]{1,0:T(4,128)(2,1)S(1)}, bf16[4,512]{1,0:T(4,128)(2,1)S(1)}, u32[]{:S(2)}, u32[]{:S(2)}) %collective-permute-start.1) | collective-permute-done | bytes 4128 | tf_op jit(solution)/shard_map/ppermute | solution.py:244
  12.2 0.0 copy-done
  12.2 0.0 collective-permute-start.2
  12.2 3.5 %collective-permute-start.3 = (bf16[16,16,512]{2,1,0:T(8,128)(2,1)S(1)}, bf16[16,16,512]{2,1,0:T(8,128)(2,1)S(1)}, u32[]{:S(2)}, u32[]{:S(2)}) collective-permute-start(bf16[16,16,512]{2,1,0:T(8,128)(2,1)S(1)} %get-tuple-element.20), channel_id=1, source_target_pairs={{1,2},{2,1},{3,4},{4,3},{5,6},{6,5},{7,8},{8,7},{9,10},{10,9},{11,... | collective-permute-start | bytes 786440 | tf_op jit(solution)/shard_map/ppermute | solution.py:244
  15.7 3.1 %collective-permute-start.4 = (bf16[16,16,512]{2,1,0:T(8,128)(2,1)S(1)}, bf16[16,16,512]{2,1,0:T(8,128)(2,1)S(1)}, u32[]{:S(2)}, u32[]{:S(2)}) collective-permute-start(bf16[16,16,512]{2,1,0:T(8,128)(2,1)S(1)} %get-tuple-element.21), channel_id=1, source_target_pairs={{1,3},{2,0},{3,5},{4,2},{5,7},{6,4},{7,9},{8,6},{9,11},{10,8},{11,... | collective-permute-start | bytes 786440 | tf_op jit(solution)/shard_map/ppermute | solution.py:244
  18.8 0.0 copy-done.1
  18.8 8.8 %own.1 = (f32[4,256,512]{2,1,0:T(8,128)S(1)}, f32[4,256,512]{2,1,0:T(8,128)S(1)}, f32[4,256,512]{2,1,0:T(8,128)S(1)}, f32[4,256,512]{2,1,0:T(8,128)S(1)}, f32[4,...) custom-call(s32[1]{0:T(128)} %bitcast.core_ref, ...), custom_call_target="tpu_custom_call" | custom-call | tf_op jit(solution)/shard_map/own/pallas_call | solution.py:273
  27.6 0.0 collective-permute-done.3.outer_own
  27.6 0.0 collective-permute-done.4.outer_other
  27.6 0.0 collective-permute-done.2
  27.7 8.9 %slab.1 = f32[16,64,512]{2,1,0:T(8,128)S(1)} custom-call(s32[1]{0:T(128)} %bitcast.core_ref, bf16[4,16,2,16,512]{4,3,2,1,0:T(8,128)(2,1)S(1)} %bitcast.13, bf16[4,16,2,16,512]{4,3,2,1,0:T(8,128)(2,1)S(1)} %bitcast.14, bf16[16,16,512]{2,1,0:T(8,128)(2,1)S(1)} %collective-permute-done.3.outer_own, bf16[16,16,512]{2,1,0:T(8,128)(2,1)S(1)} %collective-permute-done.4.outer_other, ...), custom_call_target="tpu_custom_call" | custom-call | tf_op jit(solution)/shard_map/slab/pallas_call | solution.py:285
  36.5 0.3 convert_element_type.6
  36.8 23.6 %all_to_all.5 = f16[16,64,512]{2,1,0:T(8,128)(2,1)S(1)} all-to-all(f16[16,64,512]{2,1,0:T(8,128)(2,1)S(1)} %convert_element_type.6), channel_id=1, replica_groups={{0,2,4,6,8,10,12,14,16,18,20,22,24,26,28,30},{1,3,5,7,9,11,13,15,17,19,..., dimensions={0} | all-to-all | bytes 2097152 | tf_op jit(solution)/shard_map/all_to_all | solution.py:297
  60.4 0.3 convert_element_type.7.parts
  60.7 0.9 %merge.1 = f32[4,8192]{1,0:T(4,128)} custom-call(f32[16,64,512]{2,1,0:T(8,128)S(1)} %convert_element_type.7.parts, bf16[4,128]{1,0:T(4,128)(2,1)S(1)} %copy-done.1), custom_call_target="tpu_custom_call" | custom-call | tf_op jit(solution)/shard_map/merge/pallas_call | solution.py:301
  (2 shorter events, 0.1 us)
Async XLA Ops:
  0.0 12.2 %copy-start = (bf16[4,512,512]{2,1,0:T(8,128)(2,1)S(1)}, bf16[4,512,512]{2,1,0:T(8,128)(2,1)}, u32[]{:S(2)}) copy-start(bf16[4,512,512]{2,1,0:T(8,128)(2,1)} %param.2) | copy-start | bytes 6291460
  0.0 18.8 %copy-start.1 = (bf16[4,128]{1,0:T(4,128)(2,1)S(1)}, bf16[4,128]{1,0:T(4,128)(2,1)}, u32[]{:S(2)}) copy-start(bf16[4,128]{1,0:T(4,128)(2,1)} %table.5) | copy-start | bytes 3076
  2.1 8.8 %collective-permute-start = (bf16[4,512]{1,0:T(4,128)(2,1)S(1)}, bf16[4,512]{1,0:T(4,128)(2,1)S(1)}, u32[]{:S(2)}, u32[]{:S(2)}) collective-permute-start(bf16[4,512]{1,0:T(4,128)(2,1)S(1)} %get-tuple-element.17), channel_id=1, source_target_pairs={{0,32},{2,34},{4,36},{6,38},{8,40},{10,42},{12,44},{14,46},{16,48}... | collective-permute-start | bytes 12296 | tf_op jit(solution)/shard_map/ppermute | solution.py:244
  3.4 8.8 %collective-permute-start.1 = (bf16[4,512]{1,0:T(4,128)(2,1)S(1)}, bf16[4,512]{1,0:T(4,128)(2,1)S(1)}, u32[]{:S(2)}, u32[]{:S(2)}) collective-permute-start(bf16[4,512]{1,0:T(4,128)(2,1)S(1)} %get-tuple-element.18), channel_id=1, source_target_pairs={{1,32},{3,34},{5,36},{7,38},{9,40},{11,42},{13,44},{15,46},{17,48}... | collective-permute-start | bytes 12296 | tf_op jit(solution)/shard_map/ppermute | solution.py:244
  12.2 15.5 %collective-permute-start.2 = (bf16[4,512,512]{2,1,0:T(8,128)(2,1)S(1)}, bf16[4,512,512]{2,1,0:T(8,128)(2,1)S(1)}, u32[]{:S(2)}, u32[]{:S(2)}) collective-permute-start(bf16[4,512,512]{2,1,0:T(8,128)(2,1)S(1)} %copy-done), channel_id=1, source_target_pairs={{0,1},{1,0},{2,3},{3,2},{4,5},{5,4},{6,7},{7,6},{8,9},{9,8},{10,11... | collective-permute-start | bytes 6291464 | tf_op jit(solution)/shard_map/ppermute | solution.py:260
  12.2 15.5 %collective-permute-start.3 = (bf16[16,16,512]{2,1,0:T(8,128)(2,1)S(1)}, bf16[16,16,512]{2,1,0:T(8,128)(2,1)S(1)}, u32[]{:S(2)}, u32[]{:S(2)}) collective-permute-start(bf16[16,16,512]{2,1,0:T(8,128)(2,1)S(1)} %get-tuple-element.20), channel_id=1, source_target_pairs={{1,2},{2,1},{3,4},{4,3},{5,6},{6,5},{7,8},{8,7},{9,10},{10,9},{11,... | collective-permute-start | bytes 786440 | tf_op jit(solution)/shard_map/ppermute | solution.py:244
  15.7 12.0 %collective-permute-start.4 = (bf16[16,16,512]{2,1,0:T(8,128)(2,1)S(1)}, bf16[16,16,512]{2,1,0:T(8,128)(2,1)S(1)}, u32[]{:S(2)}, u32[]{:S(2)}) collective-permute-start(bf16[16,16,512]{2,1,0:T(8,128)(2,1)S(1)} %get-tuple-element.21), channel_id=1, source_target_pairs={{1,3},{2,0},{3,5},{4,2},{5,7},{6,4},{7,9},{8,6},{9,11},{10,8},{11,... | collective-permute-start | bytes 786440 | tf_op jit(solution)/shard_map/ppermute | solution.py:244

commit v5 on v4

--- a/solution.py
+++ b/solution.py
@@ -74,7 +74,8 @@
     )
     slope[z] = 2.0 * dy + dx
     norm[z] = dx * dx + dy * dy
-    halo = edge[z : z + 1, :].astype(F32)
+    halo = edge[z].astype(F32)
+    halo = jnp.where(core == 0, halo[HALF - 1 : HALF], halo[0:1])
     top, bottom = jnp.where(core == 0, -1.0, 0.0), jnp.where(core == 0, 0.0, 1.0)
     for at, sign in ((0, top), (rows - 1, bottom)):
         dx_row = dx[at : at + 1] + halo * sign
@@ -243,24 +244,26 @@
                     pairs.append((i * depth_count + d, to_i * depth_count + to_d))
         return lax.ppermute(x, ("img", "depth"), pairs)
 
-    plane = lax.dynamic_index_in_dim(volume, (slices - 1) * core, 0, False)
-    plane = plane.reshape(blocks, 2, BLOCK, cols)
-    to_other_core = lax.dynamic_index_in_dim(plane, 1 - core, 1, False)
-    to_same_core = lax.dynamic_index_in_dim(plane, core, 1, False)
-    edge_same = lax.dynamic_index_in_dim(volume, (rows - 1) * (1 - core), 1, False)
-    edge_cross = lax.dynamic_index_in_dim(volume, (rows - 1) * core, 1, False)
-    to_other_core, to_same_core, edge_same, edge_cross = lax.optimization_barrier(
-        (to_other_core, to_same_core, edge_same, edge_cross)
-    )
-    outer_other = shift(to_same_core, lambda c: 0, lambda c: 2 if c else -2)
-    outer_own = shift(to_other_core, lambda c: 0, lambda c: 1 if c else -1)
-    edge_own = shift(edge_same, lambda c: -1 if c else 1, lambda c: 0)
-    edge_other = shift(edge_cross, lambda c: 1 if c else -1, lambda c: -1 if c else 1)
-    held = lax.optimization_barrier((volume, edge_own, edge_other))[0]
+    split = (slices, blocks, 2, BLOCK, cols)
+    own_view = volume.reshape(split)
+
+    def outer_plane(parity):
+        at = ((slices - 1) * core, 0, parity, 0, 0)
+        return lax.dynamic_slice(own_view, at, (1, blocks, 1, BLOCK, cols)).reshape(
+            blocks, BLOCK, cols
+        )
+
+    def edge_rows(at_end):
+        return lax.dynamic_slice(volume, (0, (rows - HALF) * at_end, 0), (slices, HALF, cols))
+
+    edge_own = shift(edge_rows(1 - core), lambda c: -1 if c else 1, lambda c: 0)
+    edge_other = shift(edge_rows(core), lambda c: 1 if c else -1, lambda c: -1 if c else 1)
+    outer_other = shift(outer_plane(core), lambda c: 0, lambda c: 2 if c else -2)
+    outer_own = shift(outer_plane(1 - core), lambda c: 0, lambda c: 1 if c else -1)
+    held = lax.optimization_barrier((volume, edge_own, edge_other, outer_other, outer_own))[0]
     other = lax.ppermute(held, "depth", [(d, d ^ 1) for d in range(depth_count)])
 
-    split = (slices, blocks, 2, BLOCK, cols)
-    own_view, other_view = volume.reshape(split), other.reshape(split)
+    other_view = other.reshape(split)
     core_arg = core.astype(jnp.int32).reshape(1)
     same_core = [[2 * j + c for j in range(chips)] for c in range(2)]
     vmem = pl.BlockSpec(memory_space=pltpu.MemorySpace.VMEM)

time: 61.9 us -> 62.5 us (level)
  the two profiles are of different devices: /device:TPU:1 before, /device:TPU:64 now
where the time goes in v5:
time: 62.5 us; the launch traced here: 61.8 us
  blocking collectives  24.1 us (39%)
  Pallas kernels  18.5 us (30%)
  starting transfers between devices  12.1 us (19%)
  local copies, waits for them, and re-layouts  4.53 us (7%)
  waiting for transfers between devices  1.97 us (3%)
    all_to_all x1, blocking collectives, shards(): lax.all_to_all(partial_image.astype(jnp.float16), 'depth', split_axis=0,...  24.1 us
    ppermute x4, starting transfers between devices, shift(): return lax.ppermute(x, ('img', 'depth'), pairs)  12.1 us
    pallas_call x1, Pallas kernels, shards(): pl.pallas_call(functools.partial(slab_kernel, **shares), out_shape=jax.Sh...  8.8 us
    pallas_call x1, Pallas kernels, shards(): pl.pallas_call(functools.partial(own_kernel, **shares), out_shape=(quad,...  8.71 us
    unnamed x6, local copies, waits for them, and re-layouts  2.68 us
    ppermute x4, waiting for transfers between devices, shift(): return lax.ppermute(x, ('img', 'depth'), pairs)  1.97 us
  transfers between devices with their start and end apart: 5, of which 1 were waited for; matrix products, arithmetic and copies ran while one was open for 1% of the time, Pallas kernels for 14%

profile of v5, /device:TPU:64, one launch (start us, length us, event | category | flops | bytes accessed | tf_op | source)
XLA Modules:
  0.0 61.8 jit_solution(9024393127768584264)
XLA Ops:
  0.0 1.1 %dynamic-slice_bitcast_fusion = (bf16[16,16,512]{2,1,0:T(8,128)(2,1)S(1)}, bf16[16,16,512]{2,1,0:T(8,128)(2,1)S(1)}) fusion(bf16[4,16,2,16,512]{4,3,2,1,0:T(8,128)(2,1)} %bitcast.7, s32[]{:T(128)S(6)} %select_n.26, s32[]{:T(128)S(6)} %select_n.28, s32[]{:T(128)S(6)} %select_n.27), kind=kLoop, calls=%fused_computation | loop fusion | bytes 1048588 | tf_op jit(solution)/shard_map/reshape | solution.py:252
  1.1 0.7 %collective-permute-start.3 = (bf16[16,16,512]{2,1,0:T(8,128)(2,1)S(1)}, bf16[16,16,512]{2,1,0:T(8,128)(2,1)S(1)}, u32[]{:S(2)}, u32[]{:S(2)}) collective-permute-start(bf16[16,16,512]{2,1,0:T(8,128)(2,1)S(1)} %get-tuple-element.21), channel_id=1, source_target_pairs={{1,2},{2,1},{3,4},{4,3},{5,6},{6,5},{7,8},{8,7},{9,10},{10,9},{11,... | collective-permute-start | bytes 786440 | tf_op jit(solution)/shard_map/ppermute | solution.py:245
  1.8 1.3 %collective-permute-start.2 = (bf16[16,16,512]{2,1,0:T(8,128)(2,1)S(1)}, bf16[16,16,512]{2,1,0:T(8,128)(2,1)S(1)}, u32[]{:S(2)}, u32[]{:S(2)}) collective-permute-start(bf16[16,16,512]{2,1,0:T(8,128)(2,1)S(1)} %get-tuple-element.22), channel_id=1, source_target_pairs={{1,3},{2,0},{3,5},{4,2},{5,7},{6,4},{7,9},{8,6},{9,11},{10,8},{11,... | collective-permute-start | bytes 786440 | tf_op jit(solution)/shard_map/ppermute | solution.py:245
  3.1 0.8 %constant_dynamic-slice_fusion = (bf16[4,8,512]{2,1,0:T(8,128)(2,1)S(1)}, bf16[4,8,512]{2,1,0:T(8,128)(2,1)S(1)}) fusion(bf16[4,512,512]{2,1,0:T(8,128)(2,1)} %param.2, s32[]{:T(128)S(6)} %select_n.25, s32[]{:T(128)S(6)} %select_n.24), kind=kLoop, calls=%fused_computation.2 | loop fusion | bytes 131080 | tf_op jit(solution)/shard_map/dynamic_slice | solution.py:257
  3.9 6.3 %collective-permute-start.1 = (bf16[4,8,512]{2,1,0:T(8,128)(2,1)S(1)}, bf16[4,8,512]{2,1,0:T(8,128)(2,1)S(1)}, u32[]{:S(2)}, u32[]{:S(2)}) collective-permute-start(bf16[4,8,512]{2,1,0:T(8,128)(2,1)S(1)} %get-tuple-element.23), channel_id=1, source_target_pairs={{1,32},{3,34},{5,36},{7,38},{9,40},{11,42},{13,44},{15,46},{17,48}... | collective-permute-start | bytes 98312 | tf_op jit(solution)/shard_map/ppermute | solution.py:245
  10.2 3.8 %collective-permute-start = (bf16[4,8,512]{2,1,0:T(8,128)(2,1)S(1)}, bf16[4,8,512]{2,1,0:T(8,128)(2,1)S(1)}, u32[]{:S(2)}, u32[]{:S(2)}) collective-permute-start(bf16[4,8,512]{2,1,0:T(8,128)(2,1)S(1)} %get-tuple-element.24), channel_id=1, source_target_pairs={{0,32},{2,34},{4,36},{6,38},{8,40},{10,42},{12,44},{14,46},{16,48}... | collective-permute-start | bytes 98312 | tf_op jit(solution)/shard_map/ppermute | solution.py:245
  14.0 0.0 collective-permute-done.1.edge
  14.0 2.0 %collective-permute-done.edge = bf16[4,8,512]{2,1,0:T(8,128)(2,1)S(1)} collective-permute-done((bf16[4,8,512]{2,1,0:T(8,128)(2,1)S(1)}, bf16[4,8,512]{2,1,0:T(8,128)(2,1)S(1)}, u32[]{:S(2)}, u32[]{:S(2)}) %collective-permute-start) | collective-permute-done | bytes 32800 | tf_op jit(solution)/shard_map/ppermute | solution.py:245
  16.0 0.0 collective-permute-done.3.outer_own
  16.0 0.0 collective-permute-done.2.outer_other
  16.0 0.0 collective-permute-start.4
  16.0 0.0 copy-start
  16.0 1.6 %copy-done = bf16[4,512,512]{2,1,0:T(8,128)(2,1)S(1)} copy-done((bf16[4,512,512]{2,1,0:T(8,128)(2,1)S(1)}, bf16[4,512,512]{2,1,0:T(8,128)(2,1)}, u32[]{:S(2)}) %copy-start) | copy-done | bytes 2097176
  17.6 0.0 copy-start.1
  17.6 0.7 %copy-done.1 = bf16[4,128]{1,0:T(4,128)(2,1)S(1)} copy-done((bf16[4,128]{1,0:T(4,128)(2,1)S(1)}, bf16[4,128]{1,0:T(4,128)(2,1)}, u32[]{:S(2)}) %copy-start.1) | copy-done | bytes 1048
  18.2 8.7 %own.1 = (f32[4,256,512]{2,1,0:T(8,128)S(1)}, f32[4,256,512]{2,1,0:T(8,128)S(1)}, f32[4,256,512]{2,1,0:T(8,128)S(1)}, f32[4,256,512]{2,1,0:T(8,128)S(1)}, f32[4,...) custom-call(s32[1]{0:T(128)} %bitcast.core_ref, ...), custom_call_target="tpu_custom_call" | custom-call | tf_op jit(solution)/shard_map/own/pallas_call | solution.py:276
  27.0 0.0 collective-permute-done.4
  27.0 8.8 %slab.1 = f32[16,64,512]{2,1,0:T(8,128)S(1)} custom-call(s32[1]{0:T(128)} %bitcast.core_ref, bf16[4,16,2,16,512]{4,3,2,1,0:T(8,128)(2,1)S(1)} %bitcast.9, bf16[4,16,2,16,512]{4,3,2,1,0:T(8,128)(2,1)S(1)} %bitcast.10, bf16[16,16,512]{2,1,0:T(8,128)(2,1)S(1)} %collective-permute-done.3.outer_own, bf16[16,16,512]{2,1,0:T(8,128)(2,1)S(1)} %collective-permute-done.2.outer_other, ...), custom_call_target="tpu_custom_call" | custom-call | tf_op jit(solution)/shard_map/slab/pallas_call | solution.py:288
  35.8 0.3 convert_element_type.6
  36.1 24.1 %all_to_all.5 = f16[16,64,512]{2,1,0:T(8,128)(2,1)S(1)} all-to-all(f16[16,64,512]{2,1,0:T(8,128)(2,1)S(1)} %convert_element_type.6), channel_id=1, replica_groups={{0,2,4,6,8,10,12,14,16,18,20,22,24,26,28,30},{1,3,5,7,9,11,13,15,17,19,..., dimensions={0} | all-to-all | bytes 2097152 | tf_op jit(solution)/shard_map/all_to_all | solution.py:300
  60.2 0.0 copy-start.2
  60.2 0.3 convert_element_type.7.parts
  60.4 0.4 copy-done.2
  60.9 0.9 %merge.1 = f32[4,8192]{1,0:T(4,128)} custom-call(f32[16,64,512]{2,1,0:T(8,128)S(1)} %convert_element_type.7.parts, bf16[4,128]{1,0:T(4,128)(2,1)S(1)} %copy-done.2), custom_call_target="tpu_custom_call" | custom-call | tf_op jit(solution)/shard_map/merge/pallas_call | solution.py:304
Async XLA Ops:
  1.1 14.9 %collective-permute-start.3 = (bf16[16,16,512]{2,1,0:T(8,128)(2,1)S(1)}, bf16[16,16,512]{2,1,0:T(8,128)(2,1)S(1)}, u32[]{:S(2)}, u32[]{:S(2)}) collective-permute-start(bf16[16,16,512]{2,1,0:T(8,128)(2,1)S(1)} %get-tuple-element.21), channel_id=1, source_target_pairs={{1,2},{2,1},{3,4},{4,3},{5,6},{6,5},{7,8},{8,7},{9,10},{10,9},{11,... | collective-permute-start | bytes 786440 | tf_op jit(solution)/shard_map/ppermute | solution.py:245
  1.8 14.2 %collective-permute-start.2 = (bf16[16,16,512]{2,1,0:T(8,128)(2,1)S(1)}, bf16[16,16,512]{2,1,0:T(8,128)(2,1)S(1)}, u32[]{:S(2)}, u32[]{:S(2)}) collective-permute-start(bf16[16,16,512]{2,1,0:T(8,128)(2,1)S(1)} %get-tuple-element.22), channel_id=1, source_target_pairs={{1,3},{2,0},{3,5},{4,2},{5,7},{6,4},{7,9},{8,6},{9,11},{10,8},{11,... | collective-permute-start | bytes 786440 | tf_op jit(solution)/shard_map/ppermute | solution.py:245
  3.9 10.1 %collective-permute-start.1 = (bf16[4,8,512]{2,1,0:T(8,128)(2,1)S(1)}, bf16[4,8,512]{2,1,0:T(8,128)(2,1)S(1)}, u32[]{:S(2)}, u32[]{:S(2)}) collective-permute-start(bf16[4,8,512]{2,1,0:T(8,128)(2,1)S(1)} %get-tuple-element.23), channel_id=1, source_target_pairs={{1,32},{3,34},{5,36},{7,38},{9,40},{11,42},{13,44},{15,46},{17,48}... | collective-permute-start | bytes 98312 | tf_op jit(solution)/shard_map/ppermute | solution.py:245
  10.2 5.8 %collective-permute-start = (bf16[4,8,512]{2,1,0:T(8,128)(2,1)S(1)}, bf16[4,8,512]{2,1,0:T(8,128)(2,1)S(1)}, u32[]{:S(2)}, u32[]{:S(2)}) collective-permute-start(bf16[4,8,512]{2,1,0:T(8,128)(2,1)S(1)} %get-tuple-element.24), channel_id=1, source_target_pairs={{0,32},{2,34},{4,36},{6,38},{8,40},{10,42},{12,44},{14,46},{16,48}... | collective-permute-start | bytes 98312 | tf_op jit(solution)/shard_map/ppermute | solution.py:245
  16.0 11.0 %collective-permute-start.4 = (bf16[4,512,512]{2,1,0:T(8,128)(2,1)}, bf16[4,512,512]{2,1,0:T(8,128)(2,1)S(1)}, u32[]{:S(2)}, u32[]{:S(2)}) collective-permute-start(bf16[4,512,512]{2,1,0:T(8,128)(2,1)} %param.2), channel_id=1, source_target_pairs={{0,1},{1,0},{2,3},{3,2},{4,5},{5,4},{6,7},{7,6},{8,9},{9,8},{10,11... | collective-permute-start | bytes 6291464 | tf_op jit(solution)/shard_map/ppermute | solution.py:264
  16.0 1.6 %copy-start = (bf16[4,512,512]{2,1,0:T(8,128)(2,1)S(1)}, bf16[4,512,512]{2,1,0:T(8,128)(2,1)}, u32[]{:S(2)}) copy-start(bf16[4,512,512]{2,1,0:T(8,128)(2,1)} %param.2) | copy-start | bytes 6291460
  17.6 0.7 %copy-start.1 = (bf16[4,128]{1,0:T(4,128)(2,1)S(1)}, bf16[4,128]{1,0:T(4,128)(2,1)}, u32[]{:S(2)}) copy-start(bf16[4,128]{1,0:T(4,128)(2,1)} %table.5) | copy-start | bytes 3076
  60.2 0.7 %copy-start.2 = (bf16[4,128]{1,0:T(4,128)(2,1)S(1)}, bf16[4,128]{1,0:T(4,128)(2,1)}, u32[]{:S(2)}) copy-start(bf16[4,128]{1,0:T(4,128)(2,1)} %table.5) | copy-start | bytes 3076

commit v6 on v5

v6 whole, which is shorter than its diff:
```python
import functools

import jax
import jax.numpy as jnp
import numpy as np
from jax import lax
from jax.experimental import pallas as pl
from jax.experimental.pallas import tpu as pltpu
from jax.sharding import PartitionSpec as P

F32 = jnp.float32
BF16 = jnp.bfloat16
BLOCK = 16
HALF = 8
LANES = 128
TINY = 1e-30
SLOPE = 1.4 / 3.0


def row_differences(rows, core):
    shape = (rows // 2, rows)
    local = lax.broadcasted_iota(jnp.int32, shape, 0)
    there = lax.broadcasted_iota(jnp.int32, shape, 1)
    step = there - (local + (local & -BLOCK) + core * BLOCK)
    return jnp.where(step == 1, 1.0, jnp.where(step == -1, -1.0, 0.0)).astype(BF16)


def column_differences(cols):
    step = lax.broadcasted_iota(jnp.int32, (cols, cols), 0) - lax.broadcasted_iota(
        jnp.int32, (cols, cols), 1
    )
    return jnp.where(step == 1, 1.0, jnp.where(step == -1, -1.0, 0.0)).astype(BF16)


def tops(table, slab_share):
    colour = jnp.max(jnp.max(table[0:3], axis=0, keepdims=True), axis=1, keepdims=True)
    extinction = jnp.max(table[3:4], axis=1, keepdims=True)
    return jnp.maximum(colour, TINY), jnp.maximum(extinction * slab_share, TINY)


def spread(table, slab_share, depth_total):
    entries = table.shape[1]
    colour_top, opacity_top = tops(table, slab_share)
    scale = SLOPE / (colour_top * opacity_top)
    lower = [table[c : c + 1] * scale for c in range(3)]
    lower.append(table[3:4] * float(-np.log2(np.e) / depth_total))
    lower = [jnp.broadcast_to(t, (HALF, entries)) for t in lower]
    last = lax.broadcasted_iota(jnp.int32, (HALF, entries), 1) == entries - 1
    upper = [jnp.where(last, t, pltpu.roll(t, entries - 1, 1)) for t in lower]
    return lower + upper


def look_up(table, index):
    return jnp.take_along_axis(table, index, axis=1, mode="promise_in_bounds")


def classify(centre, tabs):
    position = centre * float(tabs[0].shape[1] - 1)
    knot = position.astype(jnp.int32)
    part = position - knot.astype(F32)
    upper = part.astype(BF16).astype(F32)
    lower = (1.0 - part).astype(BF16).astype(F32)
    values = [
        lower * look_up(tabs[c], knot) + upper * look_up(tabs[c + 4], knot) for c in range(4)
    ]
    return values[:3] + [jnp.exp2(values[3])]


def shade(accum, transmit, dz, slope_xy, norm_xy, found):
    shading = 0.3 / SLOPE + jnp.abs(dz + slope_xy) * lax.rsqrt(dz * dz + norm_xy)
    left = transmit * found[3]
    gain = (transmit - left) * shading
    return [a + gain * v for a, v in zip(accum, found[:3])], left


def slope_of(dx, dy):
    return 0.5 * dx + dy


def norm_of(dx, dy):
    return dx * dx + dy * dy + 0.04


def over(near, far):
    return [n + near[3] * f for n, f in zip(near[:3], far[:3])] + [near[3] * far[3]]


def nothing():
    return [jnp.zeros((HALF, LANES), F32)] * 3, jnp.ones((HALF, LANES), F32)


def pick(condition, a, b):
    return [jnp.where(condition, x, y) for x, y in zip(a, b)]


def slices_kernel(cells, core, rows_op, cols_op, table, outs, inner_slope, inner_norm, shares):
    first, last, middle, slope, norm, edge_dx, edge_dy = outs
    slices, blocks, _, _, cols = cells.shape
    rows = blocks * BLOCK
    ends = (0, slices - 1)
    for z in range(slices):
        dx = jnp.dot(rows_op[...], cells[z].reshape(2 * rows, cols), preferred_element_type=F32)
        dy = jnp.dot(
            cells[z, :, core].reshape(rows, cols), cols_op[...], preferred_element_type=F32
        )
        to_slope, to_norm, at = (
            (slope, norm, ends.index(z)) if z in ends else (inner_slope, inner_norm, z - 1)
        )
        to_slope[at] = slope_of(dx, dy)
        to_norm[at] = norm_of(dx, dy)
        edge_dx[z] = jnp.where(core == 0, dx[:HALF], dx[rows - HALF :])
        edge_dy[z] = jnp.where(core == 0, dy[:HALF], dy[rows - HALF :])
    tabs = spread(table[...].astype(F32), **shares)

    def block(b, carry):
        for half in range(0, BLOCK, HALF):
            here = pl.ds(pl.multiple_of(b * BLOCK + half, HALF), HALF)
            rows = slice(half, half + HALF)
            for start in range(0, cols, LANES):
                lanes = slice(start, start + LANES)
                mine = [cells[z, b, core, rows, lanes].astype(F32) for z in range(slices)]
                accum, transmit = nothing()
                for z in range(slices):
                    found = classify(mine[z], tabs)
                    if z in ends:
                        ref = last if z else first
                        for c in range(4):
                            ref[c, here, lanes] = found[c]
                    else:
                        accum, transmit = shade(
                            accum, transmit, mine[z + 1] - mine[z - 1],
                            inner_slope[z - 1, here, lanes], inner_norm[z - 1, here, lanes], found,
                        )
                for c in range(3):
                    middle[c, here, lanes] = accum[c]
                middle[3, here, lanes] = transmit
        return carry

    lax.fori_loop(0, blocks, block, 0)


def own_kernel(core_ref, cells, table, *refs, shares):
    outs, rest = refs[:7], refs[7:]
    rows_op, cols_op, to_other, to_same, edge_same, edge_cross, inner_slope, inner_norm = rest
    slices, blocks, _, _, cols = cells.shape
    core = core_ref[0]
    outer = (slices - 1) * core
    to_other[...] = cells[outer, :, 1 - core]
    to_same[...] = cells[outer, :, core]

    @pl.when(core == 0)
    def _():
        edge_same[...] = cells[:, blocks - 1, 1, HALF:, :]
        edge_cross[...] = cells[:, 0, 0, :HALF, :]

    @pl.when(core != 0)
    def _():
        edge_same[...] = cells[:, 0, 0, :HALF, :]
        edge_cross[...] = cells[:, blocks - 1, 1, HALF:, :]

    rows_op[...] = row_differences(2 * blocks * BLOCK, core)
    cols_op[...] = column_differences(cols)
    slices_kernel(
        cells, core, rows_op, cols_op, table, outs, inner_slope, inner_norm, shares
    )


def other_kernel(core_ref, cells, table, rows_op, cols_op, *refs, shares):
    slices_kernel(
        cells, core_ref[0], rows_op, cols_op, table, refs[:7], refs[7], refs[8], shares
    )


def slab_kernel(
    core_ref, own, other, outer_own, outer_other, edge_own, edge_other, table, *refs, shares
):
    own_terms, other_terms, out = refs[:7], refs[7:14], refs[14]
    slices, blocks, _, _, cols = own.shape
    core = core_ref[0]
    front = core == 0
    end = slices - 1
    table_values = table[...].astype(F32)
    opacity_scale = 1.0 / tops(table_values, shares["slab_share"])[1]

    def stacks(mine, theirs, end_own, end_other):
        own_stack = (
            [jnp.where(front, end_own, theirs[end])] + mine + [jnp.where(front, theirs[0], end_own)]
        )
        other_stack = (
            [jnp.where(front, mine[end], end_other)]
            + theirs
            + [jnp.where(front, end_other, mine[0])]
        )
        return own_stack, other_stack

    def finish(own_part, other_part):
        both = over(pick(front, own_part, other_part), pick(front, other_part, own_part))
        both[3] = (1.0 - both[3]) * opacity_scale
        return both

    def block(b, carry):
        for half in range(0, BLOCK, HALF):
            here = pl.ds(pl.multiple_of(b * BLOCK + half, HALF), HALF)
            rows = slice(half, half + HALF)
            for start in range(0, cols, LANES):
                lanes = slice(start, start + LANES)

                def half_slab(stack, terms):
                    first, last, middle, slope, norm = terms[:5]
                    parts = []
                    for ref, at, z in ((first, 0, 0), (last, 1, end)):
                        accum, transmit = shade(
                            *nothing(), stack[z + 2] - stack[z],
                            slope[at, here, lanes], norm[at, here, lanes],
                            [ref[c, here, lanes] for c in range(4)],
                        )
                        parts.append(accum + [transmit])
                    inner = [middle[c, here, lanes] for c in range(4)]
                    return over(parts[0], over(inner, parts[1]))

                own_stack, other_stack = stacks(
                    [own[z, b, core, rows, lanes].astype(F32) for z in range(slices)],
                    [other[z, b, core, rows, lanes].astype(F32) for z in range(slices)],
                    outer_own[b, rows, lanes].astype(F32),
                    outer_other[b, rows, lanes].astype(F32),
                )
                both = finish(half_slab(own_stack, own_terms), half_slab(other_stack, other_terms))
                for c in range(4):
                    at = c * BLOCK + half
                    out[b, at : at + HALF, lanes] = both[c]
        return carry

    lax.fori_loop(0, blocks, block, 0)

    tabs = spread(table_values, **shares)
    b = jnp.where(front, 0, blocks - 1)
    row = lax.broadcasted_iota(jnp.int32, (HALF, LANES), 0)
    at_edge = row == jnp.where(front, 0, HALF - 1)
    for start in range(0, cols, LANES):
        lanes = slice(start, start + LANES)

        def load(ref, *index):
            top = ref[(*index, slice(0, HALF), lanes)].astype(F32)
            return jnp.where(front, top, ref[(*index, slice(HALF, BLOCK), lanes)].astype(F32))

        def half_slab(stack, terms, edge):
            accum, transmit = nothing()
            for z in range(slices):
                halo = edge[z, :, lanes].astype(F32)
                halo = jnp.where(front, -halo[HALF - 1 : HALF], halo[0:1])
                dx = terms[5][z, :, lanes] + jnp.where(at_edge, halo, 0.0)
                dy = terms[6][z, :, lanes]
                accum, transmit = shade(
                    accum, transmit, stack[z + 2] - stack[z],
                    slope_of(dx, dy), norm_of(dx, dy), classify(stack[z + 1], tabs),
                )
            return accum + [transmit]

        own_stack, other_stack = stacks(
            [load(own, z, b, core) for z in range(slices)],
            [load(other, z, b, core) for z in range(slices)],
            load(outer_own, b),
            load(outer_other, b),
        )
        both = finish(
            half_slab(own_stack, own_terms, edge_own), half_slab(other_stack, other_terms, edge_other)
        )
        for c in range(4):
            at = pl.multiple_of(c * BLOCK + core * HALF, HALF)
            out[b, pl.ds(at, HALF), lanes] = both[c]


def merge_kernel(parts, table, out, image, *, slab_share):
    cols = parts.shape[2]
    colour_top, opacity_top = tops(table[...].astype(F32), slab_share)
    for half in range(0, BLOCK, HALF):
        for start in range(0, cols, LANES):
            lanes = slice(start, start + LANES)
            accum, transmit = nothing()
            for s in range(parts.shape[0]):
                part = [
                    parts[s, c * BLOCK + half : c * BLOCK + half + HALF, lanes] for c in range(4)
                ]
                accum = [a + transmit * p for a, p in zip(accum, part[:3])]
                transmit = transmit - transmit * (part[3] * opacity_top)
            whole = [a * (colour_top * opacity_top) for a in accum] + [1.0 - transmit]
            for c in range(4):
                at = start // LANES, slice(c * BLOCK + half, c * BLOCK + half + HALF)
                image[at] = whole[c]
    for r in range(BLOCK):
        for start in range(0, cols, LANES):
            out[:, r * cols + start : r * cols + start + LANES] = image[
                start // LANES, pl.ds(r, 4, stride=BLOCK)
            ]


def shards(volume, transfer_table):
    slices, rows, cols = volume.shape
    depth_count = lax.axis_size("depth")
    img_count = lax.axis_size("img")
    chips = depth_count // 2
    depth_total = slices * depth_count
    blocks = rows // (2 * BLOCK)
    core = lax.axis_index("depth") % 2

    def shift(x, img_step, depth_step):
        pairs = []
        for i in range(img_count):
            for d in range(depth_count):
                to_i, to_d = i + img_step(d % 2), d + depth_step(d % 2)
                if 0 <= to_i < img_count and 0 <= to_d < depth_count:
                    pairs.append((i * depth_count + d, to_i * depth_count + to_d))
        return lax.ppermute(x, ("img", "depth"), pairs)

    half = rows // 2
    split = (slices, blocks, 2, BLOCK, cols)
    core_arg = core.astype(jnp.int32).reshape(1)
    same_core = [[2 * j + c for j in range(chips)] for c in range(2)]
    vmem = pl.BlockSpec(memory_space=pltpu.MemorySpace.VMEM)
    smem = pl.BlockSpec(memory_space=pltpu.MemorySpace.SMEM)
    shares = dict(slab_share=2.0 * slices / depth_total, depth_total=depth_total)
    params = pltpu.CompilerParams(vmem_limit_bytes=16 << 20)
    quad = jax.ShapeDtypeStruct((4, half, cols), F32)
    two = jax.ShapeDtypeStruct((2, half, cols), F32)
    unit = jax.ShapeDtypeStruct((slices, HALF, cols), F32)
    plane = jax.ShapeDtypeStruct((blocks, BLOCK, cols), BF16)
    edge = jax.ShapeDtypeStruct((slices, HALF, cols), BF16)
    terms = (quad, quad, quad, two, two, unit, unit)
    operators = (
        jax.ShapeDtypeStruct((half, rows), BF16), jax.ShapeDtypeStruct((cols, cols), BF16)
    )
    inner = [pltpu.VMEM((slices - 2, half, cols), F32)] * 2

    other = lax.ppermute(volume, "depth", [(d, d ^ 1) for d in range(depth_count)]).reshape(split)
    own = volume.reshape(split)
    results = pl.pallas_call(
        functools.partial(own_kernel, shares=shares),
        out_shape=(*terms, *operators, plane, plane, edge, edge),
        in_specs=[smem, vmem, vmem],
        out_specs=(vmem,) * 13,
        scratch_shapes=inner,
        compiler_params=params,
        name="own",
    )(core_arg, own, transfer_table)
    own_terms, ops, (to_other, to_same, edge_same, edge_cross) = (
        results[:7], results[7:9], results[9:]
    )
    outer_other = shift(to_same, lambda c: 0, lambda c: 2 if c else -2)
    outer_own = shift(to_other, lambda c: 0, lambda c: 1 if c else -1)
    edge_own = shift(edge_same, lambda c: -1 if c else 1, lambda c: 0)
    edge_other = shift(edge_cross, lambda c: 1 if c else -1, lambda c: -1 if c else 1)
    other_terms = pl.pallas_call(
        functools.partial(other_kernel, shares=shares),
        out_shape=terms,
        in_specs=[smem] + [vmem] * 4,
        out_specs=(vmem,) * 7,
        scratch_shapes=inner,
        compiler_params=params,
        name="other",
    )(core_arg, other, transfer_table, *ops)
    partial_image = pl.pallas_call(
        functools.partial(slab_kernel, shares=shares),
        out_shape=jax.ShapeDtypeStruct((blocks, 4 * BLOCK, cols), F32),
        in_specs=[smem] + [vmem] * 21,
        out_specs=vmem,
        compiler_params=params,
        name="slab",
    )(
        core_arg, own, other, outer_own, outer_other, edge_own, edge_other, transfer_table,
        *own_terms, *other_terms,
    )
    pieces = lax.all_to_all(
        partial_image.astype(jnp.float16), "depth", split_axis=0, concat_axis=0, tiled=True,
        axis_index_groups=same_core,
    )
    return pl.pallas_call(
        functools.partial(merge_kernel, slab_share=shares["slab_share"]),
        out_shape=jax.ShapeDtypeStruct((4, BLOCK * cols), F32),
        in_specs=[vmem, vmem],
        out_specs=vmem,
        scratch_shapes=[pltpu.VMEM((cols // LANES, 4 * BLOCK, LANES), F32)],
        compiler_params=params,
        name="merge",
    )(pieces.astype(F32), transfer_table)


def solution(mesh):
    placed = (P("depth", "img", None), P())
    return jax.shard_map(
        shards, mesh=mesh, in_specs=placed, out_specs=P(None, ("img", "depth")), check_vma=False
    )
```

time: 62.5 us -> 61.6 us (0.986)
  the two profiles are of different devices: /device:TPU:64 before, /device:TPU:33 now
where the time goes in v6:
time: 61.6 us; the launch traced here: 61.3 us
  blocking collectives  26.2 us (43%)
  Pallas kernels  21.1 us (34%)
  starting transfers between devices  10.7 us (17%)
  local copies, waits for them, and re-layouts  2.69 us (4%)
    all_to_all x1, blocking collectives, shards(): lax.all_to_all(partial_image.astype(jnp.float16), 'depth', split_axis=0,...  26.2 us
    ppermute x4, starting transfers between devices, shift(): return lax.ppermute(x, ('img', 'depth'), pairs)  9.98 us
    pallas_call x1, Pallas kernels, shards(): pl.pallas_call(functools.partial(own_kernel, shares=shares), out_shape=(*...  8.72 us
    pallas_call x1, Pallas kernels, shards(): pl.pallas_call(functools.partial(other_kernel, shares=shares), out_shape=...  8.64 us
    pallas_call x1, Pallas kernels, shards(): pl.pallas_call(functools.partial(slab_kernel, shares=shares), out_shape=j...  2.81 us
    unnamed x8, local copies, waits for them, and re-layouts  2.69 us
  transfers between devices with their start and end apart: 5, of which 0 were waited for; matrix products, arithmetic and copies ran while one was open for 0% of the time, Pallas kernels for 28%

profile of v6, /device:TPU:33, one launch (start us, length us, event | category | flops | bytes accessed | tf_op | source)
XLA Modules:
  0.0 61.3 jit_solution(6430903189901912163)
XLA Ops:
  0.0 0.7 %collective-permute-start = (bf16[4,512,512]{2,1,0:T(8,128)(2,1)}, bf16[4,512,512]{2,1,0:T(8,128)(2,1)S(1)}, u32[]{:S(2)}, u32[]{:S(2)}) collective-permute-start(bf16[4,512,512]{2,1,0:T(8,128)(2,1)} %param.2), channel_id=1, source_target_pairs={{0,1},{1,0},{2,3},{3,2},{4,5},{5,4},{6,7},{7,6},{8,9},{9,8},{10,11... | collective-permute-start | bytes 6291464 | tf_op jit(solution)/shard_map/ppermute | solution.py:334
  0.7 0.0 copy-start
  0.7 1.6 %copy-done = bf16[4,512,512]{2,1,0:T(8,128)(2,1)S(1)} copy-done((bf16[4,512,512]{2,1,0:T(8,128)(2,1)S(1)}, bf16[4,512,512]{2,1,0:T(8,128)(2,1)}, u32[]{:S(2)}) %copy-start) | copy-done | bytes 2097176
  2.3 0.0 copy-start.2
  2.3 0.7 %copy-done.2 = bf16[4,128]{1,0:T(4,128)(2,1)S(1)} copy-done((bf16[4,128]{1,0:T(4,128)(2,1)S(1)}, bf16[4,128]{1,0:T(4,128)(2,1)}, u32[]{:S(2)}) %copy-start.2) | copy-done | bytes 1048
  2.9 0.0 copy-start.1
  2.9 8.7 %own.1 = (f32[4,256,512]{2,1,0:T(8,128)S(1)}, f32[4,256,512]{2,1,0:T(8,128)S(1)}, f32[4,256,512]{2,1,0:T(8,128)S(1)}, f32[2,256,512]{2,1,0:T(8,128)S(1)}, f32[2,...) custom-call(s32[1]{0:T(128)} %bitcast.core_ref, ...), custom_call_target="tpu_custom_call" | custom-call | tf_op jit(solution)/shard_map/own/pallas_call | solution.py:336
  11.7 3.0 %collective-permute-start.1 = (bf16[16,16,512]{2,1,0:T(8,128)(2,1)S(1)}, bf16[16,16,512]{2,1,0:T(8,128)(2,1)S(1)}, u32[]{:S(2)}, u32[]{:S(2)}) collective-permute-start(bf16[16,16,512]{2,1,0:T(8,128)(2,1)S(1)} %get-tuple-element.25), channel_id=1, source_target_pairs={{1,2},{2,1},{3,4},{4,3},{5,6},{6,5},{7,8},{8,7},{9,10},{10,9},{11,... | collective-permute-start | bytes 786440 | tf_op jit(solution)/shard_map/ppermute | solution.py:313
  14.7 3.1 %collective-permute-start.2 = (bf16[16,16,512]{2,1,0:T(8,128)(2,1)S(1)}, bf16[16,16,512]{2,1,0:T(8,128)(2,1)S(1)}, u32[]{:S(2)}, u32[]{:S(2)}) collective-permute-start(bf16[16,16,512]{2,1,0:T(8,128)(2,1)S(1)} %get-tuple-element.26), channel_id=1, source_target_pairs={{1,3},{2,0},{3,5},{4,2},{5,7},{6,4},{7,9},{8,6},{9,11},{10,8},{11,... | collective-permute-start | bytes 786440 | tf_op jit(solution)/shard_map/ppermute | solution.py:313
  17.8 1.9 %collective-permute-start.3 = (bf16[4,8,512]{2,1,0:T(8,128)(2,1)S(1)}, bf16[4,8,512]{2,1,0:T(8,128)(2,1)S(1)}, u32[]{:S(2)}, u32[]{:S(2)}) collective-permute-start(bf16[4,8,512]{2,1,0:T(8,128)(2,1)S(1)} %get-tuple-element.27), channel_id=1, source_target_pairs={{0,32},{2,34},{4,36},{6,38},{8,40},{10,42},{12,44},{14,46},{16,48}... | collective-permute-start | bytes 98312 | tf_op jit(solution)/shard_map/ppermute | solution.py:313
  19.8 1.9 %collective-permute-start.4 = (bf16[4,8,512]{2,1,0:T(8,128)(2,1)S(1)}, bf16[4,8,512]{2,1,0:T(8,128)(2,1)S(1)}, u32[]{:S(2)}, u32[]{:S(2)}) collective-permute-start(bf16[4,8,512]{2,1,0:T(8,128)(2,1)S(1)} %get-tuple-element.28), channel_id=1, source_target_pairs={{1,32},{3,34},{5,36},{7,38},{9,40},{11,42},{13,44},{15,46},{17,48}... | collective-permute-start | bytes 98312 | tf_op jit(solution)/shard_map/ppermute | solution.py:313
  21.7 0.0 collective-permute-done
  21.7 8.6 %other.1 = (f32[4,256,512]{2,1,0:T(8,128)S(1)}, f32[4,256,512]{2,1,0:T(8,128)S(1)}, f32[4,256,512]{2,1,0:T(8,128)S(1)}, f32[2,256,512]{2,1,0:T(8,128)S(1)}, f32[...) custom-call(s32[1]{0:T(128)} %bitcast.core_ref, ...), custom_call_target="tpu_custom_call" | custom-call | tf_op jit(solution)/shard_map/other/pallas_call | solution.py:352
  30.3 0.0 collective-permute-done.3.edge_own
  30.4 0.0 collective-permute-done.4.edge_other
  30.4 0.0 collective-permute-done.1.outer_own
  30.4 0.0 collective-permute-done.2.outer_other
  30.4 0.0 copy-done.1
  30.4 2.8 %slab.1 = f32[16,64,512]{2,1,0:T(8,128)S(1)} custom-call(s32[1]{0:T(128)} %bitcast.core_ref, bf16[4,16,2,16,512]{4,3,2,1,0:T(8,128)(2,1)S(1)} %bitcast.4, bf16[4,16,2,16,512]{4,3,2,1,0:T(8,128)(2,1)S(1)} %bitcast.6, bf16[16,16,512]{2,1,0:T(8,128)(2,1)S(1)} %collective-permute-done.1.outer_own, bf16[16,16,512]{2,1,0:T(8,128)(2,1)S(1)} %collective-permute-done.2.outer_other, ...), custom_call_target="tpu_custom_call" | custom-call | tf_op jit(solution)/shard_map/slab/pallas_call | solution.py:361
  33.2 0.3 convert_element_type.6
  33.5 26.2 %all_to_all.5 = f16[16,64,512]{2,1,0:T(8,128)(2,1)S(1)} all-to-all(f16[16,64,512]{2,1,0:T(8,128)(2,1)S(1)} %convert_element_type.6), channel_id=1, replica_groups={{0,2,4,6,8,10,12,14,16,18,20,22,24,26,28,30},{1,3,5,7,9,11,13,15,17,19,..., dimensions={0} | all-to-all | bytes 2097152 | tf_op jit(solution)/shard_map/all_to_all | solution.py:372
  59.7 0.0 copy-start.3
  59.7 0.3 convert_element_type.7.parts
  60.0 0.4 copy-done.3
  60.4 0.9 %merge.1 = f32[4,8192]{1,0:T(4,128)} custom-call(f32[16,64,512]{2,1,0:T(8,128)S(1)} %convert_element_type.7.parts, bf16[4,128]{1,0:T(4,128)(2,1)S(1)} %copy-done.3), custom_call_target="tpu_custom_call" | custom-call | tf_op jit(solution)/shard_map/merge/pallas_call | solution.py:376
Async XLA Ops:
  0.0 21.7 %collective-permute-start = (bf16[4,512,512]{2,1,0:T(8,128)(2,1)}, bf16[4,512,512]{2,1,0:T(8,128)(2,1)S(1)}, u32[]{:S(2)}, u32[]{:S(2)}) collective-permute-start(bf16[4,512,512]{2,1,0:T(8,128)(2,1)} %param.2), channel_id=1, source_target_pairs={{0,1},{1,0},{2,3},{3,2},{4,5},{5,4},{6,7},{7,6},{8,9},{9,8},{10,11... | collective-permute-start | bytes 6291464 | tf_op jit(solution)/shard_map/ppermute | solution.py:334
  0.7 1.6 %copy-start = (bf16[4,512,512]{2,1,0:T(8,128)(2,1)S(1)}, bf16[4,512,512]{2,1,0:T(8,128)(2,1)}, u32[]{:S(2)}) copy-start(bf16[4,512,512]{2,1,0:T(8,128)(2,1)} %param.2) | copy-start | bytes 6291460
  2.3 0.7 %copy-start.2 = (bf16[4,128]{1,0:T(4,128)(2,1)S(1)}, bf16[4,128]{1,0:T(4,128)(2,1)}, u32[]{:S(2)}) copy-start(bf16[4,128]{1,0:T(4,128)(2,1)} %table.7) | copy-start | bytes 3076
  2.9 27.4 %copy-start.1 = (bf16[4,512,512]{2,1,0:T(8,128)(2,1)S(1)}, bf16[4,512,512]{2,1,0:T(8,128)(2,1)}, u32[]{:S(2)}) copy-start(bf16[4,512,512]{2,1,0:T(8,128)(2,1)} %param.2) | copy-start | bytes 6291460
  11.7 18.7 %collective-permute-start.1 = (bf16[16,16,512]{2,1,0:T(8,128)(2,1)S(1)}, bf16[16,16,512]{2,1,0:T(8,128)(2,1)S(1)}, u32[]{:S(2)}, u32[]{:S(2)}) collective-permute-start(bf16[16,16,512]{2,1,0:T(8,128)(2,1)S(1)} %get-tuple-element.25), channel_id=1, source_target_pairs={{1,2},{2,1},{3,4},{4,3},{5,6},{6,5},{7,8},{8,7},{9,10},{10,9},{11,... | collective-permute-start | bytes 786440 | tf_op jit(solution)/shard_map/ppermute | solution.py:313
  14.7 15.7 %collective-permute-start.2 = (bf16[16,16,512]{2,1,0:T(8,128)(2,1)S(1)}, bf16[16,16,512]{2,1,0:T(8,128)(2,1)S(1)}, u32[]{:S(2)}, u32[]{:S(2)}) collective-permute-start(bf16[16,16,512]{2,1,0:T(8,128)(2,1)S(1)} %get-tuple-element.26), channel_id=1, source_target_pairs={{1,3},{2,0},{3,5},{4,2},{5,7},{6,4},{7,9},{8,6},{9,11},{10,8},{11,... | collective-permute-start | bytes 786440 | tf_op jit(solution)/shard_map/ppermute | solution.py:313
  17.8 12.5 %collective-permute-start.3 = (bf16[4,8,512]{2,1,0:T(8,128)(2,1)S(1)}, bf16[4,8,512]{2,1,0:T(8,128)(2,1)S(1)}, u32[]{:S(2)}, u32[]{:S(2)}) collective-permute-start(bf16[4,8,512]{2,1,0:T(8,128)(2,1)S(1)} %get-tuple-element.27), channel_id=1, source_target_pairs={{0,32},{2,34},{4,36},{6,38},{8,40},{10,42},{12,44},{14,46},{16,48}... | collective-permute-start | bytes 98312 | tf_op jit(solution)/shard_map/ppermute | solution.py:313
  19.8 10.6 %collective-permute-start.4 = (bf16[4,8,512]{2,1,0:T(8,128)(2,1)S(1)}, bf16[4,8,512]{2,1,0:T(8,128)(2,1)S(1)}, u32[]{:S(2)}, u32[]{:S(2)}) collective-permute-start(bf16[4,8,512]{2,1,0:T(8,128)(2,1)S(1)} %get-tuple-element.28), channel_id=1, source_target_pairs={{1,32},{3,34},{5,36},{7,38},{9,40},{11,42},{13,44},{15,46},{17,48}... | collective-permute-start | bytes 98312 | tf_op jit(solution)/shard_map/ppermute | solution.py:313
  59.7 0.7 %copy-start.3 = (bf16[4,128]{1,0:T(4,128)(2,1)S(1)}, bf16[4,128]{1,0:T(4,128)(2,1)}, u32[]{:S(2)}) copy-start(bf16[4,128]{1,0:T(4,128)(2,1)} %table.7) | copy-start | bytes 3076

commit v7 on v6

--- a/solution.py
+++ b/solution.py
@@ -38,16 +38,21 @@
     return jnp.maximum(colour, TINY), jnp.maximum(extinction * slab_share, TINY)
 
 
-def spread(table, slab_share, depth_total):
+def prepare_kernel(core_ref, table_ref, rows_op, cols_op, tables, scales, *, slab_share, depth_total):
+    table = table_ref[...].astype(F32)
     entries = table.shape[1]
+    rows_op[...] = row_differences(rows_op.shape[1], core_ref[0])
+    cols_op[...] = column_differences(cols_op.shape[1])
     colour_top, opacity_top = tops(table, slab_share)
     scale = SLOPE / (colour_top * opacity_top)
-    lower = [table[c : c + 1] * scale for c in range(3)]
-    lower.append(table[3:4] * float(-np.log2(np.e) / depth_total))
-    lower = [jnp.broadcast_to(t, (HALF, entries)) for t in lower]
     last = lax.broadcasted_iota(jnp.int32, (HALF, entries), 1) == entries - 1
-    upper = [jnp.where(last, t, pltpu.roll(t, entries - 1, 1)) for t in lower]
-    return lower + upper
+    for c in range(4):
+        factor = scale if c < 3 else float(-np.log2(np.e) / depth_total)
+        lower = jnp.broadcast_to(table[c : c + 1] * factor, (HALF, entries))
+        tables[c] = lower
+        tables[c + 4] = jnp.where(last, lower, pltpu.roll(lower, entries - 1, 1))
+    for at, value in enumerate((colour_top * opacity_top, opacity_top, 1.0 / opacity_top)):
+        scales[at] = jnp.broadcast_to(value, (HALF, LANES))
 
 
 def look_up(table, index):
@@ -93,24 +98,23 @@
     return [jnp.where(condition, x, y) for x, y in zip(a, b)]
 
 
-def slices_kernel(cells, core, rows_op, cols_op, table, outs, inner_slope, inner_norm, shares):
-    first, last, middle, slope, norm, edge_dx, edge_dy = outs
+def pair_terms(cells, end, core, rows_op, cols_op, tables, outs, inner_slope, inner_norm):
+    kept, inner, slope, norm, edge_dx, edge_dy = outs
     slices, blocks, _, _, cols = cells.shape
     rows = blocks * BLOCK
-    ends = (0, slices - 1)
-    for z in range(slices):
+    near = 1 if end == 0 else end - 1
+    for at, z, to_slope, to_norm in (
+        (0, end, slope, norm), (1, near, inner_slope, inner_norm)
+    ):
         dx = jnp.dot(rows_op[...], cells[z].reshape(2 * rows, cols), preferred_element_type=F32)
         dy = jnp.dot(
             cells[z, :, core].reshape(rows, cols), cols_op[...], preferred_element_type=F32
         )
-        to_slope, to_norm, at = (
-            (slope, norm, ends.index(z)) if z in ends else (inner_slope, inner_norm, z - 1)
-        )
-        to_slope[at] = slope_of(dx, dy)
-        to_norm[at] = norm_of(dx, dy)
-        edge_dx[z] = jnp.where(core == 0, dx[:HALF], dx[rows - HALF :])
-        edge_dy[z] = jnp.where(core == 0, dy[:HALF], dy[rows - HALF :])
-    tabs = spread(table[...].astype(F32), **shares)
+        to_slope[...] = slope_of(dx, dy)
+        to_norm[...] = norm_of(dx, dy)
+        edge_dx[at] = jnp.where(core == 0, dx[:HALF], dx[rows - HALF :])
+        edge_dy[at] = jnp.where(core == 0, dy[:HALF], dy[rows - HALF :])
+    tabs = [tables[c] for c in range(8)]
 
     def block(b, carry):
         for half in range(0, BLOCK, HALF):
@@ -118,30 +122,26 @@
             rows = slice(half, half + HALF)
             for start in range(0, cols, LANES):
                 lanes = slice(start, start + LANES)
-                mine = [cells[z, b, core, rows, lanes].astype(F32) for z in range(slices)]
-                accum, transmit = nothing()
-                for z in range(slices):
-                    found = classify(mine[z], tabs)
-                    if z in ends:
-                        ref = last if z else first
-                        for c in range(4):
-                            ref[c, here, lanes] = found[c]
-                    else:
-                        accum, transmit = shade(
-                            accum, transmit, mine[z + 1] - mine[z - 1],
-                            inner_slope[z - 1, here, lanes], inner_norm[z - 1, here, lanes], found,
-                        )
+                before, after = (
+                    cells[z, b, core, rows, lanes].astype(F32) for z in (near - 1, near + 1)
+                )
+                found = classify(before if end == near - 1 else after, tabs)
+                for c in range(4):
+                    kept[c, here, lanes] = found[c]
+                accum, transmit = shade(
+                    *nothing(), after - before, inner_slope[here, lanes], inner_norm[here, lanes],
+                    classify(cells[near, b, core, rows, lanes].astype(F32), tabs),
+                )
                 for c in range(3):
-                    middle[c, here, lanes] = accum[c]
-                middle[3, here, lanes] = transmit
+                    inner[c, here, lanes] = accum[c]
+                inner[3, here, lanes] = transmit
         return carry
 
     lax.fori_loop(0, blocks, block, 0)
 
 
-def own_kernel(core_ref, cells, table, *refs, shares):
-    outs, rest = refs[:7], refs[7:]
-    rows_op, cols_op, to_other, to_same, edge_same, edge_cross, inner_slope, inner_norm = rest
+def opening_kernel(core_ref, cells, rows_op, cols_op, tables, *refs):
+    outs, (to_other, to_same, edge_same, edge_cross), inner = refs[:6], refs[6:10], refs[10:]
     slices, blocks, _, _, cols = cells.shape
     core = core_ref[0]
     outer = (slices - 1) * core
@@ -158,29 +158,22 @@
         edge_same[...] = cells[:, 0, 0, :HALF, :]
         edge_cross[...] = cells[:, blocks - 1, 1, HALF:, :]
 
-    rows_op[...] = row_differences(2 * blocks * BLOCK, core)
-    cols_op[...] = column_differences(cols)
-    slices_kernel(
-        cells, core, rows_op, cols_op, table, outs, inner_slope, inner_norm, shares
-    )
-
-
-def other_kernel(core_ref, cells, table, rows_op, cols_op, *refs, shares):
-    slices_kernel(
-        cells, core_ref[0], rows_op, cols_op, table, refs[:7], refs[7], refs[8], shares
-    )
+    pair_terms(cells, 0, core, rows_op, cols_op, tables, outs, *inner)
+
+
+def pair_kernel(core_ref, cells, rows_op, cols_op, tables, _, *refs, end):
+    pair_terms(cells, end, core_ref[0], rows_op, cols_op, tables, refs[:6], *refs[6:])
 
 
 def slab_kernel(
-    core_ref, own, other, outer_own, outer_other, edge_own, edge_other, table, *refs, shares
+    core_ref, own, other, outer_own, outer_other, edge_own, edge_other, tables, scales, *refs
 ):
-    own_terms, other_terms, out = refs[:7], refs[7:14], refs[14]
+    own_terms, other_terms, out = (refs[0:6], refs[6:12]), (refs[12:18], refs[18:24]), refs[24]
     slices, blocks, _, _, cols = own.shape
     core = core_ref[0]
     front = core == 0
     end = slices - 1
-    table_values = table[...].astype(F32)
-    opacity_scale = 1.0 / tops(table_values, shares["slab_share"])[1]
+    opacity_scale = scales[2]
 
     def stacks(mine, theirs, end_own, end_other):
         own_stack = (
@@ -206,17 +199,16 @@
                 lanes = slice(start, start + LANES)
 
                 def half_slab(stack, terms):
-                    first, last, middle, slope, norm = terms[:5]
-                    parts = []
-                    for ref, at, z in ((first, 0, 0), (last, 1, end)):
+                    ends, inners = [], []
+                    for (kept, inner, slope, norm, _, _), z in zip(terms, (0, end)):
                         accum, transmit = shade(
                             *nothing(), stack[z + 2] - stack[z],
-                            slope[at, here, lanes], norm[at, here, lanes],
-                            [ref[c, here, lanes] for c in range(4)],
+                            slope[here, lanes], norm[here, lanes],
+                            [kept[c, here, lanes] for c in range(4)],
                         )
-                        parts.append(accum + [transmit])
-                    inner = [middle[c, here, lanes] for c in range(4)]
-                    return over(parts[0], over(inner, parts[1]))
+                        ends.append(accum + [transmit])
+                        inners.append([inner[c, here, lanes] for c in range(4)])
+                    return over(over(ends[0], inners[0]), over(inners[1], ends[1]))
 
                 own_stack, other_stack = stacks(
                     [own[z, b, core, rows, lanes].astype(F32) for z in range(slices)],
@@ -232,7 +224,7 @@
 
     lax.fori_loop(0, blocks, block, 0)
 
-    tabs = spread(table_values, **shares)
+    tabs = [tables[c] for c in range(8)]
     b = jnp.where(front, 0, blocks - 1)
     row = lax.broadcasted_iota(jnp.int32, (HALF, LANES), 0)
     at_edge = row == jnp.where(front, 0, HALF - 1)
@@ -248,8 +240,10 @@
             for z in range(slices):
                 halo = edge[z, :, lanes].astype(F32)
                 halo = jnp.where(front, -halo[HALF - 1 : HALF], halo[0:1])
-                dx = terms[5][z, :, lanes] + jnp.where(at_edge, halo, 0.0)
-                dy = terms[6][z, :, lanes]
+                _, _, _, _, edge_dx, edge_dy = terms[z // 2]
+                at = 0 if z in (0, end) else 1
+                dx = edge_dx[at, :, lanes] + jnp.where(at_edge, halo, 0.0)
+                dy = edge_dy[at, :, lanes]
                 accum, transmit = shade(
                     accum, transmit, stack[z + 2] - stack[z],
                     slope_of(dx, dy), norm_of(dx, dy), classify(stack[z + 1], tabs),
@@ -270,9 +264,9 @@
             out[b, pl.ds(at, HALF), lanes] = both[c]
 
 
-def merge_kernel(parts, table, out, image, *, slab_share):
+def merge_kernel(parts, scales, out, image):
     cols = parts.shape[2]
-    colour_top, opacity_top = tops(table[...].astype(F32), slab_share)
+    colour_scale, opacity_top = scales[0], scales[1]
     for half in range(0, BLOCK, HALF):
         for start in range(0, cols, LANES):
             lanes = slice(start, start + LANES)
@@ -283,7 +277,7 @@
                 ]
                 accum = [a + transmit * p for a, p in zip(accum, part[:3])]
                 transmit = transmit - transmit * (part[3] * opacity_top)
-            whole = [a * (colour_top * opacity_top) for a in accum] + [1.0 - transmit]
+            whole = [a * colour_scale for a in accum] + [1.0 - transmit]
             for c in range(4):
                 at = start // LANES, slice(c * BLOCK + half, c * BLOCK + half + HALF)
                 image[at] = whole[c]
@@ -318,70 +312,89 @@
     same_core = [[2 * j + c for j in range(chips)] for c in range(2)]
     vmem = pl.BlockSpec(memory_space=pltpu.MemorySpace.VMEM)
     smem = pl.BlockSpec(memory_space=pltpu.MemorySpace.SMEM)
-    shares = dict(slab_share=2.0 * slices / depth_total, depth_total=depth_total)
     params = pltpu.CompilerParams(vmem_limit_bytes=16 << 20)
     quad = jax.ShapeDtypeStruct((4, half, cols), F32)
-    two = jax.ShapeDtypeStruct((2, half, cols), F32)
-    unit = jax.ShapeDtypeStruct((slices, HALF, cols), F32)
+    flat = jax.ShapeDtypeStruct((half, cols), F32)
+    unit = jax.ShapeDtypeStruct((2, HALF, cols), F32)
     plane = jax.ShapeDtypeStruct((blocks, BLOCK, cols), BF16)
     edge = jax.ShapeDtypeStruct((slices, HALF, cols), BF16)
-    terms = (quad, quad, quad, two, two, unit, unit)
-    operators = (
-        jax.ShapeDtypeStruct((half, rows), BF16), jax.ShapeDtypeStruct((cols, cols), BF16)
-    )
-    inner = [pltpu.VMEM((slices - 2, half, cols), F32)] * 2
+    terms = (quad, quad, flat, flat, unit, unit)
+    inner = [pltpu.VMEM((half, cols), F32)] * 2
 
     other = lax.ppermute(volume, "depth", [(d, d ^ 1) for d in range(depth_count)]).reshape(split)
     own = volume.reshape(split)
+    entries = transfer_table.shape[1]
+    *ops, scales = pl.pallas_call(
+        functools.partial(
+            prepare_kernel, slab_share=2.0 * slices / depth_total, depth_total=depth_total
+        ),
+        out_shape=(
+            jax.ShapeDtypeStruct((half, rows), BF16),
+            jax.ShapeDtypeStruct((cols, cols), BF16),
+            jax.ShapeDtypeStruct((8, HALF, entries), F32),
+            jax.ShapeDtypeStruct((3, HALF, LANES), F32),
+        ),
+        in_specs=[smem, vmem],
+        out_specs=(vmem,) * 4,
+        compiler_params=params,
+        name="prepare",
+    )(core_arg, transfer_table)
     results = pl.pallas_call(
-        functools.partial(own_kernel, shares=shares),
-        out_shape=(*terms, *operators, plane, plane, edge, edge),
-        in_specs=[smem, vmem, vmem],
-        out_specs=(vmem,) * 13,
+        opening_kernel,
+        out_shape=(*terms, plane, plane, edge, edge),
+        in_specs=[smem] + [vmem] * 4,
+        out_specs=(vmem,) * 10,
         scratch_shapes=inner,
         compiler_params=params,
-        name="own",
-    )(core_arg, own, transfer_table)
-    own_terms, ops, (to_other, to_same, edge_same, edge_cross) = (
-        results[:7], results[7:9], results[9:]
-    )
+        name="opening",
+    )(core_arg, own, *ops)
+    to_other, to_same, edge_same, edge_cross = results[6:]
+
+    def slice_pair(cells, end, previous, name):
+        return pl.pallas_call(
+            functools.partial(pair_kernel, end=end),
+            out_shape=terms,
+            in_specs=[smem] + [vmem] * 5,
+            out_specs=(vmem,) * 6,
+            scratch_shapes=inner,
+            compiler_params=params,
+            name=name,
+        )(core_arg, cells, *ops, previous[5])
+
+    own_terms = [results[:6]]
+    outer_own = shift(to_other, lambda c: 0, lambda c: 1 if c else -1)
+    own_terms.append(slice_pair(own, slices - 1, own_terms[0], "own_far"))
+    to_same, _ = lax.optimization_barrier((to_same, own_terms[1][5]))
     outer_other = shift(to_same, lambda c: 0, lambda c: 2 if c else -2)
-    outer_own = shift(to_other, lambda c: 0, lambda c: 1 if c else -1)
+    other_terms = [slice_pair(other, 0, own_terms[1], "other_near")]
+    edge_same, edge_cross, _ = lax.optimization_barrier((edge_same, edge_cross, other_terms[0][5]))
     edge_own = shift(edge_same, lambda c: -1 if c else 1, lambda c: 0)
     edge_other = shift(edge_cross, lambda c: 1 if c else -1, lambda c: -1 if c else 1)
-    other_terms = pl.pallas_call(
-        functools.partial(other_kernel, shares=shares),
-        out_shape=terms,
-        in_specs=[smem] + [vmem] * 4,
-        out_specs=(vmem,) * 7,
-        scratch_shapes=inner,
-        compiler_params=params,
-        name="other",
-    )(core_arg, other, transfer_table, *ops)
+    other_terms.append(slice_pair(other, slices - 1, other_terms[0], "other_far"))
     partial_image = pl.pallas_call(
-        functools.partial(slab_kernel, shares=shares),
+        slab_kernel,
         out_shape=jax.ShapeDtypeStruct((blocks, 4 * BLOCK, cols), F32),
-        in_specs=[smem] + [vmem] * 21,
+        in_specs=[smem] + [vmem] * 32,
         out_specs=vmem,
         compiler_params=params,
         name="slab",
     )(
-        core_arg, own, other, outer_own, outer_other, edge_own, edge_other, transfer_table,
-        *own_terms, *other_terms,
+        core_arg, own, other, outer_own, outer_other, edge_own, edge_other, ops[2], scales,
+        *own_terms[0], *own_terms[1], *other_terms[0], *other_terms[1],
     )
     pieces = lax.all_to_all(
         partial_image.astype(jnp.float16), "depth", split_axis=0, concat_axis=0, tiled=True,
         axis_index_groups=same_core,
     )
     return pl.pallas_call(
-        functools.partial(merge_kernel, slab_share=shares["slab_share"]),
+        merge_kernel,
         out_shape=jax.ShapeDtypeStruct((4, BLOCK * cols), F32),
         in_specs=[vmem, vmem],
         out_specs=vmem,
         scratch_shapes=[pltpu.VMEM((cols // LANES, 4 * BLOCK, LANES), F32)],
         compiler_params=params,
         name="merge",
-    )(pieces.astype(F32), transfer_table)
+    )(pieces.astype(F32), scales)
 
 
 def solution(mesh):

time: 61.6 us -> 65 us (1.055)
  Pallas kernels: 21.1 us -> 24.8 us
    pallas_call x4 -> x7, Pallas kernels: 21.1 us -> 24.8 us  [the longest x3 15.3 us: slice_pair(): pl.pallas_call(functools.partial(pair_kernel, end=end), out_shape=terms,...]
    unnamed x8 -> x6, local copies, waits for them, and re-layouts: 2.69 us -> 2.27 us
  transfers between devices with their start and end apart: 5 -> 5, of which waited for: 0 -> 0; matrix products, arithmetic and copies ran while one was open for 0% -> 0% of each run, Pallas kernels for 28% -> 32%
where the time goes in v7:
time: 65 us; the launch traced here: 64.8 us
  blocking collectives  26.2 us (40%)
  Pallas kernels  24.8 us (38%)
  starting transfers between devices  10.8 us (17%)
  local copies, waits for them, and re-layouts  2.27 us (3%)
    all_to_all x1, blocking collectives, shards(): lax.all_to_all(partial_image.astype(jnp.float16), 'depth', split_axis=0,...  26.2 us
    pallas_call x3, Pallas kernels, slice_pair(): pl.pallas_call(functools.partial(pair_kernel, end=end), out_shape=terms,...  15.3 us
    ppermute x4, starting transfers between devices, shift(): return lax.ppermute(x, ('img', 'depth'), pairs)  10.1 us
    pallas_call x1, Pallas kernels, shards(): pl.pallas_call(opening_kernel, out_shape=(*terms, plane, plane, edge, edg...  5.13 us
    pallas_call x1, Pallas kernels, shards(): pl.pallas_call(slab_kernel, out_shape=jax.ShapeDtypeStruct((blocks, 4 * B...  3.18 us
    unnamed x6, local copies, waits for them, and re-layouts  2.27 us
  transfers between devices with their start and end apart: 5, of which 0 were waited for; matrix products, arithmetic and copies ran while one was open for 0% of the time, Pallas kernels for 32%

profile of v7, /device:TPU:33, one launch (start us, length us, event | category | flops | bytes accessed | tf_op | source)
XLA Modules:
  0.0 64.8 jit_solution(5904382610165689450)
XLA Ops:
  0.0 0.7 %collective-permute-start = (bf16[4,512,512]{2,1,0:T(8,128)(2,1)}, bf16[4,512,512]{2,1,0:T(8,128)(2,1)S(1)}, u32[]{:S(2)}, u32[]{:S(2)}) collective-permute-start(bf16[4,512,512]{2,1,0:T(8,128)(2,1)} %param.2), channel_id=1, source_target_pairs={{0,1},{1,0},{2,3},{3,2},{4,5},{5,4},{6,7},{7,6},{8,9},{9,8},{10,11... | collective-permute-start | bytes 6291464 | tf_op jit(solution)/shard_map/ppermute | solution.py:324
  0.7 0.0 copy-start.2
  0.7 0.7 %copy-done.2 = bf16[4,128]{1,0:T(4,128)(2,1)S(1)} copy-done((bf16[4,128]{1,0:T(4,128)(2,1)S(1)}, bf16[4,128]{1,0:T(4,128)(2,1)}, u32[]{:S(2)}) %copy-start.2) | copy-done | bytes 1048
  1.4 0.4 prepare.1
  1.7 0.0 copy-start
  1.7 1.6 %copy-done = bf16[4,512,512]{2,1,0:T(8,128)(2,1)S(1)} copy-done((bf16[4,512,512]{2,1,0:T(8,128)(2,1)S(1)}, bf16[4,512,512]{2,1,0:T(8,128)(2,1)}, u32[]{:S(2)}) %copy-start) | copy-done | bytes 2097176
  3.3 5.1 %opening.1 = (f32[4,256,512]{2,1,0:T(8,128)S(1)}, f32[4,256,512]{2,1,0:T(8,128)S(1)}, f32[256,512]{1,0:T(8,128)S(1)}, f32[256,512]{1,0:T(8,128)S(1)}, f32[2,8,51...) custom-call(s32[1]{0:T(128)} %bitcast.core_ref, ...), custom_call_target="tpu_custom_call" | custom-call | tf_op jit(solution)/shard_map/opening/pallas_call | solution.py:342
  8.4 3.0 %collective-permute-start.1 = (bf16[16,16,512]{2,1,0:T(8,128)(2,1)S(1)}, bf16[16,16,512]{2,1,0:T(8,128)(2,1)S(1)}, u32[]{:S(2)}, u32[]{:S(2)}) collective-permute-start(bf16[16,16,512]{2,1,0:T(8,128)(2,1)S(1)} %get-tuple-element.43), channel_id=1, source_target_pairs={{1,2},{2,1},{3,4},{4,3},{5,6},{6,5},{7,8},{8,7},{9,10},{10,9},{11,... | collective-permute-start | bytes 786440 | tf_op jit(solution)/shard_map/ppermute | solution.py:307
  11.5 5.1 %own_far.1 = (f32[4,256,512]{2,1,0:T(8,128)S(1)}, f32[4,256,512]{2,1,0:T(8,128)S(1)}, f32[256,512]{1,0:T(8,128)S(1)}, f32[256,512]{1,0:T(8,128)S(1)}, f32[2,8,51...) custom-call(s32[1]{0:T(128)} %bitcast.core_ref, bf16[4,16,2,16,512]{4,3,2,1,0:T(8,128)(2,1)S(1)} %bitcast.4, ...), custom_call_target="tpu_custom_call" | custom-call | tf_op jit(solution)/shard_map/own_far/pallas_call | solution.py:354
  16.6 3.1 %collective-permute-start.2 = (bf16[16,16,512]{2,1,0:T(8,128)(2,1)S(1)}, bf16[16,16,512]{2,1,0:T(8,128)(2,1)S(1)}, u32[]{:S(2)}, u32[]{:S(2)}) collective-permute-start(bf16[16,16,512]{2,1,0:T(8,128)(2,1)S(1)} %get-tuple-element.47), channel_id=1, source_target_pairs={{1,3},{2,0},{3,5},{4,2},{5,7},{6,4},{7,9},{8,6},{9,11},{10,8},{11,... | collective-permute-start | bytes 786440 | tf_op jit(solution)/shard_map/ppermute | solution.py:307
  19.7 0.0 collective-permute-done
  19.7 5.1 %other_near.1 = (f32[4,256,512]{2,1,0:T(8,128)S(1)}, f32[4,256,512]{2,1,0:T(8,128)S(1)}, f32[256,512]{1,0:T(8,128)S(1)}, f32[256,512]{1,0:T(8,128)S(1)}, f32[2,8...) custom-call(s32[1]{0:T(128)} %bitcast.core_ref, bf16[4,16,2,16,512]{4,3,2,1,0:T(8,128)(2,1)S(1)} %bitcast.6, ...), custom_call_target="tpu_custom_call" | custom-call | tf_op jit(solution)/shard_map/other_near/pallas_call | solution.py:354
  24.8 0.0 copy-start.1
  24.8 2.1 %collective-permute-start.3 = (bf16[4,8,512]{2,1,0:T(8,128)(2,1)S(1)}, bf16[4,8,512]{2,1,0:T(8,128)(2,1)S(1)}, u32[]{:S(2)}, u32[]{:S(2)}) collective-permute-start(bf16[4,8,512]{2,1,0:T(8,128)(2,1)S(1)} %get-tuple-element.51), channel_id=1, source_target_pairs={{0,32},{2,34},{4,36},{6,38},{8,40},{10,42},{12,44},{14,46},{16,48}... | collective-permute-start | bytes 98312 | tf_op jit(solution)/shard_map/ppermute | solution.py:307
  26.9 1.9 %collective-permute-start.4 = (bf16[4,8,512]{2,1,0:T(8,128)(2,1)S(1)}, bf16[4,8,512]{2,1,0:T(8,128)(2,1)S(1)}, u32[]{:S(2)}, u32[]{:S(2)}) collective-permute-start(bf16[4,8,512]{2,1,0:T(8,128)(2,1)S(1)} %get-tuple-element.52), channel_id=1, source_target_pairs={{1,32},{3,34},{5,36},{7,38},{9,40},{11,42},{13,44},{15,46},{17,48}... | collective-permute-start | bytes 98312 | tf_op jit(solution)/shard_map/ppermute | solution.py:307
  28.8 5.1 %other_far.1 = (f32[4,256,512]{2,1,0:T(8,128)S(1)}, f32[4,256,512]{2,1,0:T(8,128)S(1)}, f32[256,512]{1,0:T(8,128)S(1)}, f32[256,512]{1,0:T(8,128)S(1)}, f32[2,8,...) custom-call(s32[1]{0:T(128)} %bitcast.core_ref, bf16[4,16,2,16,512]{4,3,2,1,0:T(8,128)(2,1)S(1)} %bitcast.7, ...), custom_call_target="tpu_custom_call" | custom-call | tf_op jit(solution)/shard_map/other_far/pallas_call | solution.py:354
  33.9 0.0 collective-permute-done.1.outer_own
  33.9 0.0 collective-permute-done.2.outer_other
  33.9 0.0 collective-permute-done.3.edge_own
  33.9 0.0 collective-permute-done.4.edge_other
  34.0 0.0 copy-done.1
  34.0 3.2 %slab.1 = f32[16,64,512]{2,1,0:T(8,128)S(1)} custom-call(s32[1]{0:T(128)} %bitcast.core_ref, bf16[4,16,2,16,512]{4,3,2,1,0:T(8,128)(2,1)S(1)} %bitcast.5, bf16[4,16,2,16,512]{4,3,2,1,0:T(8,128)(2,1)S(1)} %bitcast.8, bf16[16,16,512]{2,1,0:T(8,128)(2,1)S(1)} %collective-permute-done.1.outer_own, bf16[16,16,512]{2,1,0:T(8,128)(2,1)S(1)} %collective-permute-done.2.outer_other, ...), custom_call_target="tpu_custom_call" | custom-call | tf_op jit(solution)/shard_map/slab/pallas_call | solution.py:374
  37.2 0.3 convert_element_type.6
  37.4 26.2 %all_to_all.5 = f16[16,64,512]{2,1,0:T(8,128)(2,1)S(1)} all-to-all(f16[16,64,512]{2,1,0:T(8,128)(2,1)S(1)} %convert_element_type.6), channel_id=1, replica_groups={{0,2,4,6,8,10,12,14,16,18,20,22,24,26,28,30},{1,3,5,7,9,11,13,15,17,19,..., dimensions={0} | all-to-all | bytes 2097152 | tf_op jit(solution)/shard_map/all_to_all | solution.py:385
  63.6 0.3 convert_element_type.7.parts
  63.9 0.9 %merge.1 = f32[4,8192]{1,0:T(4,128)} custom-call(f32[16,64,512]{2,1,0:T(8,128)S(1)} %convert_element_type.7.parts, f32[3,8,128]{2,1,0:T(8,128)S(1)} %get-tuple-element.53.scales), custom_call_target="tpu_custom_call" | custom-call | tf_op jit(solution)/shard_map/merge/pallas_call | solution.py:389
Async XLA Ops:
  0.0 19.7 %collective-permute-start = (bf16[4,512,512]{2,1,0:T(8,128)(2,1)}, bf16[4,512,512]{2,1,0:T(8,128)(2,1)S(1)}, u32[]{:S(2)}, u32[]{:S(2)}) collective-permute-start(bf16[4,512,512]{2,1,0:T(8,128)(2,1)} %param.2), channel_id=1, source_target_pairs={{0,1},{1,0},{2,3},{3,2},{4,5},{5,4},{6,7},{7,6},{8,9},{9,8},{10,11... | collective-permute-start | bytes 6291464 | tf_op jit(solution)/shard_map/ppermute | solution.py:324
  0.7 0.7 %copy-start.2 = (bf16[4,128]{1,0:T(4,128)(2,1)S(1)}, bf16[4,128]{1,0:T(4,128)(2,1)}, u32[]{:S(2)}) copy-start(bf16[4,128]{1,0:T(4,128)(2,1)} %table_ref.1) | copy-start | bytes 3076
  1.7 1.6 %copy-start = (bf16[4,512,512]{2,1,0:T(8,128)(2,1)S(1)}, bf16[4,512,512]{2,1,0:T(8,128)(2,1)}, u32[]{:S(2)}) copy-start(bf16[4,512,512]{2,1,0:T(8,128)(2,1)} %param.2) | copy-start | bytes 6291460
  8.4 25.5 %collective-permute-start.1 = (bf16[16,16,512]{2,1,0:T(8,128)(2,1)S(1)}, bf16[16,16,512]{2,1,0:T(8,128)(2,1)S(1)}, u32[]{:S(2)}, u32[]{:S(2)}) collective-permute-start(bf16[16,16,512]{2,1,0:T(8,128)(2,1)S(1)} %get-tuple-element.43), channel_id=1, source_target_pairs={{1,2},{2,1},{3,4},{4,3},{5,6},{6,5},{7,8},{8,7},{9,10},{10,9},{11,... | collective-permute-start | bytes 786440 | tf_op jit(solution)/shard_map/ppermute | solution.py:307
  16.6 17.4 %collective-permute-start.2 = (bf16[16,16,512]{2,1,0:T(8,128)(2,1)S(1)}, bf16[16,16,512]{2,1,0:T(8,128)(2,1)S(1)}, u32[]{:S(2)}, u32[]{:S(2)}) collective-permute-start(bf16[16,16,512]{2,1,0:T(8,128)(2,1)S(1)} %get-tuple-element.47), channel_id=1, source_target_pairs={{1,3},{2,0},{3,5},{4,2},{5,7},{6,4},{7,9},{8,6},{9,11},{10,8},{11,... | collective-permute-start | bytes 786440 | tf_op jit(solution)/shard_map/ppermute | solution.py:307
  24.8 9.1 %copy-start.1 = (bf16[4,512,512]{2,1,0:T(8,128)(2,1)S(1)}, bf16[4,512,512]{2,1,0:T(8,128)(2,1)}, u32[]{:S(2)}) copy-start(bf16[4,512,512]{2,1,0:T(8,128)(2,1)} %param.2) | copy-start | bytes 6291460
  24.8 9.1 %collective-permute-start.3 = (bf16[4,8,512]{2,1,0:T(8,128)(2,1)S(1)}, bf16[4,8,512]{2,1,0:T(8,128)(2,1)S(1)}, u32[]{:S(2)}, u32[]{:S(2)}) collective-permute-start(bf16[4,8,512]{2,1,0:T(8,128)(2,1)S(1)} %get-tuple-element.51), channel_id=1, source_target_pairs={{0,32},{2,34},{4,36},{6,38},{8,40},{10,42},{12,44},{14,46},{16,48}... | collective-permute-start | bytes 98312 | tf_op jit(solution)/shard_map/ppermute | solution.py:307
  26.9 7.1 %collective-permute-start.4 = (bf16[4,8,512]{2,1,0:T(8,128)(2,1)S(1)}, bf16[4,8,512]{2,1,0:T(8,128)(2,1)S(1)}, u32[]{:S(2)}, u32[]{:S(2)}) collective-permute-start(bf16[4,8,512]{2,1,0:T(8,128)(2,1)S(1)} %get-tuple-element.52), channel_id=1, source_target_pairs={{1,32},{3,34},{5,36},{7,38},{9,40},{11,42},{13,44},{15,46},{17,48}... | collective-permute-start | bytes 98312 | tf_op jit(solution)/shard_map/ppermute | solution.py:307

commit v8 on v6

--- a/solution.py
+++ b/solution.py
@@ -38,16 +38,21 @@
     return jnp.maximum(colour, TINY), jnp.maximum(extinction * slab_share, TINY)
 
 
-def spread(table, slab_share, depth_total):
+def prepare_kernel(core_ref, table_ref, rows_op, cols_op, tables, scales, *, slab_share, depth_total):
+    table = table_ref[...].astype(F32)
     entries = table.shape[1]
+    rows_op[...] = row_differences(rows_op.shape[1], core_ref[0])
+    cols_op[...] = column_differences(cols_op.shape[1])
     colour_top, opacity_top = tops(table, slab_share)
     scale = SLOPE / (colour_top * opacity_top)
-    lower = [table[c : c + 1] * scale for c in range(3)]
-    lower.append(table[3:4] * float(-np.log2(np.e) / depth_total))
-    lower = [jnp.broadcast_to(t, (HALF, entries)) for t in lower]
     last = lax.broadcasted_iota(jnp.int32, (HALF, entries), 1) == entries - 1
-    upper = [jnp.where(last, t, pltpu.roll(t, entries - 1, 1)) for t in lower]
-    return lower + upper
+    for c in range(4):
+        factor = scale if c < 3 else float(-np.log2(np.e) / depth_total)
+        lower = jnp.broadcast_to(table[c : c + 1] * factor, (HALF, entries))
+        tables[c] = lower
+        tables[c + 4] = jnp.where(last, lower, pltpu.roll(lower, entries - 1, 1))
+    for at, value in enumerate((colour_top * opacity_top, opacity_top, 1.0 / opacity_top)):
+        scales[at] = jnp.broadcast_to(value, (HALF, LANES))
 
 
 def look_up(table, index):
@@ -93,8 +98,9 @@
     return [jnp.where(condition, x, y) for x, y in zip(a, b)]
 
 
-def slices_kernel(cells, core, rows_op, cols_op, table, outs, inner_slope, inner_norm, shares):
-    first, last, middle, slope, norm, edge_dx, edge_dy = outs
+def slices_kernel(core_ref, cells, rows_op, cols_op, tables, *refs):
+    first, last, middle, slope, norm, edge_dx, edge_dy, inner_slope, inner_norm = refs[-9:]
+    core = core_ref[0]
     slices, blocks, _, _, cols = cells.shape
     rows = blocks * BLOCK
     ends = (0, slices - 1)
@@ -110,7 +116,7 @@
         to_norm[at] = norm_of(dx, dy)
         edge_dx[z] = jnp.where(core == 0, dx[:HALF], dx[rows - HALF :])
         edge_dy[z] = jnp.where(core == 0, dy[:HALF], dy[rows - HALF :])
-    tabs = spread(table[...].astype(F32), **shares)
+    tabs = [tables[c] for c in range(8)]
 
     def block(b, carry):
         for half in range(0, BLOCK, HALF):
@@ -139,48 +145,35 @@
     lax.fori_loop(0, blocks, block, 0)
 
 
-def own_kernel(core_ref, cells, table, *refs, shares):
-    outs, rest = refs[:7], refs[7:]
-    rows_op, cols_op, to_other, to_same, edge_same, edge_cross, inner_slope, inner_norm = rest
-    slices, blocks, _, _, cols = cells.shape
+def relay_kernel(core_ref, outer, top, bottom, out):
+    blocks = outer.shape[0]
     core = core_ref[0]
-    outer = (slices - 1) * core
-    to_other[...] = cells[outer, :, 1 - core]
-    to_same[...] = cells[outer, :, core]
+    out[:blocks] = outer[:, 1 - core]
+
+    def edges(ref):
+        for z in range(0, ref.shape[0], 2):
+            at = blocks + z // 2
+            out[at, :HALF, :] = ref[z]
+            out[at, HALF:, :] = ref[z + 1]
 
     @pl.when(core == 0)
     def _():
-        edge_same[...] = cells[:, blocks - 1, 1, HALF:, :]
-        edge_cross[...] = cells[:, 0, 0, :HALF, :]
+        edges(bottom)
 
     @pl.when(core != 0)
     def _():
-        edge_same[...] = cells[:, 0, 0, :HALF, :]
-        edge_cross[...] = cells[:, blocks - 1, 1, HALF:, :]
-
-    rows_op[...] = row_differences(2 * blocks * BLOCK, core)
-    cols_op[...] = column_differences(cols)
-    slices_kernel(
-        cells, core, rows_op, cols_op, table, outs, inner_slope, inner_norm, shares
-    )
-
-
-def other_kernel(core_ref, cells, table, rows_op, cols_op, *refs, shares):
-    slices_kernel(
-        cells, core_ref[0], rows_op, cols_op, table, refs[:7], refs[7], refs[8], shares
-    )
+        edges(top)
 
 
 def slab_kernel(
-    core_ref, own, other, outer_own, outer_other, edge_own, edge_other, table, *refs, shares
+    core_ref, own, other, outer, relayed, top, bottom, tables, scales, *refs
 ):
     own_terms, other_terms, out = refs[:7], refs[7:14], refs[14]
     slices, blocks, _, _, cols = own.shape
     core = core_ref[0]
     front = core == 0
     end = slices - 1
-    table_values = table[...].astype(F32)
-    opacity_scale = 1.0 / tops(table_values, shares["slab_share"])[1]
+    opacity_scale = scales[2]
 
     def stacks(mine, theirs, end_own, end_other):
         own_stack = (
@@ -221,8 +214,8 @@
                 own_stack, other_stack = stacks(
                     [own[z, b, core, rows, lanes].astype(F32) for z in range(slices)],
                     [other[z, b, core, rows, lanes].astype(F32) for z in range(slices)],
-                    outer_own[b, rows, lanes].astype(F32),
-                    outer_other[b, rows, lanes].astype(F32),
+                    outer[b, core, rows, lanes].astype(F32),
+                    relayed[b, rows, lanes].astype(F32),
                 )
                 both = finish(half_slab(own_stack, own_terms), half_slab(other_stack, other_terms))
                 for c in range(4):
@@ -232,7 +225,7 @@
 
     lax.fori_loop(0, blocks, block, 0)
 
-    tabs = spread(table_values, **shares)
+    tabs = [tables[c] for c in range(8)]
     b = jnp.where(front, 0, blocks - 1)
     row = lax.broadcasted_iota(jnp.int32, (HALF, LANES), 0)
     at_edge = row == jnp.where(front, 0, HALF - 1)
@@ -243,12 +236,18 @@
             top = ref[(*index, slice(0, HALF), lanes)].astype(F32)
             return jnp.where(front, top, ref[(*index, slice(HALF, BLOCK), lanes)].astype(F32))
 
+        def edge_own(z):
+            upper = top[z, :, lanes].astype(F32)[HALF - 1 :]
+            return jnp.where(front, -upper, bottom[z, :, lanes].astype(F32)[0:1])
+
+        def edge_other(z):
+            sent = relayed[blocks + z // 2, z % 2 * HALF : (z % 2 + 1) * HALF, lanes].astype(F32)
+            return jnp.where(front, -sent[HALF - 1 :], sent[0:1])
+
         def half_slab(stack, terms, edge):
             accum, transmit = nothing()
             for z in range(slices):
-                halo = edge[z, :, lanes].astype(F32)
-                halo = jnp.where(front, -halo[HALF - 1 : HALF], halo[0:1])
-                dx = terms[5][z, :, lanes] + jnp.where(at_edge, halo, 0.0)
+                dx = terms[5][z, :, lanes] + jnp.where(at_edge, edge(z), 0.0)
                 dy = terms[6][z, :, lanes]
                 accum, transmit = shade(
                     accum, transmit, stack[z + 2] - stack[z],
@@ -259,8 +258,8 @@
         own_stack, other_stack = stacks(
             [load(own, z, b, core) for z in range(slices)],
             [load(other, z, b, core) for z in range(slices)],
-            load(outer_own, b),
-            load(outer_other, b),
+            load(outer, b, core),
+            load(relayed, b),
         )
         both = finish(
             half_slab(own_stack, own_terms, edge_own), half_slab(other_stack, other_terms, edge_other)
@@ -270,9 +269,9 @@
             out[b, pl.ds(at, HALF), lanes] = both[c]
 
 
-def merge_kernel(parts, table, out, image, *, slab_share):
+def merge_kernel(parts, scales, out, image):
     cols = parts.shape[2]
-    colour_top, opacity_top = tops(table[...].astype(F32), slab_share)
+    colour_scale, opacity_top = scales[0], scales[1]
     for half in range(0, BLOCK, HALF):
         for start in range(0, cols, LANES):
             lanes = slice(start, start + LANES)
@@ -283,7 +282,7 @@
                 ]
                 accum = [a + transmit * p for a, p in zip(accum, part[:3])]
                 transmit = transmit - transmit * (part[3] * opacity_top)
-            whole = [a * (colour_top * opacity_top) for a in accum] + [1.0 - transmit]
+            whole = [a * colour_scale for a in accum] + [1.0 - transmit]
             for c in range(4):
                 at = start // LANES, slice(c * BLOCK + half, c * BLOCK + half + HALF)
                 image[at] = whole[c]
@@ -303,85 +302,91 @@
     blocks = rows // (2 * BLOCK)
     core = lax.axis_index("depth") % 2
 
-    def shift(x, img_step, depth_step):
-        pairs = []
-        for i in range(img_count):
-            for d in range(depth_count):
-                to_i, to_d = i + img_step(d % 2), d + depth_step(d % 2)
-                if 0 <= to_i < img_count and 0 <= to_d < depth_count:
-                    pairs.append((i * depth_count + d, to_i * depth_count + to_d))
-        return lax.ppermute(x, ("img", "depth"), pairs)
-
     half = rows // 2
     split = (slices, blocks, 2, BLOCK, cols)
     core_arg = core.astype(jnp.int32).reshape(1)
     same_core = [[2 * j + c for j in range(chips)] for c in range(2)]
     vmem = pl.BlockSpec(memory_space=pltpu.MemorySpace.VMEM)
     smem = pl.BlockSpec(memory_space=pltpu.MemorySpace.SMEM)
-    shares = dict(slab_share=2.0 * slices / depth_total, depth_total=depth_total)
     params = pltpu.CompilerParams(vmem_limit_bytes=16 << 20)
     quad = jax.ShapeDtypeStruct((4, half, cols), F32)
     two = jax.ShapeDtypeStruct((2, half, cols), F32)
     unit = jax.ShapeDtypeStruct((slices, HALF, cols), F32)
-    plane = jax.ShapeDtypeStruct((blocks, BLOCK, cols), BF16)
-    edge = jax.ShapeDtypeStruct((slices, HALF, cols), BF16)
     terms = (quad, quad, quad, two, two, unit, unit)
-    operators = (
-        jax.ShapeDtypeStruct((half, rows), BF16), jax.ShapeDtypeStruct((cols, cols), BF16)
-    )
-    inner = [pltpu.VMEM((slices - 2, half, cols), F32)] * 2
-
-    other = lax.ppermute(volume, "depth", [(d, d ^ 1) for d in range(depth_count)]).reshape(split)
+
+    partner = [(d, d ^ 1) for d in range(depth_count)]
+    other = lax.ppermute(volume, "depth", partner).reshape(split)
+    outer = lax.ppermute(
+        lax.dynamic_index_in_dim(volume, (slices - 1) * core, 0, False), "depth",
+        [(d, d + 1) for d in range(1, depth_count - 1, 2)]
+        + [(d + 1, d) for d in range(1, depth_count - 1, 2)],
+    ).reshape(split[1:])
+    down = [(i, i + 1) for i in range(img_count - 1)]
+    top = lax.ppermute(volume[:, rows - HALF :], "img", down)
+    bottom = lax.ppermute(volume[:, :HALF], "img", [(to, at) for at, to in down])
     own = volume.reshape(split)
-    results = pl.pallas_call(
-        functools.partial(own_kernel, shares=shares),
-        out_shape=(*terms, *operators, plane, plane, edge, edge),
-        in_specs=[smem, vmem, vmem],
-        out_specs=(vmem,) * 13,
-        scratch_shapes=inner,
+    entries = transfer_table.shape[1]
+    *ops, scales = pl.pallas_call(
+        functools.partial(
+            prepare_kernel, slab_share=2.0 * slices / depth_total, depth_total=depth_total
+        ),
+        out_shape=(
+            jax.ShapeDtypeStruct((half, rows), BF16),
+            jax.ShapeDtypeStruct((cols, cols), BF16),
+            jax.ShapeDtypeStruct((8, HALF, entries), F32),
+            jax.ShapeDtypeStruct((3, HALF, LANES), F32),
+        ),
+        in_specs=[smem, vmem],
+        out_specs=(vmem,) * 4,
         compiler_params=params,
-        name="own",
-    )(core_arg, own, transfer_table)
-    own_terms, ops, (to_other, to_same, edge_same, edge_cross) = (
-        results[:7], results[7:9], results[9:]
-    )
-    outer_other = shift(to_same, lambda c: 0, lambda c: 2 if c else -2)
-    outer_own = shift(to_other, lambda c: 0, lambda c: 1 if c else -1)
-    edge_own = shift(edge_same, lambda c: -1 if c else 1, lambda c: 0)
-    edge_other = shift(edge_cross, lambda c: 1 if c else -1, lambda c: -1 if c else 1)
-    other_terms = pl.pallas_call(
-        functools.partial(other_kernel, shares=shares),
-        out_shape=terms,
-        in_specs=[smem] + [vmem] * 4,
-        out_specs=(vmem,) * 7,
-        scratch_shapes=inner,
+        name="prepare",
+    )(core_arg, transfer_table)
+    def slices_terms(cells, previous, name):
+        return pl.pallas_call(
+            slices_kernel,
+            out_shape=terms,
+            in_specs=[smem] + [vmem] * (4 + len(previous)),
+            out_specs=(vmem,) * 7,
+            scratch_shapes=[pltpu.VMEM((slices - 2, half, cols), F32)] * 2,
+            compiler_params=params,
+            name=name,
+        )(core_arg, cells, *ops, *previous)
+
+    own_terms = slices_terms(own, (), "own")
+    outer, top, bottom, _ = lax.optimization_barrier((outer, top, bottom, own_terms[6]))
+    relayed = pl.pallas_call(
+        relay_kernel,
+        out_shape=jax.ShapeDtypeStruct((blocks + slices // 2, BLOCK, cols), BF16),
+        in_specs=[smem] + [vmem] * 3,
+        out_specs=vmem,
         compiler_params=params,
-        name="other",
-    )(core_arg, other, transfer_table, *ops)
+        name="relay",
+    )(core_arg, outer, top, bottom)
+    other_terms = slices_terms(other, (relayed,), "other")
+    relayed = lax.ppermute(relayed, "depth", partner)
     partial_image = pl.pallas_call(
-        functools.partial(slab_kernel, shares=shares),
+        slab_kernel,
         out_shape=jax.ShapeDtypeStruct((blocks, 4 * BLOCK, cols), F32),
-        in_specs=[smem] + [vmem] * 21,
+        in_specs=[smem] + [vmem] * 22,
         out_specs=vmem,
         compiler_params=params,
         name="slab",
     )(
-        core_arg, own, other, outer_own, outer_other, edge_own, edge_other, transfer_table,
-        *own_terms, *other_terms,
+        core_arg, own, other, outer, relayed, top, bottom, ops[2], scales, *own_terms, *other_terms,
     )
     pieces = lax.all_to_all(
         partial_image.astype(jnp.float16), "depth", split_axis=0, concat_axis=0, tiled=True,
         axis_index_groups=same_core,
     )
     return pl.pallas_call(
-        functools.partial(merge_kernel, slab_share=shares["slab_share"]),
+        merge_kernel,
         out_shape=jax.ShapeDtypeStruct((4, BLOCK * cols), F32),
         in_specs=[vmem, vmem],
         out_specs=vmem,
         scratch_shapes=[pltpu.VMEM((cols // LANES, 4 * BLOCK, LANES), F32)],
         compiler_params=params,
         name="merge",
-    )(pieces.astype(F32), transfer_table)
+    )(pieces.astype(F32), scales)
 
 
 def solution(mesh):

time: 61.6 us -> 59.5 us (0.966)
  the two profiles are of different devices: /device:TPU:33 before, /device:TPU:64 now
where the time goes in v8:
time: 59.5 us; the launch traced here: 59.1 us
  blocking collectives  24.4 us (41%)
  Pallas kernels  21.1 us (35%)
  starting transfers between devices  8.86 us (15%)
  local copies, waits for them, and re-layouts  4.12 us (7%)
    all_to_all x1, blocking collectives, shards(): lax.all_to_all(partial_image.astype(jnp.float16), 'depth', split_axis=0,...  24.4 us
    pallas_call x2, Pallas kernels, slices_terms(): pl.pallas_call(slices_kernel, out_shape=terms, in_specs=[smem] + [vmem] *...  17.3 us
    ppermute x1, starting transfers between devices, shards(): top = lax.ppermute(volume[:, rows - HALF:], 'img', down)  3.82 us
    pallas_call x1, Pallas kernels, shards(): pl.pallas_call(slab_kernel, out_shape=jax.ShapeDtypeStruct((blocks, 4 * B...  2.6 us
    ppermute x1, starting transfers between devices, shards(): relayed = lax.ppermute(relayed, 'depth', partner)  2.34 us
    unnamed x6, local copies, waits for them, and re-layouts  2.27 us
    ppermute x1, starting transfers between devices, shards(): lax.ppermute(volume[:, :HALF], 'img', [(to, at) for at, to in down])  2 us
  transfers between devices with their start and end apart: 5, of which 0 were waited for; matrix products, arithmetic and copies ran while one was open for 3% of the time, Pallas kernels for 30%

profile of v8, /device:TPU:64, one launch (start us, length us, event | category | flops | bytes accessed | tf_op | source)
XLA Modules:
  0.0 59.1 jit_solution(14214437725537869042)
XLA Ops:
  0.0 0.0 collective-permute-start
  0.0 1.1 %dynamic-slice_bitcast_fusion = bf16[512,512]{1,0:T(8,128)(2,1)S(1)} fusion(bf16[4,512,512]{2,1,0:T(8,128)(2,1)} %param.2, s32[]{:T(128)S(6)} %select_n.12), kind=kLoop, calls=%fused_computation | loop fusion | bytes 1048580 | tf_op jit(solution)/shard_map/jit(dynamic_index_in_dim)/squeeze | solution.py:320
  1.1 0.7 %collective-permute-start.1 = (bf16[512,512]{1,0:T(8,128)(2,1)S(1)}, bf16[512,512]{1,0:T(8,128)(2,1)S(1)}, u32[]{:S(2)}, u32[]{:S(2)}) collective-permute-start(bf16[512,512]{1,0:T(8,128)(2,1)S(1)} %dynamic-slice_bitcast_fusion), channel_id=1, source_target_pairs={{1,2},{3,4},{5,6},{7,8},{9,10},{11,12},{13,14},{15,16},{17,18},{19... | collective-permute-start | bytes 1572872 | tf_op jit(solution)/shard_map/ppermute | solution.py:319
  1.8 0.8 %fusion = (bf16[4,8,512]{2,1,0:T(8,128)(2,1)S(1)}, bf16[4,8,512]{2,1,0:T(8,128)(2,1)S(1)}) fusion(bf16[4,512,512]{2,1,0:T(8,128)(2,1)} %param.2), kind=kLoop, calls=%fused_computation.1 | loop fusion | bytes 131072 | tf_op jit(solution)/shard_map/slice | solution.py:326
  2.6 2.0 %collective-permute-start.3 = (bf16[4,8,512]{2,1,0:T(8,128)(2,1)S(1)}, bf16[4,8,512]{2,1,0:T(8,128)(2,1)S(1)}, u32[]{:S(2)}, u32[]{:S(2)}) collective-permute-start(bf16[4,8,512]{2,1,0:T(8,128)(2,1)S(1)} %get-tuple-element.47), channel_id=1, source_target_pairs={{32,0},{64,32},{96,64},{33,1},{65,33},{97,65},{34,2},{66,34},{98,6... | collective-permute-start | bytes 98312 | tf_op jit(solution)/shard_map/ppermute | solution.py:326
  4.6 3.8 %collective-permute-start.2 = (bf16[4,8,512]{2,1,0:T(8,128)(2,1)S(1)}, bf16[4,8,512]{2,1,0:T(8,128)(2,1)S(1)}, u32[]{:S(2)}, u32[]{:S(2)}) collective-permute-start(bf16[4,8,512]{2,1,0:T(8,128)(2,1)S(1)} %get-tuple-element.48), channel_id=1, source_target_pairs={{0,32},{32,64},{64,96},{1,33},{33,65},{65,97},{2,34},{34,66},{66,9... | collective-permute-start | bytes 98312 | tf_op jit(solution)/shard_map/ppermute | solution.py:325
  8.4 0.0 copy-start.2
  8.4 0.7 %copy-done.2 = bf16[4,128]{1,0:T(4,128)(2,1)S(1)} copy-done((bf16[4,128]{1,0:T(4,128)(2,1)S(1)}, bf16[4,128]{1,0:T(4,128)(2,1)}, u32[]{:S(2)}) %copy-start.2) | copy-done | bytes 1048
  9.1 0.4 prepare.1
  9.5 0.0 copy-start
  9.5 1.6 %copy-done = bf16[4,512,512]{2,1,0:T(8,128)(2,1)S(1)} copy-done((bf16[4,512,512]{2,1,0:T(8,128)(2,1)S(1)}, bf16[4,512,512]{2,1,0:T(8,128)(2,1)}, u32[]{:S(2)}) %copy-start) | copy-done | bytes 2097176
  11.1 8.7 %own.1 = (f32[4,256,512]{2,1,0:T(8,128)S(1)}, f32[4,256,512]{2,1,0:T(8,128)S(1)}, f32[4,256,512]{2,1,0:T(8,128)S(1)}, f32[2,256,512]{2,1,0:T(8,128)S(1)}, f32[2,...) custom-call(s32[1]{0:T(128)} %bitcast.core_ref, ...), custom_call_target="tpu_custom_call" | custom-call | tf_op jit(solution)/shard_map/own/pallas_call | solution.py:345
  19.7 0.0 copy-start.1
  19.7 0.0 collective-permute-done.3.bottom
  19.7 0.0 collective-permute-done.2.top
  19.7 0.0 collective-permute-done.1
  19.8 2.3 %collective-permute-start.4 = (bf16[18,16,512]{2,1,0:T(8,128)(2,1)S(1)}, bf16[18,16,512]{2,1,0:T(8,128)(2,1)S(1)}, u32[]{:S(2)}, u32[]{:S(2)}) collective-permute-start(bf16[18,16,512]{2,1,0:T(8,128)(2,1)S(1)} %relay.1.refs_0_), channel_id=1, source_target_pairs={{0,1},{1,0},{2,3},{3,2},{4,5},{5,4},{6,7},{7,6},{8,9},{9,8},{10,11... | collective-permute-start | bytes 884744 | tf_op jit(solution)/shard_map/ppermute | solution.py:366
  22.1 0.0 collective-permute-done
  22.1 8.6 %other.1 = (f32[4,256,512]{2,1,0:T(8,128)S(1)}, f32[4,256,512]{2,1,0:T(8,128)S(1)}, f32[4,256,512]{2,1,0:T(8,128)S(1)}, f32[2,256,512]{2,1,0:T(8,128)S(1)}, f32[...) custom-call(s32[1]{0:T(128)} %bitcast.core_ref, ...), custom_call_target="tpu_custom_call" | custom-call | tf_op jit(solution)/shard_map/other/pallas_call | solution.py:345
  30.8 0.0 collective-permute-done.4.relayed
  30.8 0.0 copy-done.1
  30.8 2.6 %slab.1 = f32[16,64,512]{2,1,0:T(8,128)S(1)} custom-call(s32[1]{0:T(128)} %bitcast.core_ref, bf16[4,16,2,16,512]{4,3,2,1,0:T(8,128)(2,1)S(1)} %bitcast.7, bf16[4,16,2,16,512]{4,3,2,1,0:T(8,128)(2,1)S(1)} %bitcast.9, bf16[16,2,16,512]{3,2,1,0:T(8,128)(2,1)S(1)} %bitcast.11, bf16[18,16,512]{2,1,0:T(8,128)(2,1)S(1)} %collective-permute-done.4.relayed, ...), custom_call_target="tpu_custom_call" | custom-call | tf_op jit(solution)/shard_map/slab/pallas_call | solution.py:367
  33.4 0.3 convert_element_type.6
  33.7 24.4 %all_to_all.5 = f16[16,64,512]{2,1,0:T(8,128)(2,1)S(1)} all-to-all(f16[16,64,512]{2,1,0:T(8,128)(2,1)S(1)} %convert_element_type.6), channel_id=1, replica_groups={{0,2,4,6,8,10,12,14,16,18,20,22,24,26,28,30},{1,3,5,7,9,11,13,15,17,19,..., dimensions={0} | all-to-all | bytes 2097152 | tf_op jit(solution)/shard_map/all_to_all | solution.py:377
  58.0 0.3 convert_element_type.7.parts
  58.3 0.9 %merge.1 = f32[4,8192]{1,0:T(4,128)} custom-call(f32[16,64,512]{2,1,0:T(8,128)S(1)} %convert_element_type.7.parts, f32[3,8,128]{2,1,0:T(8,128)S(1)} %get-tuple-element.33.scales), custom_call_target="tpu_custom_call" | custom-call | tf_op jit(solution)/shard_map/merge/pallas_call | solution.py:381
  (1 shorter events, 0.0 us)
Async XLA Ops:
  0.0 22.1 %collective-permute-start = (bf16[4,512,512]{2,1,0:T(8,128)(2,1)}, bf16[4,512,512]{2,1,0:T(8,128)(2,1)S(1)}, u32[]{:S(2)}, u32[]{:S(2)}) collective-permute-start(bf16[4,512,512]{2,1,0:T(8,128)(2,1)} %param.2), channel_id=1, source_target_pairs={{0,1},{1,0},{2,3},{3,2},{4,5},{5,4},{6,7},{7,6},{8,9},{9,8},{10,11... | collective-permute-start | bytes 6291464 | tf_op jit(solution)/shard_map/ppermute | solution.py:318
  1.1 18.7 %collective-permute-start.1 = (bf16[512,512]{1,0:T(8,128)(2,1)S(1)}, bf16[512,512]{1,0:T(8,128)(2,1)S(1)}, u32[]{:S(2)}, u32[]{:S(2)}) collective-permute-start(bf16[512,512]{1,0:T(8,128)(2,1)S(1)} %dynamic-slice_bitcast_fusion), channel_id=1, source_target_pairs={{1,2},{3,4},{5,6},{7,8},{9,10},{11,12},{13,14},{15,16},{17,18},{19... | collective-permute-start | bytes 1572872 | tf_op jit(solution)/shard_map/ppermute | solution.py:319
  2.6 17.2 %collective-permute-start.3 = (bf16[4,8,512]{2,1,0:T(8,128)(2,1)S(1)}, bf16[4,8,512]{2,1,0:T(8,128)(2,1)S(1)}, u32[]{:S(2)}, u32[]{:S(2)}) collective-permute-start(bf16[4,8,512]{2,1,0:T(8,128)(2,1)S(1)} %get-tuple-element.47), channel_id=1, source_target_pairs={{32,0},{64,32},{96,64},{33,1},{65,33},{97,65},{34,2},{66,34},{98,6... | collective-permute-start | bytes 98312 | tf_op jit(solution)/shard_map/ppermute | solution.py:326
  4.6 15.2 %collective-permute-start.2 = (bf16[4,8,512]{2,1,0:T(8,128)(2,1)S(1)}, bf16[4,8,512]{2,1,0:T(8,128)(2,1)S(1)}, u32[]{:S(2)}, u32[]{:S(2)}) collective-permute-start(bf16[4,8,512]{2,1,0:T(8,128)(2,1)S(1)} %get-tuple-element.48), channel_id=1, source_target_pairs={{0,32},{32,64},{64,96},{1,33},{33,65},{65,97},{2,34},{34,66},{66,9... | collective-permute-start | bytes 98312 | tf_op jit(solution)/shard_map/ppermute | solution.py:325
  8.4 0.7 %copy-start.2 = (bf16[4,128]{1,0:T(4,128)(2,1)S(1)}, bf16[4,128]{1,0:T(4,128)(2,1)}, u32[]{:S(2)}) copy-start(bf16[4,128]{1,0:T(4,128)(2,1)} %table_ref.1) | copy-start | bytes 3076
  9.5 1.6 %copy-start = (bf16[4,512,512]{2,1,0:T(8,128)(2,1)S(1)}, bf16[4,512,512]{2,1,0:T(8,128)(2,1)}, u32[]{:S(2)}) copy-start(bf16[4,512,512]{2,1,0:T(8,128)(2,1)} %param.2) | copy-start | bytes 6291460
  19.7 11.1 %copy-start.1 = (bf16[4,512,512]{2,1,0:T(8,128)(2,1)S(1)}, bf16[4,512,512]{2,1,0:T(8,128)(2,1)}, u32[]{:S(2)}) copy-start(bf16[4,512,512]{2,1,0:T(8,128)(2,1)} %param.2) | copy-start | bytes 6291460
  19.8 11.0 %collective-permute-start.4 = (bf16[18,16,512]{2,1,0:T(8,128)(2,1)S(1)}, bf16[18,16,512]{2,1,0:T(8,128)(2,1)S(1)}, u32[]{:S(2)}, u32[]{:S(2)}) collective-permute-start(bf16[18,16,512]{2,1,0:T(8,128)(2,1)S(1)} %relay.1.refs_0_), channel_id=1, source_target_pairs={{0,1},{1,0},{2,3},{3,2},{4,5},{5,4},{6,7},{7,6},{8,9},{9,8},{10,11... | collective-permute-start | bytes 884744 | tf_op jit(solution)/shard_map/ppermute | solution.py:366

commit v9 on v8

--- a/solution.py
+++ b/solution.py
@@ -38,7 +38,14 @@
     return jnp.maximum(colour, TINY), jnp.maximum(extinction * slab_share, TINY)
 
 
-def prepare_kernel(core_ref, table_ref, rows_op, cols_op, tables, scales, *, slab_share, depth_total):
+def prepare_kernel(
+    core_ref, cells, table_ref, rows_op, cols_op, tables, scales, outer, upper_edge, lower_edge,
+    *, slab_share, depth_total,
+):
+    rows = cells.shape[1]
+    outer[...] = cells[(cells.shape[0] - 1) * core_ref[0]]
+    upper_edge[...] = cells[:, :HALF]
+    lower_edge[...] = cells[:, rows - HALF :]
     table = table_ref[...].astype(F32)
     entries = table.shape[1]
     rows_op[...] = row_differences(rows_op.shape[1], core_ref[0])
@@ -118,7 +125,9 @@
         edge_dy[z] = jnp.where(core == 0, dy[:HALF], dy[rows - HALF :])
     tabs = [tables[c] for c in range(8)]
 
-    def block(b, carry):
+    def block(bb, carry):
+      for sub in range(2):
+        b = bb * 2 + sub
         for half in range(0, BLOCK, HALF):
             here = pl.ds(pl.multiple_of(b * BLOCK + half, HALF), HALF)
             rows = slice(half, half + HALF)
@@ -140,9 +149,9 @@
                 for c in range(3):
                     middle[c, here, lanes] = accum[c]
                 middle[3, here, lanes] = transmit
-        return carry
-
-    lax.fori_loop(0, blocks, block, 0)
+      return carry
+
+    lax.fori_loop(0, blocks // 2, block, 0)
 
 
 def relay_kernel(core_ref, outer, top, bottom, out):
@@ -312,21 +321,14 @@
     quad = jax.ShapeDtypeStruct((4, half, cols), F32)
     two = jax.ShapeDtypeStruct((2, half, cols), F32)
     unit = jax.ShapeDtypeStruct((slices, HALF, cols), F32)
+    edge = jax.ShapeDtypeStruct((slices, HALF, cols), BF16)
     terms = (quad, quad, quad, two, two, unit, unit)
 
     partner = [(d, d ^ 1) for d in range(depth_count)]
     other = lax.ppermute(volume, "depth", partner).reshape(split)
-    outer = lax.ppermute(
-        lax.dynamic_index_in_dim(volume, (slices - 1) * core, 0, False), "depth",
-        [(d, d + 1) for d in range(1, depth_count - 1, 2)]
-        + [(d + 1, d) for d in range(1, depth_count - 1, 2)],
-    ).reshape(split[1:])
-    down = [(i, i + 1) for i in range(img_count - 1)]
-    top = lax.ppermute(volume[:, rows - HALF :], "img", down)
-    bottom = lax.ppermute(volume[:, :HALF], "img", [(to, at) for at, to in down])
     own = volume.reshape(split)
     entries = transfer_table.shape[1]
-    *ops, scales = pl.pallas_call(
+    *ops, scales, outer, upper_edge, lower_edge = pl.pallas_call(
         functools.partial(
             prepare_kernel, slab_share=2.0 * slices / depth_total, depth_total=depth_total
         ),
@@ -335,12 +337,23 @@
             jax.ShapeDtypeStruct((cols, cols), BF16),
             jax.ShapeDtypeStruct((8, HALF, entries), F32),
             jax.ShapeDtypeStruct((3, HALF, LANES), F32),
+            jax.ShapeDtypeStruct((rows, cols), BF16),
+            edge,
+            edge,
         ),
-        in_specs=[smem, vmem],
-        out_specs=(vmem,) * 4,
+        in_specs=[smem, vmem, vmem],
+        out_specs=(vmem,) * 7,
         compiler_params=params,
         name="prepare",
-    )(core_arg, transfer_table)
+    )(core_arg, volume, transfer_table)
+    outer = lax.ppermute(
+        outer, "depth",
+        [(d, d + 1) for d in range(1, depth_count - 1, 2)]
+        + [(d + 1, d) for d in range(1, depth_count - 1, 2)],
+    ).reshape(split[1:])
+    down = [(i, i + 1) for i in range(img_count - 1)]
+    top = lax.ppermute(lower_edge, "img", down)
+    bottom = lax.ppermute(upper_edge, "img", [(to, at) for at, to in down])
     def slices_terms(cells, previous, name):
         return pl.pallas_call(
             slices_kernel,

time: 59.5 us -> 56.2 us (0.945)
  local copies, waits for them, and re-layouts: 4.12 us -> 2.28 us
  Pallas kernels: 21.1 us -> 19.8 us
    pallas_call x2, Pallas kernels: 17.3 us -> 16 us  [slices_terms(): pl.pallas_call(slices_kernel, out_shape=terms, in_specs=[smem] + [vmem] *...]
    squeeze x1 -> x0, local copies, waits for them, and re-layouts: 1.08 us -> none  [shards(): lax.dynamic_index_in_dim(volume, (slices - 1) * core, 0, False)]
    slice x1 -> x0, local copies, waits for them, and re-layouts: 0.78 us -> none  [shards(): volume[:, :HALF]]
  transfers between devices with their start and end apart: 5 -> 5, of which waited for: 0 -> 0; matrix products, arithmetic and copies ran while one was open for 3% -> 0% of each run, Pallas kernels for 30% -> 29%
where the time goes in v9:
time: 56.2 us; the launch traced here: 56 us
  blocking collectives  24.4 us (43%)
  Pallas kernels  19.8 us (35%)
  starting transfers between devices  8.88 us (16%)
  local copies, waits for them, and re-layouts  2.28 us (4%)
    all_to_all x1, blocking collectives, shards(): lax.all_to_all(partial_image.astype(jnp.float16), 'depth', split_axis=0,...  24.4 us
    pallas_call x2, Pallas kernels, slices_terms(): pl.pallas_call(slices_kernel, out_shape=terms, in_specs=[smem] + [vmem] *...  16 us
    ppermute x1, starting transfers between devices, shards(): top = lax.ppermute(lower_edge, 'img', down)  3.53 us
    pallas_call x1, Pallas kernels, shards(): pl.pallas_call(slab_kernel, out_shape=jax.ShapeDtypeStruct((blocks, 4 * B...  2.59 us
    ppermute x1, starting transfers between devices, shards(): relayed = lax.ppermute(relayed, 'depth', partner)  2.34 us
    ppermute x1, starting transfers between devices, shards(): bottom = lax.ppermute(upper_edge, 'img', [(to, at) for at, to in down])  2.31 us
    unnamed x6, local copies, waits for them, and re-layouts  2.28 us
  transfers between devices with their start and end apart: 5, of which 0 were waited for; matrix products, arithmetic and copies ran while one was open for 0% of the time, Pallas kernels for 29%

profile of v9, /device:TPU:64, one launch (start us, length us, event | category | flops | bytes accessed | tf_op | source)
XLA Modules:
  0.0 56.0 jit_solution(6435495062602332317)
XLA Ops:
  0.0 0.0 collective-permute-start
  0.0 0.0 copy-start
  0.0 1.6 %copy-done = bf16[4,512,512]{2,1,0:T(8,128)(2,1)S(1)} copy-done((bf16[4,512,512]{2,1,0:T(8,128)(2,1)S(1)}, bf16[4,512,512]{2,1,0:T(8,128)(2,1)}, u32[]{:S(2)}) %copy-start) | copy-done | bytes 2097176
  1.6 0.0 copy-start.2
  1.6 0.7 %copy-done.2 = bf16[4,128]{1,0:T(4,128)(2,1)S(1)} copy-done((bf16[4,128]{1,0:T(4,128)(2,1)S(1)}, bf16[4,128]{1,0:T(4,128)(2,1)}, u32[]{:S(2)}) %copy-start.2) | copy-done | bytes 1048
  2.3 0.4 prepare.1
  2.6 0.7 %collective-permute-start.1 = (bf16[512,512]{1,0:T(8,128)(2,1)S(1)}, bf16[512,512]{1,0:T(8,128)(2,1)S(1)}, u32[]{:S(2)}, u32[]{:S(2)}) collective-permute-start(bf16[512,512]{1,0:T(8,128)(2,1)S(1)} %get-tuple-element.29), channel_id=1, source_target_pairs={{1,2},{3,4},{5,6},{7,8},{9,10},{11,12},{13,14},{15,16},{17,18},{19... | collective-permute-start | bytes 1572872 | tf_op jit(solution)/shard_map/ppermute | solution.py:349
  3.3 3.5 %collective-permute-start.2 = (bf16[4,8,512]{2,1,0:T(8,128)(2,1)S(1)}, bf16[4,8,512]{2,1,0:T(8,128)(2,1)S(1)}, u32[]{:S(2)}, u32[]{:S(2)}) collective-permute-start(bf16[4,8,512]{2,1,0:T(8,128)(2,1)S(1)} %get-tuple-element.30), channel_id=1, source_target_pairs={{0,32},{32,64},{64,96},{1,33},{33,65},{65,97},{2,34},{34,66},{66,9... | collective-permute-start | bytes 98312 | tf_op jit(solution)/shard_map/ppermute | solution.py:355
  6.9 2.3 %collective-permute-start.3 = (bf16[4,8,512]{2,1,0:T(8,128)(2,1)S(1)}, bf16[4,8,512]{2,1,0:T(8,128)(2,1)S(1)}, u32[]{:S(2)}, u32[]{:S(2)}) collective-permute-start(bf16[4,8,512]{2,1,0:T(8,128)(2,1)S(1)} %get-tuple-element.31), channel_id=1, source_target_pairs={{32,0},{64,32},{96,64},{33,1},{65,33},{97,65},{34,2},{66,34},{98,6... | collective-permute-start | bytes 98312 | tf_op jit(solution)/shard_map/ppermute | solution.py:356
  9.2 8.0 %own.1 = (f32[4,256,512]{2,1,0:T(8,128)S(1)}, f32[4,256,512]{2,1,0:T(8,128)S(1)}, f32[4,256,512]{2,1,0:T(8,128)S(1)}, f32[2,256,512]{2,1,0:T(8,128)S(1)}, f32[2,...) custom-call(s32[1]{0:T(128)} %bitcast.core_ref, ...), custom_call_target="tpu_custom_call" | custom-call | tf_op jit(solution)/shard_map/own/pallas_call | solution.py:358
  17.2 0.0 copy-start.1
  17.2 0.0 collective-permute-done.2.top
  17.2 0.0 collective-permute-done.3.bottom
  17.3 0.0 collective-permute-done.1
  17.3 2.3 %collective-permute-start.4 = (bf16[18,16,512]{2,1,0:T(8,128)(2,1)S(1)}, bf16[18,16,512]{2,1,0:T(8,128)(2,1)S(1)}, u32[]{:S(2)}, u32[]{:S(2)}) collective-permute-start(bf16[18,16,512]{2,1,0:T(8,128)(2,1)S(1)} %relay.1.refs_0_), channel_id=1, source_target_pairs={{0,1},{1,0},{2,3},{3,2},{4,5},{5,4},{6,7},{7,6},{8,9},{9,8},{10,11... | collective-permute-start | bytes 884744 | tf_op jit(solution)/shard_map/ppermute | solution.py:379
  19.6 0.0 collective-permute-done
  19.6 8.0 %other.1 = (f32[4,256,512]{2,1,0:T(8,128)S(1)}, f32[4,256,512]{2,1,0:T(8,128)S(1)}, f32[4,256,512]{2,1,0:T(8,128)S(1)}, f32[2,256,512]{2,1,0:T(8,128)S(1)}, f32[...) custom-call(s32[1]{0:T(128)} %bitcast.core_ref, ...), custom_call_target="tpu_custom_call" | custom-call | tf_op jit(solution)/shard_map/other/pallas_call | solution.py:358
  27.6 0.0 collective-permute-done.4.relayed
  27.6 0.0 copy-done.1
  27.6 2.6 %slab.1 = f32[16,64,512]{2,1,0:T(8,128)S(1)} custom-call(s32[1]{0:T(128)} %bitcast.core_ref, bf16[4,16,2,16,512]{4,3,2,1,0:T(8,128)(2,1)S(1)} %bitcast.5, bf16[4,16,2,16,512]{4,3,2,1,0:T(8,128)(2,1)S(1)} %bitcast.7, bf16[16,2,16,512]{3,2,1,0:T(8,128)(2,1)S(1)} %bitcast.9, bf16[18,16,512]{2,1,0:T(8,128)(2,1)S(1)} %collective-permute-done.4.relayed, ...), custom_call_target="tpu_custom_call" | custom-call | tf_op jit(solution)/shard_map/slab/pallas_call | solution.py:380
  30.2 0.3 convert_element_type.6
  30.5 24.4 %all_to_all.5 = f16[16,64,512]{2,1,0:T(8,128)(2,1)S(1)} all-to-all(f16[16,64,512]{2,1,0:T(8,128)(2,1)S(1)} %convert_element_type.6), channel_id=1, replica_groups={{0,2,4,6,8,10,12,14,16,18,20,22,24,26,28,30},{1,3,5,7,9,11,13,15,17,19,..., dimensions={0} | all-to-all | bytes 2097152 | tf_op jit(solution)/shard_map/all_to_all | solution.py:390
  54.9 0.3 convert_element_type.7.parts
  55.1 0.9 %merge.1 = f32[4,8192]{1,0:T(4,128)} custom-call(f32[16,64,512]{2,1,0:T(8,128)S(1)} %convert_element_type.7.parts, f32[3,8,128]{2,1,0:T(8,128)S(1)} %get-tuple-element.39.scales), custom_call_target="tpu_custom_call" | custom-call | tf_op jit(solution)/shard_map/merge/pallas_call | solution.py:394
  (1 shorter events, 0.0 us)
Async XLA Ops:
  0.0 19.6 %collective-permute-start = (bf16[4,512,512]{2,1,0:T(8,128)(2,1)}, bf16[4,512,512]{2,1,0:T(8,128)(2,1)S(1)}, u32[]{:S(2)}, u32[]{:S(2)}) collective-permute-start(bf16[4,512,512]{2,1,0:T(8,128)(2,1)} %cells.1), channel_id=1, source_target_pairs={{0,1},{1,0},{2,3},{3,2},{4,5},{5,4},{6,7},{7,6},{8,9},{9,8},{10,11... | collective-permute-start | bytes 6291464 | tf_op jit(solution)/shard_map/ppermute | solution.py:328
  0.0 1.6 %copy-start = (bf16[4,512,512]{2,1,0:T(8,128)(2,1)S(1)}, bf16[4,512,512]{2,1,0:T(8,128)(2,1)}, u32[]{:S(2)}) copy-start(bf16[4,512,512]{2,1,0:T(8,128)(2,1)} %cells.1) | copy-start | bytes 6291460
  1.6 0.7 %copy-start.2 = (bf16[4,128]{1,0:T(4,128)(2,1)S(1)}, bf16[4,128]{1,0:T(4,128)(2,1)}, u32[]{:S(2)}) copy-start(bf16[4,128]{1,0:T(4,128)(2,1)} %table_ref.1) | copy-start | bytes 3076
  2.6 14.6 %collective-permute-start.1 = (bf16[512,512]{1,0:T(8,128)(2,1)S(1)}, bf16[512,512]{1,0:T(8,128)(2,1)S(1)}, u32[]{:S(2)}, u32[]{:S(2)}) collective-permute-start(bf16[512,512]{1,0:T(8,128)(2,1)S(1)} %get-tuple-element.29), channel_id=1, source_target_pairs={{1,2},{3,4},{5,6},{7,8},{9,10},{11,12},{13,14},{15,16},{17,18},{19... | collective-permute-start | bytes 1572872 | tf_op jit(solution)/shard_map/ppermute | solution.py:349
  3.3 13.9 %collective-permute-start.2 = (bf16[4,8,512]{2,1,0:T(8,128)(2,1)S(1)}, bf16[4,8,512]{2,1,0:T(8,128)(2,1)S(1)}, u32[]{:S(2)}, u32[]{:S(2)}) collective-permute-start(bf16[4,8,512]{2,1,0:T(8,128)(2,1)S(1)} %get-tuple-element.30), channel_id=1, source_target_pairs={{0,32},{32,64},{64,96},{1,33},{33,65},{65,97},{2,34},{34,66},{66,9... | collective-permute-start | bytes 98312 | tf_op jit(solution)/shard_map/ppermute | solution.py:355
  6.9 10.4 %collective-permute-start.3 = (bf16[4,8,512]{2,1,0:T(8,128)(2,1)S(1)}, bf16[4,8,512]{2,1,0:T(8,128)(2,1)S(1)}, u32[]{:S(2)}, u32[]{:S(2)}) collective-permute-start(bf16[4,8,512]{2,1,0:T(8,128)(2,1)S(1)} %get-tuple-element.31), channel_id=1, source_target_pairs={{32,0},{64,32},{96,64},{33,1},{65,33},{97,65},{34,2},{66,34},{98,6... | collective-permute-start | bytes 98312 | tf_op jit(solution)/shard_map/ppermute | solution.py:356
  17.2 10.4 %copy-start.1 = (bf16[4,512,512]{2,1,0:T(8,128)(2,1)S(1)}, bf16[4,512,512]{2,1,0:T(8,128)(2,1)}, u32[]{:S(2)}) copy-start(bf16[4,512,512]{2,1,0:T(8,128)(2,1)} %cells.1) | copy-start | bytes 6291460
  17.3 10.3 %collective-permute-start.4 = (bf16[18,16,512]{2,1,0:T(8,128)(2,1)S(1)}, bf16[18,16,512]{2,1,0:T(8,128)(2,1)S(1)}, u32[]{:S(2)}, u32[]{:S(2)}) collective-permute-start(bf16[18,16,512]{2,1,0:T(8,128)(2,1)S(1)} %relay.1.refs_0_), channel_id=1, source_target_pairs={{0,1},{1,0},{2,3},{3,2},{4,5},{5,4},{6,7},{7,6},{8,9},{9,8},{10,11... | collective-permute-start | bytes 884744 | tf_op jit(solution)/shard_map/ppermute | solution.py:379

commit v10 on v9

--- a/solution.py
+++ b/solution.py
@@ -39,13 +39,10 @@
 
 
 def prepare_kernel(
-    core_ref, cells, table_ref, rows_op, cols_op, tables, scales, outer, upper_edge, lower_edge,
+    core_ref, cells, table_ref, rows_op, cols_op, tables, scales, outer,
     *, slab_share, depth_total,
 ):
-    rows = cells.shape[1]
     outer[...] = cells[(cells.shape[0] - 1) * core_ref[0]]
-    upper_edge[...] = cells[:, :HALF]
-    lower_edge[...] = cells[:, rows - HALF :]
     table = table_ref[...].astype(F32)
     entries = table.shape[1]
     rows_op[...] = row_differences(rows_op.shape[1], core_ref[0])
@@ -154,28 +151,24 @@
     lax.fori_loop(0, blocks // 2, block, 0)
 
 
-def relay_kernel(core_ref, outer, top, bottom, out):
-    blocks = outer.shape[0]
+def relay_kernel(core_ref, own, other, outer, relayed, edge):
+    slices, blocks, _, _, _ = own.shape
     core = core_ref[0]
-    out[:blocks] = outer[:, 1 - core]
-
-    def edges(ref):
-        for z in range(0, ref.shape[0], 2):
-            at = blocks + z // 2
-            out[at, :HALF, :] = ref[z]
-            out[at, HALF:, :] = ref[z + 1]
+    relayed[...] = outer[:, 1 - core]
 
     @pl.when(core == 0)
     def _():
-        edges(bottom)
+        edge[:slices] = own[:, blocks - 1, 1, HALF:, :]
+        edge[slices:] = other[:, blocks - 1, 1, HALF:, :]
 
     @pl.when(core != 0)
     def _():
-        edges(top)
+        edge[:slices] = own[:, 0, 0, :HALF, :]
+        edge[slices:] = other[:, 0, 0, :HALF, :]
 
 
 def slab_kernel(
-    core_ref, own, other, outer, relayed, top, bottom, tables, scales, *refs
+    core_ref, own, other, outer, relayed, edges, tables, scales, *refs
 ):
     own_terms, other_terms, out = refs[:7], refs[7:14], refs[14]
     slices, blocks, _, _, cols = own.shape
@@ -245,18 +238,12 @@
             top = ref[(*index, slice(0, HALF), lanes)].astype(F32)
             return jnp.where(front, top, ref[(*index, slice(HALF, BLOCK), lanes)].astype(F32))
 
-        def edge_own(z):
-            upper = top[z, :, lanes].astype(F32)[HALF - 1 :]
-            return jnp.where(front, -upper, bottom[z, :, lanes].astype(F32)[0:1])
-
-        def edge_other(z):
-            sent = relayed[blocks + z // 2, z % 2 * HALF : (z % 2 + 1) * HALF, lanes].astype(F32)
-            return jnp.where(front, -sent[HALF - 1 :], sent[0:1])
-
-        def half_slab(stack, terms, edge):
+        def half_slab(stack, terms, at):
             accum, transmit = nothing()
             for z in range(slices):
-                dx = terms[5][z, :, lanes] + jnp.where(at_edge, edge(z), 0.0)
+                halo = edges[at + z, :, lanes].astype(F32)
+                halo = jnp.where(front, -halo[HALF - 1 :], halo[0:1])
+                dx = terms[5][z, :, lanes] + jnp.where(at_edge, halo, 0.0)
                 dy = terms[6][z, :, lanes]
                 accum, transmit = shade(
                     accum, transmit, stack[z + 2] - stack[z],
@@ -271,7 +258,7 @@
             load(relayed, b),
         )
         both = finish(
-            half_slab(own_stack, own_terms, edge_own), half_slab(other_stack, other_terms, edge_other)
+            half_slab(own_stack, own_terms, 0), half_slab(other_stack, other_terms, slices)
         )
         for c in range(4):
             at = pl.multiple_of(c * BLOCK + core * HALF, HALF)
@@ -321,14 +308,14 @@
     quad = jax.ShapeDtypeStruct((4, half, cols), F32)
     two = jax.ShapeDtypeStruct((2, half, cols), F32)
     unit = jax.ShapeDtypeStruct((slices, HALF, cols), F32)
-    edge = jax.ShapeDtypeStruct((slices, HALF, cols), BF16)
+    plane = jax.ShapeDtypeStruct((blocks, BLOCK, cols), BF16)
+    edge = jax.ShapeDtypeStruct((2 * slices, HALF, cols), BF16)
     terms = (quad, quad, quad, two, two, unit, unit)
 
     partner = [(d, d ^ 1) for d in range(depth_count)]
-    other = lax.ppermute(volume, "depth", partner).reshape(split)
     own = volume.reshape(split)
     entries = transfer_table.shape[1]
-    *ops, scales, outer, upper_edge, lower_edge = pl.pallas_call(
+    *ops, scales, outer = pl.pallas_call(
         functools.partial(
             prepare_kernel, slab_share=2.0 * slices / depth_total, depth_total=depth_total
         ),
@@ -338,11 +325,9 @@
             jax.ShapeDtypeStruct((8, HALF, entries), F32),
             jax.ShapeDtypeStruct((3, HALF, LANES), F32),
             jax.ShapeDtypeStruct((rows, cols), BF16),
-            edge,
-            edge,
         ),
         in_specs=[smem, vmem, vmem],
-        out_specs=(vmem,) * 7,
+        out_specs=(vmem,) * 5,
         compiler_params=params,
         name="prepare",
     )(core_arg, volume, transfer_table)
@@ -351,9 +336,8 @@
         [(d, d + 1) for d in range(1, depth_count - 1, 2)]
         + [(d + 1, d) for d in range(1, depth_count - 1, 2)],
     ).reshape(split[1:])
-    down = [(i, i + 1) for i in range(img_count - 1)]
-    top = lax.ppermute(lower_edge, "img", down)
-    bottom = lax.ppermute(upper_edge, "img", [(to, at) for at, to in down])
+    other = lax.ppermute(volume, "depth", partner).reshape(split)
+
     def slices_terms(cells, previous, name):
         return pl.pallas_call(
             slices_kernel,
@@ -366,26 +350,35 @@
         )(core_arg, cells, *ops, *previous)
 
     own_terms = slices_terms(own, (), "own")
-    outer, top, bottom, _ = lax.optimization_barrier((outer, top, bottom, own_terms[6]))
-    relayed = pl.pallas_call(
+    outer, _ = lax.optimization_barrier((outer, own_terms[6]))
+    relayed, edges = pl.pallas_call(
         relay_kernel,
-        out_shape=jax.ShapeDtypeStruct((blocks + slices // 2, BLOCK, cols), BF16),
+        out_shape=(plane, edge),
         in_specs=[smem] + [vmem] * 3,
-        out_specs=vmem,
+        out_specs=(vmem, vmem),
         compiler_params=params,
         name="relay",
-    )(core_arg, outer, top, bottom)
+    )(core_arg, own, other, outer)
     other_terms = slices_terms(other, (relayed,), "other")
     relayed = lax.ppermute(relayed, "depth", partner)
+    edges = lax.ppermute(
+        edges, ("img", "depth"),
+        [
+            (at * depth_count + d, to * depth_count + d)
+            for i in range(img_count - 1)
+            for d in range(depth_count)
+            for at, to in [((i + 1, i) if d % 2 else (i, i + 1))]
+        ],
+    )
     partial_image = pl.pallas_call(
         slab_kernel,
         out_shape=jax.ShapeDtypeStruct((blocks, 4 * BLOCK, cols), F32),
-        in_specs=[smem] + [vmem] * 22,
+        in_specs=[smem] + [vmem] * 21,
         out_specs=vmem,
         compiler_params=params,
         name="slab",
     )(
-        core_arg, own, other, outer, relayed, top, bottom, ops[2], scales, *own_terms, *other_terms,
+        core_arg, own, other, outer, relayed, edges, ops[2], scales, *own_terms, *other_terms,
     )
     pieces = lax.all_to_all(
         partial_image.astype(jnp.float16), "depth", split_axis=0, concat_axis=0, tiled=True,

time: 56.2 us -> 54.7 us (0.973)
  starting transfers between devices: 8.88 us -> 7.11 us
    ppermute x2 -> x1, starting transfers between devices: 5.84 us -> 3.52 us  [shards(): lax.ppermute(edges, ('img', 'depth'), [(at * depth_count + d, to * depth_...]
  transfers between devices with their start and end apart: 5 -> 4, of which waited for: 0 -> 0; matrix products, arithmetic and copies ran while one was open for 0% -> 0% of each run, Pallas kernels for 29% -> 30%
where the time goes in v10:
time: 54.7 us; the launch traced here: 54.5 us
  blocking collectives  24.4 us (45%)
  Pallas kernels  20.1 us (37%)
  starting transfers between devices  7.11 us (13%)
  local copies, waits for them, and re-layouts  2.28 us (4%)
    all_to_all x1, blocking collectives, shards(): lax.all_to_all(partial_image.astype(jnp.float16), 'depth', split_axis=0,...  24.4 us
    pallas_call x2, Pallas kernels, slices_terms(): pl.pallas_call(slices_kernel, out_shape=terms, in_specs=[smem] + [vmem] *...  16.1 us
    ppermute x1, starting transfers between devices, shards(): lax.ppermute(edges, ('img', 'depth'), [(at * depth_count + d, to * depth_...  3.52 us
    ppermute x1, starting transfers between devices, shards(): relayed = lax.ppermute(relayed, 'depth', partner)  2.9 us
    pallas_call x1, Pallas kernels, shards(): pl.pallas_call(slab_kernel, out_shape=jax.ShapeDtypeStruct((blocks, 4 * B...  2.74 us
    unnamed x6, local copies, waits for them, and re-layouts  2.28 us
  transfers between devices with their start and end apart: 4, of which 0 were waited for; matrix products, arithmetic and copies ran while one was open for 0% of the time, Pallas kernels for 30%

profile of v10, /device:TPU:64, one launch (start us, length us, event | category | flops | bytes accessed | tf_op | source)
XLA Modules:
  0.0 54.5 jit_solution(8922244429525272511)
XLA Ops:
  0.0 0.0 collective-permute-start
  0.0 0.0 copy-start
  0.0 1.6 %copy-done = bf16[4,512,512]{2,1,0:T(8,128)(2,1)S(1)} copy-done((bf16[4,512,512]{2,1,0:T(8,128)(2,1)S(1)}, bf16[4,512,512]{2,1,0:T(8,128)(2,1)}, u32[]{:S(2)}) %copy-start) | copy-done | bytes 2097176
  1.6 0.0 copy-start.2
  1.6 0.7 %copy-done.2 = bf16[4,128]{1,0:T(4,128)(2,1)S(1)} copy-done((bf16[4,128]{1,0:T(4,128)(2,1)S(1)}, bf16[4,128]{1,0:T(4,128)(2,1)}, u32[]{:S(2)}) %copy-start.2) | copy-done | bytes 1048
  2.3 0.4 prepare.1
  2.6 0.7 %collective-permute-start.1 = (bf16[512,512]{1,0:T(8,128)(2,1)S(1)}, bf16[512,512]{1,0:T(8,128)(2,1)S(1)}, u32[]{:S(2)}, u32[]{:S(2)}) collective-permute-start(bf16[512,512]{1,0:T(8,128)(2,1)S(1)} %get-tuple-element.27), channel_id=1, source_target_pairs={{1,2},{3,4},{5,6},{7,8},{9,10},{11,12},{13,14},{15,16},{17,18},{19... | collective-permute-start | bytes 1572872 | tf_op jit(solution)/shard_map/ppermute | solution.py:334
  3.3 8.0 %own.1 = (f32[4,256,512]{2,1,0:T(8,128)S(1)}, f32[4,256,512]{2,1,0:T(8,128)S(1)}, f32[4,256,512]{2,1,0:T(8,128)S(1)}, f32[2,256,512]{2,1,0:T(8,128)S(1)}, f32[2,...) custom-call(s32[1]{0:T(128)} %bitcast.core_ref, ...), custom_call_target="tpu_custom_call" | custom-call | tf_op jit(solution)/shard_map/own/pallas_call | solution.py:342
  11.4 0.0 collective-permute-done.1
  11.4 0.0 collective-permute-done
  11.4 0.0 copy-start.1
  11.5 2.9 %collective-permute-start.2 = (bf16[16,16,512]{2,1,0:T(8,128)(2,1)S(1)}, bf16[16,16,512]{2,1,0:T(8,128)(2,1)S(1)}, u32[]{:S(2)}, u32[]{:S(2)}) collective-permute-start(bf16[16,16,512]{2,1,0:T(8,128)(2,1)S(1)} %get-tuple-element.33.refs_0_), channel_id=1, source_target_pairs={{0,1},{1,0},{2,3},{3,2},{4,5},{5,4},{6,7},{7,6},{8,9},{9,8},{10,11... | collective-permute-start | bytes 786440 | tf_op jit(solution)/shard_map/ppermute | solution.py:363
  14.4 3.5 %collective-permute-start.3 = (bf16[8,8,512]{2,1,0:T(8,128)(2,1)S(1)}, bf16[8,8,512]{2,1,0:T(8,128)(2,1)S(1)}, u32[]{:S(2)}, u32[]{:S(2)}) collective-permute-start(bf16[8,8,512]{2,1,0:T(8,128)(2,1)S(1)} %get-tuple-element.34), channel_id=1, source_target_pairs={{0,32},{33,1},{2,34},{35,3},{4,36},{37,5},{6,38},{39,7},{8,40},{41... | collective-permute-start | bytes 196616 | tf_op jit(solution)/shard_map/ppermute | solution.py:364
  17.9 8.0 %other.1 = (f32[4,256,512]{2,1,0:T(8,128)S(1)}, f32[4,256,512]{2,1,0:T(8,128)S(1)}, f32[4,256,512]{2,1,0:T(8,128)S(1)}, f32[2,256,512]{2,1,0:T(8,128)S(1)}, f32[...) custom-call(s32[1]{0:T(128)} %bitcast.core_ref, ...), custom_call_target="tpu_custom_call" | custom-call | tf_op jit(solution)/shard_map/other/pallas_call | solution.py:342
  25.9 0.0 collective-permute-done.3.edges
  25.9 0.0 collective-permute-done.2.relayed
  25.9 0.0 copy-done.1
  25.9 2.7 %slab.1 = f32[16,64,512]{2,1,0:T(8,128)S(1)} custom-call(s32[1]{0:T(128)} %bitcast.core_ref, bf16[4,16,2,16,512]{4,3,2,1,0:T(8,128)(2,1)S(1)} %bitcast.6, bf16[4,16,2,16,512]{4,3,2,1,0:T(8,128)(2,1)S(1)} %bitcast.9, bf16[16,2,16,512]{3,2,1,0:T(8,128)(2,1)S(1)} %bitcast.11, bf16[16,16,512]{2,1,0:T(8,128)(2,1)S(1)} %collective-permute-done.2.relayed, ...), custom_call_target="tpu_custom_call" | custom-call | tf_op jit(solution)/shard_map/slab/pallas_call | solution.py:373
  28.7 0.3 convert_element_type.6
  28.9 24.4 %all_to_all.5 = f16[16,64,512]{2,1,0:T(8,128)(2,1)S(1)} all-to-all(f16[16,64,512]{2,1,0:T(8,128)(2,1)S(1)} %convert_element_type.6), channel_id=1, replica_groups={{0,2,4,6,8,10,12,14,16,18,20,22,24,26,28,30},{1,3,5,7,9,11,13,15,17,19,..., dimensions={0} | all-to-all | bytes 2097152 | tf_op jit(solution)/shard_map/all_to_all | solution.py:383
  53.3 0.3 convert_element_type.7.parts
  53.6 0.9 %merge.1 = f32[4,8192]{1,0:T(4,128)} custom-call(f32[16,64,512]{2,1,0:T(8,128)S(1)} %convert_element_type.7.parts, f32[3,8,128]{2,1,0:T(8,128)S(1)} %get-tuple-element.35.scales), custom_call_target="tpu_custom_call" | custom-call | tf_op jit(solution)/shard_map/merge/pallas_call | solution.py:387
  (1 shorter events, 0.0 us)
Async XLA Ops:
  0.0 11.4 %collective-permute-start = (bf16[4,512,512]{2,1,0:T(8,128)(2,1)}, bf16[4,512,512]{2,1,0:T(8,128)(2,1)S(1)}, u32[]{:S(2)}, u32[]{:S(2)}) collective-permute-start(bf16[4,512,512]{2,1,0:T(8,128)(2,1)} %cells.1), channel_id=1, source_target_pairs={{0,1},{1,0},{2,3},{3,2},{4,5},{5,4},{6,7},{7,6},{8,9},{9,8},{10,11... | collective-permute-start | bytes 6291464 | tf_op jit(solution)/shard_map/ppermute | solution.py:339
  0.0 1.6 %copy-start = (bf16[4,512,512]{2,1,0:T(8,128)(2,1)S(1)}, bf16[4,512,512]{2,1,0:T(8,128)(2,1)}, u32[]{:S(2)}) copy-start(bf16[4,512,512]{2,1,0:T(8,128)(2,1)} %cells.1) | copy-start | bytes 6291460
  1.6 0.7 %copy-start.2 = (bf16[4,128]{1,0:T(4,128)(2,1)S(1)}, bf16[4,128]{1,0:T(4,128)(2,1)}, u32[]{:S(2)}) copy-start(bf16[4,128]{1,0:T(4,128)(2,1)} %table_ref.1) | copy-start | bytes 3076
  2.6 8.7 %collective-permute-start.1 = (bf16[512,512]{1,0:T(8,128)(2,1)S(1)}, bf16[512,512]{1,0:T(8,128)(2,1)S(1)}, u32[]{:S(2)}, u32[]{:S(2)}) collective-permute-start(bf16[512,512]{1,0:T(8,128)(2,1)S(1)} %get-tuple-element.27), channel_id=1, source_target_pairs={{1,2},{3,4},{5,6},{7,8},{9,10},{11,12},{13,14},{15,16},{17,18},{19... | collective-permute-start | bytes 1572872 | tf_op jit(solution)/shard_map/ppermute | solution.py:334
  11.4 14.5 %copy-start.1 = (bf16[4,512,512]{2,1,0:T(8,128)(2,1)S(1)}, bf16[4,512,512]{2,1,0:T(8,128)(2,1)}, u32[]{:S(2)}) copy-start(bf16[4,512,512]{2,1,0:T(8,128)(2,1)} %cells.1) | copy-start | bytes 6291460
  11.5 14.5 %collective-permute-start.2 = (bf16[16,16,512]{2,1,0:T(8,128)(2,1)S(1)}, bf16[16,16,512]{2,1,0:T(8,128)(2,1)S(1)}, u32[]{:S(2)}, u32[]{:S(2)}) collective-permute-start(bf16[16,16,512]{2,1,0:T(8,128)(2,1)S(1)} %get-tuple-element.33.refs_0_), channel_id=1, source_target_pairs={{0,1},{1,0},{2,3},{3,2},{4,5},{5,4},{6,7},{7,6},{8,9},{9,8},{10,11... | collective-permute-start | bytes 786440 | tf_op jit(solution)/shard_map/ppermute | solution.py:363
  14.4 11.6 %collective-permute-start.3 = (bf16[8,8,512]{2,1,0:T(8,128)(2,1)S(1)}, bf16[8,8,512]{2,1,0:T(8,128)(2,1)S(1)}, u32[]{:S(2)}, u32[]{:S(2)}) collective-permute-start(bf16[8,8,512]{2,1,0:T(8,128)(2,1)S(1)} %get-tuple-element.34), channel_id=1, source_target_pairs={{0,32},{33,1},{2,34},{35,3},{4,36},{37,5},{6,38},{39,7},{8,40},{41... | collective-permute-start | bytes 196616 | tf_op jit(solution)/shard_map/ppermute | solution.py:364

commit v11 on v10

--- a/solution.py
+++ b/solution.py
@@ -336,7 +336,8 @@
         [(d, d + 1) for d in range(1, depth_count - 1, 2)]
         + [(d + 1, d) for d in range(1, depth_count - 1, 2)],
     ).reshape(split[1:])
-    other = lax.ppermute(volume, "depth", partner).reshape(split)
+    held = lax.optimization_barrier((volume, scales))[0]
+    other = lax.ppermute(held, "depth", partner).reshape(split)
 
     def slices_terms(cells, previous, name):
         return pl.pallas_call(

time: 54.7 us -> 54.7 us (level)
  transfers between devices with their start and end apart: 4 -> 4, of which waited for: 0 -> 0; matrix products, arithmetic and copies ran while one was open for 0% -> 0% of each run, Pallas kernels for 30% -> 29%
where the time goes in v11:
time: 54.7 us; the launch traced here: 54.5 us
  blocking collectives  24.3 us (44%)
  Pallas kernels  20.1 us (37%)
  starting transfers between devices  7.19 us (13%)
  local copies, waits for them, and re-layouts  2.28 us (4%)
    all_to_all x1, blocking collectives, shards(): lax.all_to_all(partial_image.astype(jnp.float16), 'depth', split_axis=0,...  24.3 us
    pallas_call x2, Pallas kernels, slices_terms(): pl.pallas_call(slices_kernel, out_shape=terms, in_specs=[smem] + [vmem] *...  16.1 us
    ppermute x1, starting transfers between devices, shards(): lax.ppermute(edges, ('img', 'depth'), [(at * depth_count + d, to * depth_...  3.52 us
    ppermute x1, starting transfers between devices, shards(): relayed = lax.ppermute(relayed, 'depth', partner)  2.9 us
    pallas_call x1, Pallas kernels, shards(): pl.pallas_call(slab_kernel, out_shape=jax.ShapeDtypeStruct((blocks, 4 * B...  2.74 us
    unnamed x6, local copies, waits for them, and re-layouts  2.28 us
  transfers between devices with their start and end apart: 4, of which 0 were waited for; matrix products, arithmetic and copies ran while one was open for 0% of the time, Pallas kernels for 29%

profile of v11, /device:TPU:64, one launch (start us, length us, event | category | flops | bytes accessed | tf_op | source)
XLA Modules:
  0.0 54.5 jit_solution(16606143585892810799)
XLA Ops:
  0.0 0.0 copy-start
  0.0 1.6 %copy-done = bf16[4,512,512]{2,1,0:T(8,128)(2,1)S(1)} copy-done((bf16[4,512,512]{2,1,0:T(8,128)(2,1)S(1)}, bf16[4,512,512]{2,1,0:T(8,128)(2,1)}, u32[]{:S(2)}) %copy-start) | copy-done | bytes 2097176
  1.6 0.0 copy-start.2
  1.6 0.7 %copy-done.2 = bf16[4,128]{1,0:T(4,128)(2,1)S(1)} copy-done((bf16[4,128]{1,0:T(4,128)(2,1)S(1)}, bf16[4,128]{1,0:T(4,128)(2,1)}, u32[]{:S(2)}) %copy-start.2) | copy-done | bytes 1048
  2.3 0.4 prepare.1
  2.6 0.1 collective-permute-start
  2.7 0.7 %collective-permute-start.1 = (bf16[512,512]{1,0:T(8,128)(2,1)S(1)}, bf16[512,512]{1,0:T(8,128)(2,1)S(1)}, u32[]{:S(2)}, u32[]{:S(2)}) collective-permute-start(bf16[512,512]{1,0:T(8,128)(2,1)S(1)} %get-tuple-element.30), channel_id=1, source_target_pairs={{1,2},{3,4},{5,6},{7,8},{9,10},{11,12},{13,14},{15,16},{17,18},{19... | collective-permute-start | bytes 1572872 | tf_op jit(solution)/shard_map/ppermute | solution.py:334
  3.4 8.0 %own.1 = (f32[4,256,512]{2,1,0:T(8,128)S(1)}, f32[4,256,512]{2,1,0:T(8,128)S(1)}, f32[4,256,512]{2,1,0:T(8,128)S(1)}, f32[2,256,512]{2,1,0:T(8,128)S(1)}, f32[2,...) custom-call(s32[1]{0:T(128)} %bitcast.core_ref, ...), custom_call_target="tpu_custom_call" | custom-call | tf_op jit(solution)/shard_map/own/pallas_call | solution.py:343
  11.5 0.0 collective-permute-done.1
  11.5 0.0 collective-permute-done
  11.5 0.0 copy-start.1
  11.5 2.9 %collective-permute-start.2 = (bf16[16,16,512]{2,1,0:T(8,128)(2,1)S(1)}, bf16[16,16,512]{2,1,0:T(8,128)(2,1)S(1)}, u32[]{:S(2)}, u32[]{:S(2)}) collective-permute-start(bf16[16,16,512]{2,1,0:T(8,128)(2,1)S(1)} %get-tuple-element.36.refs_0_), channel_id=1, source_target_pairs={{0,1},{1,0},{2,3},{3,2},{4,5},{5,4},{6,7},{7,6},{8,9},{9,8},{10,11... | collective-permute-start | bytes 786440 | tf_op jit(solution)/shard_map/ppermute | solution.py:364
  14.4 3.5 %collective-permute-start.3 = (bf16[8,8,512]{2,1,0:T(8,128)(2,1)S(1)}, bf16[8,8,512]{2,1,0:T(8,128)(2,1)S(1)}, u32[]{:S(2)}, u32[]{:S(2)}) collective-permute-start(bf16[8,8,512]{2,1,0:T(8,128)(2,1)S(1)} %get-tuple-element.37), channel_id=1, source_target_pairs={{0,32},{33,1},{2,34},{35,3},{4,36},{37,5},{6,38},{39,7},{8,40},{41... | collective-permute-start | bytes 196616 | tf_op jit(solution)/shard_map/ppermute | solution.py:365
  18.0 8.0 %other.1 = (f32[4,256,512]{2,1,0:T(8,128)S(1)}, f32[4,256,512]{2,1,0:T(8,128)S(1)}, f32[4,256,512]{2,1,0:T(8,128)S(1)}, f32[2,256,512]{2,1,0:T(8,128)S(1)}, f32[...) custom-call(s32[1]{0:T(128)} %bitcast.core_ref, ...), custom_call_target="tpu_custom_call" | custom-call | tf_op jit(solution)/shard_map/other/pallas_call | solution.py:343
  26.0 0.0 collective-permute-done.3.edges
  26.0 0.0 collective-permute-done.2.relayed
  26.0 0.0 copy-done.1
  26.0 2.7 %slab.1 = f32[16,64,512]{2,1,0:T(8,128)S(1)} custom-call(s32[1]{0:T(128)} %bitcast.core_ref, bf16[4,16,2,16,512]{4,3,2,1,0:T(8,128)(2,1)S(1)} %bitcast.6, bf16[4,16,2,16,512]{4,3,2,1,0:T(8,128)(2,1)S(1)} %bitcast.9, bf16[16,2,16,512]{3,2,1,0:T(8,128)(2,1)S(1)} %bitcast.11, bf16[16,16,512]{2,1,0:T(8,128)(2,1)S(1)} %collective-permute-done.2.relayed, ...), custom_call_target="tpu_custom_call" | custom-call | tf_op jit(solution)/shard_map/slab/pallas_call | solution.py:374
  28.8 0.3 convert_element_type.6
  29.0 24.3 %all_to_all.5 = f16[16,64,512]{2,1,0:T(8,128)(2,1)S(1)} all-to-all(f16[16,64,512]{2,1,0:T(8,128)(2,1)S(1)} %convert_element_type.6), channel_id=1, replica_groups={{0,2,4,6,8,10,12,14,16,18,20,22,24,26,28,30},{1,3,5,7,9,11,13,15,17,19,..., dimensions={0} | all-to-all | bytes 2097152 | tf_op jit(solution)/shard_map/all_to_all | solution.py:384
  53.4 0.3 convert_element_type.7.parts
  53.6 0.9 %merge.1 = f32[4,8192]{1,0:T(4,128)} custom-call(f32[16,64,512]{2,1,0:T(8,128)S(1)} %convert_element_type.7.parts, f32[3,8,128]{2,1,0:T(8,128)S(1)} %get-tuple-element.28.scales), custom_call_target="tpu_custom_call" | custom-call | tf_op jit(solution)/shard_map/merge/pallas_call | solution.py:388
  (1 shorter events, 0.0 us)
Async XLA Ops:
  0.0 1.6 %copy-start = (bf16[4,512,512]{2,1,0:T(8,128)(2,1)S(1)}, bf16[4,512,512]{2,1,0:T(8,128)(2,1)}, u32[]{:S(2)}) copy-start(bf16[4,512,512]{2,1,0:T(8,128)(2,1)} %cells.1) | copy-start | bytes 6291460
  1.6 0.7 %copy-start.2 = (bf16[4,128]{1,0:T(4,128)(2,1)S(1)}, bf16[4,128]{1,0:T(4,128)(2,1)}, u32[]{:S(2)}) copy-start(bf16[4,128]{1,0:T(4,128)(2,1)} %table_ref.1) | copy-start | bytes 3076
  2.6 8.8 %collective-permute-start = (bf16[4,512,512]{2,1,0:T(8,128)(2,1)S(1)}, bf16[4,512,512]{2,1,0:T(8,128)(2,1)S(1)}, u32[]{:S(2)}, u32[]{:S(2)}) collective-permute-start(bf16[4,512,512]{2,1,0:T(8,128)(2,1)S(1)} %copy-done), channel_id=1, source_target_pairs={{0,1},{1,0},{2,3},{3,2},{4,5},{5,4},{6,7},{7,6},{8,9},{9,8},{10,11... | collective-permute-start | bytes 6291464 | tf_op jit(solution)/shard_map/ppermute | solution.py:340
  2.7 8.7 %collective-permute-start.1 = (bf16[512,512]{1,0:T(8,128)(2,1)S(1)}, bf16[512,512]{1,0:T(8,128)(2,1)S(1)}, u32[]{:S(2)}, u32[]{:S(2)}) collective-permute-start(bf16[512,512]{1,0:T(8,128)(2,1)S(1)} %get-tuple-element.30), channel_id=1, source_target_pairs={{1,2},{3,4},{5,6},{7,8},{9,10},{11,12},{13,14},{15,16},{17,18},{19... | collective-permute-start | bytes 1572872 | tf_op jit(solution)/shard_map/ppermute | solution.py:334
  11.5 14.5 %copy-start.1 = (bf16[4,512,512]{2,1,0:T(8,128)(2,1)S(1)}, bf16[4,512,512]{2,1,0:T(8,128)(2,1)}, u32[]{:S(2)}) copy-start(bf16[4,512,512]{2,1,0:T(8,128)(2,1)} %cells.1) | copy-start | bytes 6291460
  11.5 14.5 %collective-permute-start.2 = (bf16[16,16,512]{2,1,0:T(8,128)(2,1)S(1)}, bf16[16,16,512]{2,1,0:T(8,128)(2,1)S(1)}, u32[]{:S(2)}, u32[]{:S(2)}) collective-permute-start(bf16[16,16,512]{2,1,0:T(8,128)(2,1)S(1)} %get-tuple-element.36.refs_0_), channel_id=1, source_target_pairs={{0,1},{1,0},{2,3},{3,2},{4,5},{5,4},{6,7},{7,6},{8,9},{9,8},{10,11... | collective-permute-start | bytes 786440 | tf_op jit(solution)/shard_map/ppermute | solution.py:364
  14.4 11.6 %collective-permute-start.3 = (bf16[8,8,512]{2,1,0:T(8,128)(2,1)S(1)}, bf16[8,8,512]{2,1,0:T(8,128)(2,1)S(1)}, u32[]{:S(2)}, u32[]{:S(2)}) collective-permute-start(bf16[8,8,512]{2,1,0:T(8,128)(2,1)S(1)} %get-tuple-element.37), channel_id=1, source_target_pairs={{0,32},{33,1},{2,34},{35,3},{4,36},{37,5},{6,38},{39,7},{8,40},{41... | collective-permute-start | bytes 196616 | tf_op jit(solution)/shard_map/ppermute | solution.py:365

commit v12 on v10

--- a/solution.py
+++ b/solution.py
@@ -39,14 +39,19 @@
 
 
 def prepare_kernel(
-    core_ref, cells, table_ref, rows_op, cols_op, tables, scales, outer,
+    core_ref, volume, table_hbm, rows_op, cols_op, tables, scales, outer, table_ref, sems,
     *, slab_share, depth_total,
 ):
-    outer[...] = cells[(cells.shape[0] - 1) * core_ref[0]]
+    outer_slice = (volume.shape[0] - 1) * core_ref[0]
+    table_copy = pltpu.make_async_copy(table_hbm, table_ref, sems.at[0])
+    outer_copy = pltpu.make_async_copy(volume.at[outer_slice], outer, sems.at[1])
+    table_copy.start()
+    outer_copy.start()
+    rows_op[...] = row_differences(rows_op.shape[1], core_ref[0])
+    cols_op[...] = column_differences(cols_op.shape[1])
+    table_copy.wait()
     table = table_ref[...].astype(F32)
     entries = table.shape[1]
-    rows_op[...] = row_differences(rows_op.shape[1], core_ref[0])
-    cols_op[...] = column_differences(cols_op.shape[1])
     colour_top, opacity_top = tops(table, slab_share)
     scale = SLOPE / (colour_top * opacity_top)
     last = lax.broadcasted_iota(jnp.int32, (HALF, entries), 1) == entries - 1
@@ -57,6 +62,7 @@
         tables[c + 4] = jnp.where(last, lower, pltpu.roll(lower, entries - 1, 1))
     for at, value in enumerate((colour_top * opacity_top, opacity_top, 1.0 / opacity_top)):
         scales[at] = jnp.broadcast_to(value, (HALF, LANES))
+    outer_copy.wait()
 
 
 def look_up(table, index):
@@ -102,13 +108,25 @@
     return [jnp.where(condition, x, y) for x, y in zip(a, b)]
 
 
-def slices_kernel(core_ref, cells, rows_op, cols_op, tables, *refs):
+def own_kernel(core_ref, volume, rows_op, cols_op, tables, *refs):
+    cells, sems = refs[7], refs[-1]
+    copies = [
+        pltpu.make_async_copy(volume.at[z], cells.at[z], sems.at[z]) for z in range(cells.shape[0])
+    ]
+    for copy in copies:
+        copy.start()
+    slices_kernel(core_ref, cells, rows_op, cols_op, tables, *refs[:7], *refs[8:10], copies=copies)
+
+
+def slices_kernel(core_ref, cells, rows_op, cols_op, tables, *refs, copies=()):
     first, last, middle, slope, norm, edge_dx, edge_dy, inner_slope, inner_norm = refs[-9:]
     core = core_ref[0]
     slices, blocks, _, _, cols = cells.shape
     rows = blocks * BLOCK
     ends = (0, slices - 1)
     for z in range(slices):
+        if copies:
+            copies[z].wait()
         dx = jnp.dot(rows_op[...], cells[z].reshape(2 * rows, cols), preferred_element_type=F32)
         dy = jnp.dot(
             cells[z, :, core].reshape(rows, cols), cols_op[...], preferred_element_type=F32
@@ -303,6 +321,8 @@
     core_arg = core.astype(jnp.int32).reshape(1)
     same_core = [[2 * j + c for j in range(chips)] for c in range(2)]
     vmem = pl.BlockSpec(memory_space=pltpu.MemorySpace.VMEM)
+    hbm = pl.BlockSpec(memory_space=pltpu.MemorySpace.HBM)
+    in_hbm = functools.partial(pltpu.with_memory_space_constraint, memory_space=pltpu.MemorySpace.HBM)
     smem = pl.BlockSpec(memory_space=pltpu.MemorySpace.SMEM)
     params = pltpu.CompilerParams(vmem_limit_bytes=16 << 20)
     quad = jax.ShapeDtypeStruct((4, half, cols), F32)
@@ -313,7 +333,6 @@
     terms = (quad, quad, quad, two, two, unit, unit)
 
     partner = [(d, d ^ 1) for d in range(depth_count)]
-    own = volume.reshape(split)
     entries = transfer_table.shape[1]
     *ops, scales, outer = pl.pallas_call(
         functools.partial(
@@ -326,11 +345,16 @@
             jax.ShapeDtypeStruct((3, HALF, LANES), F32),
             jax.ShapeDtypeStruct((rows, cols), BF16),
         ),
-        in_specs=[smem, vmem, vmem],
+        in_specs=[smem, hbm, hbm],
         out_specs=(vmem,) * 5,
+        scratch_shapes=[
+            pltpu.VMEM(transfer_table.shape, BF16), pltpu.SemaphoreType.DMA((2,)),
+        ],
         compiler_params=params,
         name="prepare",
-    )(core_arg, volume, transfer_table)
+    )(
+        core_arg, in_hbm(volume), in_hbm(transfer_table)
+    )
     outer = lax.ppermute(
         outer, "depth",
         [(d, d + 1) for d in range(1, depth_count - 1, 2)]
@@ -349,7 +373,16 @@
             name=name,
         )(core_arg, cells, *ops, *previous)
 
-    own_terms = slices_terms(own, (), "own")
+    *own_terms, own = pl.pallas_call(
+        own_kernel,
+        out_shape=(*terms, jax.ShapeDtypeStruct(split, BF16)),
+        in_specs=[smem, hbm] + [vmem] * 3,
+        out_specs=(vmem,) * 8,
+        scratch_shapes=[pltpu.VMEM((slices - 2, half, cols), F32)] * 2
+        + [pltpu.SemaphoreType.DMA((slices,))],
+        compiler_params=params,
+        name="own",
+    )(core_arg, in_hbm(volume.reshape(split)), *ops)
     outer, _ = lax.optimization_barrier((outer, own_terms[6]))
     relayed, edges = pl.pallas_call(
         relay_kernel,

time: 54.7 us -> 52.8 us (0.965)
  local copies, waits for them, and re-layouts: 2.28 us -> 0 us
  Pallas kernels: 20.1 us -> 22.2 us
  blocking collectives: 24.4 us -> 22.7 us
    pallas_call x0 -> x1, Pallas kernels: none -> 9.52 us  [shards(): pl.pallas_call(own_kernel, out_shape=(*terms, jax.ShapeDtypeStruct(split,...]
    pallas_call x2 -> x1, Pallas kernels: 16.1 us -> 8.05 us  [slices_terms(): pl.pallas_call(slices_kernel, out_shape=terms, in_specs=[smem] + [vmem] *...]
    unnamed x6 -> x0, local copies, waits for them, and re-layouts: 2.28 us -> none
    all_to_all x1, blocking collectives: 24.4 us -> 22.7 us  [shards(): lax.all_to_all(partial_image.astype(jnp.float16), 'depth', split_axis=0,...]
    pallas_call x1, Pallas kernels: 0.36 us -> 1.08 us  [shards(): pl.pallas_call(functools.partial(prepare_kernel, slab_share=2.0 * slices...]
  transfers between devices with their start and end apart: 4 -> 4, of which waited for: 0 -> 0; matrix products, arithmetic and copies ran while one was open for 0% -> 0% of each run, Pallas kernels for 30% -> 35%
where the time goes in v12:
time: 52.8 us; the launch traced here: 52.6 us
  blocking collectives  22.7 us (43%)
  Pallas kernels  22.2 us (42%)
  starting transfers between devices  7.11 us (13%)
    all_to_all x1, blocking collectives, shards(): lax.all_to_all(partial_image.astype(jnp.float16), 'depth', split_axis=0,...  22.7 us
    pallas_call x1, Pallas kernels, shards(): pl.pallas_call(own_kernel, out_shape=(*terms, jax.ShapeDtypeStruct(split,...  9.52 us
    pallas_call x1, Pallas kernels, slices_terms(): pl.pallas_call(slices_kernel, out_shape=terms, in_specs=[smem] + [vmem] *...  8.05 us
    ppermute x1, starting transfers between devices, shards(): lax.ppermute(edges, ('img', 'depth'), [(at * depth_count + d, to * depth_...  3.52 us
    ppermute x1, starting transfers between devices, shards(): relayed = lax.ppermute(relayed, 'depth', partner)  2.9 us
    pallas_call x1, Pallas kernels, shards(): pl.pallas_call(slab_kernel, out_shape=jax.ShapeDtypeStruct((blocks, 4 * B...  2.6 us
    pallas_call x1, Pallas kernels, shards(): pl.pallas_call(functools.partial(prepare_kernel, slab_share=2.0 * slices...  1.08 us
  transfers between devices with their start and end apart: 4, of which 0 were waited for; matrix products, arithmetic and copies ran while one was open for 0% of the time, Pallas kernels for 35%

profile of v12, /device:TPU:64, one launch (start us, length us, event | category | flops | bytes accessed | tf_op | source)
XLA Modules:
  0.0 52.6 jit_solution(1404176862273437764)
XLA Ops:
  0.0 0.0 collective-permute-start
  0.0 1.1 %prepare.1 = (bf16[256,512]{1,0:T(8,128)(2,1)S(1)}, bf16[512,512]{1,0:T(8,128)(2,1)S(1)}, f32[8,8,128]{2,1,0:T(8,128)S(1)}, f32[3,8,128]{2,1,0:T(8,128)S(1)}, bf16[512,512]{1,0:T(8,128)(2,1)S(1)}) custom-call(s32[1]{0:T(128)} %bitcast.core_ref, bf16[4,512,512]{2,1,0:T(8,128)(2,1)} %volume.1, bf16[4,128]{1,0:T(4,128)(2,1)} %table_hbm.1), custom_call_target="tpu_custom_call" | custom-call | tf_op jit(solution)/shard_map/prepare/pallas_call | solution.py:337
  1.1 0.7 %collective-permute-start.1 = (bf16[512,512]{1,0:T(8,128)(2,1)S(1)}, bf16[512,512]{1,0:T(8,128)(2,1)S(1)}, u32[]{:S(2)}, u32[]{:S(2)}) collective-permute-start(bf16[512,512]{1,0:T(8,128)(2,1)S(1)} %get-tuple-element.32), channel_id=1, source_target_pairs={{1,2},{3,4},{5,6},{7,8},{9,10},{11,12},{13,14},{15,16},{17,18},{19... | collective-permute-start | bytes 1572872 | tf_op jit(solution)/shard_map/ppermute | solution.py:358
  1.8 9.5 %own.1 = (f32[4,256,512]{2,1,0:T(8,128)S(1)}, f32[4,256,512]{2,1,0:T(8,128)S(1)}, f32[4,256,512]{2,1,0:T(8,128)S(1)}, f32[2,256,512]{2,1,0:T(8,128)S(1)}, f32[2,...) custom-call(s32[1]{0:T(128)} %bitcast.core_ref, ...), custom_call_target="tpu_custom_call" | custom-call | tf_op jit(solution)/shard_map/own/pallas_call | solution.py:376
  11.3 0.0 collective-permute-done.1
  11.3 0.0 collective-permute-done
  11.4 2.9 %collective-permute-start.2 = (bf16[16,16,512]{2,1,0:T(8,128)(2,1)S(1)}, bf16[16,16,512]{2,1,0:T(8,128)(2,1)S(1)}, u32[]{:S(2)}, u32[]{:S(2)}) collective-permute-start(bf16[16,16,512]{2,1,0:T(8,128)(2,1)S(1)} %get-tuple-element.35.refs_0_), channel_id=1, source_target_pairs={{0,1},{1,0},{2,3},{3,2},{4,5},{5,4},{6,7},{7,6},{8,9},{9,8},{10,11... | collective-permute-start | bytes 786440 | tf_op jit(solution)/shard_map/ppermute | solution.py:396
  14.3 3.5 %collective-permute-start.3 = (bf16[8,8,512]{2,1,0:T(8,128)(2,1)S(1)}, bf16[8,8,512]{2,1,0:T(8,128)(2,1)S(1)}, u32[]{:S(2)}, u32[]{:S(2)}) collective-permute-start(bf16[8,8,512]{2,1,0:T(8,128)(2,1)S(1)} %get-tuple-element.36), channel_id=1, source_target_pairs={{0,32},{33,1},{2,34},{35,3},{4,36},{37,5},{6,38},{39,7},{8,40},{41... | collective-permute-start | bytes 196616 | tf_op jit(solution)/shard_map/ppermute | solution.py:397
  17.8 8.1 %other.1 = (f32[4,256,512]{2,1,0:T(8,128)S(1)}, f32[4,256,512]{2,1,0:T(8,128)S(1)}, f32[4,256,512]{2,1,0:T(8,128)S(1)}, f32[2,256,512]{2,1,0:T(8,128)S(1)}, f32[...) custom-call(s32[1]{0:T(128)} %bitcast.core_ref, ...), custom_call_target="tpu_custom_call" | custom-call | tf_op jit(solution)/shard_map/other/pallas_call | solution.py:366
  25.9 0.0 collective-permute-done.3.edges
  25.9 0.0 collective-permute-done.2.relayed
  25.9 2.6 %slab.1 = f32[16,64,512]{2,1,0:T(8,128)S(1)} custom-call(s32[1]{0:T(128)} %bitcast.core_ref, bf16[4,16,2,16,512]{4,3,2,1,0:T(8,128)(2,1)S(1)} %get-tuple-element.31.own, bf16[4,16,2,16,512]{4,3,2,1,0:T(8,128)(2,1)S(1)} %bitcast.6, bf16[16,2,16,512]{3,2,1,0:T(8,128)(2,1)S(1)} %bitcast.8, bf16[16,16,512]{2,1,0:T(8,128)(2,1)S(1)} %collective-permute-done.2.relayed, ...), custom_call_target="tpu_custom_call" | custom-call | tf_op jit(solution)/shard_map/slab/pallas_call | solution.py:406
  28.5 0.3 convert_element_type.6
  28.8 22.7 %all_to_all.5 = f16[16,64,512]{2,1,0:T(8,128)(2,1)S(1)} all-to-all(f16[16,64,512]{2,1,0:T(8,128)(2,1)S(1)} %convert_element_type.6), channel_id=1, replica_groups={{0,2,4,6,8,10,12,14,16,18,20,22,24,26,28,30},{1,3,5,7,9,11,13,15,17,19,..., dimensions={0} | all-to-all | bytes 2097152 | tf_op jit(solution)/shard_map/all_to_all | solution.py:416
  51.5 0.3 convert_element_type.7.parts
  51.8 0.9 %merge.1 = f32[4,8192]{1,0:T(4,128)} custom-call(f32[16,64,512]{2,1,0:T(8,128)S(1)} %convert_element_type.7.parts, f32[3,8,128]{2,1,0:T(8,128)S(1)} %get-tuple-element.37.scales), custom_call_target="tpu_custom_call" | custom-call | tf_op jit(solution)/shard_map/merge/pallas_call | solution.py:420
  (1 shorter events, 0.0 us)
Async XLA Ops:
  0.0 11.3 %collective-permute-start = (bf16[4,512,512]{2,1,0:T(8,128)(2,1)}, bf16[4,512,512]{2,1,0:T(8,128)(2,1)S(1)}, u32[]{:S(2)}, u32[]{:S(2)}) collective-permute-start(bf16[4,512,512]{2,1,0:T(8,128)(2,1)} %volume.1), channel_id=1, source_target_pairs={{0,1},{1,0},{2,3},{3,2},{4,5},{5,4},{6,7},{7,6},{8,9},{9,8},{10,11... | collective-permute-start | bytes 6291464 | tf_op jit(solution)/shard_map/ppermute | solution.py:363
  1.1 10.2 %collective-permute-start.1 = (bf16[512,512]{1,0:T(8,128)(2,1)S(1)}, bf16[512,512]{1,0:T(8,128)(2,1)S(1)}, u32[]{:S(2)}, u32[]{:S(2)}) collective-permute-start(bf16[512,512]{1,0:T(8,128)(2,1)S(1)} %get-tuple-element.32), channel_id=1, source_target_pairs={{1,2},{3,4},{5,6},{7,8},{9,10},{11,12},{13,14},{15,16},{17,18},{19... | collective-permute-start | bytes 1572872 | tf_op jit(solution)/shard_map/ppermute | solution.py:358
  11.4 14.5 %collective-permute-start.2 = (bf16[16,16,512]{2,1,0:T(8,128)(2,1)S(1)}, bf16[16,16,512]{2,1,0:T(8,128)(2,1)S(1)}, u32[]{:S(2)}, u32[]{:S(2)}) collective-permute-start(bf16[16,16,512]{2,1,0:T(8,128)(2,1)S(1)} %get-tuple-element.35.refs_0_), channel_id=1, source_target_pairs={{0,1},{1,0},{2,3},{3,2},{4,5},{5,4},{6,7},{7,6},{8,9},{9,8},{10,11... | collective-permute-start | bytes 786440 | tf_op jit(solution)/shard_map/ppermute | solution.py:396
  14.3 11.6 %collective-permute-start.3 = (bf16[8,8,512]{2,1,0:T(8,128)(2,1)S(1)}, bf16[8,8,512]{2,1,0:T(8,128)(2,1)S(1)}, u32[]{:S(2)}, u32[]{:S(2)}) collective-permute-start(bf16[8,8,512]{2,1,0:T(8,128)(2,1)S(1)} %get-tuple-element.36), channel_id=1, source_target_pairs={{0,32},{33,1},{2,34},{35,3},{4,36},{37,5},{6,38},{39,7},{8,40},{41... | collective-permute-start | bytes 196616 | tf_op jit(solution)/shard_map/ppermute | solution.py:397

commit v13 on v12

--- a/solution.py
+++ b/solution.py
@@ -108,31 +108,67 @@
     return [jnp.where(condition, x, y) for x, y in zip(a, b)]
 
 
+def each_block(blocks, unroll, body):
+    def step(at, carry):
+        for sub in range(unroll):
+            body(at * unroll + sub)
+        return carry
+
+    lax.fori_loop(0, blocks // unroll, step, 0)
+
+
+def each_unit(cols):
+    for half in range(0, BLOCK, HALF):
+        for start in range(0, cols, LANES):
+            yield half, slice(half, half + HALF), slice(start, start + LANES)
+
+
+def keep(ref, centre, tabs, here, lanes):
+    for c, value in enumerate(classify(centre, tabs)):
+        ref[c, here, lanes] = value
+
+
 def own_kernel(core_ref, volume, rows_op, cols_op, tables, *refs):
-    cells, sems = refs[7], refs[-1]
+    first, cells, sems = refs[0], refs[7], refs[-1]
+    slices, blocks, _, _, cols = cells.shape
     copies = [
-        pltpu.make_async_copy(volume.at[z], cells.at[z], sems.at[z]) for z in range(cells.shape[0])
+        pltpu.make_async_copy(volume.at[z], cells.at[z], sems.at[z]) for z in range(slices)
     ]
     for copy in copies:
         copy.start()
-    slices_kernel(core_ref, cells, rows_op, cols_op, tables, *refs[:7], *refs[8:10], copies=copies)
-
-
-def slices_kernel(core_ref, cells, rows_op, cols_op, tables, *refs, copies=()):
-    first, last, middle, slope, norm, edge_dx, edge_dy, inner_slope, inner_norm = refs[-9:]
+    copies[0].wait()
+    tabs = [tables[c] for c in range(8)]
+
+    def look_up_first(b):
+        for half, rows, lanes in each_unit(cols):
+            here = pl.ds(pl.multiple_of(b * BLOCK + half, HALF), HALF)
+            keep(first, cells[0, b, core_ref[0], rows, lanes].astype(F32), tabs, here, lanes)
+
+    each_block(blocks, 4, look_up_first)
+    for copy in copies[1:]:
+        copy.wait()
+    later_slices(core_ref, cells, rows_op, cols_op, tables, *refs[:7], *refs[8:10], first_done=True)
+
+
+def slices_kernel(*refs):
+    later_slices(*refs[:5], *refs[-9:], first_done=False)
+
+
+def later_slices(
+    core_ref, cells, rows_op, cols_op, tables,
+    first, last, middle, slope, norm, edge_dx, edge_dy, inner_slope, inner_norm, *, first_done,
+):
     core = core_ref[0]
     slices, blocks, _, _, cols = cells.shape
     rows = blocks * BLOCK
-    ends = (0, slices - 1)
+    end = slices - 1
     for z in range(slices):
-        if copies:
-            copies[z].wait()
         dx = jnp.dot(rows_op[...], cells[z].reshape(2 * rows, cols), preferred_element_type=F32)
         dy = jnp.dot(
             cells[z, :, core].reshape(rows, cols), cols_op[...], preferred_element_type=F32
         )
         to_slope, to_norm, at = (
-            (slope, norm, ends.index(z)) if z in ends else (inner_slope, inner_norm, z - 1)
+            (slope, norm, z // end) if z in (0, end) else (inner_slope, inner_norm, z - 1)
         )
         to_slope[at] = slope_of(dx, dy)
         to_norm[at] = norm_of(dx, dy)
@@ -140,33 +176,24 @@
         edge_dy[z] = jnp.where(core == 0, dy[:HALF], dy[rows - HALF :])
     tabs = [tables[c] for c in range(8)]
 
-    def block(bb, carry):
-      for sub in range(2):
-        b = bb * 2 + sub
-        for half in range(0, BLOCK, HALF):
+    def block(b):
+        for half, rows, lanes in each_unit(cols):
             here = pl.ds(pl.multiple_of(b * BLOCK + half, HALF), HALF)
-            rows = slice(half, half + HALF)
-            for start in range(0, cols, LANES):
-                lanes = slice(start, start + LANES)
-                mine = [cells[z, b, core, rows, lanes].astype(F32) for z in range(slices)]
-                accum, transmit = nothing()
-                for z in range(slices):
-                    found = classify(mine[z], tabs)
-                    if z in ends:
-                        ref = last if z else first
-                        for c in range(4):
-                            ref[c, here, lanes] = found[c]
-                    else:
-                        accum, transmit = shade(
-                            accum, transmit, mine[z + 1] - mine[z - 1],
-                            inner_slope[z - 1, here, lanes], inner_norm[z - 1, here, lanes], found,
-                        )
-                for c in range(3):
-                    middle[c, here, lanes] = accum[c]
-                middle[3, here, lanes] = transmit
-      return carry
-
-    lax.fori_loop(0, blocks // 2, block, 0)
+            mine = [cells[z, b, core, rows, lanes].astype(F32) for z in range(slices)]
+            if not first_done:
+                keep(first, mine[0], tabs, here, lanes)
+            accum, transmit = nothing()
+            for z in range(1, end):
+                accum, transmit = shade(
+                    accum, transmit, mine[z + 1] - mine[z - 1],
+                    inner_slope[z - 1, here, lanes], inner_norm[z - 1, here, lanes],
+                    classify(mine[z], tabs),
+                )
+            keep(last, mine[end], tabs, here, lanes)
+            for c, value in enumerate(accum + [transmit]):
+                middle[c, here, lanes] = value
+
+    each_block(blocks, 2, block)
 
 
 def relay_kernel(core_ref, own, other, outer, relayed, edge):
@@ -211,39 +238,35 @@
         both[3] = (1.0 - both[3]) * opacity_scale
         return both
 
-    def block(b, carry):
-        for half in range(0, BLOCK, HALF):
+    def block(b):
+        for half, rows, lanes in each_unit(cols):
             here = pl.ds(pl.multiple_of(b * BLOCK + half, HALF), HALF)
-            rows = slice(half, half + HALF)
-            for start in range(0, cols, LANES):
-                lanes = slice(start, start + LANES)
-
-                def half_slab(stack, terms):
-                    first, last, middle, slope, norm = terms[:5]
-                    parts = []
-                    for ref, at, z in ((first, 0, 0), (last, 1, end)):
-                        accum, transmit = shade(
-                            *nothing(), stack[z + 2] - stack[z],
-                            slope[at, here, lanes], norm[at, here, lanes],
-                            [ref[c, here, lanes] for c in range(4)],
-                        )
-                        parts.append(accum + [transmit])
-                    inner = [middle[c, here, lanes] for c in range(4)]
-                    return over(parts[0], over(inner, parts[1]))
-
-                own_stack, other_stack = stacks(
-                    [own[z, b, core, rows, lanes].astype(F32) for z in range(slices)],
-                    [other[z, b, core, rows, lanes].astype(F32) for z in range(slices)],
-                    outer[b, core, rows, lanes].astype(F32),
-                    relayed[b, rows, lanes].astype(F32),
-                )
-                both = finish(half_slab(own_stack, own_terms), half_slab(other_stack, other_terms))
-                for c in range(4):
-                    at = c * BLOCK + half
-                    out[b, at : at + HALF, lanes] = both[c]
-        return carry
-
-    lax.fori_loop(0, blocks, block, 0)
+
+            def half_slab(stack, terms):
+                first, last, middle, slope, norm = terms[:5]
+                parts = []
+                for ref, at, z in ((first, 0, 0), (last, 1, end)):
+                    accum, transmit = shade(
+                        *nothing(), stack[z + 2] - stack[z],
+                        slope[at, here, lanes], norm[at, here, lanes],
+                        [ref[c, here, lanes] for c in range(4)],
+                    )
+                    parts.append(accum + [transmit])
+                inner = [middle[c, here, lanes] for c in range(4)]
+                return over(parts[0], over(inner, parts[1]))
+
+            own_stack, other_stack = stacks(
+                [own[z, b, core, rows, lanes].astype(F32) for z in range(slices)],
+                [other[z, b, core, rows, lanes].astype(F32) for z in range(slices)],
+                outer[b, core, rows, lanes].astype(F32),
+                relayed[b, rows, lanes].astype(F32),
+            )
+            both = finish(half_slab(own_stack, own_terms), half_slab(other_stack, other_terms))
+            for c in range(4):
+                at = c * BLOCK + half
+                out[b, at : at + HALF, lanes] = both[c]
+
+    each_block(blocks, 2, block)
 
     tabs = [tables[c] for c in range(8)]
     b = jnp.where(front, 0, blocks - 1)

time: 52.8 us -> 52.8 us (level)
  no operation moved by 1% of the time
where the time goes in v13:
time: 52.8 us; the launch traced here: 52.6 us
  blocking collectives  22.8 us (43%)
  Pallas kernels  22.1 us (42%)
  starting transfers between devices  7.11 us (13%)
    all_to_all x1, blocking collectives, shards(): lax.all_to_all(partial_image.astype(jnp.float16), 'depth', split_axis=0,...  22.8 us
    pallas_call x1, Pallas kernels, shards(): pl.pallas_call(own_kernel, out_shape=(*terms, jax.ShapeDtypeStruct(split,...  9.5 us
    pallas_call x1, Pallas kernels, slices_terms(): pl.pallas_call(slices_kernel, out_shape=terms, in_specs=[smem] + [vmem] *...  8.05 us
    ppermute x1, starting transfers between devices, shards(): lax.ppermute(edges, ('img', 'depth'), [(at * depth_count + d, to * depth_...  3.52 us
    ppermute x1, starting transfers between devices, shards(): relayed = lax.ppermute(relayed, 'depth', partner)  2.89 us
    pallas_call x1, Pallas kernels, shards(): pl.pallas_call(slab_kernel, out_shape=jax.ShapeDtypeStruct((blocks, 4 * B...  2.57 us
    pallas_call x1, Pallas kernels, shards(): pl.pallas_call(functools.partial(prepare_kernel, slab_share=2.0 * slices...  1.08 us
  transfers between devices with their start and end apart: 4, of which 0 were waited for; matrix products, arithmetic and copies ran while one was open for 0% of the time, Pallas kernels for 35%

profile of v13, /device:TPU:64, one launch (start us, length us, event | category | flops | bytes accessed | tf_op | source)
XLA Modules:
  0.0 52.6 jit_solution(2371129753975937027)
XLA Ops:
  0.0 0.0 collective-permute-start
  0.0 1.1 %prepare.1 = (bf16[256,512]{1,0:T(8,128)(2,1)S(1)}, bf16[512,512]{1,0:T(8,128)(2,1)S(1)}, f32[8,8,128]{2,1,0:T(8,128)S(1)}, f32[3,8,128]{2,1,0:T(8,128)S(1)}, bf16[512,512]{1,0:T(8,128)(2,1)S(1)}) custom-call(s32[1]{0:T(128)} %bitcast.core_ref.refs_0_, bf16[4,512,512]{2,1,0:T(8,128)(2,1)} %volume.1, bf16[4,128]{1,0:T(4,128)(2,1)} %table_hbm.1), custom_call_target="tpu_custom_call" | custom-call | tf_op jit(solution)/shard_map/prepare/pallas_call | solution.py:360
  1.1 0.7 %collective-permute-start.1 = (bf16[512,512]{1,0:T(8,128)(2,1)S(1)}, bf16[512,512]{1,0:T(8,128)(2,1)S(1)}, u32[]{:S(2)}, u32[]{:S(2)}) collective-permute-start(bf16[512,512]{1,0:T(8,128)(2,1)S(1)} %get-tuple-element.32), channel_id=1, source_target_pairs={{1,2},{3,4},{5,6},{7,8},{9,10},{11,12},{13,14},{15,16},{17,18},{19... | collective-permute-start | bytes 1572872 | tf_op jit(solution)/shard_map/ppermute | solution.py:381
  1.8 9.5 %own.1 = (f32[4,256,512]{2,1,0:T(8,128)S(1)}, f32[4,256,512]{2,1,0:T(8,128)S(1)}, f32[4,256,512]{2,1,0:T(8,128)S(1)}, f32[2,256,512]{2,1,0:T(8,128)S(1)}, f32[2,...) custom-call(s32[1]{0:T(128)} %bitcast.core_ref.refs_0_, ...), custom_call_target="tpu_custom_call" | custom-call | tf_op jit(solution)/shard_map/own/pallas_call | solution.py:399
  11.3 0.0 collective-permute-done.1
  11.3 0.0 collective-permute-done
  11.4 2.9 %collective-permute-start.2 = (bf16[16,16,512]{2,1,0:T(8,128)(2,1)S(1)}, bf16[16,16,512]{2,1,0:T(8,128)(2,1)S(1)}, u32[]{:S(2)}, u32[]{:S(2)}) collective-permute-start(bf16[16,16,512]{2,1,0:T(8,128)(2,1)S(1)} %get-tuple-element.35.refs_5_), channel_id=1, source_target_pairs={{0,1},{1,0},{2,3},{3,2},{4,5},{5,4},{6,7},{7,6},{8,9},{9,8},{10,11... | collective-permute-start | bytes 786440 | tf_op jit(solution)/shard_map/ppermute | solution.py:419
  14.3 3.5 %collective-permute-start.3 = (bf16[8,8,512]{2,1,0:T(8,128)(2,1)S(1)}, bf16[8,8,512]{2,1,0:T(8,128)(2,1)S(1)}, u32[]{:S(2)}, u32[]{:S(2)}) collective-permute-start(bf16[8,8,512]{2,1,0:T(8,128)(2,1)S(1)} %get-tuple-element.36), channel_id=1, source_target_pairs={{0,32},{33,1},{2,34},{35,3},{4,36},{37,5},{6,38},{39,7},{8,40},{41... | collective-permute-start | bytes 196616 | tf_op jit(solution)/shard_map/ppermute | solution.py:420
  17.8 8.1 %other.1 = (f32[4,256,512]{2,1,0:T(8,128)S(1)}, f32[4,256,512]{2,1,0:T(8,128)S(1)}, f32[4,256,512]{2,1,0:T(8,128)S(1)}, f32[2,256,512]{2,1,0:T(8,128)S(1)}, f32[...) custom-call(s32[1]{0:T(128)} %bitcast.core_ref.refs_0_, ...), custom_call_target="tpu_custom_call" | custom-call | tf_op jit(solution)/shard_map/other/pallas_call | solution.py:389
  25.8 0.0 collective-permute-done.3.edges
  25.9 0.0 collective-permute-done.2.relayed
  25.9 2.6 %slab.1 = f32[16,64,512]{2,1,0:T(8,128)S(1)} custom-call(s32[1]{0:T(128)} %bitcast.core_ref.refs_0_, bf16[4,16,2,16,512]{4,3,2,1,0:T(8,128)(2,1)S(1)} %get-tuple-element.31.own, bf16[4,16,2,16,512]{4,3,2,1,0:T(8,128)(2,1)S(1)} %bitcast.6, bf16[16,2,16,512]{3,2,1,0:T(8,128)(2,1)S(1)} %bitcast.8, bf16[16,16,512]{2,1,0:T(8,128)(2,1)S(1)} %collective-permute-done.2.relayed, ...), custom_call_target="tpu_custom_call" | custom-call | tf_op jit(solution)/shard_map/slab/pallas_call | solution.py:429
  28.4 0.3 convert_element_type.6
  28.7 22.8 %all_to_all.5 = f16[16,64,512]{2,1,0:T(8,128)(2,1)S(1)} all-to-all(f16[16,64,512]{2,1,0:T(8,128)(2,1)S(1)} %convert_element_type.6), channel_id=1, replica_groups={{0,2,4,6,8,10,12,14,16,18,20,22,24,26,28,30},{1,3,5,7,9,11,13,15,17,19,..., dimensions={0} | all-to-all | bytes 2097152 | tf_op jit(solution)/shard_map/all_to_all | solution.py:439
  51.5 0.3 convert_element_type.7.parts
  51.7 0.9 %merge.1 = f32[4,8192]{1,0:T(4,128)} custom-call(f32[16,64,512]{2,1,0:T(8,128)S(1)} %convert_element_type.7.parts, f32[3,8,128]{2,1,0:T(8,128)S(1)} %get-tuple-element.37.scales), custom_call_target="tpu_custom_call" | custom-call | tf_op jit(solution)/shard_map/merge/pallas_call | solution.py:443
  (1 shorter events, 0.0 us)
Async XLA Ops:
  0.0 11.3 %collective-permute-start = (bf16[4,512,512]{2,1,0:T(8,128)(2,1)}, bf16[4,512,512]{2,1,0:T(8,128)(2,1)S(1)}, u32[]{:S(2)}, u32[]{:S(2)}) collective-permute-start(bf16[4,512,512]{2,1,0:T(8,128)(2,1)} %volume.1), channel_id=1, source_target_pairs={{0,1},{1,0},{2,3},{3,2},{4,5},{5,4},{6,7},{7,6},{8,9},{9,8},{10,11... | collective-permute-start | bytes 6291464 | tf_op jit(solution)/shard_map/ppermute | solution.py:386
  1.1 10.2 %collective-permute-start.1 = (bf16[512,512]{1,0:T(8,128)(2,1)S(1)}, bf16[512,512]{1,0:T(8,128)(2,1)S(1)}, u32[]{:S(2)}, u32[]{:S(2)}) collective-permute-start(bf16[512,512]{1,0:T(8,128)(2,1)S(1)} %get-tuple-element.32), channel_id=1, source_target_pairs={{1,2},{3,4},{5,6},{7,8},{9,10},{11,12},{13,14},{15,16},{17,18},{19... | collective-permute-start | bytes 1572872 | tf_op jit(solution)/shard_map/ppermute | solution.py:381
  11.4 14.5 %collective-permute-start.2 = (bf16[16,16,512]{2,1,0:T(8,128)(2,1)S(1)}, bf16[16,16,512]{2,1,0:T(8,128)(2,1)S(1)}, u32[]{:S(2)}, u32[]{:S(2)}) collective-permute-start(bf16[16,16,512]{2,1,0:T(8,128)(2,1)S(1)} %get-tuple-element.35.refs_5_), channel_id=1, source_target_pairs={{0,1},{1,0},{2,3},{3,2},{4,5},{5,4},{6,7},{7,6},{8,9},{9,8},{10,11... | collective-permute-start | bytes 786440 | tf_op jit(solution)/shard_map/ppermute | solution.py:419
  14.3 11.6 %collective-permute-start.3 = (bf16[8,8,512]{2,1,0:T(8,128)(2,1)S(1)}, bf16[8,8,512]{2,1,0:T(8,128)(2,1)S(1)}, u32[]{:S(2)}, u32[]{:S(2)}) collective-permute-start(bf16[8,8,512]{2,1,0:T(8,128)(2,1)S(1)} %get-tuple-element.36), channel_id=1, source_target_pairs={{0,32},{33,1},{2,34},{35,3},{4,36},{37,5},{6,38},{39,7},{8,40},{41... | collective-permute-start | bytes 196616 | tf_op jit(solution)/shard_map/ppermute | solution.py:420

commit v14 on v13

--- a/solution.py
+++ b/solution.py
@@ -134,9 +134,10 @@
     copies = [
         pltpu.make_async_copy(volume.at[z], cells.at[z], sems.at[z]) for z in range(slices)
     ]
-    for copy in copies:
+    copies[0].start()
+    copies[0].wait()
+    for copy in copies[1:]:
         copy.start()
-    copies[0].wait()
     tabs = [tables[c] for c in range(8)]
 
     def look_up_first(b):

time: 52.8 us -> 52.8 us (level)
  no operation moved by 1% of the time
where the time goes in v14:
time: 52.8 us; the launch traced here: 52.6 us
  blocking collectives  22.8 us (43%)
  Pallas kernels  22.1 us (42%)
  starting transfers between devices  7.11 us (13%)
    all_to_all x1, blocking collectives, shards(): lax.all_to_all(partial_image.astype(jnp.float16), 'depth', split_axis=0,...  22.8 us
    pallas_call x1, Pallas kernels, shards(): pl.pallas_call(own_kernel, out_shape=(*terms, jax.ShapeDtypeStruct(split,...  9.5 us
    pallas_call x1, Pallas kernels, slices_terms(): pl.pallas_call(slices_kernel, out_shape=terms, in_specs=[smem] + [vmem] *...  8.05 us
    ppermute x1, starting transfers between devices, shards(): lax.ppermute(edges, ('img', 'depth'), [(at * depth_count + d, to * depth_...  3.52 us
    ppermute x1, starting transfers between devices, shards(): relayed = lax.ppermute(relayed, 'depth', partner)  2.89 us
    pallas_call x1, Pallas kernels, shards(): pl.pallas_call(slab_kernel, out_shape=jax.ShapeDtypeStruct((blocks, 4 * B...  2.57 us
    pallas_call x1, Pallas kernels, shards(): pl.pallas_call(functools.partial(prepare_kernel, slab_share=2.0 * slices...  1.08 us
  transfers between devices with their start and end apart: 4, of which 0 were waited for; matrix products, arithmetic and copies ran while one was open for 0% of the time, Pallas kernels for 35%

profile of v14, /device:TPU:64, one launch (start us, length us, event | category | flops | bytes accessed | tf_op | source)
XLA Modules:
  0.0 52.6 jit_solution(5681494330683450092)
XLA Ops:
  0.0 0.0 collective-permute-start
  0.0 1.1 %prepare.1 = (bf16[256,512]{1,0:T(8,128)(2,1)S(1)}, bf16[512,512]{1,0:T(8,128)(2,1)S(1)}, f32[8,8,128]{2,1,0:T(8,128)S(1)}, f32[3,8,128]{2,1,0:T(8,128)S(1)}, bf16[512,512]{1,0:T(8,128)(2,1)S(1)}) custom-call(s32[1]{0:T(128)} %bitcast.core_ref.refs_0_, bf16[4,512,512]{2,1,0:T(8,128)(2,1)} %volume.1, bf16[4,128]{1,0:T(4,128)(2,1)} %table_hbm.1), custom_call_target="tpu_custom_call" | custom-call | tf_op jit(solution)/shard_map/prepare/pallas_call | solution.py:361
  1.1 0.7 %collective-permute-start.1 = (bf16[512,512]{1,0:T(8,128)(2,1)S(1)}, bf16[512,512]{1,0:T(8,128)(2,1)S(1)}, u32[]{:S(2)}, u32[]{:S(2)}) collective-permute-start(bf16[512,512]{1,0:T(8,128)(2,1)S(1)} %get-tuple-element.32), channel_id=1, source_target_pairs={{1,2},{3,4},{5,6},{7,8},{9,10},{11,12},{13,14},{15,16},{17,18},{19... | collective-permute-start | bytes 1572872 | tf_op jit(solution)/shard_map/ppermute | solution.py:382
  1.8 9.5 %own.1 = (f32[4,256,512]{2,1,0:T(8,128)S(1)}, f32[4,256,512]{2,1,0:T(8,128)S(1)}, f32[4,256,512]{2,1,0:T(8,128)S(1)}, f32[2,256,512]{2,1,0:T(8,128)S(1)}, f32[2,...) custom-call(s32[1]{0:T(128)} %bitcast.core_ref.refs_0_, ...), custom_call_target="tpu_custom_call" | custom-call | tf_op jit(solution)/shard_map/own/pallas_call | solution.py:400
  11.3 0.0 collective-permute-done.1
  11.3 0.0 collective-permute-done
  11.4 2.9 %collective-permute-start.2 = (bf16[16,16,512]{2,1,0:T(8,128)(2,1)S(1)}, bf16[16,16,512]{2,1,0:T(8,128)(2,1)S(1)}, u32[]{:S(2)}, u32[]{:S(2)}) collective-permute-start(bf16[16,16,512]{2,1,0:T(8,128)(2,1)S(1)} %get-tuple-element.35.refs_5_), channel_id=1, source_target_pairs={{0,1},{1,0},{2,3},{3,2},{4,5},{5,4},{6,7},{7,6},{8,9},{9,8},{10,11... | collective-permute-start | bytes 786440 | tf_op jit(solution)/shard_map/ppermute | solution.py:420
  14.3 3.5 %collective-permute-start.3 = (bf16[8,8,512]{2,1,0:T(8,128)(2,1)S(1)}, bf16[8,8,512]{2,1,0:T(8,128)(2,1)S(1)}, u32[]{:S(2)}, u32[]{:S(2)}) collective-permute-start(bf16[8,8,512]{2,1,0:T(8,128)(2,1)S(1)} %get-tuple-element.36), channel_id=1, source_target_pairs={{0,32},{33,1},{2,34},{35,3},{4,36},{37,5},{6,38},{39,7},{8,40},{41... | collective-permute-start | bytes 196616 | tf_op jit(solution)/shard_map/ppermute | solution.py:421
  17.8 8.1 %other.1 = (f32[4,256,512]{2,1,0:T(8,128)S(1)}, f32[4,256,512]{2,1,0:T(8,128)S(1)}, f32[4,256,512]{2,1,0:T(8,128)S(1)}, f32[2,256,512]{2,1,0:T(8,128)S(1)}, f32[...) custom-call(s32[1]{0:T(128)} %bitcast.core_ref.refs_0_, ...), custom_call_target="tpu_custom_call" | custom-call | tf_op jit(solution)/shard_map/other/pallas_call | solution.py:390
  25.8 0.0 collective-permute-done.3.edges
  25.9 0.0 collective-permute-done.2.relayed
  25.9 2.6 %slab.1 = f32[16,64,512]{2,1,0:T(8,128)S(1)} custom-call(s32[1]{0:T(128)} %bitcast.core_ref.refs_0_, bf16[4,16,2,16,512]{4,3,2,1,0:T(8,128)(2,1)S(1)} %get-tuple-element.31.own, bf16[4,16,2,16,512]{4,3,2,1,0:T(8,128)(2,1)S(1)} %bitcast.6, bf16[16,2,16,512]{3,2,1,0:T(8,128)(2,1)S(1)} %bitcast.8, bf16[16,16,512]{2,1,0:T(8,128)(2,1)S(1)} %collective-permute-done.2.relayed, ...), custom_call_target="tpu_custom_call" | custom-call | tf_op jit(solution)/shard_map/slab/pallas_call | solution.py:430
  28.4 0.3 convert_element_type.6
  28.7 22.8 %all_to_all.5 = f16[16,64,512]{2,1,0:T(8,128)(2,1)S(1)} all-to-all(f16[16,64,512]{2,1,0:T(8,128)(2,1)S(1)} %convert_element_type.6), channel_id=1, replica_groups={{0,2,4,6,8,10,12,14,16,18,20,22,24,26,28,30},{1,3,5,7,9,11,13,15,17,19,..., dimensions={0} | all-to-all | bytes 2097152 | tf_op jit(solution)/shard_map/all_to_all | solution.py:440
  51.5 0.3 convert_element_type.7.parts
  51.7 0.9 %merge.1 = f32[4,8192]{1,0:T(4,128)} custom-call(f32[16,64,512]{2,1,0:T(8,128)S(1)} %convert_element_type.7.parts, f32[3,8,128]{2,1,0:T(8,128)S(1)} %get-tuple-element.37.scales), custom_call_target="tpu_custom_call" | custom-call | tf_op jit(solution)/shard_map/merge/pallas_call | solution.py:444
  (1 shorter events, 0.0 us)
Async XLA Ops:
  0.0 11.3 %collective-permute-start = (bf16[4,512,512]{2,1,0:T(8,128)(2,1)}, bf16[4,512,512]{2,1,0:T(8,128)(2,1)S(1)}, u32[]{:S(2)}, u32[]{:S(2)}) collective-permute-start(bf16[4,512,512]{2,1,0:T(8,128)(2,1)} %volume.1), channel_id=1, source_target_pairs={{0,1},{1,0},{2,3},{3,2},{4,5},{5,4},{6,7},{7,6},{8,9},{9,8},{10,11... | collective-permute-start | bytes 6291464 | tf_op jit(solution)/shard_map/ppermute | solution.py:387
  1.1 10.2 %collective-permute-start.1 = (bf16[512,512]{1,0:T(8,128)(2,1)S(1)}, bf16[512,512]{1,0:T(8,128)(2,1)S(1)}, u32[]{:S(2)}, u32[]{:S(2)}) collective-permute-start(bf16[512,512]{1,0:T(8,128)(2,1)S(1)} %get-tuple-element.32), channel_id=1, source_target_pairs={{1,2},{3,4},{5,6},{7,8},{9,10},{11,12},{13,14},{15,16},{17,18},{19... | collective-permute-start | bytes 1572872 | tf_op jit(solution)/shard_map/ppermute | solution.py:382
  11.4 14.5 %collective-permute-start.2 = (bf16[16,16,512]{2,1,0:T(8,128)(2,1)S(1)}, bf16[16,16,512]{2,1,0:T(8,128)(2,1)S(1)}, u32[]{:S(2)}, u32[]{:S(2)}) collective-permute-start(bf16[16,16,512]{2,1,0:T(8,128)(2,1)S(1)} %get-tuple-element.35.refs_5_), channel_id=1, source_target_pairs={{0,1},{1,0},{2,3},{3,2},{4,5},{5,4},{6,7},{7,6},{8,9},{9,8},{10,11... | collective-permute-start | bytes 786440 | tf_op jit(solution)/shard_map/ppermute | solution.py:420
  14.3 11.6 %collective-permute-start.3 = (bf16[8,8,512]{2,1,0:T(8,128)(2,1)S(1)}, bf16[8,8,512]{2,1,0:T(8,128)(2,1)S(1)}, u32[]{:S(2)}, u32[]{:S(2)}) collective-permute-start(bf16[8,8,512]{2,1,0:T(8,128)(2,1)S(1)} %get-tuple-element.36), channel_id=1, source_target_pairs={{0,32},{33,1},{2,34},{35,3},{4,36},{37,5},{6,38},{39,7},{8,40},{41... | collective-permute-start | bytes 196616 | tf_op jit(solution)/shard_map/ppermute | solution.py:421

commit v15 on v13

--- a/solution.py
+++ b/solution.py
@@ -39,14 +39,15 @@
 
 
 def prepare_kernel(
-    core_ref, volume, table_hbm, rows_op, cols_op, tables, scales, outer, table_ref, sems,
+    core_ref, volume, table_hbm, rows_op, cols_op, tables, scales, outer, cells, table_ref, sems,
     *, slab_share, depth_total,
 ):
-    outer_slice = (volume.shape[0] - 1) * core_ref[0]
-    table_copy = pltpu.make_async_copy(table_hbm, table_ref, sems.at[0])
-    outer_copy = pltpu.make_async_copy(volume.at[outer_slice], outer, sems.at[1])
+    slices = volume.shape[0]
+    table_copy = pltpu.make_async_copy(table_hbm, table_ref, sems.at[slices])
+    copies = [pltpu.make_async_copy(volume.at[z], cells.at[z], sems.at[z]) for z in range(slices)]
     table_copy.start()
-    outer_copy.start()
+    for copy in copies:
+        copy.start()
     rows_op[...] = row_differences(rows_op.shape[1], core_ref[0])
     cols_op[...] = column_differences(cols_op.shape[1])
     table_copy.wait()
@@ -62,7 +63,9 @@
         tables[c + 4] = jnp.where(last, lower, pltpu.roll(lower, entries - 1, 1))
     for at, value in enumerate((colour_top * opacity_top, opacity_top, 1.0 / opacity_top)):
         scales[at] = jnp.broadcast_to(value, (HALF, LANES))
-    outer_copy.wait()
+    for copy in copies:
+        copy.wait()
+    outer[...] = cells[(slices - 1) * core_ref[0]]
 
 
 def look_up(table, index):
@@ -128,36 +131,10 @@
         ref[c, here, lanes] = value
 
 
-def own_kernel(core_ref, volume, rows_op, cols_op, tables, *refs):
-    first, cells, sems = refs[0], refs[7], refs[-1]
-    slices, blocks, _, _, cols = cells.shape
-    copies = [
-        pltpu.make_async_copy(volume.at[z], cells.at[z], sems.at[z]) for z in range(slices)
-    ]
-    for copy in copies:
-        copy.start()
-    copies[0].wait()
-    tabs = [tables[c] for c in range(8)]
-
-    def look_up_first(b):
-        for half, rows, lanes in each_unit(cols):
-            here = pl.ds(pl.multiple_of(b * BLOCK + half, HALF), HALF)
-            keep(first, cells[0, b, core_ref[0], rows, lanes].astype(F32), tabs, here, lanes)
-
-    each_block(blocks, 4, look_up_first)
-    for copy in copies[1:]:
-        copy.wait()
-    later_slices(core_ref, cells, rows_op, cols_op, tables, *refs[:7], *refs[8:10], first_done=True)
-
-
-def slices_kernel(*refs):
-    later_slices(*refs[:5], *refs[-9:], first_done=False)
-
-
-def later_slices(
-    core_ref, cells, rows_op, cols_op, tables,
-    first, last, middle, slope, norm, edge_dx, edge_dy, inner_slope, inner_norm, *, first_done,
+def slices_kernel(
+    core_ref, cells, rows_op, cols_op, tables, *refs
 ):
+    first, last, middle, slope, norm, edge_dx, edge_dy, inner_slope, inner_norm = refs[-9:]
     core = core_ref[0]
     slices, blocks, _, _, cols = cells.shape
     rows = blocks * BLOCK
@@ -180,8 +157,7 @@
         for half, rows, lanes in each_unit(cols):
             here = pl.ds(pl.multiple_of(b * BLOCK + half, HALF), HALF)
             mine = [cells[z, b, core, rows, lanes].astype(F32) for z in range(slices)]
-            if not first_done:
-                keep(first, mine[0], tabs, here, lanes)
+            keep(first, mine[0], tabs, here, lanes)
             accum, transmit = nothing()
             for z in range(1, end):
                 accum, transmit = shade(
@@ -193,7 +169,7 @@
             for c, value in enumerate(accum + [transmit]):
                 middle[c, here, lanes] = value
 
-    each_block(blocks, 2, block)
+    each_block(blocks, 4, block)
 
 
 def relay_kernel(core_ref, own, other, outer, relayed, edge):
@@ -357,7 +333,7 @@
 
     partner = [(d, d ^ 1) for d in range(depth_count)]
     entries = transfer_table.shape[1]
-    *ops, scales, outer = pl.pallas_call(
+    *ops, scales, outer, own = pl.pallas_call(
         functools.partial(
             prepare_kernel, slab_share=2.0 * slices / depth_total, depth_total=depth_total
         ),
@@ -367,11 +343,12 @@
             jax.ShapeDtypeStruct((8, HALF, entries), F32),
             jax.ShapeDtypeStruct((3, HALF, LANES), F32),
             jax.ShapeDtypeStruct((rows, cols), BF16),
+            jax.ShapeDtypeStruct(volume.shape, BF16),
         ),
         in_specs=[smem, hbm, hbm],
-        out_specs=(vmem,) * 5,
+        out_specs=(vmem,) * 6,
         scratch_shapes=[
-            pltpu.VMEM(transfer_table.shape, BF16), pltpu.SemaphoreType.DMA((2,)),
+            pltpu.VMEM(transfer_table.shape, BF16), pltpu.SemaphoreType.DMA((slices + 1,)),
         ],
         compiler_params=params,
         name="prepare",
@@ -396,16 +373,8 @@
             name=name,
         )(core_arg, cells, *ops, *previous)
 
-    *own_terms, own = pl.pallas_call(
-        own_kernel,
-        out_shape=(*terms, jax.ShapeDtypeStruct(split, BF16)),
-        in_specs=[smem, hbm] + [vmem] * 3,
-        out_specs=(vmem,) * 8,
-        scratch_shapes=[pltpu.VMEM((slices - 2, half, cols), F32)] * 2
-        + [pltpu.SemaphoreType.DMA((slices,))],
-        compiler_params=params,
-        name="own",
-    )(core_arg, in_hbm(volume.reshape(split)), *ops)
+    own = own.reshape(split)
+    own_terms = slices_terms(own, (), "own")
     outer, _ = lax.optimization_barrier((outer, own_terms[6]))
     relayed, edges = pl.pallas_call(
         relay_kernel,

time: 52.8 us -> 53 us (level)
  blocking collectives: 22.8 us -> 24.6 us
  Pallas kernels: 22.1 us -> 20.5 us
    pallas_call x1 -> x0, Pallas kernels: 9.5 us -> none  [shards(): pl.pallas_call(own_kernel, out_shape=(*terms, jax.ShapeDtypeStruct(split,...]
    pallas_call x1 -> x2, Pallas kernels: 8.05 us -> 15.4 us  [slices_terms(): pl.pallas_call(slices_kernel, out_shape=terms, in_specs=[smem] + [vmem] *...]
    all_to_all x1, blocking collectives: 22.8 us -> 24.6 us  [shards(): lax.all_to_all(partial_image.astype(jnp.float16), 'depth', split_axis=0,...]
    pallas_call x1, Pallas kernels: 1.08 us -> 1.61 us  [shards(): pl.pallas_call(functools.partial(prepare_kernel, slab_share=2.0 * slices...]
  transfers between devices with their start and end apart: 4 -> 4, of which waited for: 0 -> 0; matrix products, arithmetic and copies ran while one was open for 0% -> 0% of each run, Pallas kernels for 35% -> 32%
where the time goes in v15:
time: 53 us; the launch traced here: 52.8 us
  blocking collectives  24.6 us (46%)
  Pallas kernels  20.5 us (39%)
  starting transfers between devices  7.11 us (13%)
    all_to_all x1, blocking collectives, shards(): lax.all_to_all(partial_image.astype(jnp.float16), 'depth', split_axis=0,...  24.6 us
    pallas_call x2, Pallas kernels, slices_terms(): pl.pallas_call(slices_kernel, out_shape=terms, in_specs=[smem] + [vmem] *...  15.4 us
    ppermute x1, starting transfers between devices, shards(): lax.ppermute(edges, ('img', 'depth'), [(at * depth_count + d, to * depth_...  3.52 us
    ppermute x1, starting transfers between devices, shards(): relayed = lax.ppermute(relayed, 'depth', partner)  2.9 us
    pallas_call x1, Pallas kernels, shards(): pl.pallas_call(slab_kernel, out_shape=jax.ShapeDtypeStruct((blocks, 4 * B...  2.65 us
    pallas_call x1, Pallas kernels, shards(): pl.pallas_call(functools.partial(prepare_kernel, slab_share=2.0 * slices...  1.61 us
  transfers between devices with their start and end apart: 4, of which 0 were waited for; matrix products, arithmetic and copies ran while one was open for 0% of the time, Pallas kernels for 32%

profile of v15, /device:TPU:64, one launch (start us, length us, event | category | flops | bytes accessed | tf_op | source)
XLA Modules:
  0.0 52.8 jit_solution(11211758124568403951)
XLA Ops:
  0.0 0.0 collective-permute-start
  0.0 1.6 %prepare.1 = (bf16[256,512]{1,0:T(8,128)(2,1)S(1)}, bf16[512,512]{1,0:T(8,128)(2,1)S(1)}, f32[8,8,128]{2,1,0:T(8,128)S(1)}, f32[3,8,128]{2,1,0:T(8,128)S(1)}, bf...) custom-call(s32[1]{0:T(128)} %bitcast.core_ref, bf16[4,512,512]{2,1,0:T(8,128)(2,1)} %volume.1, ...), custom_call_target="tpu_custom_call" | custom-call | tf_op jit(solution)/shard_map/prepare/pallas_call | solution.py:336
  1.6 0.7 %collective-permute-start.1 = (bf16[512,512]{1,0:T(8,128)(2,1)S(1)}, bf16[512,512]{1,0:T(8,128)(2,1)S(1)}, u32[]{:S(2)}, u32[]{:S(2)}) collective-permute-start(bf16[512,512]{1,0:T(8,128)(2,1)S(1)} %get-tuple-element.29), channel_id=1, source_target_pairs={{1,2},{3,4},{5,6},{7,8},{9,10},{11,12},{13,14},{15,16},{17,18},{19... | collective-permute-start | bytes 1572872 | tf_op jit(solution)/shard_map/ppermute | solution.py:358
  2.3 7.7 %own.1 = (f32[4,256,512]{2,1,0:T(8,128)S(1)}, f32[4,256,512]{2,1,0:T(8,128)S(1)}, f32[4,256,512]{2,1,0:T(8,128)S(1)}, f32[2,256,512]{2,1,0:T(8,128)S(1)}, f32[2,...) custom-call(s32[1]{0:T(128)} %bitcast.core_ref, ...), custom_call_target="tpu_custom_call" | custom-call | tf_op jit(solution)/shard_map/own/pallas_call | solution.py:366
  10.0 0.0 collective-permute-done.1
  10.0 0.0 collective-permute-done
  10.1 2.9 %collective-permute-start.2 = (bf16[16,16,512]{2,1,0:T(8,128)(2,1)S(1)}, bf16[16,16,512]{2,1,0:T(8,128)(2,1)S(1)}, u32[]{:S(2)}, u32[]{:S(2)}) collective-permute-start(bf16[16,16,512]{2,1,0:T(8,128)(2,1)S(1)} %get-tuple-element.35.refs_0_), channel_id=1, source_target_pairs={{0,1},{1,0},{2,3},{3,2},{4,5},{5,4},{6,7},{7,6},{8,9},{9,8},{10,11... | collective-permute-start | bytes 786440 | tf_op jit(solution)/shard_map/ppermute | solution.py:388
  13.0 3.5 %collective-permute-start.3 = (bf16[8,8,512]{2,1,0:T(8,128)(2,1)S(1)}, bf16[8,8,512]{2,1,0:T(8,128)(2,1)S(1)}, u32[]{:S(2)}, u32[]{:S(2)}) collective-permute-start(bf16[8,8,512]{2,1,0:T(8,128)(2,1)S(1)} %get-tuple-element.36), channel_id=1, source_target_pairs={{0,32},{33,1},{2,34},{35,3},{4,36},{37,5},{6,38},{39,7},{8,40},{41... | collective-permute-start | bytes 196616 | tf_op jit(solution)/shard_map/ppermute | solution.py:389
  16.5 7.7 %other.1 = (f32[4,256,512]{2,1,0:T(8,128)S(1)}, f32[4,256,512]{2,1,0:T(8,128)S(1)}, f32[4,256,512]{2,1,0:T(8,128)S(1)}, f32[2,256,512]{2,1,0:T(8,128)S(1)}, f32[...) custom-call(s32[1]{0:T(128)} %bitcast.core_ref, ...), custom_call_target="tpu_custom_call" | custom-call | tf_op jit(solution)/shard_map/other/pallas_call | solution.py:366
  24.2 0.0 collective-permute-done.3.edges
  24.2 0.0 collective-permute-done.2.relayed
  24.2 2.6 %slab.1 = f32[16,64,512]{2,1,0:T(8,128)S(1)} custom-call(s32[1]{0:T(128)} %bitcast.core_ref, bf16[4,16,2,16,512]{4,3,2,1,0:T(8,128)(2,1)S(1)} %bitcast.6, bf16[4,16,2,16,512]{4,3,2,1,0:T(8,128)(2,1)S(1)} %bitcast.9, bf16[16,2,16,512]{3,2,1,0:T(8,128)(2,1)S(1)} %bitcast.11, bf16[16,16,512]{2,1,0:T(8,128)(2,1)S(1)} %collective-permute-done.2.relayed, ...), custom_call_target="tpu_custom_call" | custom-call | tf_op jit(solution)/shard_map/slab/pallas_call | solution.py:398
  26.9 0.3 convert_element_type.6
  27.1 24.6 %all_to_all.5 = f16[16,64,512]{2,1,0:T(8,128)(2,1)S(1)} all-to-all(f16[16,64,512]{2,1,0:T(8,128)(2,1)S(1)} %convert_element_type.6), channel_id=1, replica_groups={{0,2,4,6,8,10,12,14,16,18,20,22,24,26,28,30},{1,3,5,7,9,11,13,15,17,19,..., dimensions={0} | all-to-all | bytes 2097152 | tf_op jit(solution)/shard_map/all_to_all | solution.py:408
  51.7 0.3 convert_element_type.7.parts
  52.0 0.9 %merge.1 = f32[4,8192]{1,0:T(4,128)} custom-call(f32[16,64,512]{2,1,0:T(8,128)S(1)} %convert_element_type.7.parts, f32[3,8,128]{2,1,0:T(8,128)S(1)} %get-tuple-element.37.scales), custom_call_target="tpu_custom_call" | custom-call | tf_op jit(solution)/shard_map/merge/pallas_call | solution.py:412
  (1 shorter events, 0.0 us)
Async XLA Ops:
  0.0 10.0 %collective-permute-start = (bf16[4,512,512]{2,1,0:T(8,128)(2,1)}, bf16[4,512,512]{2,1,0:T(8,128)(2,1)S(1)}, u32[]{:S(2)}, u32[]{:S(2)}) collective-permute-start(bf16[4,512,512]{2,1,0:T(8,128)(2,1)} %volume.1), channel_id=1, source_target_pairs={{0,1},{1,0},{2,3},{3,2},{4,5},{5,4},{6,7},{7,6},{8,9},{9,8},{10,11... | collective-permute-start | bytes 6291464 | tf_op jit(solution)/shard_map/ppermute | solution.py:363
  1.6 8.4 %collective-permute-start.1 = (bf16[512,512]{1,0:T(8,128)(2,1)S(1)}, bf16[512,512]{1,0:T(8,128)(2,1)S(1)}, u32[]{:S(2)}, u32[]{:S(2)}) collective-permute-start(bf16[512,512]{1,0:T(8,128)(2,1)S(1)} %get-tuple-element.29), channel_id=1, source_target_pairs={{1,2},{3,4},{5,6},{7,8},{9,10},{11,12},{13,14},{15,16},{17,18},{19... | collective-permute-start | bytes 1572872 | tf_op jit(solution)/shard_map/ppermute | solution.py:358
  10.1 14.1 %collective-permute-start.2 = (bf16[16,16,512]{2,1,0:T(8,128)(2,1)S(1)}, bf16[16,16,512]{2,1,0:T(8,128)(2,1)S(1)}, u32[]{:S(2)}, u32[]{:S(2)}) collective-permute-start(bf16[16,16,512]{2,1,0:T(8,128)(2,1)S(1)} %get-tuple-element.35.refs_0_), channel_id=1, source_target_pairs={{0,1},{1,0},{2,3},{3,2},{4,5},{5,4},{6,7},{7,6},{8,9},{9,8},{10,11... | collective-permute-start | bytes 786440 | tf_op jit(solution)/shard_map/ppermute | solution.py:388
  13.0 11.2 %collective-permute-start.3 = (bf16[8,8,512]{2,1,0:T(8,128)(2,1)S(1)}, bf16[8,8,512]{2,1,0:T(8,128)(2,1)S(1)}, u32[]{:S(2)}, u32[]{:S(2)}) collective-permute-start(bf16[8,8,512]{2,1,0:T(8,128)(2,1)S(1)} %get-tuple-element.36), channel_id=1, source_target_pairs={{0,32},{33,1},{2,34},{35,3},{4,36},{37,5},{6,38},{39,7},{8,40},{41... | collective-permute-start | bytes 196616 | tf_op jit(solution)/shard_map/ppermute | solution.py:389

commit v16 on v15

--- a/solution.py
+++ b/solution.py
@@ -38,8 +38,15 @@
     return jnp.maximum(colour, TINY), jnp.maximum(extinction * slab_share, TINY)
 
 
+def plane_kernel(core_ref, volume, outer, sem):
+    at = (volume.shape[0] - 1) * core_ref[0]
+    copy = pltpu.make_async_copy(volume.at[at], outer, sem.at[0])
+    copy.start()
+    copy.wait()
+
+
 def prepare_kernel(
-    core_ref, volume, table_hbm, rows_op, cols_op, tables, scales, outer, cells, table_ref, sems,
+    core_ref, volume, table_hbm, _, rows_op, cols_op, tables, scales, cells, table_ref, sems,
     *, slab_share, depth_total,
 ):
     slices = volume.shape[0]
@@ -65,7 +72,6 @@
         scales[at] = jnp.broadcast_to(value, (HALF, LANES))
     for copy in copies:
         copy.wait()
-    outer[...] = cells[(slices - 1) * core_ref[0]]
 
 
 def look_up(table, index):
@@ -333,7 +339,16 @@
 
     partner = [(d, d ^ 1) for d in range(depth_count)]
     entries = transfer_table.shape[1]
-    *ops, scales, outer, own = pl.pallas_call(
+    outer = pl.pallas_call(
+        plane_kernel,
+        out_shape=jax.ShapeDtypeStruct((rows, cols), BF16),
+        in_specs=[smem, hbm],
+        out_specs=vmem,
+        scratch_shapes=[pltpu.SemaphoreType.DMA((1,))],
+        compiler_params=params,
+        name="plane",
+    )(core_arg, in_hbm(volume))
+    *ops, scales, own = pl.pallas_call(
         functools.partial(
             prepare_kernel, slab_share=2.0 * slices / depth_total, depth_total=depth_total
         ),
@@ -342,18 +357,17 @@
             jax.ShapeDtypeStruct((cols, cols), BF16),
             jax.ShapeDtypeStruct((8, HALF, entries), F32),
             jax.ShapeDtypeStruct((3, HALF, LANES), F32),
-            jax.ShapeDtypeStruct((rows, cols), BF16),
             jax.ShapeDtypeStruct(volume.shape, BF16),
         ),
-        in_specs=[smem, hbm, hbm],
-        out_specs=(vmem,) * 6,
+        in_specs=[smem, hbm, hbm, vmem],
+        out_specs=(vmem,) * 5,
         scratch_shapes=[
             pltpu.VMEM(transfer_table.shape, BF16), pltpu.SemaphoreType.DMA((slices + 1,)),
         ],
         compiler_params=params,
         name="prepare",
     )(
-        core_arg, in_hbm(volume), in_hbm(transfer_table)
+        core_arg, in_hbm(volume), in_hbm(transfer_table), outer
     )
     outer = lax.ppermute(
         outer, "depth",

time: 53 us -> 52.5 us (level)
  blocking collectives: 24.6 us -> 23 us
  Pallas kernels: 20.5 us -> 21.5 us
    all_to_all x1, blocking collectives: 24.6 us -> 23 us  [shards(): lax.all_to_all(partial_image.astype(jnp.float16), 'depth', split_axis=0,...]
    pallas_call x0 -> x1, Pallas kernels: none -> 1.05 us  [shards(): pl.pallas_call(plane_kernel, out_shape=jax.ShapeDtypeStruct((rows, cols),...]
  transfers between devices with their start and end apart: 4 -> 4, of which waited for: 0 -> 0; matrix products, arithmetic and copies ran while one was open for 0% -> 0% of each run, Pallas kernels for 32% -> 34%
where the time goes in v16:
time: 52.5 us; the launch traced here: 52.3 us
  blocking collectives  23 us (44%)
  Pallas kernels  21.5 us (41%)
  starting transfers between devices  7.11 us (14%)
    all_to_all x1, blocking collectives, shards(): lax.all_to_all(partial_image.astype(jnp.float16), 'depth', split_axis=0,...  23 us
    pallas_call x2, Pallas kernels, slices_terms(): pl.pallas_call(slices_kernel, out_shape=terms, in_specs=[smem] + [vmem] *...  15.4 us
    ppermute x1, starting transfers between devices, shards(): lax.ppermute(edges, ('img', 'depth'), [(at * depth_count + d, to * depth_...  3.52 us
    ppermute x1, starting transfers between devices, shards(): relayed = lax.ppermute(relayed, 'depth', partner)  2.9 us
    pallas_call x1, Pallas kernels, shards(): pl.pallas_call(slab_kernel, out_shape=jax.ShapeDtypeStruct((blocks, 4 * B...  2.64 us
    pallas_call x1, Pallas kernels, shards(): pl.pallas_call(functools.partial(prepare_kernel, slab_share=2.0 * slices...  1.58 us
  transfers between devices with their start and end apart: 4, of which 0 were waited for; matrix products, arithmetic and copies ran while one was open for 0% of the time, Pallas kernels for 34%

profile of v16, /device:TPU:64, one launch (start us, length us, event | category | flops | bytes accessed | tf_op | source)
XLA Modules:
  0.0 52.3 jit_solution(2406267349700314215)
XLA Ops:
  0.0 0.0 collective-permute-start
  0.0 1.0 %plane.1._ = bf16[512,512]{1,0:T(8,128)(2,1)S(1)} custom-call(s32[1]{0:T(128)} %bitcast.core_ref, bf16[4,512,512]{2,1,0:T(8,128)(2,1)} %volume.3), custom_call_target="tpu_custom_call" | custom-call | tf_op jit(solution)/shard_map/plane/pallas_call | solution.py:342
  1.1 0.7 %collective-permute-start.1 = (bf16[512,512]{1,0:T(8,128)(2,1)S(1)}, bf16[512,512]{1,0:T(8,128)(2,1)S(1)}, u32[]{:S(2)}, u32[]{:S(2)}) collective-permute-start(bf16[512,512]{1,0:T(8,128)(2,1)S(1)} %plane.1._), channel_id=1, source_target_pairs={{1,2},{3,4},{5,6},{7,8},{9,10},{11,12},{13,14},{15,16},{17,18},{19... | collective-permute-start | bytes 1572872 | tf_op jit(solution)/shard_map/ppermute | solution.py:372
  1.8 1.6 %prepare.1 = (bf16[256,512]{1,0:T(8,128)(2,1)S(1)}, bf16[512,512]{1,0:T(8,128)(2,1)S(1)}, f32[8,8,128]{2,1,0:T(8,128)S(1)}, f32[3,8,128]{2,1,0:T(8,128)S(1)}, bf16[4,512,512]{2,1,0:T(8,128)(2,1)S(1)}) custom-call(s32[1]{0:T(128)} %bitcast.core_ref, bf16[4,512,512]{2,1,0:T(8,128)(2,1)} %volume.3, bf16[4,128]{1,0:T(4,128)(2,1)} %table_hbm.1, ...), custom_call_target="tpu_custom_call" | custom-call | tf_op jit(solution)/shard_map/prepare/pallas_call | solution.py:351
  3.3 7.7 %own.1 = (f32[4,256,512]{2,1,0:T(8,128)S(1)}, f32[4,256,512]{2,1,0:T(8,128)S(1)}, f32[4,256,512]{2,1,0:T(8,128)S(1)}, f32[2,256,512]{2,1,0:T(8,128)S(1)}, f32[2,...) custom-call(s32[1]{0:T(128)} %bitcast.core_ref, ...), custom_call_target="tpu_custom_call" | custom-call | tf_op jit(solution)/shard_map/own/pallas_call | solution.py:380
  11.0 0.0 collective-permute-done.1
  11.0 0.0 collective-permute-done
  11.1 2.9 %collective-permute-start.2 = (bf16[16,16,512]{2,1,0:T(8,128)(2,1)S(1)}, bf16[16,16,512]{2,1,0:T(8,128)(2,1)S(1)}, u32[]{:S(2)}, u32[]{:S(2)}) collective-permute-start(bf16[16,16,512]{2,1,0:T(8,128)(2,1)S(1)} %get-tuple-element.33.refs_0_), channel_id=1, source_target_pairs={{0,1},{1,0},{2,3},{3,2},{4,5},{5,4},{6,7},{7,6},{8,9},{9,8},{10,11... | collective-permute-start | bytes 786440 | tf_op jit(solution)/shard_map/ppermute | solution.py:402
  14.0 3.5 %collective-permute-start.3 = (bf16[8,8,512]{2,1,0:T(8,128)(2,1)S(1)}, bf16[8,8,512]{2,1,0:T(8,128)(2,1)S(1)}, u32[]{:S(2)}, u32[]{:S(2)}) collective-permute-start(bf16[8,8,512]{2,1,0:T(8,128)(2,1)S(1)} %get-tuple-element.34), channel_id=1, source_target_pairs={{0,32},{33,1},{2,34},{35,3},{4,36},{37,5},{6,38},{39,7},{8,40},{41... | collective-permute-start | bytes 196616 | tf_op jit(solution)/shard_map/ppermute | solution.py:403
  17.5 7.7 %other.1 = (f32[4,256,512]{2,1,0:T(8,128)S(1)}, f32[4,256,512]{2,1,0:T(8,128)S(1)}, f32[4,256,512]{2,1,0:T(8,128)S(1)}, f32[2,256,512]{2,1,0:T(8,128)S(1)}, f32[...) custom-call(s32[1]{0:T(128)} %bitcast.core_ref, ...), custom_call_target="tpu_custom_call" | custom-call | tf_op jit(solution)/shard_map/other/pallas_call | solution.py:380
  25.2 0.0 collective-permute-done.3.edges
  25.2 0.0 collective-permute-done.2.relayed
  25.2 2.6 %slab.1 = f32[16,64,512]{2,1,0:T(8,128)S(1)} custom-call(s32[1]{0:T(128)} %bitcast.core_ref, bf16[4,16,2,16,512]{4,3,2,1,0:T(8,128)(2,1)S(1)} %bitcast.6, bf16[4,16,2,16,512]{4,3,2,1,0:T(8,128)(2,1)S(1)} %bitcast.9, bf16[16,2,16,512]{3,2,1,0:T(8,128)(2,1)S(1)} %bitcast.11, bf16[16,16,512]{2,1,0:T(8,128)(2,1)S(1)} %collective-permute-done.2.relayed, ...), custom_call_target="tpu_custom_call" | custom-call | tf_op jit(solution)/shard_map/slab/pallas_call | solution.py:412
  27.9 0.3 convert_element_type.6
  28.1 23.0 %all_to_all.5 = f16[16,64,512]{2,1,0:T(8,128)(2,1)S(1)} all-to-all(f16[16,64,512]{2,1,0:T(8,128)(2,1)S(1)} %convert_element_type.6), channel_id=1, replica_groups={{0,2,4,6,8,10,12,14,16,18,20,22,24,26,28,30},{1,3,5,7,9,11,13,15,17,19,..., dimensions={0} | all-to-all | bytes 2097152 | tf_op jit(solution)/shard_map/all_to_all | solution.py:422
  51.1 0.3 convert_element_type.7.parts
  51.4 0.9 %merge.1 = f32[4,8192]{1,0:T(4,128)} custom-call(f32[16,64,512]{2,1,0:T(8,128)S(1)} %convert_element_type.7.parts, f32[3,8,128]{2,1,0:T(8,128)S(1)} %get-tuple-element.35.scales), custom_call_target="tpu_custom_call" | custom-call | tf_op jit(solution)/shard_map/merge/pallas_call | solution.py:426
  (1 shorter events, 0.0 us)
Async XLA Ops:
  0.0 11.0 %collective-permute-start = (bf16[4,512,512]{2,1,0:T(8,128)(2,1)}, bf16[4,512,512]{2,1,0:T(8,128)(2,1)S(1)}, u32[]{:S(2)}, u32[]{:S(2)}) collective-permute-start(bf16[4,512,512]{2,1,0:T(8,128)(2,1)} %volume.3), channel_id=1, source_target_pairs={{0,1},{1,0},{2,3},{3,2},{4,5},{5,4},{6,7},{7,6},{8,9},{9,8},{10,11... | collective-permute-start | bytes 6291464 | tf_op jit(solution)/shard_map/ppermute | solution.py:377
  1.1 10.0 %collective-permute-start.1 = (bf16[512,512]{1,0:T(8,128)(2,1)S(1)}, bf16[512,512]{1,0:T(8,128)(2,1)S(1)}, u32[]{:S(2)}, u32[]{:S(2)}) collective-permute-start(bf16[512,512]{1,0:T(8,128)(2,1)S(1)} %plane.1._), channel_id=1, source_target_pairs={{1,2},{3,4},{5,6},{7,8},{9,10},{11,12},{13,14},{15,16},{17,18},{19... | collective-permute-start | bytes 1572872 | tf_op jit(solution)/shard_map/ppermute | solution.py:372
  11.1 14.1 %collective-permute-start.2 = (bf16[16,16,512]{2,1,0:T(8,128)(2,1)S(1)}, bf16[16,16,512]{2,1,0:T(8,128)(2,1)S(1)}, u32[]{:S(2)}, u32[]{:S(2)}) collective-permute-start(bf16[16,16,512]{2,1,0:T(8,128)(2,1)S(1)} %get-tuple-element.33.refs_0_), channel_id=1, source_target_pairs={{0,1},{1,0},{2,3},{3,2},{4,5},{5,4},{6,7},{7,6},{8,9},{9,8},{10,11... | collective-permute-start | bytes 786440 | tf_op jit(solution)/shard_map/ppermute | solution.py:402
  14.0 11.2 %collective-permute-start.3 = (bf16[8,8,512]{2,1,0:T(8,128)(2,1)S(1)}, bf16[8,8,512]{2,1,0:T(8,128)(2,1)S(1)}, u32[]{:S(2)}, u32[]{:S(2)}) collective-permute-start(bf16[8,8,512]{2,1,0:T(8,128)(2,1)S(1)} %get-tuple-element.34), channel_id=1, source_target_pairs={{0,32},{33,1},{2,34},{35,3},{4,36},{37,5},{6,38},{39,7},{8,40},{41... | collective-permute-start | bytes 196616 | tf_op jit(solution)/shard_map/ppermute | solution.py:403

commit v17 on v16

--- a/solution.py
+++ b/solution.py
@@ -348,6 +348,8 @@
         compiler_params=params,
         name="plane",
     )(core_arg, in_hbm(volume))
+    held = lax.optimization_barrier((volume, outer))[0]
+    other = lax.ppermute(held, "depth", partner).reshape(split)
     *ops, scales, own = pl.pallas_call(
         functools.partial(
             prepare_kernel, slab_share=2.0 * slices / depth_total, depth_total=depth_total
@@ -374,7 +376,6 @@
         [(d, d + 1) for d in range(1, depth_count - 1, 2)]
         + [(d + 1, d) for d in range(1, depth_count - 1, 2)],
     ).reshape(split[1:])
-    other = lax.ppermute(volume, "depth", partner).reshape(split)
 
     def slices_terms(cells, previous, name):
         return pl.pallas_call(

time: 52.5 us -> 53.2 us (1.013)
  local copies, waits for them, and re-layouts: 0 us -> 0.54 us
    unnamed x0 -> x2, local copies, waits for them, and re-layouts: none -> 0.54 us
  transfers between devices with their start and end apart: 4 -> 4, of which waited for: 0 -> 0; matrix products, arithmetic and copies ran while one was open for 0% -> 0% of each run, Pallas kernels for 34% -> 32%
where the time goes in v17:
time: 53.2 us; the launch traced here: 53 us
  blocking collectives  23 us (43%)
  Pallas kernels  21.7 us (41%)
  starting transfers between devices  7.1 us (13%)
  local copies, waits for them, and re-layouts  0.54 us (1%)
    all_to_all x1, blocking collectives, shards(): lax.all_to_all(partial_image.astype(jnp.float16), 'depth', split_axis=0,...  23 us
    pallas_call x2, Pallas kernels, slices_terms(): pl.pallas_call(slices_kernel, out_shape=terms, in_specs=[smem] + [vmem] *...  15.4 us
    ppermute x1, starting transfers between devices, shards(): lax.ppermute(edges, ('img', 'depth'), [(at * depth_count + d, to * depth_...  3.52 us
    ppermute x1, starting transfers between devices, shards(): relayed = lax.ppermute(relayed, 'depth', partner)  2.9 us
    pallas_call x1, Pallas kernels, shards(): pl.pallas_call(slab_kernel, out_shape=jax.ShapeDtypeStruct((blocks, 4 * B...  2.64 us
    pallas_call x1, Pallas kernels, shards(): pl.pallas_call(functools.partial(prepare_kernel, slab_share=2.0 * slices...  1.58 us
    pallas_call x1, Pallas kernels, shards(): pl.pallas_call(plane_kernel, out_shape=jax.ShapeDtypeStruct((rows, cols),...  1.2 us
  transfers between devices with their start and end apart: 4, of which 0 were waited for; matrix products, arithmetic and copies ran while one was open for 0% of the time, Pallas kernels for 32%

profile of v17, /device:TPU:64, one launch (start us, length us, event | category | flops | bytes accessed | tf_op | source)
XLA Modules:
  0.0 53.0 jit_solution(12703164512820212511)
XLA Ops:
  0.0 0.0 copy-start
  0.0 1.2 %plane.1._ = bf16[512,512]{1,0:T(8,128)(2,1)S(1)} custom-call(s32[1]{0:T(128)} %bitcast.core_ref, bf16[4,512,512]{2,1,0:T(8,128)(2,1)} %volume.3), custom_call_target="tpu_custom_call" | custom-call | tf_op jit(solution)/shard_map/plane/pallas_call | solution.py:342
  1.2 0.5 %copy-done = bf16[4,512,512]{2,1,0:T(8,128)(2,1)S(1)} copy-done((bf16[4,512,512]{2,1,0:T(8,128)(2,1)S(1)}, bf16[4,512,512]{2,1,0:T(8,128)(2,1)}, u32[]{:S(2)}) %copy-start) | copy-done | bytes 2097176
  1.7 0.0 collective-permute-start
  1.8 0.7 %collective-permute-start.1 = (bf16[512,512]{1,0:T(8,128)(2,1)S(1)}, bf16[512,512]{1,0:T(8,128)(2,1)S(1)}, u32[]{:S(2)}, u32[]{:S(2)}) collective-permute-start(bf16[512,512]{1,0:T(8,128)(2,1)S(1)} %plane.1._), channel_id=1, source_target_pairs={{1,2},{3,4},{5,6},{7,8},{9,10},{11,12},{13,14},{15,16},{17,18},{19... | collective-permute-start | bytes 1572872 | tf_op jit(solution)/shard_map/ppermute | solution.py:374
  2.4 1.6 %prepare.1 = (bf16[256,512]{1,0:T(8,128)(2,1)S(1)}, bf16[512,512]{1,0:T(8,128)(2,1)S(1)}, f32[8,8,128]{2,1,0:T(8,128)S(1)}, f32[3,8,128]{2,1,0:T(8,128)S(1)}, bf16[4,512,512]{2,1,0:T(8,128)(2,1)S(1)}) custom-call(s32[1]{0:T(128)} %bitcast.core_ref, bf16[4,512,512]{2,1,0:T(8,128)(2,1)} %volume.3, bf16[4,128]{1,0:T(4,128)(2,1)} %table_hbm.1, ...), custom_call_target="tpu_custom_call" | custom-call | tf_op jit(solution)/shard_map/prepare/pallas_call | solution.py:353
  4.0 7.7 %own.1 = (f32[4,256,512]{2,1,0:T(8,128)S(1)}, f32[4,256,512]{2,1,0:T(8,128)S(1)}, f32[4,256,512]{2,1,0:T(8,128)S(1)}, f32[2,256,512]{2,1,0:T(8,128)S(1)}, f32[2,...) custom-call(s32[1]{0:T(128)} %bitcast.core_ref, ...), custom_call_target="tpu_custom_call" | custom-call | tf_op jit(solution)/shard_map/own/pallas_call | solution.py:381
  11.7 0.0 collective-permute-done.1
  11.7 0.0 collective-permute-done
  11.8 2.9 %collective-permute-start.2 = (bf16[16,16,512]{2,1,0:T(8,128)(2,1)S(1)}, bf16[16,16,512]{2,1,0:T(8,128)(2,1)S(1)}, u32[]{:S(2)}, u32[]{:S(2)}) collective-permute-start(bf16[16,16,512]{2,1,0:T(8,128)(2,1)S(1)} %get-tuple-element.35.refs_0_), channel_id=1, source_target_pairs={{0,1},{1,0},{2,3},{3,2},{4,5},{5,4},{6,7},{7,6},{8,9},{9,8},{10,11... | collective-permute-start | bytes 786440 | tf_op jit(solution)/shard_map/ppermute | solution.py:403
  14.7 3.5 %collective-permute-start.3 = (bf16[8,8,512]{2,1,0:T(8,128)(2,1)S(1)}, bf16[8,8,512]{2,1,0:T(8,128)(2,1)S(1)}, u32[]{:S(2)}, u32[]{:S(2)}) collective-permute-start(bf16[8,8,512]{2,1,0:T(8,128)(2,1)S(1)} %get-tuple-element.36), channel_id=1, source_target_pairs={{0,32},{33,1},{2,34},{35,3},{4,36},{37,5},{6,38},{39,7},{8,40},{41... | collective-permute-start | bytes 196616 | tf_op jit(solution)/shard_map/ppermute | solution.py:404
  18.2 7.7 %other.1 = (f32[4,256,512]{2,1,0:T(8,128)S(1)}, f32[4,256,512]{2,1,0:T(8,128)S(1)}, f32[4,256,512]{2,1,0:T(8,128)S(1)}, f32[2,256,512]{2,1,0:T(8,128)S(1)}, f32[...) custom-call(s32[1]{0:T(128)} %bitcast.core_ref, ...), custom_call_target="tpu_custom_call" | custom-call | tf_op jit(solution)/shard_map/other/pallas_call | solution.py:381
  25.9 0.0 collective-permute-done.3.edges
  25.9 0.0 collective-permute-done.2.relayed
  25.9 2.6 %slab.1 = f32[16,64,512]{2,1,0:T(8,128)S(1)} custom-call(s32[1]{0:T(128)} %bitcast.core_ref, bf16[4,16,2,16,512]{4,3,2,1,0:T(8,128)(2,1)S(1)} %bitcast.6, bf16[4,16,2,16,512]{4,3,2,1,0:T(8,128)(2,1)S(1)} %bitcast.9, bf16[16,2,16,512]{3,2,1,0:T(8,128)(2,1)S(1)} %bitcast.11, bf16[16,16,512]{2,1,0:T(8,128)(2,1)S(1)} %collective-permute-done.2.relayed, ...), custom_call_target="tpu_custom_call" | custom-call | tf_op jit(solution)/shard_map/slab/pallas_call | solution.py:413
  28.6 0.3 convert_element_type.6
  28.8 23.0 %all_to_all.5 = f16[16,64,512]{2,1,0:T(8,128)(2,1)S(1)} all-to-all(f16[16,64,512]{2,1,0:T(8,128)(2,1)S(1)} %convert_element_type.6), channel_id=1, replica_groups={{0,2,4,6,8,10,12,14,16,18,20,22,24,26,28,30},{1,3,5,7,9,11,13,15,17,19,..., dimensions={0} | all-to-all | bytes 2097152 | tf_op jit(solution)/shard_map/all_to_all | solution.py:423
  51.8 0.3 convert_element_type.7.parts
  52.1 0.9 %merge.1 = f32[4,8192]{1,0:T(4,128)} custom-call(f32[16,64,512]{2,1,0:T(8,128)S(1)} %convert_element_type.7.parts, f32[3,8,128]{2,1,0:T(8,128)S(1)} %get-tuple-element.37.scales), custom_call_target="tpu_custom_call" | custom-call | tf_op jit(solution)/shard_map/merge/pallas_call | solution.py:427
  (1 shorter events, 0.0 us)
Async XLA Ops:
  0.0 1.7 %copy-start = (bf16[4,512,512]{2,1,0:T(8,128)(2,1)S(1)}, bf16[4,512,512]{2,1,0:T(8,128)(2,1)}, u32[]{:S(2)}) copy-start(bf16[4,512,512]{2,1,0:T(8,128)(2,1)} %volume.3) | copy-start | bytes 6291460
  1.7 10.0 %collective-permute-start = (bf16[4,512,512]{2,1,0:T(8,128)(2,1)S(1)}, bf16[4,512,512]{2,1,0:T(8,128)(2,1)S(1)}, u32[]{:S(2)}, u32[]{:S(2)}) collective-permute-start(bf16[4,512,512]{2,1,0:T(8,128)(2,1)S(1)} %copy-done), channel_id=1, source_target_pairs={{0,1},{1,0},{2,3},{3,2},{4,5},{5,4},{6,7},{7,6},{8,9},{9,8},{10,11... | collective-permute-start | bytes 6291464 | tf_op jit(solution)/shard_map/ppermute | solution.py:352
  1.8 10.0 %collective-permute-start.1 = (bf16[512,512]{1,0:T(8,128)(2,1)S(1)}, bf16[512,512]{1,0:T(8,128)(2,1)S(1)}, u32[]{:S(2)}, u32[]{:S(2)}) collective-permute-start(bf16[512,512]{1,0:T(8,128)(2,1)S(1)} %plane.1._), channel_id=1, source_target_pairs={{1,2},{3,4},{5,6},{7,8},{9,10},{11,12},{13,14},{15,16},{17,18},{19... | collective-permute-start | bytes 1572872 | tf_op jit(solution)/shard_map/ppermute | solution.py:374
  11.8 14.1 %collective-permute-start.2 = (bf16[16,16,512]{2,1,0:T(8,128)(2,1)S(1)}, bf16[16,16,512]{2,1,0:T(8,128)(2,1)S(1)}, u32[]{:S(2)}, u32[]{:S(2)}) collective-permute-start(bf16[16,16,512]{2,1,0:T(8,128)(2,1)S(1)} %get-tuple-element.35.refs_0_), channel_id=1, source_target_pairs={{0,1},{1,0},{2,3},{3,2},{4,5},{5,4},{6,7},{7,6},{8,9},{9,8},{10,11... | collective-permute-start | bytes 786440 | tf_op jit(solution)/shard_map/ppermute | solution.py:403
  14.7 11.2 %collective-permute-start.3 = (bf16[8,8,512]{2,1,0:T(8,128)(2,1)S(1)}, bf16[8,8,512]{2,1,0:T(8,128)(2,1)S(1)}, u32[]{:S(2)}, u32[]{:S(2)}) collective-permute-start(bf16[8,8,512]{2,1,0:T(8,128)(2,1)S(1)} %get-tuple-element.36), channel_id=1, source_target_pairs={{0,32},{33,1},{2,34},{35,3},{4,36},{37,5},{6,38},{39,7},{8,40},{41... | collective-permute-start | bytes 196616 | tf_op jit(solution)/shard_map/ppermute | solution.py:404

commit v18 on v16

--- a/solution.py
+++ b/solution.py
@@ -13,6 +13,7 @@
 BLOCK = 16
 HALF = 8
 LANES = 128
+PARTS = 4
 TINY = 1e-30
 SLOPE = 1.4 / 3.0
 
@@ -38,11 +39,20 @@
     return jnp.maximum(colour, TINY), jnp.maximum(extinction * slab_share, TINY)
 
 
-def plane_kernel(core_ref, volume, outer, sem):
+def plane_kernel(core_ref, volume, outer, sems):
     at = (volume.shape[0] - 1) * core_ref[0]
-    copy = pltpu.make_async_copy(volume.at[at], outer, sem.at[0])
-    copy.start()
-    copy.wait()
+    parts = sems.shape[0]
+    size = outer.shape[0] // parts
+    copies = [
+        pltpu.make_async_copy(
+            volume.at[at, pl.ds(p * size, size)], outer.at[pl.ds(p * size, size)], sems.at[p]
+        )
+        for p in range(parts)
+    ]
+    for copy in copies:
+        copy.start()
+    for copy in copies:
+        copy.wait()
 
 
 def prepare_kernel(
@@ -50,8 +60,17 @@
     *, slab_share, depth_total,
 ):
     slices = volume.shape[0]
-    table_copy = pltpu.make_async_copy(table_hbm, table_ref, sems.at[slices])
-    copies = [pltpu.make_async_copy(volume.at[z], cells.at[z], sems.at[z]) for z in range(slices)]
+    table_copy = pltpu.make_async_copy(table_hbm, table_ref, sems.at[slices * PARTS])
+    size = volume.shape[1] // PARTS
+    copies = [
+        pltpu.make_async_copy(
+            volume.at[z, pl.ds(p * size, size)],
+            cells.at[z, pl.ds(p * size, size)],
+            sems.at[z * PARTS + p],
+        )
+        for z in range(slices)
+        for p in range(PARTS)
+    ]
     table_copy.start()
     for copy in copies:
         copy.start()
@@ -344,7 +363,7 @@
         out_shape=jax.ShapeDtypeStruct((rows, cols), BF16),
         in_specs=[smem, hbm],
         out_specs=vmem,
-        scratch_shapes=[pltpu.SemaphoreType.DMA((1,))],
+        scratch_shapes=[pltpu.SemaphoreType.DMA((2 * PARTS,))],
         compiler_params=params,
         name="plane",
     )(core_arg, in_hbm(volume))
@@ -362,7 +381,7 @@
         in_specs=[smem, hbm, hbm, vmem],
         out_specs=(vmem,) * 5,
         scratch_shapes=[
-            pltpu.VMEM(transfer_table.shape, BF16), pltpu.SemaphoreType.DMA((slices + 1,)),
+            pltpu.VMEM(transfer_table.shape, BF16), pltpu.SemaphoreType.DMA((slices * PARTS + 1,)),
         ],
         compiler_params=params,
         name="prepare",

time: 52.5 us -> 52.6 us (level)
  transfers between devices with their start and end apart: 4 -> 4, of which waited for: 0 -> 0; matrix products, arithmetic and copies ran while one was open for 0% -> 0% of each run, Pallas kernels for 34% -> 35%
where the time goes in v18:
time: 52.6 us; the launch traced here: 52.4 us
  blocking collectives  22.8 us (43%)
  Pallas kernels  21.8 us (41%)
  starting transfers between devices  7.11 us (14%)
    all_to_all x1, blocking collectives, shards(): lax.all_to_all(partial_image.astype(jnp.float16), 'depth', split_axis=0,...  22.8 us
    pallas_call x2, Pallas kernels, slices_terms(): pl.pallas_call(slices_kernel, out_shape=terms, in_specs=[smem] + [vmem] *...  15.4 us
    ppermute x1, starting transfers between devices, shards(): lax.ppermute(edges, ('img', 'depth'), [(at * depth_count + d, to * depth_...  3.52 us
    ppermute x1, starting transfers between devices, shards(): relayed = lax.ppermute(relayed, 'depth', partner)  2.9 us
    pallas_call x1, Pallas kernels, shards(): pl.pallas_call(slab_kernel, out_shape=jax.ShapeDtypeStruct((blocks, 4 * B...  2.64 us
    pallas_call x1, Pallas kernels, shards(): pl.pallas_call(functools.partial(prepare_kernel, slab_share=2.0 * slices...  1.76 us
    pallas_call x1, Pallas kernels, shards(): pl.pallas_call(plane_kernel, out_shape=jax.ShapeDtypeStruct((rows, cols),...  1.13 us
  transfers between devices with their start and end apart: 4, of which 0 were waited for; matrix products, arithmetic and copies ran while one was open for 0% of the time, Pallas kernels for 35%

profile of v18, /device:TPU:64, one launch (start us, length us, event | category | flops | bytes accessed | tf_op | source)
XLA Modules:
  0.0 52.4 jit_solution(13094340770540711566)
XLA Ops:
  0.0 0.0 collective-permute-start
  0.0 1.1 %plane.1._ = bf16[512,512]{1,0:T(8,128)(2,1)S(1)} custom-call(s32[1]{0:T(128)} %bitcast.core_ref, bf16[4,512,512]{2,1,0:T(8,128)(2,1)} %volume.3), custom_call_target="tpu_custom_call" | custom-call | tf_op jit(solution)/shard_map/plane/pallas_call | solution.py:361
  1.1 0.7 %collective-permute-start.1 = (bf16[512,512]{1,0:T(8,128)(2,1)S(1)}, bf16[512,512]{1,0:T(8,128)(2,1)S(1)}, u32[]{:S(2)}, u32[]{:S(2)}) collective-permute-start(bf16[512,512]{1,0:T(8,128)(2,1)S(1)} %plane.1._), channel_id=1, source_target_pairs={{1,2},{3,4},{5,6},{7,8},{9,10},{11,12},{13,14},{15,16},{17,18},{19... | collective-permute-start | bytes 1572872 | tf_op jit(solution)/shard_map/ppermute | solution.py:391
  1.8 1.8 %prepare.1 = (bf16[256,512]{1,0:T(8,128)(2,1)S(1)}, bf16[512,512]{1,0:T(8,128)(2,1)S(1)}, f32[8,8,128]{2,1,0:T(8,128)S(1)}, f32[3,8,128]{2,1,0:T(8,128)S(1)}, bf16[4,512,512]{2,1,0:T(8,128)(2,1)S(1)}) custom-call(s32[1]{0:T(128)} %bitcast.core_ref, bf16[4,512,512]{2,1,0:T(8,128)(2,1)} %volume.3, bf16[4,128]{1,0:T(4,128)(2,1)} %table_hbm.1, ...), custom_call_target="tpu_custom_call" | custom-call | tf_op jit(solution)/shard_map/prepare/pallas_call | solution.py:370
  3.6 7.7 %own.1 = (f32[4,256,512]{2,1,0:T(8,128)S(1)}, f32[4,256,512]{2,1,0:T(8,128)S(1)}, f32[4,256,512]{2,1,0:T(8,128)S(1)}, f32[2,256,512]{2,1,0:T(8,128)S(1)}, f32[2,...) custom-call(s32[1]{0:T(128)} %bitcast.core_ref, ...), custom_call_target="tpu_custom_call" | custom-call | tf_op jit(solution)/shard_map/own/pallas_call | solution.py:399
  11.3 0.0 collective-permute-done.1
  11.3 0.0 collective-permute-done
  11.4 2.9 %collective-permute-start.2 = (bf16[16,16,512]{2,1,0:T(8,128)(2,1)S(1)}, bf16[16,16,512]{2,1,0:T(8,128)(2,1)S(1)}, u32[]{:S(2)}, u32[]{:S(2)}) collective-permute-start(bf16[16,16,512]{2,1,0:T(8,128)(2,1)S(1)} %get-tuple-element.33.refs_0_), channel_id=1, source_target_pairs={{0,1},{1,0},{2,3},{3,2},{4,5},{5,4},{6,7},{7,6},{8,9},{9,8},{10,11... | collective-permute-start | bytes 786440 | tf_op jit(solution)/shard_map/ppermute | solution.py:421
  14.3 3.5 %collective-permute-start.3 = (bf16[8,8,512]{2,1,0:T(8,128)(2,1)S(1)}, bf16[8,8,512]{2,1,0:T(8,128)(2,1)S(1)}, u32[]{:S(2)}, u32[]{:S(2)}) collective-permute-start(bf16[8,8,512]{2,1,0:T(8,128)(2,1)S(1)} %get-tuple-element.34), channel_id=1, source_target_pairs={{0,32},{33,1},{2,34},{35,3},{4,36},{37,5},{6,38},{39,7},{8,40},{41... | collective-permute-start | bytes 196616 | tf_op jit(solution)/shard_map/ppermute | solution.py:422
  17.8 7.7 %other.1 = (f32[4,256,512]{2,1,0:T(8,128)S(1)}, f32[4,256,512]{2,1,0:T(8,128)S(1)}, f32[4,256,512]{2,1,0:T(8,128)S(1)}, f32[2,256,512]{2,1,0:T(8,128)S(1)}, f32[...) custom-call(s32[1]{0:T(128)} %bitcast.core_ref, ...), custom_call_target="tpu_custom_call" | custom-call | tf_op jit(solution)/shard_map/other/pallas_call | solution.py:399
  25.5 0.0 collective-permute-done.3.edges
  25.5 0.0 collective-permute-done.2.relayed
  25.5 2.6 %slab.1 = f32[16,64,512]{2,1,0:T(8,128)S(1)} custom-call(s32[1]{0:T(128)} %bitcast.core_ref, bf16[4,16,2,16,512]{4,3,2,1,0:T(8,128)(2,1)S(1)} %bitcast.6, bf16[4,16,2,16,512]{4,3,2,1,0:T(8,128)(2,1)S(1)} %bitcast.9, bf16[16,2,16,512]{3,2,1,0:T(8,128)(2,1)S(1)} %bitcast.11, bf16[16,16,512]{2,1,0:T(8,128)(2,1)S(1)} %collective-permute-done.2.relayed, ...), custom_call_target="tpu_custom_call" | custom-call | tf_op jit(solution)/shard_map/slab/pallas_call | solution.py:431
  28.1 0.3 convert_element_type.6
  28.4 22.8 %all_to_all.5 = f16[16,64,512]{2,1,0:T(8,128)(2,1)S(1)} all-to-all(f16[16,64,512]{2,1,0:T(8,128)(2,1)S(1)} %convert_element_type.6), channel_id=1, replica_groups={{0,2,4,6,8,10,12,14,16,18,20,22,24,26,28,30},{1,3,5,7,9,11,13,15,17,19,..., dimensions={0} | all-to-all | bytes 2097152 | tf_op jit(solution)/shard_map/all_to_all | solution.py:441
  51.2 0.3 convert_element_type.7.parts
  51.5 0.9 %merge.1 = f32[4,8192]{1,0:T(4,128)} custom-call(f32[16,64,512]{2,1,0:T(8,128)S(1)} %convert_element_type.7.parts, f32[3,8,128]{2,1,0:T(8,128)S(1)} %get-tuple-element.35.scales), custom_call_target="tpu_custom_call" | custom-call | tf_op jit(solution)/shard_map/merge/pallas_call | solution.py:445
  (1 shorter events, 0.0 us)
Async XLA Ops:
  0.0 11.3 %collective-permute-start = (bf16[4,512,512]{2,1,0:T(8,128)(2,1)}, bf16[4,512,512]{2,1,0:T(8,128)(2,1)S(1)}, u32[]{:S(2)}, u32[]{:S(2)}) collective-permute-start(bf16[4,512,512]{2,1,0:T(8,128)(2,1)} %volume.3), channel_id=1, source_target_pairs={{0,1},{1,0},{2,3},{3,2},{4,5},{5,4},{6,7},{7,6},{8,9},{9,8},{10,11... | collective-permute-start | bytes 6291464 | tf_op jit(solution)/shard_map/ppermute | solution.py:396
  1.1 10.2 %collective-permute-start.1 = (bf16[512,512]{1,0:T(8,128)(2,1)S(1)}, bf16[512,512]{1,0:T(8,128)(2,1)S(1)}, u32[]{:S(2)}, u32[]{:S(2)}) collective-permute-start(bf16[512,512]{1,0:T(8,128)(2,1)S(1)} %plane.1._), channel_id=1, source_target_pairs={{1,2},{3,4},{5,6},{7,8},{9,10},{11,12},{13,14},{15,16},{17,18},{19... | collective-permute-start | bytes 1572872 | tf_op jit(solution)/shard_map/ppermute | solution.py:391
  11.4 14.1 %collective-permute-start.2 = (bf16[16,16,512]{2,1,0:T(8,128)(2,1)S(1)}, bf16[16,16,512]{2,1,0:T(8,128)(2,1)S(1)}, u32[]{:S(2)}, u32[]{:S(2)}) collective-permute-start(bf16[16,16,512]{2,1,0:T(8,128)(2,1)S(1)} %get-tuple-element.33.refs_0_), channel_id=1, source_target_pairs={{0,1},{1,0},{2,3},{3,2},{4,5},{5,4},{6,7},{7,6},{8,9},{9,8},{10,11... | collective-permute-start | bytes 786440 | tf_op jit(solution)/shard_map/ppermute | solution.py:421
  14.3 11.2 %collective-permute-start.3 = (bf16[8,8,512]{2,1,0:T(8,128)(2,1)S(1)}, bf16[8,8,512]{2,1,0:T(8,128)(2,1)S(1)}, u32[]{:S(2)}, u32[]{:S(2)}) collective-permute-start(bf16[8,8,512]{2,1,0:T(8,128)(2,1)S(1)} %get-tuple-element.34), channel_id=1, source_target_pairs={{0,32},{33,1},{2,34},{35,3},{4,36},{37,5},{6,38},{39,7},{8,40},{41... | collective-permute-start | bytes 196616 | tf_op jit(solution)/shard_map/ppermute | solution.py:422

commit v19 on v16

--- a/solution.py
+++ b/solution.py
@@ -178,10 +178,13 @@
     each_block(blocks, 4, block)
 
 
-def relay_kernel(core_ref, own, other, outer, relayed, edge):
+def relay_kernel(core_ref, outer, relayed):
+    relayed[...] = outer[:, 1 - core_ref[0]]
+
+
+def edge_kernel(core_ref, own, other, _, edge):
     slices, blocks, _, _, _ = own.shape
     core = core_ref[0]
-    relayed[...] = outer[:, 1 - core]
 
     @pl.when(core == 0)
     def _():
@@ -389,15 +392,23 @@
 
     own = own.reshape(split)
     own_terms = slices_terms(own, (), "own")
-    outer, _ = lax.optimization_barrier((outer, own_terms[6]))
-    relayed, edges = pl.pallas_call(
+    edges = pl.pallas_call(
+        edge_kernel,
+        out_shape=edge,
+        in_specs=[smem] + [vmem] * 3,
+        out_specs=vmem,
+        compiler_params=params,
+        name="edge",
+    )(core_arg, own, other, own_terms[6])
+    outer, _ = lax.optimization_barrier((outer, edges))
+    relayed = pl.pallas_call(
         relay_kernel,
-        out_shape=(plane, edge),
-        in_specs=[smem] + [vmem] * 3,
-        out_specs=(vmem, vmem),
+        out_shape=plane,
+        in_specs=[smem, vmem],
+        out_specs=vmem,
         compiler_params=params,
         name="relay",
-    )(core_arg, own, other, outer)
+    )(core_arg, outer)
     other_terms = slices_terms(other, (relayed,), "other")
     relayed = lax.ppermute(relayed, "depth", partner)
     edges = lax.ppermute(

time: 52.5 us -> 52.4 us (level)
  transfers between devices with their start and end apart: 4 -> 4, of which waited for: 0 -> 0; matrix products, arithmetic and copies ran while one was open for 0% -> 0% of each run, Pallas kernels for 34% -> 35%
where the time goes in v19:
time: 52.4 us; the launch traced here: 52.1 us
  blocking collectives  22.9 us (44%)
  Pallas kernels  21.5 us (41%)
  starting transfers between devices  7.12 us (14%)
    all_to_all x1, blocking collectives, shards(): lax.all_to_all(partial_image.astype(jnp.float16), 'depth', split_axis=0,...  22.9 us
    pallas_call x2, Pallas kernels, slices_terms(): pl.pallas_call(slices_kernel, out_shape=terms, in_specs=[smem] + [vmem] *...  15.5 us
    ppermute x1, starting transfers between devices, shards(): lax.ppermute(edges, ('img', 'depth'), [(at * depth_count + d, to * depth_...  3.52 us
    ppermute x1, starting transfers between devices, shards(): relayed = lax.ppermute(relayed, 'depth', partner)  2.9 us
    pallas_call x1, Pallas kernels, shards(): pl.pallas_call(slab_kernel, out_shape=jax.ShapeDtypeStruct((blocks, 4 * B...  2.47 us
    pallas_call x1, Pallas kernels, shards(): pl.pallas_call(functools.partial(prepare_kernel, slab_share=2.0 * slices...  1.58 us
    pallas_call x1, Pallas kernels, shards(): pl.pallas_call(plane_kernel, out_shape=jax.ShapeDtypeStruct((rows, cols),...  1.05 us
  transfers between devices with their start and end apart: 4, of which 0 were waited for; matrix products, arithmetic and copies ran while one was open for 0% of the time, Pallas kernels for 35%

profile of v19, /device:TPU:64, one launch (start us, length us, event | category | flops | bytes accessed | tf_op | source)
XLA Modules:
  0.0 52.1 jit_solution(10032979322938031379)
XLA Ops:
  0.0 0.0 collective-permute-start
  0.0 1.0 %plane.1._ = bf16[512,512]{1,0:T(8,128)(2,1)S(1)} custom-call(s32[1]{0:T(128)} %bitcast.core_ref, bf16[4,512,512]{2,1,0:T(8,128)(2,1)} %volume.3), custom_call_target="tpu_custom_call" | custom-call | tf_op jit(solution)/shard_map/plane/pallas_call | solution.py:345
  1.1 0.7 %collective-permute-start.1 = (bf16[512,512]{1,0:T(8,128)(2,1)S(1)}, bf16[512,512]{1,0:T(8,128)(2,1)S(1)}, u32[]{:S(2)}, u32[]{:S(2)}) collective-permute-start(bf16[512,512]{1,0:T(8,128)(2,1)S(1)} %plane.1._), channel_id=1, source_target_pairs={{1,2},{3,4},{5,6},{7,8},{9,10},{11,12},{13,14},{15,16},{17,18},{19... | collective-permute-start | bytes 1572872 | tf_op jit(solution)/shard_map/ppermute | solution.py:375
  1.8 1.6 %prepare.1 = (bf16[256,512]{1,0:T(8,128)(2,1)S(1)}, bf16[512,512]{1,0:T(8,128)(2,1)S(1)}, f32[8,8,128]{2,1,0:T(8,128)S(1)}, f32[3,8,128]{2,1,0:T(8,128)S(1)}, bf16[4,512,512]{2,1,0:T(8,128)(2,1)S(1)}) custom-call(s32[1]{0:T(128)} %bitcast.core_ref, bf16[4,512,512]{2,1,0:T(8,128)(2,1)} %volume.3, bf16[4,128]{1,0:T(4,128)(2,1)} %table_hbm.1, ...), custom_call_target="tpu_custom_call" | custom-call | tf_op jit(solution)/shard_map/prepare/pallas_call | solution.py:354
  3.3 7.7 %own.1 = (f32[4,256,512]{2,1,0:T(8,128)S(1)}, f32[4,256,512]{2,1,0:T(8,128)S(1)}, f32[4,256,512]{2,1,0:T(8,128)S(1)}, f32[2,256,512]{2,1,0:T(8,128)S(1)}, f32[2,...) custom-call(s32[1]{0:T(128)} %bitcast.core_ref, ...), custom_call_target="tpu_custom_call" | custom-call | tf_op jit(solution)/shard_map/own/pallas_call | solution.py:383
  11.1 0.0 collective-permute-done
  11.1 0.0 collective-permute-done.1
  11.2 2.9 %collective-permute-start.2 = (bf16[16,16,512]{2,1,0:T(8,128)(2,1)S(1)}, bf16[16,16,512]{2,1,0:T(8,128)(2,1)S(1)}, u32[]{:S(2)}, u32[]{:S(2)}) collective-permute-start(bf16[16,16,512]{2,1,0:T(8,128)(2,1)S(1)} %relay.1.refs_0_), channel_id=1, source_target_pairs={{0,1},{1,0},{2,3},{3,2},{4,5},{5,4},{6,7},{7,6},{8,9},{9,8},{10,11... | collective-permute-start | bytes 786440 | tf_op jit(solution)/shard_map/ppermute | solution.py:413
  14.1 3.5 %collective-permute-start.3 = (bf16[8,8,512]{2,1,0:T(8,128)(2,1)S(1)}, bf16[8,8,512]{2,1,0:T(8,128)(2,1)S(1)}, u32[]{:S(2)}, u32[]{:S(2)}) collective-permute-start(bf16[8,8,512]{2,1,0:T(8,128)(2,1)S(1)} %edge.1), channel_id=1, source_target_pairs={{0,32},{33,1},{2,34},{35,3},{4,36},{37,5},{6,38},{39,7},{8,40},{41... | collective-permute-start | bytes 196616 | tf_op jit(solution)/shard_map/ppermute | solution.py:414
  17.6 7.7 %other.1 = (f32[4,256,512]{2,1,0:T(8,128)S(1)}, f32[4,256,512]{2,1,0:T(8,128)S(1)}, f32[4,256,512]{2,1,0:T(8,128)S(1)}, f32[2,256,512]{2,1,0:T(8,128)S(1)}, f32[...) custom-call(s32[1]{0:T(128)} %bitcast.core_ref, ...), custom_call_target="tpu_custom_call" | custom-call | tf_op jit(solution)/shard_map/other/pallas_call | solution.py:383
  25.3 0.0 collective-permute-done.3.edges
  25.3 0.0 collective-permute-done.2.relayed
  25.3 2.5 %slab.1 = f32[16,64,512]{2,1,0:T(8,128)S(1)} custom-call(s32[1]{0:T(128)} %bitcast.core_ref, bf16[4,16,2,16,512]{4,3,2,1,0:T(8,128)(2,1)S(1)} %bitcast.9, bf16[4,16,2,16,512]{4,3,2,1,0:T(8,128)(2,1)S(1)} %bitcast.6, bf16[16,2,16,512]{3,2,1,0:T(8,128)(2,1)S(1)} %bitcast.11, bf16[16,16,512]{2,1,0:T(8,128)(2,1)S(1)} %collective-permute-done.2.relayed, ...), custom_call_target="tpu_custom_call" | custom-call | tf_op jit(solution)/shard_map/slab/pallas_call | solution.py:423
  27.8 0.3 convert_element_type.6
  28.1 22.9 %all_to_all.5 = f16[16,64,512]{2,1,0:T(8,128)(2,1)S(1)} all-to-all(f16[16,64,512]{2,1,0:T(8,128)(2,1)S(1)} %convert_element_type.6), channel_id=1, replica_groups={{0,2,4,6,8,10,12,14,16,18,20,22,24,26,28,30},{1,3,5,7,9,11,13,15,17,19,..., dimensions={0} | all-to-all | bytes 2097152 | tf_op jit(solution)/shard_map/all_to_all | solution.py:433
  51.0 0.3 convert_element_type.7.parts
  51.3 0.9 %merge.1 = f32[4,8192]{1,0:T(4,128)} custom-call(f32[16,64,512]{2,1,0:T(8,128)S(1)} %convert_element_type.7.parts, f32[3,8,128]{2,1,0:T(8,128)S(1)} %get-tuple-element.31.scales), custom_call_target="tpu_custom_call" | custom-call | tf_op jit(solution)/shard_map/merge/pallas_call | solution.py:437
  (2 shorter events, 0.0 us)
Async XLA Ops:
  0.0 11.1 %collective-permute-start = (bf16[4,512,512]{2,1,0:T(8,128)(2,1)}, bf16[4,512,512]{2,1,0:T(8,128)(2,1)S(1)}, u32[]{:S(2)}, u32[]{:S(2)}) collective-permute-start(bf16[4,512,512]{2,1,0:T(8,128)(2,1)} %volume.3), channel_id=1, source_target_pairs={{0,1},{1,0},{2,3},{3,2},{4,5},{5,4},{6,7},{7,6},{8,9},{9,8},{10,11... | collective-permute-start | bytes 6291464 | tf_op jit(solution)/shard_map/ppermute | solution.py:380
  1.1 10.1 %collective-permute-start.1 = (bf16[512,512]{1,0:T(8,128)(2,1)S(1)}, bf16[512,512]{1,0:T(8,128)(2,1)S(1)}, u32[]{:S(2)}, u32[]{:S(2)}) collective-permute-start(bf16[512,512]{1,0:T(8,128)(2,1)S(1)} %plane.1._), channel_id=1, source_target_pairs={{1,2},{3,4},{5,6},{7,8},{9,10},{11,12},{13,14},{15,16},{17,18},{19... | collective-permute-start | bytes 1572872 | tf_op jit(solution)/shard_map/ppermute | solution.py:375
  11.2 14.2 %collective-permute-start.2 = (bf16[16,16,512]{2,1,0:T(8,128)(2,1)S(1)}, bf16[16,16,512]{2,1,0:T(8,128)(2,1)S(1)}, u32[]{:S(2)}, u32[]{:S(2)}) collective-permute-start(bf16[16,16,512]{2,1,0:T(8,128)(2,1)S(1)} %relay.1.refs_0_), channel_id=1, source_target_pairs={{0,1},{1,0},{2,3},{3,2},{4,5},{5,4},{6,7},{7,6},{8,9},{9,8},{10,11... | collective-permute-start | bytes 786440 | tf_op jit(solution)/shard_map/ppermute | solution.py:413
  14.1 11.3 %collective-permute-start.3 = (bf16[8,8,512]{2,1,0:T(8,128)(2,1)S(1)}, bf16[8,8,512]{2,1,0:T(8,128)(2,1)S(1)}, u32[]{:S(2)}, u32[]{:S(2)}) collective-permute-start(bf16[8,8,512]{2,1,0:T(8,128)(2,1)S(1)} %edge.1), channel_id=1, source_target_pairs={{0,32},{33,1},{2,34},{35,3},{4,36},{37,5},{6,38},{39,7},{8,40},{41... | collective-permute-start | bytes 196616 | tf_op jit(solution)/shard_map/ppermute | solution.py:414

commit v20 on v16

--- a/solution.py
+++ b/solution.py
@@ -175,7 +175,7 @@
             for c, value in enumerate(accum + [transmit]):
                 middle[c, here, lanes] = value
 
-    each_block(blocks, 4, block)
+    each_block(blocks, 8, block)
 
 
 def relay_kernel(core_ref, own, other, outer, relayed, edge):

time: 52.5 us -> 52.4 us (level)
  no operation moved by 1% of the time
where the time goes in v20:
time: 52.4 us; the launch traced here: 52.1 us
  blocking collectives  23.2 us (44%)
  Pallas kernels  21.2 us (40%)
  starting transfers between devices  7.11 us (14%)
    all_to_all x1, blocking collectives, shards(): lax.all_to_all(partial_image.astype(jnp.float16), 'depth', split_axis=0,...  23.2 us
    pallas_call x2, Pallas kernels, slices_terms(): pl.pallas_call(slices_kernel, out_shape=terms, in_specs=[smem] + [vmem] *...  15 us
    ppermute x1, starting transfers between devices, shards(): lax.ppermute(edges, ('img', 'depth'), [(at * depth_count + d, to * depth_...  3.52 us
    ppermute x1, starting transfers between devices, shards(): relayed = lax.ppermute(relayed, 'depth', partner)  2.9 us
    pallas_call x1, Pallas kernels, shards(): pl.pallas_call(slab_kernel, out_shape=jax.ShapeDtypeStruct((blocks, 4 * B...  2.64 us
    pallas_call x1, Pallas kernels, shards(): pl.pallas_call(functools.partial(prepare_kernel, slab_share=2.0 * slices...  1.58 us
    pallas_call x1, Pallas kernels, shards(): pl.pallas_call(plane_kernel, out_shape=jax.ShapeDtypeStruct((rows, cols),...  1.05 us
  transfers between devices with their start and end apart: 4, of which 0 were waited for; matrix products, arithmetic and copies ran while one was open for 0% of the time, Pallas kernels for 34%

profile of v20, /device:TPU:64, one launch (start us, length us, event | category | flops | bytes accessed | tf_op | source)
XLA Modules:
  0.0 52.1 jit_solution(12264780606180538220)
XLA Ops:
  0.0 0.0 collective-permute-start
  0.0 1.0 %plane.1._ = bf16[512,512]{1,0:T(8,128)(2,1)S(1)} custom-call(s32[1]{0:T(128)} %bitcast.core_ref, bf16[4,512,512]{2,1,0:T(8,128)(2,1)} %volume.3), custom_call_target="tpu_custom_call" | custom-call | tf_op jit(solution)/shard_map/plane/pallas_call | solution.py:342
  1.1 0.7 %collective-permute-start.1 = (bf16[512,512]{1,0:T(8,128)(2,1)S(1)}, bf16[512,512]{1,0:T(8,128)(2,1)S(1)}, u32[]{:S(2)}, u32[]{:S(2)}) collective-permute-start(bf16[512,512]{1,0:T(8,128)(2,1)S(1)} %plane.1._), channel_id=1, source_target_pairs={{1,2},{3,4},{5,6},{7,8},{9,10},{11,12},{13,14},{15,16},{17,18},{19... | collective-permute-start | bytes 1572872 | tf_op jit(solution)/shard_map/ppermute | solution.py:372
  1.8 1.6 %prepare.1 = (bf16[256,512]{1,0:T(8,128)(2,1)S(1)}, bf16[512,512]{1,0:T(8,128)(2,1)S(1)}, f32[8,8,128]{2,1,0:T(8,128)S(1)}, f32[3,8,128]{2,1,0:T(8,128)S(1)}, bf16[4,512,512]{2,1,0:T(8,128)(2,1)S(1)}) custom-call(s32[1]{0:T(128)} %bitcast.core_ref, bf16[4,512,512]{2,1,0:T(8,128)(2,1)} %volume.3, bf16[4,128]{1,0:T(4,128)(2,1)} %table_hbm.1, ...), custom_call_target="tpu_custom_call" | custom-call | tf_op jit(solution)/shard_map/prepare/pallas_call | solution.py:351
  3.3 7.5 %own.1 = (f32[4,256,512]{2,1,0:T(8,128)S(1)}, f32[4,256,512]{2,1,0:T(8,128)S(1)}, f32[4,256,512]{2,1,0:T(8,128)S(1)}, f32[2,256,512]{2,1,0:T(8,128)S(1)}, f32[2,...) custom-call(s32[1]{0:T(128)} %bitcast.core_ref, ...), custom_call_target="tpu_custom_call" | custom-call | tf_op jit(solution)/shard_map/own/pallas_call | solution.py:380
  10.9 0.0 collective-permute-done.1
  10.9 0.0 collective-permute-done
  10.9 2.9 %collective-permute-start.2 = (bf16[16,16,512]{2,1,0:T(8,128)(2,1)S(1)}, bf16[16,16,512]{2,1,0:T(8,128)(2,1)S(1)}, u32[]{:S(2)}, u32[]{:S(2)}) collective-permute-start(bf16[16,16,512]{2,1,0:T(8,128)(2,1)S(1)} %get-tuple-element.33.refs_0_), channel_id=1, source_target_pairs={{0,1},{1,0},{2,3},{3,2},{4,5},{5,4},{6,7},{7,6},{8,9},{9,8},{10,11... | collective-permute-start | bytes 786440 | tf_op jit(solution)/shard_map/ppermute | solution.py:402
  13.8 3.5 %collective-permute-start.3 = (bf16[8,8,512]{2,1,0:T(8,128)(2,1)S(1)}, bf16[8,8,512]{2,1,0:T(8,128)(2,1)S(1)}, u32[]{:S(2)}, u32[]{:S(2)}) collective-permute-start(bf16[8,8,512]{2,1,0:T(8,128)(2,1)S(1)} %get-tuple-element.34), channel_id=1, source_target_pairs={{0,32},{33,1},{2,34},{35,3},{4,36},{37,5},{6,38},{39,7},{8,40},{41... | collective-permute-start | bytes 196616 | tf_op jit(solution)/shard_map/ppermute | solution.py:403
  17.4 7.5 %other.1 = (f32[4,256,512]{2,1,0:T(8,128)S(1)}, f32[4,256,512]{2,1,0:T(8,128)S(1)}, f32[4,256,512]{2,1,0:T(8,128)S(1)}, f32[2,256,512]{2,1,0:T(8,128)S(1)}, f32[...) custom-call(s32[1]{0:T(128)} %bitcast.core_ref, ...), custom_call_target="tpu_custom_call" | custom-call | tf_op jit(solution)/shard_map/other/pallas_call | solution.py:380
  24.9 0.0 collective-permute-done.3.edges
  24.9 0.0 collective-permute-done.2.relayed
  24.9 2.6 %slab.1 = f32[16,64,512]{2,1,0:T(8,128)S(1)} custom-call(s32[1]{0:T(128)} %bitcast.core_ref, bf16[4,16,2,16,512]{4,3,2,1,0:T(8,128)(2,1)S(1)} %bitcast.6, bf16[4,16,2,16,512]{4,3,2,1,0:T(8,128)(2,1)S(1)} %bitcast.9, bf16[16,2,16,512]{3,2,1,0:T(8,128)(2,1)S(1)} %bitcast.11, bf16[16,16,512]{2,1,0:T(8,128)(2,1)S(1)} %collective-permute-done.2.relayed, ...), custom_call_target="tpu_custom_call" | custom-call | tf_op jit(solution)/shard_map/slab/pallas_call | solution.py:412
  27.5 0.3 convert_element_type.6
  27.8 23.2 %all_to_all.5 = f16[16,64,512]{2,1,0:T(8,128)(2,1)S(1)} all-to-all(f16[16,64,512]{2,1,0:T(8,128)(2,1)S(1)} %convert_element_type.6), channel_id=1, replica_groups={{0,2,4,6,8,10,12,14,16,18,20,22,24,26,28,30},{1,3,5,7,9,11,13,15,17,19,..., dimensions={0} | all-to-all | bytes 2097152 | tf_op jit(solution)/shard_map/all_to_all | solution.py:422
  51.0 0.3 convert_element_type.7.parts
  51.2 0.9 %merge.1 = f32[4,8192]{1,0:T(4,128)} custom-call(f32[16,64,512]{2,1,0:T(8,128)S(1)} %convert_element_type.7.parts, f32[3,8,128]{2,1,0:T(8,128)S(1)} %get-tuple-element.35.scales), custom_call_target="tpu_custom_call" | custom-call | tf_op jit(solution)/shard_map/merge/pallas_call | solution.py:426
  (1 shorter events, 0.0 us)
Async XLA Ops:
  0.0 10.9 %collective-permute-start = (bf16[4,512,512]{2,1,0:T(8,128)(2,1)}, bf16[4,512,512]{2,1,0:T(8,128)(2,1)S(1)}, u32[]{:S(2)}, u32[]{:S(2)}) collective-permute-start(bf16[4,512,512]{2,1,0:T(8,128)(2,1)} %volume.3), channel_id=1, source_target_pairs={{0,1},{1,0},{2,3},{3,2},{4,5},{5,4},{6,7},{7,6},{8,9},{9,8},{10,11... | collective-permute-start | bytes 6291464 | tf_op jit(solution)/shard_map/ppermute | solution.py:377
  1.1 9.8 %collective-permute-start.1 = (bf16[512,512]{1,0:T(8,128)(2,1)S(1)}, bf16[512,512]{1,0:T(8,128)(2,1)S(1)}, u32[]{:S(2)}, u32[]{:S(2)}) collective-permute-start(bf16[512,512]{1,0:T(8,128)(2,1)S(1)} %plane.1._), channel_id=1, source_target_pairs={{1,2},{3,4},{5,6},{7,8},{9,10},{11,12},{13,14},{15,16},{17,18},{19... | collective-permute-start | bytes 1572872 | tf_op jit(solution)/shard_map/ppermute | solution.py:372
  10.9 14.0 %collective-permute-start.2 = (bf16[16,16,512]{2,1,0:T(8,128)(2,1)S(1)}, bf16[16,16,512]{2,1,0:T(8,128)(2,1)S(1)}, u32[]{:S(2)}, u32[]{:S(2)}) collective-permute-start(bf16[16,16,512]{2,1,0:T(8,128)(2,1)S(1)} %get-tuple-element.33.refs_0_), channel_id=1, source_target_pairs={{0,1},{1,0},{2,3},{3,2},{4,5},{5,4},{6,7},{7,6},{8,9},{9,8},{10,11... | collective-permute-start | bytes 786440 | tf_op jit(solution)/shard_map/ppermute | solution.py:402
  13.8 11.1 %collective-permute-start.3 = (bf16[8,8,512]{2,1,0:T(8,128)(2,1)S(1)}, bf16[8,8,512]{2,1,0:T(8,128)(2,1)S(1)}, u32[]{:S(2)}, u32[]{:S(2)}) collective-permute-start(bf16[8,8,512]{2,1,0:T(8,128)(2,1)S(1)} %get-tuple-element.34), channel_id=1, source_target_pairs={{0,32},{33,1},{2,34},{35,3},{4,36},{37,5},{6,38},{39,7},{8,40},{41... | collective-permute-start | bytes 196616 | tf_op jit(solution)/shard_map/ppermute | solution.py:403
